TPU v7x, 512 devices: a whole 4x4x16 slice. The times are simulated.
512 devices in a mesh: row: 8 (over z_lo), col: 16 (over x, y), depth: 4 (over z_hi, core).
Axes of the slice: x: 4, y: 4, z: 16 (z_hi: 2, z_lo: 8; z = z_hi * 8 + z_lo), core: 2. Of those that a mesh axis runs over, the one named last changes fastest.
Arguments:
- tokens: bfloat16 [512, 12288], P(('col', 'depth'), 'row'), may hold values from -6 to 6
- cotangent: bfloat16 [512, 12288], P(('col', 'depth'), 'row'), may hold values from -0.375 to 0.375
- w_in: bfloat16 [12288, 24576], P('row', ('col', 'depth')), may hold values from -0.0546875 to 0.0546875
- b_in: float32 [24576], P('col'), may hold values from -4 to 4
- w_out: bfloat16 [24576, 12288], P('col', ('row', 'depth')), may hold values from -0.0390625 to 0.0390625
Outputs:
- input_grad: bfloat16 [512, 12288], P(('col', 'depth'), 'row')
- w_in_grad: bfloat16 [12288, 24576], P('row', ('col', 'depth'))
- b_in_grad: float32 [24576], P(('col', 'depth'))
- w_out_grad: bfloat16 [24576, 12288], P('col', ('row', 'depth'))
All inputs are finite; a program needn't handle non-finite values.
Results may differ from a plain program's by a relative error of at most 0.0065.
Values may be sent and summed in bfloat16 or wider, within the bound.
No kernel may reach another device: no remote copies, remote signals or barrier semaphores. Data moves between devices by JAX's collectives and lax.ppermute only.
A program may use at most 64 MiB of HBM per device.

v0:
```python
import jax
import jax.numpy as jnp
from jax import lax
from jax.sharding import PartitionSpec as P

coef = 0.7978845608


def gelu_pair(pre):
    inner = coef * (pre + 0.044715 * pre * pre * pre)
    tanh_v = jnp.tanh(inner)
    act = 0.5 * pre * (1.0 + tanh_v)
    slope = 0.5 * (1.0 + tanh_v) + 0.5 * pre * (1.0 - tanh_v * tanh_v) * coef * (
        1.0 + 0.134145 * pre * pre
    )
    return (act, slope)


def against(left, right):
    return lax.dot_general(
        left, right, (((1,), (1,)), ((), ())), preferred_element_type=jnp.float32
    )


def shards(tokens, cotangent, w_in, b_in, w_out):
    n_rows = lax.axis_size("row")
    n_cols = lax.axis_size("col")
    n_depth = lax.axis_size("depth")
    depth_at = lax.axis_index("depth")
    tok_dev = tokens.shape[0]
    feat_cols = tokens.shape[1]
    tile_hidden = b_in.shape[0]
    quarter_h = w_in.shape[1]
    quarter_d = w_out.shape[1]
    every_x, every_g = (
        lax.all_gather(tokens, ("col", "depth"), axis=0, tiled=True),
        lax.all_gather(cotangent, ("col", "depth"), axis=0, tiled=True),
    )

    def own_copy(whole):
        shaped = whole.reshape(n_cols, n_depth, tok_dev, feat_cols)
        picked = lax.dynamic_index_in_dim(shaped, depth_at, 1, keepdims=False)
        return picked.reshape(n_cols * tok_dev, feat_cols)

    copy_x = own_copy(every_x)
    copy_g = own_copy(every_g)
    tile_in, tile_out = (
        lax.all_gather(w_in, "depth", axis=1, tiled=True),
        lax.all_gather(w_out, "depth", axis=1, tiled=True),
    )
    pre_part = jnp.dot(copy_x, tile_in, preferred_element_type=jnp.float32)
    back_part = against(copy_g, tile_out)
    pre_rows, back_rows = (
        lax.psum_scatter(pre_part, "row", scatter_dimension=0, tiled=True),
        lax.psum_scatter(back_part, "row", scatter_dimension=0, tiled=True),
    )
    pre_rows = pre_rows + b_in
    act_f, slope = gelu_pair(pre_rows)
    act = act_f.astype(jnp.bfloat16)
    grad_pre = (back_rows * slope).astype(jnp.bfloat16)
    rows_here = pre_rows.shape[0]
    per_row = rows_here // tok_dev
    all_act, all_grad = (
        lax.all_gather(act, ("row", "depth"), axis=0, tiled=True),
        lax.all_gather(grad_pre, ("row", "depth"), axis=0, tiled=True),
    )
    grid_grad = all_grad.reshape(n_rows, n_depth, rows_here, tile_hidden)
    copy_grad = lax.dynamic_index_in_dim(grid_grad, depth_at, 1, keepdims=False).reshape(
        n_rows * rows_here, tile_hidden
    )
    quarter_grad = lax.dynamic_slice_in_dim(all_grad, depth_at * quarter_h, quarter_h, 1)
    tok_grid = every_x.reshape(n_rows, per_row, n_depth, tok_dev, feat_cols)
    grad_grid = quarter_grad.reshape(n_rows, n_depth, per_row, tok_dev, quarter_h)
    w_in_sum = jnp.einsum(
        "rcdtk,rdctn->kn", tok_grid, grad_grid, preferred_element_type=jnp.float32
    )
    quarter_g = lax.dynamic_slice_in_dim(every_g, depth_at * quarter_d, quarter_d, 1)
    cot_grid = quarter_g.reshape(n_rows, per_row, n_depth, tok_dev, quarter_d)
    act_grid = all_act.reshape(n_rows, n_depth, per_row, tok_dev, tile_hidden)
    w_out_sum = jnp.einsum(
        "rdctk,rcdtn->kn", act_grid, cot_grid, preferred_element_type=jnp.float32
    )
    b_in_grad = jnp.sum(quarter_grad.astype(jnp.float32), axis=0)
    input_part = against(copy_grad, tile_in)
    input_grad = lax.psum_scatter(input_part, "col", scatter_dimension=0, tiled=True).astype(
        jnp.bfloat16
    )
    return (input_grad, w_in_sum.astype(jnp.bfloat16), b_in_grad, w_out_sum.astype(jnp.bfloat16))


def solution(mesh):
    return jax.shard_map(
        shards,
        mesh=mesh,
        in_specs=(
            P(("col", "depth"), "row"),
            P(("col", "depth"), "row"),
            P("row", ("col", "depth")),
            P("col"),
            P("col", ("row", "depth")),
        ),
        out_specs=(
            P(("col", "depth"), "row"),
            P("row", ("col", "depth")),
            P(("col", "depth")),
            P("col", ("row", "depth")),
        ),
        check_vma=False,
    )
```

profile of v0, /device:TPU:1, one launch (start us, length us, event | category | flops | bytes accessed | tf_op | source)
XLA Modules:
  0.0 1060.4 jit_solution(3046231269290413314)
XLA Ops:
  7.2 0.0 all-gather.7.cloned.1.call-start
  7.2 0.7 all-gather.7.cloned.1.call-update
  7.9 0.0 all-gather.9.cloned.1.call-start
  7.9 0.7 all-gather.9.cloned.1.call-update
  8.6 0.0 all-gather.11.cloned.1.call-start
  8.7 0.7 all-gather.11.cloned.1.call-update
  9.4 0.0 all-gather.13.cloned.1.call-start
  9.4 0.5 all-gather.13.cloned.1.call-update
  10.0 0.0 reduce-scatter.3.cloned.1.call-start
  10.0 115.5 %all-gather.7.cloned.1.call-done = bf16[512,1536]{1,0:T(8,128)(2,1)} async-done(((bf16[8,1536]{1,0:T(8,128)(2,1)}), bf16[512,1536]{1,0:T(8,128)(2,1)}) %all-gather.7.cloned.1.call-update) | async-done | bytes 1572880 | tf_op jit(solution)/shard_map/all_gather | solution.py:37
  125.5 118.3 %all-gather.9.cloned.1.call-done = bf16[1536,1536]{1,0:T(8,128)(2,1)} async-done(((bf16[1536,384]{1,0:T(8,128)(2,1)}), bf16[1536,1536]{1,0:T(8,128)(2,1)}) %all-gather.9.cloned.1.call-update) | async-done | bytes 4718608 | tf_op jit(solution)/shard_map/all_gather | solution.py:49
  243.8 5.0 fusion.7
  248.8 0.0 reduce-scatter.3.cloned.1.call-update
  248.8 0.0 reduce-scatter.5.cloned.1.call-start
  248.9 104.8 %all-gather.11.cloned.1.call-done = bf16[512,1536]{1,0:T(8,128)(2,1)} async-done(((bf16[8,1536]{1,0:T(8,128)(2,1)}), bf16[512,1536]{1,0:T(8,128)(2,1)}) %all-gather.11.cloned.1.call-update) | async-done | bytes 1572880 | tf_op jit(solution)/shard_map/all_gather | solution.py:36
  353.6 118.2 %all-gather.13.cloned.1.call-done = bf16[1536,1536]{1,0:T(8,128)(2,1)} async-done(((bf16[1536,384]{1,0:T(8,128)(2,1)}), bf16[1536,1536]{1,0:T(8,128)(2,1)}) %all-gather.13.cloned.1.call-update) | async-done | bytes 4718608 | tf_op jit(solution)/shard_map/all_gather | solution.py:48
  471.8 0.0 copy-start.1
  471.8 4.1 fusion.5
  475.9 0.0 reduce-scatter.5.cloned.1.call-update
  475.9 0.0 all-gather.15.cloned.1.call-start
  476.0 57.5 %reduce-scatter.3.cloned.1.call-done = f32[16,1536]{1,0:T(8,128)} async-done(((f32[128,1536]{1,0:T(8,128)}), f32[16,1536]{1,0:T(8,128)}) %reduce-scatter.3.cloned.1.call-update) | async-done | bytes 98320 | tf_op jit(solution)/shard_map/reduce_scatter | solution.py:55
  533.5 62.9 %reduce-scatter.5.cloned.1.call-done = f32[16,1536]{1,0:T(8,128)} async-done(((f32[128,1536]{1,0:T(8,128)}), f32[16,1536]{1,0:T(8,128)}) %reduce-scatter.5.cloned.1.call-update) | async-done | bytes 98320 | tf_op jit(solution)/shard_map/reduce_scatter | solution.py:54
  596.5 0.0 copy-done.1
  596.5 1.6 multiply_convert_fusion
  598.1 0.0 all-gather.15.cloned.1.call-update
  598.1 0.0 all-gather.17.cloned.1.call-start
  598.2 1.3 dynamic-slice
  600.1 1.0 constant_dynamic-slice_fusion
  601.1 0.0 all-gather.17.cloned.1.call-update
  601.2 224.3 %all-gather.15.cloned.1.call-done = bf16[512,1536]{1,0:T(8,128)(2,1)} async-done(((bf16[16,1536]{1,0:T(8,128)(2,1)}), bf16[512,1536]{1,0:T(8,128)(2,1)}) %all-gather.15.cloned.1.call-update) | async-done | bytes 1572880 | tf_op jit(solution)/shard_map/all_gather | solution.py:65
  825.4 1.0 constant_dynamic-slice_fusion.2
  826.5 0.0 copy-start
  826.5 4.1 fusion.22
  830.6 1.7 convert_reduce_fusion
  832.3 0.0 copy-done
  832.3 0.8 fusion.2
  833.1 1.4 copy.20
  834.5 68.4 %all-reduce.2 = bf16[128,1536]{1,0:T(8,128)(2,1)S(1)} all-reduce(f32[128,1536]{1,0:T(8,128)S(1)} %fusion.22), channel_id=4, replica_groups=mesh['row'=8,'col'=16,'depth'=4] {'col'}, use_global_device_ids=true, to_apply=%region_2.3.clone | all-reduce | flops 196608 | bytes 1179648
  902.9 146.6 %all-gather.17.cloned.1.call-done = bf16[512,1536]{1,0:T(8,128)(2,1)} async-done(((bf16[16,1536]{1,0:T(8,128)(2,1)}), bf16[512,1536]{1,0:T(8,128)(2,1)}) %all-gather.17.cloned.1.call-update) | async-done | bytes 1572880 | tf_op jit(solution)/shard_map/all_gather | solution.py:64
  1049.5 3.5 fusion.1
  1052.9 0.6 dynamic-slice_convert_fusion
Async XLA Ops:
  7.2 118.4 %all-gather.7.cloned.1.call-start = ((), (), s32[]{:S(2)}) async-start(), calls=%async_computation.2 | async-start | bytes 1597440 | tf_op jit(solution)/shard_map/all_gather | solution.py:37
  7.9 235.9 %all-gather.9.cloned.1.call-start = ((), (), s32[]{:S(2)}) async-start(), calls=%async_computation.3 | async-start | bytes 5898240 | tf_op jit(solution)/shard_map/all_gather | solution.py:49
  8.6 345.0 %all-gather.11.cloned.1.call-start = ((), (), s32[]{:S(2)}) async-start(), calls=%async_computation.5 | async-start | bytes 1597440 | tf_op jit(solution)/shard_map/all_gather | solution.py:36
  9.4 462.4 %all-gather.13.cloned.1.call-start = ((), (), s32[]{:S(2)}) async-start(), calls=%async_computation.6 | async-start | bytes 5898240 | tf_op jit(solution)/shard_map/all_gather | solution.py:48
  10.0 523.6 %reduce-scatter.3.cloned.1.call-start = ((), (), s32[]{:S(2)}) async-start(), calls=%async_computation.4 | async-start | bytes 884736 | tf_op jit(solution)/shard_map/reduce_scatter | solution.py:55
  248.8 347.6 %reduce-scatter.5.cloned.1.call-start = ((), (), s32[]{:S(2)}) async-start(), calls=%async_computation.7 | async-start | bytes 884736 | tf_op jit(solution)/shard_map/reduce_scatter | solution.py:54
  471.8 124.7 %copy-start.1 = (f32[1536]{0:T(1024)S(1)}, f32[1536]{0:T(1024)}, u32[]{:S(2)}) copy-start(f32[1536]{0:T(1024)} %param.8) | copy-start | bytes 18436
  475.9 349.5 %all-gather.15.cloned.1.call-start = ((), (), s32[]{:S(2)}) async-start(), calls=%async_computation.8 | async-start | bytes 1622016 | tf_op jit(solution)/shard_map/all_gather | solution.py:65
  598.1 451.3 %all-gather.17.cloned.1.call-start = ((), (), s32[]{:S(2)}) async-start(), calls=%async_computation.9 | async-start | bytes 1622016 | tf_op jit(solution)/shard_map/all_gather | solution.py:64
  826.5 5.8 copy-start
Sparse Core Ops, SparseCore 0:
  12.4 113.1 all-gather.6
  127.6 116.1 all-gather.8
  248.2 105.3 all-gather.10
  355.6 116.1 all-gather.12
  475.0 58.4 reduce-scatter.2
  537.0 59.3 reduce-scatter.4
  599.1 226.2 all-gather.14
  828.1 221.3 all-gather.16
where the time goes:
time: 1060 us
  waiting for transfers between devices  951 us (90%)
  blocking collectives  68.4 us (6%)
  matrix products  17.5 us (2%)
  between operations  14.8 us (1%)
    all_gather x1, waiting for transfers between devices, shards(): lax.all_gather(grad_pre, ('row', 'depth'), axis=0, tiled=True)  224 us
    all_gather x1, waiting for transfers between devices, shards(): lax.all_gather(act, ('row', 'depth'), axis=0, tiled=True)  147 us
    all_gather x1, waiting for transfers between devices, shards(): lax.all_gather(w_out, 'depth', axis=1, tiled=True)  118 us
    all_gather x1, waiting for transfers between devices, shards(): lax.all_gather(w_in, 'depth', axis=1, tiled=True)  118 us
    all_gather x1, waiting for transfers between devices, shards(): lax.all_gather(cotangent, ('col', 'depth'), axis=0, tiled=True)  116 us
    all_gather x1, waiting for transfers between devices, shards(): lax.all_gather(tokens, ('col', 'depth'), axis=0, tiled=True)  105 us
    unnamed x1, blocking collectives  68.4 us
    reduce_scatter x1, waiting for transfers between devices, shards(): lax.psum_scatter(pre_part, 'row', scatter_dimension=0, tiled=True)  62.9 us
  transfers between devices with their start and end apart: 8, of which 8 were waited for; matrix products, arithmetic and copies ran while one was open for 2% of the time, Pallas kernels for 0%

commit v1 on v0

v1 whole, which is shorter than its diff:
```python
import jax
import jax.numpy as jnp
from jax import lax
from jax.sharding import Mesh, PartitionSpec as P

coef = 0.7978845608
bf16 = jnp.bfloat16
f32 = jnp.float32
SWAP = [(0, 1), (1, 0)]
GRID = ("x", "y")


def gelu_pair(pre):
    inner = coef * (pre + 0.044715 * pre * pre * pre)
    tanh_v = jnp.tanh(inner)
    act = 0.5 * pre * (1.0 + tanh_v)
    slope = 0.5 * (1.0 + tanh_v) + 0.5 * pre * (1.0 - tanh_v * tanh_v) * coef * (
        1.0 + 0.134145 * pre * pre
    )
    return (act, slope)


def dot(left, right):
    return jnp.dot(left, right, preferred_element_type=f32)


def against(left, right):
    return lax.dot_general(left, right, (((1,), (1,)), ((), ())), preferred_element_type=f32)


def over_rows(left, right):
    return lax.dot_general(left, right, (((0,), (0,)), ((), ())), preferred_element_type=f32)


def part_of(whole, at, size, dim):
    return lax.dynamic_slice_in_dim(whole, at * size, size, dim)


def swap(value, axis):
    return lax.ppermute(value, axis, SWAP)


def join(mine, other, axis, dim):
    first = lax.axis_index(axis) == 0
    return jnp.where(
        first,
        jnp.concatenate([mine, other], dim),
        jnp.concatenate([other, mine], dim),
    )


def widen(mine, axis, dim):
    return join(mine, swap(mine, axis), axis, dim)


def halve(part, axis, dim=0):
    size = part.shape[dim] // 2
    at = lax.axis_index(axis)
    out = part_of(part, 1 - at, size, dim).astype(bf16)
    return part_of(part, at, size, dim) + swap(out, axis).astype(f32)


def spread(rows):
    n = lax.axis_size("x") * lax.axis_size("y")
    sent = jnp.broadcast_to(rows[None], (n,) + rows.shape)
    got = lax.all_to_all(sent, GRID, 0, 0, tiled=True)
    return got.reshape(n * rows.shape[0], rows.shape[1])


def shards(tokens, cotangent, w_in, b_in, w_out):
    zh = lax.axis_index("zh")
    core = lax.axis_index("core")
    feat = tokens.shape[1]
    quarter = w_in.shape[1]
    half_h = 2 * quarter
    half_d = 2 * w_out.shape[1]

    in_pair = lax.all_gather(w_in, "core", axis=1, tiled=True)
    out_pair = lax.all_gather(w_out, "core", axis=1, tiled=True)

    sent = jnp.concatenate([tokens, part_of(cotangent, 1 - zh, half_d, 1)], 1)
    kept = jnp.concatenate([tokens, part_of(cotangent, zh, half_d, 1)], 1)
    both = join(kept, swap(sent, "zh"), "zh", 0)
    every_g = spread(both[:, feat:])
    every_x = spread(both[:, :feat])

    back = against(every_g, out_pair)
    pre = dot(every_x, in_pair)
    for axis in ("rl", "rm", "rh"):
        back = halve(back, axis)
        pre = halve(pre, axis)
    back = halve(back, "zh", 1)

    act_f, slope = gelu_pair(pre + part_of(b_in, zh, half_h, 0))
    act = act_f.astype(bf16)
    grad = (back * slope).astype(bf16)

    for axis in ("rh", "rm", "rl"):
        grad = widen(grad, axis, 0)

    part = against(grad, in_pair).astype(bf16)
    n = lax.axis_size("x") * lax.axis_size("y")
    got = lax.all_to_all(part.reshape(n, -1, feat), GRID, 0, 0, tiled=True)
    summed = jnp.sum(got.astype(f32), axis=0)
    input_grad = halve(summed, "zh").astype(bf16)

    pair_x = swap(every_x, "core")
    own_grad = part_of(grad, core, quarter, 1)
    pair_grad = swap(part_of(grad, 1 - core, quarter, 1), "core")
    w_in_grad = (over_rows(every_x, own_grad) + over_rows(pair_x, pair_grad)).astype(bf16)
    b_in_grad = jnp.sum(own_grad.astype(f32), 0) + jnp.sum(pair_grad.astype(f32), 0)

    act = widen(act, "zh", 1)
    for axis in ("rh", "rm", "rl"):
        act = widen(act, axis, 0)
    pair_act = swap(act, "core")
    own_g = part_of(every_g, core, w_out.shape[1], 1)
    pair_g = swap(part_of(every_g, 1 - core, w_out.shape[1], 1), "core")
    w_out_grad = (over_rows(act, own_g) + over_rows(pair_act, pair_g)).astype(bf16)
    return (input_grad, w_in_grad, b_in_grad, w_out_grad)


def solution(mesh):
    grid = Mesh(
        mesh.devices.reshape(2, 2, 2, 4, 4, 2, 2), ("rh", "rm", "rl", "x", "y", "zh", "core")
    )
    row, col, depth = ("rh", "rm", "rl"), ("x", "y"), ("zh", "core")
    return jax.shard_map(
        shards,
        mesh=grid,
        in_specs=(
            P(col + depth, row),
            P(col + depth, row),
            P(row, col + depth),
            P(col),
            P(col, row + depth),
        ),
        out_specs=(
            P(col + depth, row),
            P(row, col + depth),
            P(col + depth),
            P(col, row + depth),
        ),
        check_vma=False,
    )
```

time: 1060 us -> 225 us (0.21)
  waiting for transfers between devices: 951 us -> 82.8 us
  starting transfers between devices: 0.32 us -> 105 us
  blocking collectives: 68.4 us -> 0 us
    all_gather x6 -> x2, waiting for transfers between devices: 828 us -> 3.51 us  [the longest x1 3.49 us: shards(): out_pair = lax.all_gather(w_out, 'core', axis=1, tiled=True)]
    reduce_scatter x2 -> x0, waiting for transfers between devices: 120 us -> none  [the longest x1 62.9 us: shards(): lax.psum_scatter(pre_part, 'row', scatter_dimension=0, tiled=True)]
    ppermute x0 -> x20, starting transfers between devices: none -> 90.1 us  [swap(): return lax.ppermute(value, axis, SWAP)]
    unnamed x1 -> x0, blocking collectives: 68.4 us -> none
    ppermute x0 -> x20, waiting for transfers between devices: none -> 62.8 us  [swap(): return lax.ppermute(value, axis, SWAP)]
    all_to_all x0 -> x3, waiting for transfers between devices: none -> 15.1 us  [the longest x2 15.1 us: spread(): got = lax.all_to_all(sent, GRID, 0, 0, tiled=True)]
    all_to_all x0 -> x3, starting transfers between devices: none -> 14.4 us  [the longest x2 10.8 us: spread(): got = lax.all_to_all(sent, GRID, 0, 0, tiled=True)]
  transfers between devices with their start and end apart: 8 -> 25, of which waited for: 8 -> 13; matrix products, arithmetic and copies ran while one was open for 2% -> 8% of each run, Pallas kernels for 0% -> 0%
where the time goes in v1:
time: 225 us; the launch traced here: 223 us
  starting transfers between devices  105 us (47%)
  waiting for transfers between devices  82.8 us (37%)
  between operations  14.6 us (6%)
  matrix products  12 us (5%)
  other arithmetic  5.12 us (2%)
  local copies, waits for them, and re-layouts  4.2 us (2%)
    ppermute x20, starting transfers between devices, swap(): return lax.ppermute(value, axis, SWAP)  90.1 us
    ppermute x20, waiting for transfers between devices, swap(): return lax.ppermute(value, axis, SWAP)  62.8 us
    all_to_all x2, waiting for transfers between devices, spread(): got = lax.all_to_all(sent, GRID, 0, 0, tiled=True)  15.1 us
    all_to_all x2, starting transfers between devices, spread(): got = lax.all_to_all(sent, GRID, 0, 0, tiled=True)  10.8 us
    dot_general x4, matrix products, over_rows(): lax.dot_general(left, right, (((0,), (0,)), ((), ())), preferred_element_...  5.42 us
  transfers between devices with their start and end apart: 25, of which 13 were waited for; matrix products, arithmetic and copies ran while one was open for 8% of the time, Pallas kernels for 0%

profile of v1, /device:TPU:1, one launch (start us, length us, event | category | flops | bytes accessed | tf_op | source)
XLA Modules:
  0.0 223.3 jit_solution(4178569922878870104)
XLA Ops:
  7.2 0.0 all-gather.5.cloned.1.call-start
  7.2 0.7 all-gather.5.cloned.1.call-update
  7.9 0.0 all-gather.3.cloned.1.call-start
  8.0 0.7 all-gather.3.cloned.1.call-update
  8.7 16.3 %collective-permute-start = (bf16[8,2304]{1,0:T(8,128)(2,1)S(1)}, bf16[8,2304]{1,0:T(8,128)(2,1)S(1)}, u32[]{:S(2)}, u32[]{:S(2)}) collective-permute-start(bf16[8,2304]{1,0:T(8,128)(2,1)S(1)} %pad_maximum_fusion), channel_id=1, source_target_pairs={{0,2},{2,0},{1,3},{3,1},{4,6},{6,4},{5,7},{7,5},{8,10},{10,8},{9,1... | collective-permute-start | bytes 110600 | tf_op jit(solution)/shard_map/ppermute | solution.py:40
  25.0 1.5 collective-permute-done
  26.5 1.0 broadcast_in_dim.5
  27.5 6.8 %all-to-all-start.1 = ((bf16[16,16,1536]{2,1,0:T(8,128)(2,1)}), bf16[16,16,1536]{2,1,0:T(8,128)(2,1)S(1)}, u32[]{:S(2)}, u32[]{:S(2)}) async-start(bf16[16,16,1536]{2,1,0:T(8,128)(2,1)} %broadcast_in_dim.5), calls=%async_computation.1 | async-start | bytes 1572864 | tf_op jit(solution)/shard_map/all_to_all | solution.py:66
  34.3 12.5 %all-to-all-done.1 = bf16[16,16,1536]{2,1,0:T(8,128)(2,1)S(1)} async-done(((bf16[16,16,1536]{2,1,0:T(8,128)(2,1)}), bf16[16,16,1536]{2,1,0:T(8,128)(2,1)S(1)}, u32[]{:S(2)}, u32[]{:S(2)}) %all-to-all-start.1) | async-done | bytes 786464 | tf_op jit(solution)/shard_map/all_to_all | solution.py:66
  46.8 0.8 broadcast_in_dim.4
  47.5 4.0 %all-to-all-start = ((bf16[16,16,768]{2,1,0:T(8,128)(2,1)}), bf16[16,16,768]{2,1,0:T(8,128)(2,1)S(1)}, u32[]{:S(2)}, u32[]{:S(2)}) async-start(bf16[16,16,768]{2,1,0:T(8,128)(2,1)} %broadcast_in_dim.4), calls=%async_computation | async-start | bytes 786432 | tf_op jit(solution)/shard_map/all_to_all | solution.py:66
  51.6 2.4 %fusion.14 = f32[256,768]{1,0:T(8,128)S(1)} fusion(bf16[256,1536]{1,0:T(8,128)(2,1)S(1)} %bitcast.18, bf16[1536,768]{1,0:T(8,128)(2,1)} %all-gather.5.cloned.1.call-done), kind=kOutput, calls=%fused_computation.51 | convolution fusion | flops 603979776 | bytes 3932160 | tf_op jit(solution)/shard_map/dot_general | solution.py:24
  54.0 0.7 dynamic-slice_convert_fusion.1
  54.8 2.2 collective-permute-start.5
  57.0 2.6 %all-to-all-done = bf16[16,16,768]{2,1,0:T(8,128)(2,1)S(1)} async-done(((bf16[16,16,768]{2,1,0:T(8,128)(2,1)}), bf16[16,16,768]{2,1,0:T(8,128)(2,1)S(1)}, u32[]{:S(2)}, u32[]{:S(2)}) %all-to-all-start) | async-done | bytes 393248 | tf_op jit(solution)/shard_map/all_to_all | solution.py:66
  59.6 3.5 %all-gather.3.cloned.1.call-done = bf16[1536,768]{1,0:T(8,128)(2,1)} async-done(((bf16[1536,384]{1,0:T(8,128)(2,1)}), bf16[1536,768]{1,0:T(8,128)(2,1)}) %all-gather.3.cloned.1.call-update) | async-done | bytes 2359312 | tf_op jit(solution)/shard_map/all_gather | solution.py:79
  63.1 2.5 %fusion.13 = f32[256,1536]{1,0:T(8,128)S(1)} fusion(bf16[256,768]{1,0:T(8,128)(2,1)S(1)} %bitcast.15, bf16[1536,768]{1,0:T(8,128)(2,1)} %all-gather.3.cloned.1.call-done), kind=kOutput, calls=%fused_computation.50 | convolution fusion | flops 603979776 | bytes 4325376 | tf_op jit(solution)/shard_map/dot_general | solution.py:28
  65.5 0.8 dynamic-slice_convert_fusion
  66.3 2.2 collective-permute-start.1
  68.5 1.0 convert_add_fusion.1
  69.6 4.2 %collective-permute-start.6 = (bf16[64,768]{1,0:T(8,128)(2,1)S(1)}, bf16[64,768]{1,0:T(8,128)(2,1)S(1)}, u32[]{:S(2)}, u32[]{:S(2)}) collective-permute-start(bf16[64,768]{1,0:T(8,128)(2,1)S(1)} %dynamic-slice_convert_fusion.3), channel_id=1, source_target_pairs={{0,128},{128,0},{1,129},{129,1},{2,130},{130,2},{3,131},{131,3},{4... | collective-permute-start | bytes 294920 | tf_op jit(solution)/shard_map/ppermute | solution.py:40
  73.8 7.4 %collective-permute-done.1 = bf16[128,1536]{1,0:T(8,128)(2,1)} collective-permute-done((bf16[128,1536]{1,0:T(8,128)(2,1)}, bf16[128,1536]{1,0:T(8,128)(2,1)}, u32[]{:S(2)}, u32[]{:S(2)}) %collective-permute-start.1) | collective-permute-done | bytes 393248 | tf_op jit(solution)/shard_map/ppermute | solution.py:40
  81.2 1.1 convert_add_fusion
  82.3 2.3 %collective-permute-start.2 = (bf16[64,1536]{1,0:T(8,128)(2,1)S(1)}, bf16[64,1536]{1,0:T(8,128)(2,1)S(1)}, u32[]{:S(2)}, u32[]{:S(2)}) collective-permute-start(bf16[64,1536]{1,0:T(8,128)(2,1)S(1)} %dynamic-slice_convert_fusion.2), channel_id=1, source_target_pairs={{0,128},{128,0},{1,129},{129,1},{2,130},{130,2},{3,131},{131,3},{4... | collective-permute-start | bytes 589832 | tf_op jit(solution)/shard_map/ppermute | solution.py:40
  84.6 11.4 %collective-permute-done.2 = bf16[64,1536]{1,0:T(8,128)(2,1)S(1)} collective-permute-done((bf16[64,1536]{1,0:T(8,128)(2,1)S(1)}, bf16[64,1536]{1,0:T(8,128)(2,1)S(1)}, u32[]{:S(2)}, u32[]{:S(2)}) %collective-permute-start.2) | collective-permute-done | bytes 196640 | tf_op jit(solution)/shard_map/ppermute | solution.py:40
  96.1 5.7 %collective-permute-start.3 = (bf16[32,1536]{1,0:T(8,128)(2,1)S(1)}, bf16[32,1536]{1,0:T(8,128)(2,1)S(1)}, u32[]{:S(2)}, u32[]{:S(2)}) collective-permute-start(bf16[32,1536]{1,0:T(8,128)(2,1)S(1)} %dynamic-slice_convert_fusion.4), channel_id=1, source_target_pairs={{0,256},{256,0},{1,257},{257,1},{2,258},{258,2},{3,259},{259,3},{4... | collective-permute-start | bytes 294920 | tf_op jit(solution)/shard_map/ppermute | solution.py:40
  101.9 3.5 %collective-permute-start.7 = (bf16[32,768]{1,0:T(8,128)(2,1)S(1)}, bf16[32,768]{1,0:T(8,128)(2,1)S(1)}, u32[]{:S(2)}, u32[]{:S(2)}) collective-permute-start(bf16[32,768]{1,0:T(8,128)(2,1)S(1)} %dynamic-slice_convert_fusion.5), channel_id=1, source_target_pairs={{0,256},{256,0},{1,257},{257,1},{2,258},{258,2},{3,259},{259,3},{4... | collective-permute-start | bytes 147464 | tf_op jit(solution)/shard_map/ppermute | solution.py:40
  105.3 9.5 %collective-permute-done.3 = bf16[32,1536]{1,0:T(8,128)(2,1)S(1)} collective-permute-done((bf16[32,1536]{1,0:T(8,128)(2,1)S(1)}, bf16[32,1536]{1,0:T(8,128)(2,1)S(1)}, u32[]{:S(2)}, u32[]{:S(2)}) %collective-permute-start.3) | collective-permute-done | bytes 98336 | tf_op jit(solution)/shard_map/ppermute | solution.py:40
  114.9 8.2 %collective-permute-start.4 = (bf16[32,768]{1,0:T(8,128)(2,1)S(1)}, bf16[32,768]{1,0:T(8,128)(2,1)S(1)}, u32[]{:S(2)}, u32[]{:S(2)}) collective-permute-start(bf16[32,768]{1,0:T(8,128)(2,1)S(1)} %dynamic-slice_convert_fusion.6), channel_id=1, source_target_pairs={{0,2},{2,0},{1,3},{3,1},{4,6},{6,4},{5,7},{7,5},{8,10},{10,8},{9,1... | collective-permute-start | bytes 147464 | tf_op jit(solution)/shard_map/ppermute | solution.py:40
  123.2 0.1 dynamic_slice.85
  123.2 7.9 %collective-permute-done.4 = bf16[32,768]{1,0:T(8,128)(2,1)S(1)} collective-permute-done((bf16[32,768]{1,0:T(8,128)(2,1)S(1)}, bf16[32,768]{1,0:T(8,128)(2,1)S(1)}, u32[]{:S(2)}, u32[]{:S(2)}) %collective-permute-start.4) | collective-permute-done | bytes 49184 | tf_op jit(solution)/shard_map/ppermute | solution.py:40
  131.2 0.1 multiply_convert_fusion
  131.3 1.9 collective-permute-start.8
  133.2 0.7 constant_dynamic-slice_fusion
  133.9 2.4 %collective-permute-start.19 = (bf16[256,384]{1,0:T(8,128)(2,1)}, bf16[256,384]{1,0:T(8,128)(2,1)}, u32[]{:S(2)}, u32[]{:S(2)}) collective-permute-start(bf16[256,384]{1,0:T(8,128)(2,1)} %constant_dynamic-slice_fusion), channel_id=1, source_target_pairs={{0,1},{1,0},{2,3},{3,2},{4,5},{5,4},{6,7},{7,6},{8,9},{9,8},{10,11... | collective-permute-start | bytes 589832 | tf_op jit(solution)/shard_map/ppermute | solution.py:40
  136.3 1.9 collective-permute-start.12
  138.2 6.8 %collective-permute-start.14 = (bf16[32,768]{1,0:T(8,128)(2,1)S(1)}, bf16[32,768]{1,0:T(8,128)(2,1)S(1)}, u32[]{:S(2)}, u32[]{:S(2)}) collective-permute-start(bf16[32,768]{1,0:T(8,128)(2,1)S(1)} %get-tuple-element.4), channel_id=1, source_target_pairs={{0,2},{2,0},{1,3},{3,1},{4,6},{6,4},{5,7},{7,5},{8,10},{10,8},{9,1... | collective-permute-start | bytes 147464 | tf_op jit(solution)/shard_map/ppermute | solution.py:40
  145.1 1.9 collective-permute-start.9
  147.0 6.7 %collective-permute-done.14 = bf16[32,768]{1,0:T(8,128)(2,1)S(1)} collective-permute-done((bf16[32,768]{1,0:T(8,128)(2,1)S(1)}, bf16[32,768]{1,0:T(8,128)(2,1)S(1)}, u32[]{:S(2)}, u32[]{:S(2)}) %collective-permute-start.14) | collective-permute-done | bytes 49184 | tf_op jit(solution)/shard_map/ppermute | solution.py:40
  153.8 8.1 %collective-permute-start.15 = (bf16[32,1536]{1,0:T(8,128)(2,1)S(1)}, bf16[32,1536]{1,0:T(8,128)(2,1)S(1)}, u32[]{:S(2)}, u32[]{:S(2)}) collective-permute-start(bf16[32,1536]{1,0:T(8,128)(2,1)S(1)} %maximum_select_fusion.6), channel_id=1, source_target_pairs={{0,256},{256,0},{1,257},{257,1},{2,258},{258,2},{3,259},{259,3},{4... | collective-permute-start | bytes 294920 | tf_op jit(solution)/shard_map/ppermute | solution.py:40
  161.9 1.9 collective-permute-start.10
  163.8 2.7 %collective-permute-done.15 = bf16[32,1536]{1,0:T(8,128)(2,1)S(1)} collective-permute-done((bf16[32,1536]{1,0:T(8,128)(2,1)S(1)}, bf16[32,1536]{1,0:T(8,128)(2,1)S(1)}, u32[]{:S(2)}, u32[]{:S(2)}) %collective-permute-start.15) | collective-permute-done | bytes 98336 | tf_op jit(solution)/shard_map/ppermute | solution.py:40
  166.6 1.9 collective-permute-start.16
  168.5 2.6 %collective-permute-done.10 = bf16[128,768]{1,0:T(8,128)(2,1)S(1)} collective-permute-done((bf16[128,768]{1,0:T(8,128)(2,1)S(1)}, bf16[128,768]{1,0:T(8,128)(2,1)S(1)}, u32[]{:S(2)}, u32[]{:S(2)}) %collective-permute-start.10) | collective-permute-done | bytes 196640 | tf_op jit(solution)/shard_map/ppermute | solution.py:40
  171.1 0.1 maximum_select_fusion.1
  171.2 1.7 convolution_convert_fusion
  172.9 3.6 %all-to-all-start.2 = ((bf16[16,16,1536]{2,1,0:T(8,128)(2,1)}), bf16[16,16,1536]{2,1,0:T(8,128)(2,1)S(1)}, u32[]{:S(2)}, u32[]{:S(2)}) async-start(bf16[16,16,1536]{2,1,0:T(8,128)(2,1)} %bitcast.2), calls=%async_computation.2 | async-start | bytes 1572864 | tf_op jit(solution)/shard_map/all_to_all | solution.py:103
  176.5 6.1 %collective-permute-start.13 = (bf16[256,384]{1,0:T(8,128)(2,1)S(1)}, bf16[256,384]{1,0:T(8,128)(2,1)S(1)}, u32[]{:S(2)}, u32[]{:S(2)}) collective-permute-start(bf16[256,384]{1,0:T(8,128)(2,1)S(1)} %constant_dynamic-slice_fusion.1), channel_id=1, source_target_pairs={{0,1},{1,0},{2,3},{3,2},{4,5},{5,4},{6,7},{7,6},{8,9},{9,8},{10,11... | collective-permute-start | bytes 589832 | tf_op jit(solution)/shard_map/ppermute | solution.py:40
  182.6 1.1 maximum_select_fusion.2
  183.7 2.6 %collective-permute-start.17 = (bf16[128,1536]{1,0:T(8,128)(2,1)S(1)}, bf16[128,1536]{1,0:T(8,128)(2,1)S(1)}, u32[]{:S(2)}, u32[]{:S(2)}) collective-permute-start(bf16[128,1536]{1,0:T(8,128)(2,1)S(1)} %maximum_select_fusion.2), channel_id=1, source_target_pairs={{0,64},{64,0},{1,65},{65,1},{2,66},{66,2},{3,67},{67,3},{4,68},{68... | collective-permute-start | bytes 1179656 | tf_op jit(solution)/shard_map/ppermute | solution.py:40
  186.4 0.1 convert_reduce_fusion.2
  186.4 0.6 fusion.15
  187.0 1.6 fusion
  188.7 7.7 %collective-permute-done.17 = bf16[128,1536]{1,0:T(8,128)(2,1)S(1)} collective-permute-done((bf16[128,1536]{1,0:T(8,128)(2,1)S(1)}, bf16[128,1536]{1,0:T(8,128)(2,1)S(1)}, u32[]{:S(2)}, u32[]{:S(2)}) %collective-permute-start.17) | collective-permute-done | bytes 393248 | tf_op jit(solution)/shard_map/ppermute | solution.py:40
  196.4 0.2 maximum_select_fusion
  196.5 2.7 %collective-permute-start.18 = (bf16[256,1536]{1,0:T(8,128)(2,1)S(1)}, bf16[256,1536]{1,0:T(8,128)(2,1)S(1)}, u32[]{:S(2)}, u32[]{:S(2)}) collective-permute-start(bf16[256,1536]{1,0:T(8,128)(2,1)S(1)} %maximum_select_fusion), channel_id=1, source_target_pairs={{0,1},{1,0},{2,3},{3,2},{4,5},{5,4},{6,7},{7,6},{8,9},{9,8},{10,11... | collective-permute-start | bytes 2359304 | tf_op jit(solution)/shard_map/ppermute | solution.py:40
  199.2 0.1 convert_reduce_fusion
  199.4 7.3 %collective-permute-start.11 = (bf16[8,1536]{1,0:T(8,128)(2,1)S(1)}, bf16[8,1536]{1,0:T(8,128)(2,1)S(1)}, u32[]{:S(2)}, u32[]{:S(2)}) collective-permute-start(bf16[8,1536]{1,0:T(8,128)(2,1)S(1)} %dynamic-slice_convert_fusion.7), channel_id=1, source_target_pairs={{0,2},{2,0},{1,3},{3,1},{4,6},{6,4},{5,7},{7,5},{8,10},{10,8},{9,1... | collective-permute-start | bytes 73736 | tf_op jit(solution)/shard_map/ppermute | solution.py:40
  206.7 0.1 convert_reduce_fusion.1
  206.7 0.6 add.128
  207.3 5.3 %collective-permute-done.11 = bf16[8,1536]{1,0:T(8,128)(2,1)S(1)} collective-permute-done((bf16[8,1536]{1,0:T(8,128)(2,1)S(1)}, bf16[8,1536]{1,0:T(8,128)(2,1)S(1)}, u32[]{:S(2)}, u32[]{:S(2)}) %collective-permute-start.11) | collective-permute-done | bytes 24608 | tf_op jit(solution)/shard_map/ppermute | solution.py:40
  212.7 0.6 add_convert_fusion
  213.3 1.5 fusion.16
  214.8 1.7 fusion.1
  (39 shorter events, 0.5 us)
Async XLA Ops:
  7.2 1.5 copy-start.1
  7.2 1.5 copy-start
  7.2 44.4 %all-gather.5.cloned.1.call-start = ((), (), s32[]{:S(2)}) async-start(), calls=%async_computation.4 | async-start | bytes 3538944 | tf_op jit(solution)/shard_map/all_gather | solution.py:78
  7.9 55.2 %all-gather.3.cloned.1.call-start = ((), (), s32[]{:S(2)}) async-start(), calls=%async_computation.3 | async-start | bytes 3538944 | tf_op jit(solution)/shard_map/all_gather | solution.py:79
  8.7 17.8 %collective-permute-start = (bf16[8,2304]{1,0:T(8,128)(2,1)S(1)}, bf16[8,2304]{1,0:T(8,128)(2,1)S(1)}, u32[]{:S(2)}, u32[]{:S(2)}) collective-permute-start(bf16[8,2304]{1,0:T(8,128)(2,1)S(1)} %pad_maximum_fusion), channel_id=1, source_target_pairs={{0,2},{2,0},{1,3},{3,1},{4,6},{6,4},{5,7},{7,5},{8,10},{10,8},{9,1... | collective-permute-start | bytes 110600 | tf_op jit(solution)/shard_map/ppermute | solution.py:40
  27.5 19.3 %all-to-all-start.1 = ((bf16[16,16,1536]{2,1,0:T(8,128)(2,1)}), bf16[16,16,1536]{2,1,0:T(8,128)(2,1)S(1)}, u32[]{:S(2)}, u32[]{:S(2)}) async-start(bf16[16,16,1536]{2,1,0:T(8,128)(2,1)} %broadcast_in_dim.5), calls=%async_computation.1 | async-start | bytes 1572864 | tf_op jit(solution)/shard_map/all_to_all | solution.py:66
  47.5 12.1 %all-to-all-start = ((bf16[16,16,768]{2,1,0:T(8,128)(2,1)}), bf16[16,16,768]{2,1,0:T(8,128)(2,1)S(1)}, u32[]{:S(2)}, u32[]{:S(2)}) async-start(bf16[16,16,768]{2,1,0:T(8,128)(2,1)} %broadcast_in_dim.4), calls=%async_computation | async-start | bytes 786432 | tf_op jit(solution)/shard_map/all_to_all | solution.py:66
  54.8 13.8 %collective-permute-start.5 = (bf16[128,768]{1,0:T(8,128)(2,1)}, bf16[128,768]{1,0:T(8,128)(2,1)}, u32[]{:S(2)}, u32[]{:S(2)}) collective-permute-start(bf16[128,768]{1,0:T(8,128)(2,1)} %dynamic-slice_convert_fusion.1), channel_id=1, source_target_pairs={{0,64},{64,0},{1,65},{65,1},{2,66},{66,2},{3,67},{67,3},{4,68},{68... | collective-permute-start | bytes 589832 | tf_op jit(solution)/shard_map/ppermute | solution.py:40
  66.3 14.8 %collective-permute-start.1 = (bf16[128,1536]{1,0:T(8,128)(2,1)}, bf16[128,1536]{1,0:T(8,128)(2,1)}, u32[]{:S(2)}, u32[]{:S(2)}) collective-permute-start(bf16[128,1536]{1,0:T(8,128)(2,1)} %dynamic-slice_convert_fusion), channel_id=1, source_target_pairs={{0,64},{64,0},{1,65},{65,1},{2,66},{66,2},{3,67},{67,3},{4,68},{68... | collective-permute-start | bytes 1179656 | tf_op jit(solution)/shard_map/ppermute | solution.py:40
  69.5 53.6 %copy-start.2 = (f32[1536]{0:T(1024)S(1)}, f32[1536]{0:T(1024)}, u32[]{:S(2)}) copy-start(f32[1536]{0:T(1024)} %param.8) | copy-start | bytes 18436
  69.6 15.0 %collective-permute-start.6 = (bf16[64,768]{1,0:T(8,128)(2,1)S(1)}, bf16[64,768]{1,0:T(8,128)(2,1)S(1)}, u32[]{:S(2)}, u32[]{:S(2)}) collective-permute-start(bf16[64,768]{1,0:T(8,128)(2,1)S(1)} %dynamic-slice_convert_fusion.3), channel_id=1, source_target_pairs={{0,128},{128,0},{1,129},{129,1},{2,130},{130,2},{3,131},{131,3},{4... | collective-permute-start | bytes 294920 | tf_op jit(solution)/shard_map/ppermute | solution.py:40
  82.3 13.7 %collective-permute-start.2 = (bf16[64,1536]{1,0:T(8,128)(2,1)S(1)}, bf16[64,1536]{1,0:T(8,128)(2,1)S(1)}, u32[]{:S(2)}, u32[]{:S(2)}) collective-permute-start(bf16[64,1536]{1,0:T(8,128)(2,1)S(1)} %dynamic-slice_convert_fusion.2), channel_id=1, source_target_pairs={{0,128},{128,0},{1,129},{129,1},{2,130},{130,2},{3,131},{131,3},{4... | collective-permute-start | bytes 589832 | tf_op jit(solution)/shard_map/ppermute | solution.py:40
  96.1 18.8 %collective-permute-start.3 = (bf16[32,1536]{1,0:T(8,128)(2,1)S(1)}, bf16[32,1536]{1,0:T(8,128)(2,1)S(1)}, u32[]{:S(2)}, u32[]{:S(2)}) collective-permute-start(bf16[32,1536]{1,0:T(8,128)(2,1)S(1)} %dynamic-slice_convert_fusion.4), channel_id=1, source_target_pairs={{0,256},{256,0},{1,257},{257,1},{2,258},{258,2},{3,259},{259,3},{4... | collective-permute-start | bytes 294920 | tf_op jit(solution)/shard_map/ppermute | solution.py:40
  101.9 21.4 %collective-permute-start.7 = (bf16[32,768]{1,0:T(8,128)(2,1)S(1)}, bf16[32,768]{1,0:T(8,128)(2,1)S(1)}, u32[]{:S(2)}, u32[]{:S(2)}) collective-permute-start(bf16[32,768]{1,0:T(8,128)(2,1)S(1)} %dynamic-slice_convert_fusion.5), channel_id=1, source_target_pairs={{0,256},{256,0},{1,257},{257,1},{2,258},{258,2},{3,259},{259,3},{4... | collective-permute-start | bytes 147464 | tf_op jit(solution)/shard_map/ppermute | solution.py:40
  114.9 16.3 %collective-permute-start.4 = (bf16[32,768]{1,0:T(8,128)(2,1)S(1)}, bf16[32,768]{1,0:T(8,128)(2,1)S(1)}, u32[]{:S(2)}, u32[]{:S(2)}) collective-permute-start(bf16[32,768]{1,0:T(8,128)(2,1)S(1)} %dynamic-slice_convert_fusion.6), channel_id=1, source_target_pairs={{0,2},{2,0},{1,3},{3,1},{4,6},{6,4},{5,7},{7,5},{8,10},{10,8},{9,1... | collective-permute-start | bytes 147464 | tf_op jit(solution)/shard_map/ppermute | solution.py:40
  123.2 47.9 %copy-start.3 = (bf16[1536,768]{1,0:T(8,128)(2,1)S(1)}, bf16[1536,768]{1,0:T(8,128)(2,1)}, u32[]{:S(2)}) copy-start(bf16[1536,768]{1,0:T(8,128)(2,1)} %all-gather.5.cloned.1.call-done) | copy-start | bytes 7077892
  131.3 13.8 %collective-permute-start.8 = (bf16[32,768]{1,0:T(8,128)(2,1)S(1)}, bf16[32,768]{1,0:T(8,128)(2,1)S(1)}, u32[]{:S(2)}, u32[]{:S(2)}) collective-permute-start(bf16[32,768]{1,0:T(8,128)(2,1)S(1)} %get-tuple-element.5), channel_id=1, source_target_pairs={{0,256},{256,0},{1,257},{257,1},{2,258},{258,2},{3,259},{259,3},{4... | collective-permute-start | bytes 147464 | tf_op jit(solution)/shard_map/ppermute | solution.py:40
  133.9 79.4 %collective-permute-start.19 = (bf16[256,384]{1,0:T(8,128)(2,1)}, bf16[256,384]{1,0:T(8,128)(2,1)}, u32[]{:S(2)}, u32[]{:S(2)}) collective-permute-start(bf16[256,384]{1,0:T(8,128)(2,1)} %constant_dynamic-slice_fusion), channel_id=1, source_target_pairs={{0,1},{1,0},{2,3},{3,2},{4,5},{5,4},{6,7},{7,6},{8,9},{9,8},{10,11... | collective-permute-start | bytes 589832 | tf_op jit(solution)/shard_map/ppermute | solution.py:40
  136.3 50.1 %collective-permute-start.12 = (bf16[256,1536]{1,0:T(8,128)(2,1)S(1)}, bf16[256,1536]{1,0:T(8,128)(2,1)S(1)}, u32[]{:S(2)}, u32[]{:S(2)}) collective-permute-start(bf16[256,1536]{1,0:T(8,128)(2,1)S(1)} %bitcast.19), channel_id=1, source_target_pairs={{0,1},{1,0},{2,3},{3,2},{4,5},{5,4},{6,7},{7,6},{8,9},{9,8},{10,11... | collective-permute-start | bytes 2359304 | tf_op jit(solution)/shard_map/ppermute | solution.py:40
  138.2 15.5 %collective-permute-start.14 = (bf16[32,768]{1,0:T(8,128)(2,1)S(1)}, bf16[32,768]{1,0:T(8,128)(2,1)S(1)}, u32[]{:S(2)}, u32[]{:S(2)}) collective-permute-start(bf16[32,768]{1,0:T(8,128)(2,1)S(1)} %get-tuple-element.4), channel_id=1, source_target_pairs={{0,2},{2,0},{1,3},{3,1},{4,6},{6,4},{5,7},{7,5},{8,10},{10,8},{9,1... | collective-permute-start | bytes 147464 | tf_op jit(solution)/shard_map/ppermute | solution.py:40
  145.1 16.8 %collective-permute-start.9 = (bf16[64,768]{1,0:T(8,128)(2,1)S(1)}, bf16[64,768]{1,0:T(8,128)(2,1)S(1)}, u32[]{:S(2)}, u32[]{:S(2)}) collective-permute-start(bf16[64,768]{1,0:T(8,128)(2,1)S(1)} %maximum_select_fusion.5), channel_id=1, source_target_pairs={{0,128},{128,0},{1,129},{129,1},{2,130},{130,2},{3,131},{131,3},{4... | collective-permute-start | bytes 294920 | tf_op jit(solution)/shard_map/ppermute | solution.py:40
  153.8 12.8 %collective-permute-start.15 = (bf16[32,1536]{1,0:T(8,128)(2,1)S(1)}, bf16[32,1536]{1,0:T(8,128)(2,1)S(1)}, u32[]{:S(2)}, u32[]{:S(2)}) collective-permute-start(bf16[32,1536]{1,0:T(8,128)(2,1)S(1)} %maximum_select_fusion.6), channel_id=1, source_target_pairs={{0,256},{256,0},{1,257},{257,1},{2,258},{258,2},{3,259},{259,3},{4... | collective-permute-start | bytes 294920 | tf_op jit(solution)/shard_map/ppermute | solution.py:40
  161.9 9.2 %collective-permute-start.10 = (bf16[128,768]{1,0:T(8,128)(2,1)S(1)}, bf16[128,768]{1,0:T(8,128)(2,1)S(1)}, u32[]{:S(2)}, u32[]{:S(2)}) collective-permute-start(bf16[128,768]{1,0:T(8,128)(2,1)S(1)} %maximum_select_fusion.3), channel_id=1, source_target_pairs={{0,64},{64,0},{1,65},{65,1},{2,66},{66,2},{3,67},{67,3},{4,68},{68... | collective-permute-start | bytes 589832 | tf_op jit(solution)/shard_map/ppermute | solution.py:40
  166.6 16.1 %collective-permute-start.16 = (bf16[64,1536]{1,0:T(8,128)(2,1)S(1)}, bf16[64,1536]{1,0:T(8,128)(2,1)}, u32[]{:S(2)}, u32[]{:S(2)}) collective-permute-start(bf16[64,1536]{1,0:T(8,128)(2,1)S(1)} %maximum_select_fusion.4), channel_id=1, source_target_pairs={{0,128},{128,0},{1,129},{129,1},{2,130},{130,2},{3,131},{131,3},{4... | collective-permute-start | bytes 589832 | tf_op jit(solution)/shard_map/ppermute | solution.py:40
  172.9 26.4 %all-to-all-start.2 = ((bf16[16,16,1536]{2,1,0:T(8,128)(2,1)}), bf16[16,16,1536]{2,1,0:T(8,128)(2,1)S(1)}, u32[]{:S(2)}, u32[]{:S(2)}) async-start(bf16[16,16,1536]{2,1,0:T(8,128)(2,1)} %bitcast.2), calls=%async_computation.2 | async-start | bytes 1572864 | tf_op jit(solution)/shard_map/all_to_all | solution.py:103
  176.5 9.9 %collective-permute-start.13 = (bf16[256,384]{1,0:T(8,128)(2,1)S(1)}, bf16[256,384]{1,0:T(8,128)(2,1)S(1)}, u32[]{:S(2)}, u32[]{:S(2)}) collective-permute-start(bf16[256,384]{1,0:T(8,128)(2,1)S(1)} %constant_dynamic-slice_fusion.1), channel_id=1, source_target_pairs={{0,1},{1,0},{2,3},{3,2},{4,5},{5,4},{6,7},{7,6},{8,9},{9,8},{10,11... | collective-permute-start | bytes 589832 | tf_op jit(solution)/shard_map/ppermute | solution.py:40
  183.7 12.6 %collective-permute-start.17 = (bf16[128,1536]{1,0:T(8,128)(2,1)S(1)}, bf16[128,1536]{1,0:T(8,128)(2,1)S(1)}, u32[]{:S(2)}, u32[]{:S(2)}) collective-permute-start(bf16[128,1536]{1,0:T(8,128)(2,1)S(1)} %maximum_select_fusion.2), channel_id=1, source_target_pairs={{0,64},{64,0},{1,65},{65,1},{2,66},{66,2},{3,67},{67,3},{4,68},{68... | collective-permute-start | bytes 1179656 | tf_op jit(solution)/shard_map/ppermute | solution.py:40
  196.5 16.8 %collective-permute-start.18 = (bf16[256,1536]{1,0:T(8,128)(2,1)S(1)}, bf16[256,1536]{1,0:T(8,128)(2,1)S(1)}, u32[]{:S(2)}, u32[]{:S(2)}) collective-permute-start(bf16[256,1536]{1,0:T(8,128)(2,1)S(1)} %maximum_select_fusion), channel_id=1, source_target_pairs={{0,1},{1,0},{2,3},{3,2},{4,5},{5,4},{6,7},{7,6},{8,9},{9,8},{10,11... | collective-permute-start | bytes 2359304 | tf_op jit(solution)/shard_map/ppermute | solution.py:40
  199.4 13.3 %collective-permute-start.11 = (bf16[8,1536]{1,0:T(8,128)(2,1)S(1)}, bf16[8,1536]{1,0:T(8,128)(2,1)S(1)}, u32[]{:S(2)}, u32[]{:S(2)}) collective-permute-start(bf16[8,1536]{1,0:T(8,128)(2,1)S(1)} %dynamic-slice_convert_fusion.7), channel_id=1, source_target_pairs={{0,2},{2,0},{1,3},{3,1},{4,6},{6,4},{5,7},{7,5},{8,10},{10,8},{9,1... | collective-permute-start | bytes 73736 | tf_op jit(solution)/shard_map/ppermute | solution.py:40
Sparse Core Ops, SparseCore 0:
  10.1 28.1 all-gather.4
  40.3 22.6 all-gather.2

commit v2 on v1

--- a/solution.py
+++ b/solution.py
@@ -8,6 +8,7 @@
 f32 = jnp.float32
 SWAP = [(0, 1), (1, 0)]
 GRID = ("x", "y")
+ROW4 = ("rm", "rl")
 
 
 def gelu_pair(pre):
@@ -53,69 +54,93 @@
     return join(mine, swap(mine, axis), axis, dim)
 
 
-def halve(part, axis, dim=0):
+def cut(part, axis, dim=0):
     size = part.shape[dim] // 2
     at = lax.axis_index(axis)
-    out = part_of(part, 1 - at, size, dim).astype(bf16)
-    return part_of(part, at, size, dim) + swap(out, axis).astype(f32)
+    return part_of(part, at, size, dim), part_of(part, 1 - at, size, dim).astype(bf16)
 
 
-def spread(rows):
-    n = lax.axis_size("x") * lax.axis_size("y")
+def halve(part, axis, dim=0):
+    kept, sent = cut(part, axis, dim)
+    return kept + swap(sent, axis).astype(f32)
+
+
+def spread(rows, axes):
+    n = lax.axis_size(axes)
     sent = jnp.broadcast_to(rows[None], (n,) + rows.shape)
-    got = lax.all_to_all(sent, GRID, 0, 0, tiled=True)
+    got = lax.all_to_all(sent, axes, 0, 0, tiled=True)
     return got.reshape(n * rows.shape[0], rows.shape[1])
+
+
+def deal(part, axes):
+    n = lax.axis_size(axes)
+    return lax.all_to_all(part.reshape(n, -1, part.shape[1]), axes, 0, 0, tiled=True)
+
+
+def total(parts):
+    return jnp.sum(parts.astype(f32), axis=0)
+
+
+def flip(value, axis):
+    size = value.shape[1] // 2
+    other = jnp.concatenate([value[:, size:], value[:, :size]], 1)
+    return jnp.where(lax.axis_index(axis) == 0, value, other)
 
 
 def shards(tokens, cotangent, w_in, b_in, w_out):
     zh = lax.axis_index("zh")
-    core = lax.axis_index("core")
     feat = tokens.shape[1]
     quarter = w_in.shape[1]
     half_h = 2 * quarter
-    half_d = 2 * w_out.shape[1]
-
-    in_pair = lax.all_gather(w_in, "core", axis=1, tiled=True)
-    out_pair = lax.all_gather(w_out, "core", axis=1, tiled=True)
+    quarter_d = w_out.shape[1]
+    half_d = 2 * quarter_d
 
     sent = jnp.concatenate([tokens, part_of(cotangent, 1 - zh, half_d, 1)], 1)
     kept = jnp.concatenate([tokens, part_of(cotangent, zh, half_d, 1)], 1)
-    both = join(kept, swap(sent, "zh"), "zh", 0)
-    every_g = spread(both[:, feat:])
-    every_x = spread(both[:, :feat])
+    got = swap(sent, "zh")
+    w_out, w_in, got = lax.optimization_barrier((w_out, w_in, got))
+    pair_out = swap(w_out, "core")
+    pair_in = swap(w_in, "core")
+    both = join(kept, got, "zh", 0)
 
-    back = against(every_g, out_pair)
-    pre = dot(every_x, in_pair)
-    for axis in ("rl", "rm", "rh"):
-        back = halve(back, axis)
-        pre = halve(pre, axis)
+    every_g = spread(flip(both[:, feat:], "core"), GRID)
+    own_g, other_g = every_g[:, :quarter_d], every_g[:, quarter_d:]
+    back = against(own_g, w_out) + against(other_g, pair_out)
+    back = back.reshape(2, 2, -1, back.shape[1])
+    back_kept, back_sent = cut(back, "rl", 1)
+    back_sent, x_rows = lax.optimization_barrier((back_sent, both[:, :feat]))
+    back_got = swap(back_sent, "rl")
+    every_x = spread(x_rows, GRID)
+    back_kept, back_sent = cut(back_kept + back_got.astype(f32), "rm", 0)
+    back_sent, every_x = lax.optimization_barrier((back_sent, every_x))
+    back_got = swap(back_sent, "rm")
+    pre = jnp.concatenate([dot(every_x, w_in), dot(every_x, pair_in)], 1).astype(bf16)
+    pre_parts = deal(pre, ROW4)
+    back_kept, back_sent = cut((back_kept + back_got.astype(f32))[0, 0], "rh", 0)
+    back_sent, pre_parts = lax.optimization_barrier((back_sent, pre_parts))
+    back = back_kept + swap(back_sent, "rh").astype(f32)
+    pre = halve(total(pre_parts), "rh")
     back = halve(back, "zh", 1)
 
-    act_f, slope = gelu_pair(pre + part_of(b_in, zh, half_h, 0))
+    act_f, slope = gelu_pair(flip(pre, "core") + part_of(b_in, zh, half_h, 0))
     act = act_f.astype(bf16)
-    grad = (back * slope).astype(bf16)
+    grad = flip((back * slope).astype(bf16), "core")
 
-    for axis in ("rh", "rm", "rl"):
-        grad = widen(grad, axis, 0)
-
-    part = against(grad, in_pair).astype(bf16)
-    n = lax.axis_size("x") * lax.axis_size("y")
-    got = lax.all_to_all(part.reshape(n, -1, feat), GRID, 0, 0, tiled=True)
-    summed = jnp.sum(got.astype(f32), axis=0)
-    input_grad = halve(summed, "zh").astype(bf16)
+    grad = spread(widen(grad, "rh", 0), ROW4)
+    own_grad, other_grad = grad[:, :quarter], grad[:, quarter:]
+    part = (against(own_grad, w_in) + against(other_grad, pair_in)).astype(bf16)
+    act = widen(widen(act, "zh", 1), "rh", 0)[None, None]
+    part, act = lax.optimization_barrier((part, act))
+    input_grad = halve(total(deal(part, GRID)), "zh").astype(bf16)
+    act = widen(widen(act, "rm", 0), "rl", 1).reshape(-1, act.shape[-1])
 
     pair_x = swap(every_x, "core")
-    own_grad = part_of(grad, core, quarter, 1)
-    pair_grad = swap(part_of(grad, 1 - core, quarter, 1), "core")
+    pair_grad = swap(other_grad, "core")
     w_in_grad = (over_rows(every_x, own_grad) + over_rows(pair_x, pair_grad)).astype(bf16)
     b_in_grad = jnp.sum(own_grad.astype(f32), 0) + jnp.sum(pair_grad.astype(f32), 0)
 
-    act = widen(act, "zh", 1)
-    for axis in ("rh", "rm", "rl"):
-        act = widen(act, axis, 0)
     pair_act = swap(act, "core")
-    own_g = part_of(every_g, core, w_out.shape[1], 1)
-    pair_g = swap(part_of(every_g, 1 - core, w_out.shape[1], 1), "core")
+    pair_g = swap(other_g, "core")
     w_out_grad = (over_rows(act, own_g) + over_rows(pair_act, pair_g)).astype(bf16)
     return (input_grad, w_in_grad, b_in_grad, w_out_grad)
 

time: 225 us -> 236 us (1.049)
  starting transfers between devices: 105 us -> 123 us
  between operations: 14.6 us -> 1.15 us
  matrix products: 12 us -> 16.2 us
    ppermute x20 -> x18, starting transfers between devices: 90.1 us -> 102 us  [swap(): return lax.ppermute(value, axis, SWAP)]
    all_to_all x3 -> x5, waiting for transfers between devices: 15.1 us -> 21.8 us  [the longest x3 21.8 us: spread(): got = lax.all_to_all(sent, axes, 0, 0, tiled=True)]
    all_to_all x3 -> x5, starting transfers between devices: 14.4 us -> 20.5 us  [the longest x3 11.6 us: spread(): got = lax.all_to_all(sent, axes, 0, 0, tiled=True)]
    all_gather x2 -> x0, waiting for transfers between devices: 3.51 us -> none  [the longest x1 3.49 us: shards(): out_pair = lax.all_gather(w_out, 'core', axis=1, tiled=True)]
    dot_general x2 -> x4, matrix products: 4.16 us -> 5.84 us  [against(): lax.dot_general(left, right, (((1,), (1,)), ((), ())), preferred_element_...]
    ppermute x20 -> x18, waiting for transfers between devices: 62.8 us -> 62.2 us  [swap(): return lax.ppermute(value, axis, SWAP)]
  transfers between devices with their start and end apart: 25 -> 23, of which waited for: 13 -> 12; matrix products, arithmetic and copies ran while one was open for 8% -> 7% of each run, Pallas kernels for 0% -> 0%
where the time goes in v2:
time: 236 us; the launch traced here: 235 us
  starting transfers between devices  123 us (52%)
  waiting for transfers between devices  84 us (36%)
  matrix products  16.2 us (7%)
  other arithmetic  5.31 us (2%)
  local copies, waits for them, and re-layouts  4.88 us (2%)
    ppermute x18, starting transfers between devices, swap(): return lax.ppermute(value, axis, SWAP)  102 us
    ppermute x18, waiting for transfers between devices, swap(): return lax.ppermute(value, axis, SWAP)  62.2 us
    all_to_all x3, waiting for transfers between devices, spread(): got = lax.all_to_all(sent, axes, 0, 0, tiled=True)  21.8 us
    all_to_all x3, starting transfers between devices, spread(): got = lax.all_to_all(sent, axes, 0, 0, tiled=True)  11.6 us
    all_to_all x2, starting transfers between devices, deal(): lax.all_to_all(part.reshape(n, -1, part.shape[1]), axes, 0, 0, tiled=True)  8.92 us
    dot_general x4, matrix products, over_rows(): lax.dot_general(left, right, (((0,), (0,)), ((), ())), preferred_element_...  6.73 us
    dot_general x4, matrix products, against(): lax.dot_general(left, right, (((1,), (1,)), ((), ())), preferred_element_...  5.84 us
  transfers between devices with their start and end apart: 23, of which 12 were waited for; matrix products, arithmetic and copies ran while one was open for 7% of the time, Pallas kernels for 0%

profile of v2, /device:TPU:1, one launch (start us, length us, event | category | flops | bytes accessed | tf_op | source)
XLA Modules:
  0.0 234.5 jit_solution(4931336686645910829)
XLA Ops:
  0.6 0.7 constant_dynamic-slice_fusion.1
  1.4 0.7 pad_maximum_fusion.1
  2.1 16.3 %collective-permute-start = (bf16[8,2304]{1,0:T(8,128)(2,1)S(1)}, bf16[8,2304]{1,0:T(8,128)(2,1)S(1)}, u32[]{:S(2)}, u32[]{:S(2)}) collective-permute-start(bf16[8,2304]{1,0:T(8,128)(2,1)S(1)} %pad_maximum_fusion.1), channel_id=1, source_target_pairs={{0,2},{2,0},{1,3},{3,1},{4,6},{6,4},{5,7},{7,5},{8,10},{10,8},{9,1... | collective-permute-start | bytes 110600 | tf_op jit(solution)/shard_map/ppermute | solution.py:41
  18.4 1.5 collective-permute-done
  19.9 5.6 %collective-permute-start.1 = (bf16[1536,384]{1,0:T(8,128)(2,1)}, bf16[1536,384]{1,0:T(8,128)(2,1)S(1)}, u32[]{:S(2)}, u32[]{:S(2)}) collective-permute-start(bf16[1536,384]{1,0:T(8,128)(2,1)} %param.9), channel_id=1, source_target_pairs={{0,1},{1,0},{2,3},{3,2},{4,5},{5,4},{6,7},{7,6},{8,9},{9,8},{10,11... | collective-permute-start | bytes 3538952 | tf_op jit(solution)/shard_map/ppermute | solution.py:41
  25.5 0.8 maximum_select_fusion.6
  26.3 0.8 broadcast_in_dim.6
  27.1 4.5 %all-to-all-start = ((bf16[16,16,768]{2,1,0:T(8,128)(2,1)}), bf16[16,16,768]{2,1,0:T(8,128)(2,1)S(1)}, u32[]{:S(2)}, u32[]{:S(2)}) async-start(bf16[16,16,768]{2,1,0:T(8,128)(2,1)} %broadcast_in_dim.6), calls=%async_computation | async-start | bytes 786432 | tf_op jit(solution)/shard_map/all_to_all | solution.py:71
  31.6 9.1 %all-to-all-done = bf16[16,16,768]{2,1,0:T(8,128)(2,1)S(1)} async-done(((bf16[16,16,768]{2,1,0:T(8,128)(2,1)}), bf16[16,16,768]{2,1,0:T(8,128)(2,1)S(1)}, u32[]{:S(2)}, u32[]{:S(2)}) %all-to-all-start) | async-done | bytes 393248 | tf_op jit(solution)/shard_map/all_to_all | solution.py:71
  40.7 0.6 fusion.19
  41.3 0.7 copy-done
  42.0 0.6 convolution_add_fusion.3
  42.7 3.1 %collective-permute-start.2 = (bf16[2,1,64,1536]{3,2,1,0:T(8,128)(2,1)S(1)}, bf16[2,1,64,1536]{3,2,1,0:T(8,128)(2,1)}, u32[]{:S(2)}, u32[]{:S(2)}) collective-permute-start(bf16[2,1,64,1536]{3,2,1,0:T(8,128)(2,1)S(1)} %dynamic-slice_convert_fusion), channel_id=1, source_target_pairs={{0,64},{64,0},{1,65},{65,1},{2,66},{66,2},{3,67},{67,3},{4,68},{68... | collective-permute-start | bytes 1179656 | tf_op jit(solution)/shard_map/ppermute | solution.py:41
  45.8 3.9 %collective-permute-start.4 = (bf16[1536,384]{1,0:T(8,128)(2,1)}, bf16[1536,384]{1,0:T(8,128)(2,1)}, u32[]{:S(2)}, u32[]{:S(2)}) collective-permute-start(bf16[1536,384]{1,0:T(8,128)(2,1)} %param.7), channel_id=1, source_target_pairs={{0,1},{1,0},{2,3},{3,2},{4,5},{5,4},{6,7},{7,6},{8,9},{9,8},{10,11... | collective-permute-start | bytes 3538952 | tf_op jit(solution)/shard_map/ppermute | solution.py:41
  49.7 1.0 broadcast_in_dim.7
  50.6 3.6 %all-to-all-start.1 = ((bf16[16,16,1536]{2,1,0:T(8,128)(2,1)}), bf16[16,16,1536]{2,1,0:T(8,128)(2,1)S(1)}, u32[]{:S(2)}, u32[]{:S(2)}) async-start(bf16[16,16,1536]{2,1,0:T(8,128)(2,1)} %broadcast_in_dim.7), calls=%async_computation.1 | async-start | bytes 1572864 | tf_op jit(solution)/shard_map/all_to_all | solution.py:71
  54.3 1.1 convert_add_fusion
  55.4 12.7 %all-to-all-done.1 = bf16[16,16,1536]{2,1,0:T(8,128)(2,1)S(1)} async-done(((bf16[16,16,1536]{2,1,0:T(8,128)(2,1)}), bf16[16,16,1536]{2,1,0:T(8,128)(2,1)S(1)}, u32[]{:S(2)}, u32[]{:S(2)}) %all-to-all-start.1) | async-done | bytes 786464 | tf_op jit(solution)/shard_map/all_to_all | solution.py:71
  68.1 1.8 convolution_convert_fusion.1
  70.0 1.8 convolution_convert_fusion
  71.8 0.8 pad_maximum_fusion
  72.6 3.6 %all-to-all-start.2 = ((bf16[4,64,768]{2,1,0:T(8,128)(2,1)}), bf16[4,64,768]{2,1,0:T(8,128)(2,1)S(1)}, u32[]{:S(2)}, u32[]{:S(2)}) async-start(bf16[4,64,768]{2,1,0:T(8,128)(2,1)} %pad_maximum_fusion), calls=%async_computation.2 | async-start | bytes 786432 | tf_op jit(solution)/shard_map/all_to_all | solution.py:77
  76.2 4.2 %collective-permute-start.3 = (bf16[1,1,64,1536]{3,2,1,0:T(8,128)(2,1)S(1)}, bf16[1,1,64,1536]{3,2,1,0:T(8,128)(2,1)S(1)}, u32[]{:S(2)}, u32[]{:S(2)}) collective-permute-start(bf16[1,1,64,1536]{3,2,1,0:T(8,128)(2,1)S(1)} %dynamic-slice_convert_fusion.1), channel_id=1, source_target_pairs={{0,128},{128,0},{1,129},{129,1},{2,130},{130,2},{3,131},{131,3},{4... | collective-permute-start | bytes 589832 | tf_op jit(solution)/shard_map/ppermute | solution.py:41
  80.4 15.3 %collective-permute-done.3 = bf16[1,1,64,1536]{3,2,1,0:T(8,128)(2,1)S(1)} collective-permute-done((bf16[1,1,64,1536]{3,2,1,0:T(8,128)(2,1)S(1)}, bf16[1,1,64,1536]{3,2,1,0:T(8,128)(2,1)S(1)}, u32[]{:S(2)}, u32[]{:S(2)}) %collective-permute-start.3) | collective-permute-done | bytes 196640 | tf_op jit(solution)/shard_map/ppermute | solution.py:41
  95.8 0.1 convert_reduce_fusion.1
  95.9 7.2 %collective-permute-start.7 = (bf16[32,768]{1,0:T(8,128)(2,1)S(1)}, bf16[32,768]{1,0:T(8,128)(2,1)S(1)}, u32[]{:S(2)}, u32[]{:S(2)}) collective-permute-start(bf16[32,768]{1,0:T(8,128)(2,1)S(1)} %dynamic-slice_convert_fusion.3), channel_id=1, source_target_pairs={{0,256},{256,0},{1,257},{257,1},{2,258},{258,2},{3,259},{259,3},{4... | collective-permute-start | bytes 147464 | tf_op jit(solution)/shard_map/ppermute | solution.py:41
  103.1 0.1 dynamic_slice.60
  103.2 2.0 collective-permute-start.5
  105.2 1.4 collective-permute-done.7
  106.6 11.7 %collective-permute-done.5 = bf16[32,1536]{1,0:T(8,128)(2,1)S(1)} collective-permute-done((bf16[32,1536]{1,0:T(8,128)(2,1)S(1)}, bf16[32,1536]{1,0:T(8,128)(2,1)S(1)}, u32[]{:S(2)}, u32[]{:S(2)}) %collective-permute-start.5) | collective-permute-done | bytes 98336 | tf_op jit(solution)/shard_map/ppermute | solution.py:41
  118.4 9.8 %collective-permute-start.6 = (bf16[32,768]{1,0:T(8,128)(2,1)S(1)}, bf16[32,768]{1,0:T(8,128)(2,1)S(1)}, u32[]{:S(2)}, u32[]{:S(2)}) collective-permute-start(bf16[32,768]{1,0:T(8,128)(2,1)S(1)} %dynamic-slice_convert_fusion.4), channel_id=1, source_target_pairs={{0,2},{2,0},{1,3},{3,1},{4,6},{6,4},{5,7},{7,5},{8,10},{10,8},{9,1... | collective-permute-start | bytes 147464 | tf_op jit(solution)/shard_map/ppermute | solution.py:41
  128.2 3.7 %collective-permute-done.6 = bf16[32,768]{1,0:T(8,128)(2,1)S(1)} collective-permute-done((bf16[32,768]{1,0:T(8,128)(2,1)S(1)}, bf16[32,768]{1,0:T(8,128)(2,1)S(1)}, u32[]{:S(2)}, u32[]{:S(2)}) %collective-permute-start.6) | collective-permute-done | bytes 49184 | tf_op jit(solution)/shard_map/ppermute | solution.py:41
  131.9 0.1 multiply_convert_fusion
  132.0 1.9 collective-permute-start.8
  134.0 6.8 %collective-permute-done.8 = bf16[32,768]{1,0:T(8,128)(2,1)S(1)} collective-permute-done((bf16[32,768]{1,0:T(8,128)(2,1)S(1)}, bf16[32,768]{1,0:T(8,128)(2,1)S(1)}, u32[]{:S(2)}, u32[]{:S(2)}) %collective-permute-start.8) | collective-permute-done | bytes 49184 | tf_op jit(solution)/shard_map/ppermute | solution.py:41
  140.8 0.8 broadcast_in_dim.8
  141.6 3.5 %all-to-all-start.3 = ((bf16[4,64,768]{2,1,0:T(8,128)(2,1)}), bf16[4,64,768]{2,1,0:T(8,128)(2,1)S(1)}, u32[]{:S(2)}, u32[]{:S(2)}) async-start(bf16[4,64,768]{2,1,0:T(8,128)(2,1)} %broadcast_in_dim.8), calls=%async_computation.3 | async-start | bytes 786432 | tf_op jit(solution)/shard_map/all_to_all | solution.py:71
  145.0 9.9 %collective-permute-start.9 = (bf16[32,768]{1,0:T(8,128)(2,1)S(1)}, bf16[32,768]{1,0:T(8,128)(2,1)S(1)}, u32[]{:S(2)}, u32[]{:S(2)}) collective-permute-start(bf16[32,768]{1,0:T(8,128)(2,1)S(1)} %get-tuple-element.26), channel_id=1, source_target_pairs={{0,2},{2,0},{1,3},{3,1},{4,6},{6,4},{5,7},{7,5},{8,10},{10,8},{9,1... | collective-permute-start | bytes 147464 | tf_op jit(solution)/shard_map/ppermute | solution.py:41
  155.0 4.1 %collective-permute-done.9 = bf16[32,768]{1,0:T(8,128)(2,1)S(1)} collective-permute-done((bf16[32,768]{1,0:T(8,128)(2,1)S(1)}, bf16[32,768]{1,0:T(8,128)(2,1)S(1)}, u32[]{:S(2)}, u32[]{:S(2)}) %collective-permute-start.9) | collective-permute-done | bytes 49184 | tf_op jit(solution)/shard_map/ppermute | solution.py:41
  159.1 5.3 %collective-permute-start.10 = (bf16[32,1536]{1,0:T(8,128)(2,1)S(1)}, bf16[32,1536]{1,0:T(8,128)(2,1)S(1)}, u32[]{:S(2)}, u32[]{:S(2)}) collective-permute-start(bf16[32,1536]{1,0:T(8,128)(2,1)S(1)} %maximum_select_fusion.5), channel_id=1, source_target_pairs={{0,256},{256,0},{1,257},{257,1},{2,258},{258,2},{3,259},{259,3},{4... | collective-permute-start | bytes 294920 | tf_op jit(solution)/shard_map/ppermute | solution.py:41
  164.5 5.8 %collective-permute-start.17 = (bf16[256,384]{1,0:T(8,128)(2,1)S(1)}, bf16[256,384]{1,0:T(8,128)(2,1)S(1)}, u32[]{:S(2)}, u32[]{:S(2)}) collective-permute-start(bf16[256,384]{1,0:T(8,128)(2,1)S(1)} %slice.54), channel_id=1, source_target_pairs={{0,1},{1,0},{2,3},{3,2},{4,5},{5,4},{6,7},{7,6},{8,9},{9,8},{10,11... | collective-permute-start | bytes 589832 | tf_op jit(solution)/shard_map/ppermute | solution.py:41
  170.2 1.9 collective-permute-start.12
  172.2 1.9 fusion.17
  174.1 2.8 %fusion.2 = bf16[256,1536]{1,0:T(8,128)(2,1)} fusion(f32[256,1536]{1,0:T(8,128)S(1)} %fusion.17, bf16[1536,384]{1,0:T(8,128)(2,1)} %param.7, bf16[256,768]{1,0:T(8,128)(2,1)S(1)} %bitcast.29), kind=kOutput, calls=%fused_computation.6 | convolution fusion | flops 302776320 | bytes 3735552 | tf_op jit(solution)/shard_map/dot_general | solution.py:29
  176.9 0.7 slice.61
  177.6 5.3 %all-to-all-start.4 = ((bf16[16,16,1536]{2,1,0:T(8,128)(2,1)}), bf16[16,16,1536]{2,1,0:T(8,128)(2,1)S(1)}, u32[]{:S(2)}, u32[]{:S(2)}) async-start(bf16[16,16,1536]{2,1,0:T(8,128)(2,1)} %bitcast.10), calls=%async_computation.4 | async-start | bytes 1572864 | tf_op jit(solution)/shard_map/all_to_all | solution.py:77
  182.9 3.7 %collective-permute-start.13 = (bf16[256,384]{1,0:T(8,128)(2,1)}, bf16[256,384]{1,0:T(8,128)(2,1)S(1)}, u32[]{:S(2)}, u32[]{:S(2)}) collective-permute-start(bf16[256,384]{1,0:T(8,128)(2,1)} %slice.61), channel_id=1, source_target_pairs={{0,1},{1,0},{2,3},{3,2},{4,5},{5,4},{6,7},{7,6},{8,9},{9,8},{10,11... | collective-permute-start | bytes 589832 | tf_op jit(solution)/shard_map/ppermute | solution.py:41
  186.6 5.9 %collective-permute-start.14 = (bf16[1,1,64,1536]{3,2,1,0:T(8,128)(2,1)S(1)}, bf16[1,1,64,1536]{3,2,1,0:T(8,128)(2,1)S(1)}, u32[]{:S(2)}, u32[]{:S(2)}) collective-permute-start(bf16[1,1,64,1536]{3,2,1,0:T(8,128)(2,1)S(1)} %maximum_select_fusion.2), channel_id=1, source_target_pairs={{0,128},{128,0},{1,129},{129,1},{2,130},{130,2},{3,131},{131,3},{4... | collective-permute-start | bytes 589832 | tf_op jit(solution)/shard_map/ppermute | solution.py:41
  192.5 0.6 fusion.5
  193.1 8.5 %collective-permute-done.14 = bf16[1,1,64,1536]{3,2,1,0:T(8,128)(2,1)S(1)} collective-permute-done((bf16[1,1,64,1536]{3,2,1,0:T(8,128)(2,1)S(1)}, bf16[1,1,64,1536]{3,2,1,0:T(8,128)(2,1)S(1)}, u32[]{:S(2)}, u32[]{:S(2)}) %collective-permute-start.14) | collective-permute-done | bytes 196640 | tf_op jit(solution)/shard_map/ppermute | solution.py:41
  201.7 1.9 collective-permute-start.15
  203.6 0.1 convert_reduce_fusion.3
  203.7 2.8 %fusion = bf16[1536,384]{1,0:T(8,128)(2,1)} fusion(f32[1536,384]{1,0:T(8,128)S(1)} %fusion.5, bf16[256,1536]{1,0:T(8,128)(2,1)} %collective-permute-done.12, bf16[256,384]{1,0:T(8,128)(2,1)S(1)} %collective-permute-done.13), kind=kOutput, calls=%fused_computation.2 | convolution fusion | flops 303169536 | bytes 4521984 | tf_op jit(solution)/shard_map/dot_general | solution.py:33
  206.4 7.4 %collective-permute-done.15 = bf16[2,1,64,1536]{3,2,1,0:T(8,128)(2,1)S(1)} collective-permute-done((bf16[2,1,64,1536]{3,2,1,0:T(8,128)(2,1)S(1)}, bf16[2,1,64,1536]{3,2,1,0:T(8,128)(2,1)S(1)}, u32[]{:S(2)}, u32[]{:S(2)}) %collective-permute-start.15) | collective-permute-done | bytes 393248 | tf_op jit(solution)/shard_map/ppermute | solution.py:41
  213.8 0.1 maximum_select_fusion
  213.9 3.2 %collective-permute-start.16 = (bf16[256,1536]{1,0:T(8,128)(2,1)S(1)}, bf16[256,1536]{1,0:T(8,128)(2,1)}, u32[]{:S(2)}, u32[]{:S(2)}) collective-permute-start(bf16[256,1536]{1,0:T(8,128)(2,1)S(1)} %bitcast.43), channel_id=1, source_target_pairs={{0,1},{1,0},{2,3},{3,2},{4,5},{5,4},{6,7},{7,6},{8,9},{9,8},{10,11... | collective-permute-start | bytes 2359304 | tf_op jit(solution)/shard_map/ppermute | solution.py:41
  217.1 0.1 convert_reduce_fusion
  217.3 10.9 %collective-permute-start.11 = (bf16[8,1536]{1,0:T(8,128)(2,1)S(1)}, bf16[8,1536]{1,0:T(8,128)(2,1)S(1)}, u32[]{:S(2)}, u32[]{:S(2)}) collective-permute-start(bf16[8,1536]{1,0:T(8,128)(2,1)S(1)} %dynamic-slice_convert_fusion.5), channel_id=1, source_target_pairs={{0,2},{2,0},{1,3},{3,1},{4,6},{6,4},{5,7},{7,5},{8,10},{10,8},{9,1... | collective-permute-start | bytes 73736 | tf_op jit(solution)/shard_map/ppermute | solution.py:41
  228.1 0.1 convert_reduce_fusion.2
  228.2 0.6 add.116
  228.8 1.8 collective-permute-done.11
  230.5 0.6 add_convert_fusion
  231.2 1.7 fusion.24
  232.9 1.6 fusion.1
  (34 shorter events, 0.5 us)
Async XLA Ops:
  2.1 17.7 %collective-permute-start = (bf16[8,2304]{1,0:T(8,128)(2,1)S(1)}, bf16[8,2304]{1,0:T(8,128)(2,1)S(1)}, u32[]{:S(2)}, u32[]{:S(2)}) collective-permute-start(bf16[8,2304]{1,0:T(8,128)(2,1)S(1)} %pad_maximum_fusion.1), channel_id=1, source_target_pairs={{0,2},{2,0},{1,3},{3,1},{4,6},{6,4},{5,7},{7,5},{8,10},{10,8},{9,1... | collective-permute-start | bytes 110600 | tf_op jit(solution)/shard_map/ppermute | solution.py:41
  19.9 20.9 %collective-permute-start.1 = (bf16[1536,384]{1,0:T(8,128)(2,1)}, bf16[1536,384]{1,0:T(8,128)(2,1)S(1)}, u32[]{:S(2)}, u32[]{:S(2)}) collective-permute-start(bf16[1536,384]{1,0:T(8,128)(2,1)} %param.9), channel_id=1, source_target_pairs={{0,1},{1,0},{2,3},{3,2},{4,5},{5,4},{6,7},{7,6},{8,9},{9,8},{10,11... | collective-permute-start | bytes 3538952 | tf_op jit(solution)/shard_map/ppermute | solution.py:41
  27.1 13.6 %all-to-all-start = ((bf16[16,16,768]{2,1,0:T(8,128)(2,1)}), bf16[16,16,768]{2,1,0:T(8,128)(2,1)S(1)}, u32[]{:S(2)}, u32[]{:S(2)}) async-start(bf16[16,16,768]{2,1,0:T(8,128)(2,1)} %broadcast_in_dim.6), calls=%async_computation | async-start | bytes 786432 | tf_op jit(solution)/shard_map/all_to_all | solution.py:71
  40.7 1.3 copy-start
  42.7 11.6 %collective-permute-start.2 = (bf16[2,1,64,1536]{3,2,1,0:T(8,128)(2,1)S(1)}, bf16[2,1,64,1536]{3,2,1,0:T(8,128)(2,1)}, u32[]{:S(2)}, u32[]{:S(2)}) collective-permute-start(bf16[2,1,64,1536]{3,2,1,0:T(8,128)(2,1)S(1)} %dynamic-slice_convert_fusion), channel_id=1, source_target_pairs={{0,64},{64,0},{1,65},{65,1},{2,66},{66,2},{3,67},{67,3},{4,68},{68... | collective-permute-start | bytes 1179656 | tf_op jit(solution)/shard_map/ppermute | solution.py:41
  45.8 24.2 %collective-permute-start.4 = (bf16[1536,384]{1,0:T(8,128)(2,1)}, bf16[1536,384]{1,0:T(8,128)(2,1)}, u32[]{:S(2)}, u32[]{:S(2)}) collective-permute-start(bf16[1536,384]{1,0:T(8,128)(2,1)} %param.7), channel_id=1, source_target_pairs={{0,1},{1,0},{2,3},{3,2},{4,5},{5,4},{6,7},{7,6},{8,9},{9,8},{10,11... | collective-permute-start | bytes 3538952 | tf_op jit(solution)/shard_map/ppermute | solution.py:41
  50.6 17.5 %all-to-all-start.1 = ((bf16[16,16,1536]{2,1,0:T(8,128)(2,1)}), bf16[16,16,1536]{2,1,0:T(8,128)(2,1)S(1)}, u32[]{:S(2)}, u32[]{:S(2)}) async-start(bf16[16,16,1536]{2,1,0:T(8,128)(2,1)} %broadcast_in_dim.7), calls=%async_computation.1 | async-start | bytes 1572864 | tf_op jit(solution)/shard_map/all_to_all | solution.py:71
  72.6 30.5 %copy-start.1 = (f32[1536]{0:T(1024)S(1)}, f32[1536]{0:T(1024)}, u32[]{:S(2)}) copy-start(f32[1536]{0:T(1024)} %param.8) | copy-start | bytes 18436
  72.6 23.2 %all-to-all-start.2 = ((bf16[4,64,768]{2,1,0:T(8,128)(2,1)}), bf16[4,64,768]{2,1,0:T(8,128)(2,1)S(1)}, u32[]{:S(2)}, u32[]{:S(2)}) async-start(bf16[4,64,768]{2,1,0:T(8,128)(2,1)} %pad_maximum_fusion), calls=%async_computation.2 | async-start | bytes 786432 | tf_op jit(solution)/shard_map/all_to_all | solution.py:77
  76.2 19.5 %collective-permute-start.3 = (bf16[1,1,64,1536]{3,2,1,0:T(8,128)(2,1)S(1)}, bf16[1,1,64,1536]{3,2,1,0:T(8,128)(2,1)S(1)}, u32[]{:S(2)}, u32[]{:S(2)}) collective-permute-start(bf16[1,1,64,1536]{3,2,1,0:T(8,128)(2,1)S(1)} %dynamic-slice_convert_fusion.1), channel_id=1, source_target_pairs={{0,128},{128,0},{1,129},{129,1},{2,130},{130,2},{3,131},{131,3},{4... | collective-permute-start | bytes 589832 | tf_op jit(solution)/shard_map/ppermute | solution.py:41
  95.9 10.7 %collective-permute-start.7 = (bf16[32,768]{1,0:T(8,128)(2,1)S(1)}, bf16[32,768]{1,0:T(8,128)(2,1)S(1)}, u32[]{:S(2)}, u32[]{:S(2)}) collective-permute-start(bf16[32,768]{1,0:T(8,128)(2,1)S(1)} %dynamic-slice_convert_fusion.3), channel_id=1, source_target_pairs={{0,256},{256,0},{1,257},{257,1},{2,258},{258,2},{3,259},{259,3},{4... | collective-permute-start | bytes 147464 | tf_op jit(solution)/shard_map/ppermute | solution.py:41
  103.2 15.1 %collective-permute-start.5 = (bf16[32,1536]{1,0:T(8,128)(2,1)S(1)}, bf16[32,1536]{1,0:T(8,128)(2,1)S(1)}, u32[]{:S(2)}, u32[]{:S(2)}) collective-permute-start(bf16[32,1536]{1,0:T(8,128)(2,1)S(1)} %fusion.15), channel_id=1, source_target_pairs={{0,256},{256,0},{1,257},{257,1},{2,258},{258,2},{3,259},{259,3},{4... | collective-permute-start | bytes 294920 | tf_op jit(solution)/shard_map/ppermute | solution.py:41
  118.4 13.5 %collective-permute-start.6 = (bf16[32,768]{1,0:T(8,128)(2,1)S(1)}, bf16[32,768]{1,0:T(8,128)(2,1)S(1)}, u32[]{:S(2)}, u32[]{:S(2)}) collective-permute-start(bf16[32,768]{1,0:T(8,128)(2,1)S(1)} %dynamic-slice_convert_fusion.4), channel_id=1, source_target_pairs={{0,2},{2,0},{1,3},{3,1},{4,6},{6,4},{5,7},{7,5},{8,10},{10,8},{9,1... | collective-permute-start | bytes 147464 | tf_op jit(solution)/shard_map/ppermute | solution.py:41
  132.0 8.7 %collective-permute-start.8 = (bf16[32,768]{1,0:T(8,128)(2,1)S(1)}, bf16[32,768]{1,0:T(8,128)(2,1)S(1)}, u32[]{:S(2)}, u32[]{:S(2)}) collective-permute-start(bf16[32,768]{1,0:T(8,128)(2,1)S(1)} %maximum_select_fusion.7), channel_id=1, source_target_pairs={{0,256},{256,0},{1,257},{257,1},{2,258},{258,2},{3,259},{259,3},{4... | collective-permute-start | bytes 147464 | tf_op jit(solution)/shard_map/ppermute | solution.py:41
  141.6 30.6 %all-to-all-start.3 = ((bf16[4,64,768]{2,1,0:T(8,128)(2,1)}), bf16[4,64,768]{2,1,0:T(8,128)(2,1)S(1)}, u32[]{:S(2)}, u32[]{:S(2)}) async-start(bf16[4,64,768]{2,1,0:T(8,128)(2,1)} %broadcast_in_dim.8), calls=%async_computation.3 | async-start | bytes 786432 | tf_op jit(solution)/shard_map/all_to_all | solution.py:71
  145.0 14.0 %collective-permute-start.9 = (bf16[32,768]{1,0:T(8,128)(2,1)S(1)}, bf16[32,768]{1,0:T(8,128)(2,1)S(1)}, u32[]{:S(2)}, u32[]{:S(2)}) collective-permute-start(bf16[32,768]{1,0:T(8,128)(2,1)S(1)} %get-tuple-element.26), channel_id=1, source_target_pairs={{0,2},{2,0},{1,3},{3,1},{4,6},{6,4},{5,7},{7,5},{8,10},{10,8},{9,1... | collective-permute-start | bytes 147464 | tf_op jit(solution)/shard_map/ppermute | solution.py:41
  159.1 13.1 %collective-permute-start.10 = (bf16[32,1536]{1,0:T(8,128)(2,1)S(1)}, bf16[32,1536]{1,0:T(8,128)(2,1)S(1)}, u32[]{:S(2)}, u32[]{:S(2)}) collective-permute-start(bf16[32,1536]{1,0:T(8,128)(2,1)S(1)} %maximum_select_fusion.5), channel_id=1, source_target_pairs={{0,256},{256,0},{1,257},{257,1},{2,258},{258,2},{3,259},{259,3},{4... | collective-permute-start | bytes 294920 | tf_op jit(solution)/shard_map/ppermute | solution.py:41
  164.5 66.7 %collective-permute-start.17 = (bf16[256,384]{1,0:T(8,128)(2,1)S(1)}, bf16[256,384]{1,0:T(8,128)(2,1)S(1)}, u32[]{:S(2)}, u32[]{:S(2)}) collective-permute-start(bf16[256,384]{1,0:T(8,128)(2,1)S(1)} %slice.54), channel_id=1, source_target_pairs={{0,1},{1,0},{2,3},{3,2},{4,5},{5,4},{6,7},{7,6},{8,9},{9,8},{10,11... | collective-permute-start | bytes 589832 | tf_op jit(solution)/shard_map/ppermute | solution.py:41
  170.2 33.4 %collective-permute-start.12 = (bf16[256,1536]{1,0:T(8,128)(2,1)S(1)}, bf16[256,1536]{1,0:T(8,128)(2,1)}, u32[]{:S(2)}, u32[]{:S(2)}) collective-permute-start(bf16[256,1536]{1,0:T(8,128)(2,1)S(1)} %bitcast.41), channel_id=1, source_target_pairs={{0,1},{1,0},{2,3},{3,2},{4,5},{5,4},{6,7},{7,6},{8,9},{9,8},{10,11... | collective-permute-start | bytes 2359304 | tf_op jit(solution)/shard_map/ppermute | solution.py:41
  177.6 39.5 %all-to-all-start.4 = ((bf16[16,16,1536]{2,1,0:T(8,128)(2,1)}), bf16[16,16,1536]{2,1,0:T(8,128)(2,1)S(1)}, u32[]{:S(2)}, u32[]{:S(2)}) async-start(bf16[16,16,1536]{2,1,0:T(8,128)(2,1)} %bitcast.10), calls=%async_computation.4 | async-start | bytes 1572864 | tf_op jit(solution)/shard_map/all_to_all | solution.py:77
  182.9 20.8 %collective-permute-start.13 = (bf16[256,384]{1,0:T(8,128)(2,1)}, bf16[256,384]{1,0:T(8,128)(2,1)S(1)}, u32[]{:S(2)}, u32[]{:S(2)}) collective-permute-start(bf16[256,384]{1,0:T(8,128)(2,1)} %slice.61), channel_id=1, source_target_pairs={{0,1},{1,0},{2,3},{3,2},{4,5},{5,4},{6,7},{7,6},{8,9},{9,8},{10,11... | collective-permute-start | bytes 589832 | tf_op jit(solution)/shard_map/ppermute | solution.py:41
  186.6 15.0 %collective-permute-start.14 = (bf16[1,1,64,1536]{3,2,1,0:T(8,128)(2,1)S(1)}, bf16[1,1,64,1536]{3,2,1,0:T(8,128)(2,1)S(1)}, u32[]{:S(2)}, u32[]{:S(2)}) collective-permute-start(bf16[1,1,64,1536]{3,2,1,0:T(8,128)(2,1)S(1)} %maximum_select_fusion.2), channel_id=1, source_target_pairs={{0,128},{128,0},{1,129},{129,1},{2,130},{130,2},{3,131},{131,3},{4... | collective-permute-start | bytes 589832 | tf_op jit(solution)/shard_map/ppermute | solution.py:41
  201.7 12.2 %collective-permute-start.15 = (bf16[2,1,64,1536]{3,2,1,0:T(8,128)(2,1)S(1)}, bf16[2,1,64,1536]{3,2,1,0:T(8,128)(2,1)S(1)}, u32[]{:S(2)}, u32[]{:S(2)}) collective-permute-start(bf16[2,1,64,1536]{3,2,1,0:T(8,128)(2,1)S(1)} %maximum_select_fusion.1), channel_id=1, source_target_pairs={{0,64},{64,0},{1,65},{65,1},{2,66},{66,2},{3,67},{67,3},{4,68},{68... | collective-permute-start | bytes 1179656 | tf_op jit(solution)/shard_map/ppermute | solution.py:41
  213.9 17.2 %collective-permute-start.16 = (bf16[256,1536]{1,0:T(8,128)(2,1)S(1)}, bf16[256,1536]{1,0:T(8,128)(2,1)}, u32[]{:S(2)}, u32[]{:S(2)}) collective-permute-start(bf16[256,1536]{1,0:T(8,128)(2,1)S(1)} %bitcast.43), channel_id=1, source_target_pairs={{0,1},{1,0},{2,3},{3,2},{4,5},{5,4},{6,7},{7,6},{8,9},{9,8},{10,11... | collective-permute-start | bytes 2359304 | tf_op jit(solution)/shard_map/ppermute | solution.py:41
  217.3 13.3 %collective-permute-start.11 = (bf16[8,1536]{1,0:T(8,128)(2,1)S(1)}, bf16[8,1536]{1,0:T(8,128)(2,1)S(1)}, u32[]{:S(2)}, u32[]{:S(2)}) collective-permute-start(bf16[8,1536]{1,0:T(8,128)(2,1)S(1)} %dynamic-slice_convert_fusion.5), channel_id=1, source_target_pairs={{0,2},{2,0},{1,3},{3,1},{4,6},{6,4},{5,7},{7,5},{8,10},{10,8},{9,1... | collective-permute-start | bytes 73736 | tf_op jit(solution)/shard_map/ppermute | solution.py:41

commit v3 on v1

--- a/solution.py
+++ b/solution.py
@@ -7,7 +7,9 @@
 bf16 = jnp.bfloat16
 f32 = jnp.float32
 SWAP = [(0, 1), (1, 0)]
+CROSS = [(0, 3), (1, 2), (2, 1), (3, 0)]
 GRID = ("x", "y")
+ROW4 = ("rm", "rl")
 
 
 def gelu_pair(pre):
@@ -49,60 +51,68 @@
     )
 
 
-def widen(mine, axis, dim):
-    return join(mine, swap(mine, axis), axis, dim)
+def cross(value):
+    return lax.ppermute(value, ("rh", "zh"), CROSS)
 
 
-def halve(part, axis, dim=0):
-    size = part.shape[dim] // 2
-    at = lax.axis_index(axis)
-    out = part_of(part, 1 - at, size, dim).astype(bf16)
-    return part_of(part, at, size, dim) + swap(out, axis).astype(f32)
+def both_sum(part, axis):
+    part = part.astype(bf16)
+    return part.astype(f32) + swap(part, axis).astype(f32)
 
 
-def spread(rows):
-    n = lax.axis_size("x") * lax.axis_size("y")
+def spread(rows, axes):
+    n = lax.axis_size(axes)
     sent = jnp.broadcast_to(rows[None], (n,) + rows.shape)
-    got = lax.all_to_all(sent, GRID, 0, 0, tiled=True)
+    got = lax.all_to_all(sent, axes, 0, 0, tiled=True)
     return got.reshape(n * rows.shape[0], rows.shape[1])
+
+
+def deal(part, axes):
+    n = lax.axis_size(axes)
+    got = lax.all_to_all(part.reshape(n, -1, part.shape[1]), axes, 0, 0, tiled=True)
+    return jnp.sum(got.astype(f32), axis=0)
 
 
 def shards(tokens, cotangent, w_in, b_in, w_out):
     zh = lax.axis_index("zh")
     core = lax.axis_index("core")
-    feat = tokens.shape[1]
+    tok_dev, feat = tokens.shape
     quarter = w_in.shape[1]
     half_h = 2 * quarter
-    half_d = 2 * w_out.shape[1]
-
-    in_pair = lax.all_gather(w_in, "core", axis=1, tiled=True)
-    out_pair = lax.all_gather(w_out, "core", axis=1, tiled=True)
+    quarter_d = w_out.shape[1]
+    half_d = 2 * quarter_d
 
     sent = jnp.concatenate([tokens, part_of(cotangent, 1 - zh, half_d, 1)], 1)
     kept = jnp.concatenate([tokens, part_of(cotangent, zh, half_d, 1)], 1)
-    both = join(kept, swap(sent, "zh"), "zh", 0)
-    every_g = spread(both[:, feat:])
-    every_x = spread(both[:, :feat])
+    got = swap(sent, "zh")
+    w_out, w_in, got = lax.optimization_barrier((w_out, w_in, got))
+    out_pair = join(w_out, swap(w_out, "core"), "core", 1)
+    in_pair = join(w_in, swap(w_in, "core"), "core", 1)
 
-    back = against(every_g, out_pair)
-    pre = dot(every_x, in_pair)
-    for axis in ("rl", "rm", "rh"):
-        back = halve(back, axis)
-        pre = halve(pre, axis)
-    back = halve(back, "zh", 1)
+    every = spread(join(kept, got, "zh", 0), GRID)
+    every_x, every_g = every[:, :feat], every[:, feat:]
+    pre = dot(every_x, in_pair).astype(bf16)
+    back = against(every_g, out_pair).astype(bf16)
+    sums = deal(jnp.concatenate([pre, back], 1), ROW4)
+    back = sums[:, half_h:]
+    back_kept = part_of(back, zh, half_h, 1)
+    back_sent = part_of(back, 1 - zh, half_h, 1).astype(bf16)
+    pre = both_sum(sums[:, :half_h], "rh")
+    back = both_sum(back_kept + cross(back_sent).astype(f32), "rh")
 
     act_f, slope = gelu_pair(pre + part_of(b_in, zh, half_h, 0))
     act = act_f.astype(bf16)
+    act = join(act, cross(act), "zh", 1)
     grad = (back * slope).astype(bf16)
-
-    for axis in ("rh", "rm", "rl"):
-        grad = widen(grad, axis, 0)
+    gathered = spread(jnp.concatenate([grad, act], 1), ROW4)
+    grad, act = gathered[:, :half_h], gathered[:, half_h:]
 
     part = against(grad, in_pair).astype(bf16)
-    n = lax.axis_size("x") * lax.axis_size("y")
-    got = lax.all_to_all(part.reshape(n, -1, feat), GRID, 0, 0, tiled=True)
-    summed = jnp.sum(got.astype(f32), axis=0)
-    input_grad = halve(summed, "zh").astype(bf16)
+    part, grad, act = lax.optimization_barrier((part, grad, act))
+    summed = deal(part, GRID)
+    out_rows = part_of(summed, 1 - zh, tok_dev, 0).astype(bf16)
+    own_rows = part_of(summed, zh, tok_dev, 0)
+    input_grad = (own_rows + swap(out_rows, "zh").astype(f32)).astype(bf16)
 
     pair_x = swap(every_x, "core")
     own_grad = part_of(grad, core, quarter, 1)
@@ -110,12 +120,9 @@
     w_in_grad = (over_rows(every_x, own_grad) + over_rows(pair_x, pair_grad)).astype(bf16)
     b_in_grad = jnp.sum(own_grad.astype(f32), 0) + jnp.sum(pair_grad.astype(f32), 0)
 
-    act = widen(act, "zh", 1)
-    for axis in ("rh", "rm", "rl"):
-        act = widen(act, axis, 0)
+    own_g = part_of(every_g, core, quarter_d, 1)
+    pair_g = swap(part_of(every_g, 1 - core, quarter_d, 1), "core")
     pair_act = swap(act, "core")
-    own_g = part_of(every_g, core, w_out.shape[1], 1)
-    pair_g = swap(part_of(every_g, 1 - core, w_out.shape[1], 1), "core")
     w_out_grad = (over_rows(act, own_g) + over_rows(pair_act, pair_g)).astype(bf16)
     return (input_grad, w_in_grad, b_in_grad, w_out_grad)
 

time: 225 us -> 203 us (0.902)
  blocking collectives: 0 us -> 30.4 us
  starting transfers between devices: 105 us -> 76.5 us
  waiting for transfers between devices: 82.8 us -> 66.9 us
  between operations: 14.6 us -> 1 us
  matrix products: 12 us -> 16.2 us
    ppermute x20 -> x10, waiting for transfers between devices: 62.8 us -> 16.6 us  [swap(): return lax.ppermute(value, axis, SWAP)]
    ppermute x20 -> x10, starting transfers between devices: 90.1 us -> 53.2 us  [swap(): return lax.ppermute(value, axis, SWAP)]
    all_to_all x0 -> x1, blocking collectives: none -> 30.4 us  [deal(): lax.all_to_all(part.reshape(n, -1, part.shape[1]), axes, 0, 0, tiled=True)]
    all_to_all x3, waiting for transfers between devices: 15.1 us -> 39.5 us  [the longest x2 37.4 us: spread(): got = lax.all_to_all(sent, axes, 0, 0, tiled=True)]
    ppermute x0 -> x2, starting transfers between devices: none -> 11.6 us  [cross(): return lax.ppermute(value, ('rh', 'zh'), CROSS)]
    ppermute x0 -> x2, waiting for transfers between devices: none -> 10.8 us  [cross(): return lax.ppermute(value, ('rh', 'zh'), CROSS)]
    all_gather x2 -> x0, waiting for transfers between devices: 3.51 us -> none  [the longest x1 3.49 us: shards(): out_pair = lax.all_gather(w_out, 'core', axis=1, tiled=True)]
    all_to_all x3, starting transfers between devices: 14.4 us -> 11.6 us  [the longest x2 8.03 us: spread(): got = lax.all_to_all(sent, axes, 0, 0, tiled=True)]
  transfers between devices with their start and end apart: 25 -> 15, of which waited for: 13 -> 8; matrix products, arithmetic and copies ran while one was open for 8% -> 9% of each run, Pallas kernels for 0% -> 0%
where the time goes in v3:
time: 203 us; the launch traced here: 201 us
  starting transfers between devices  76.5 us (38%)
  waiting for transfers between devices  66.9 us (33%)
  blocking collectives  30.4 us (15%)
  matrix products  16.2 us (8%)
  local copies, waits for them, and re-layouts  5.98 us (3%)
  other arithmetic  4.44 us (2%)
    ppermute x10, starting transfers between devices, swap(): return lax.ppermute(value, axis, SWAP)  53.2 us
    all_to_all x2, waiting for transfers between devices, spread(): got = lax.all_to_all(sent, axes, 0, 0, tiled=True)  37.4 us
    all_to_all x1, blocking collectives, deal(): lax.all_to_all(part.reshape(n, -1, part.shape[1]), axes, 0, 0, tiled=True)  30.4 us
    ppermute x10, waiting for transfers between devices, swap(): return lax.ppermute(value, axis, SWAP)  16.6 us
    ppermute x2, starting transfers between devices, cross(): return lax.ppermute(value, ('rh', 'zh'), CROSS)  11.6 us
    ppermute x2, waiting for transfers between devices, cross(): return lax.ppermute(value, ('rh', 'zh'), CROSS)  10.8 us
    all_to_all x2, starting transfers between devices, spread(): got = lax.all_to_all(sent, axes, 0, 0, tiled=True)  8.03 us
    dot_general x4, matrix products, over_rows(): lax.dot_general(left, right, (((0,), (0,)), ((), ())), preferred_element_...  7.92 us
  transfers between devices with their start and end apart: 15, of which 8 were waited for; matrix products, arithmetic and copies ran while one was open for 9% of the time, Pallas kernels for 0%

profile of v3, /device:TPU:1, one launch (start us, length us, event | category | flops | bytes accessed | tf_op | source)
XLA Modules:
  0.0 201.4 jit_solution(121218131197696405)
XLA Ops:
  0.6 0.0 copy-start.3
  0.6 0.0 copy-start.4
  0.7 0.9 constant_dynamic-slice_fusion.3
  1.5 0.7 pad_maximum_fusion.2
  2.3 16.3 %collective-permute-start = (bf16[8,2304]{1,0:T(8,128)(2,1)S(1)}, bf16[8,2304]{1,0:T(8,128)(2,1)S(1)}, u32[]{:S(2)}, u32[]{:S(2)}) collective-permute-start(bf16[8,2304]{1,0:T(8,128)(2,1)S(1)} %pad_maximum_fusion.2), channel_id=1, source_target_pairs={{0,2},{2,0},{1,3},{3,1},{4,6},{6,4},{5,7},{7,5},{8,10},{10,8},{9,1... | collective-permute-start | bytes 110600 | tf_op jit(solution)/shard_map/ppermute | solution.py:42
  18.6 1.5 collective-permute-done
  20.0 5.6 %collective-permute-start.2 = (bf16[1536,384]{1,0:T(8,128)(2,1)}, bf16[1536,384]{1,0:T(8,128)(2,1)}, u32[]{:S(2)}, u32[]{:S(2)}) collective-permute-start(bf16[1536,384]{1,0:T(8,128)(2,1)} %param.9), channel_id=1, source_target_pairs={{0,1},{1,0},{2,3},{3,2},{4,5},{5,4},{6,7},{7,6},{8,9},{9,8},{10,11... | collective-permute-start | bytes 3538952 | tf_op jit(solution)/shard_map/ppermute | solution.py:42
  25.6 0.8 maximum_select_fusion.6
  26.5 1.1 broadcast_in_dim.4
  27.6 4.5 %all-to-all-start = ((bf16[16,16,2304]{2,1,0:T(8,128)(2,1)}), bf16[16,16,2304]{2,1,0:T(8,128)(2,1)S(1)}, u32[]{:S(2)}, u32[]{:S(2)}) async-start(bf16[16,16,2304]{2,1,0:T(8,128)(2,1)} %broadcast_in_dim.4), calls=%async_computation | async-start | bytes 2359296 | tf_op jit(solution)/shard_map/all_to_all | solution.py:66
  32.1 0.0 copy-done.4
  32.1 2.2 %collective-permute-start.1 = (bf16[1536,384]{1,0:T(8,128)(2,1)S(1)}, bf16[1536,384]{1,0:T(8,128)(2,1)}, u32[]{:S(2)}, u32[]{:S(2)}) collective-permute-start(bf16[1536,384]{1,0:T(8,128)(2,1)S(1)} %copy-done.4), channel_id=1, source_target_pairs={{0,1},{1,0},{2,3},{3,2},{4,5},{5,4},{6,7},{7,6},{8,9},{9,8},{10,11... | collective-permute-start | bytes 3538952 | tf_op jit(solution)/shard_map/ppermute | solution.py:42
  34.3 16.5 %all-to-all-done = bf16[16,16,2304]{2,1,0:T(8,128)(2,1)S(1)} async-done(((bf16[16,16,2304]{2,1,0:T(8,128)(2,1)}), bf16[16,16,2304]{2,1,0:T(8,128)(2,1)S(1)}, u32[]{:S(2)}, u32[]{:S(2)}) %all-to-all-start) | async-done | bytes 1179680 | tf_op jit(solution)/shard_map/all_to_all | solution.py:66
  50.8 0.0 collective-permute-done.2
  50.8 0.0 copy-done.3
  50.8 2.5 %convolution_convert_fusion.1 = bf16[256,1536]{1,0:T(8,128)(2,1)S(1)} fusion(bf16[1536,384]{1,0:T(8,128)(2,1)} %collective-permute-done.2, bf16[1536,384]{1,0:T(8,128)(2,1)S(1)} %copy-done.3, pred[]{:T(512)S(6)} %eq.9, bf16[256,2304]{1,0:T(8,128)(2,1)S(1)} %bitcast.9), kind=kOutput, calls=%fused_computation.5 | convolution fusion | flops 614989824 | bytes 3538945 | tf_op jit(solution)/shard_map/dot_general | solution.py:30
  53.2 0.0 collective-permute-done.1
  53.3 2.5 %convolution_convert_fusion.2 = bf16[256,768]{1,0:T(8,128)(2,1)S(1)} fusion(bf16[1536,384]{1,0:T(8,128)(2,1)} %collective-permute-done.1, bf16[1536,384]{1,0:T(8,128)(2,1)S(1)} %copy-done.4, pred[]{:T(512)S(6)} %eq.9, bf16[256,2304]{1,0:T(8,128)(2,1)S(1)} %bitcast.10), kind=kOutput, calls=%fused_computation.16 | convolution fusion | flops 614793216 | bytes 3538945 | tf_op jit(solution)/shard_map/dot_general | solution.py:26
  55.7 0.1 pad_maximum_fusion
  55.8 0.0 copy-start.2
  55.8 30.4 %all_to_all.20 = bf16[4,64,2304]{2,1,0:T(8,128)(2,1)S(1)} all-to-all(bf16[4,64,2304]{2,1,0:T(8,128)(2,1)S(1)} %bitcast.17), channel_id=1, replica_groups=mesh['rh'=2,'rm'=2,'rl'=2,'x'=4,'y'=4,'zh'=2,'core'=2] {'rm','rl'}, dimensions={0} | all-to-all | bytes 2359296 | tf_op jit(solution)/shard_map/all_to_all | solution.py:72
  86.3 0.2 convert_reduce_fusion
  86.5 9.7 %collective-permute-start.3 = (bf16[64,768]{1,0:T(8,128)(2,1)S(1)}, bf16[64,768]{1,0:T(8,128)(2,1)S(1)}, u32[]{:S(2)}, u32[]{:S(2)}) collective-permute-start(bf16[64,768]{1,0:T(8,128)(2,1)S(1)} %dynamic-slice_convert_fusion), channel_id=1, source_target_pairs={{0,258},{2,256},{256,2},{258,0},{1,259},{3,257},{257,3},{259,1},{4... | collective-permute-start | bytes 294920 | tf_op jit(solution)/shard_map/ppermute | solution.py:55
  96.2 5.0 %collective-permute-start.5 = (bf16[64,768]{1,0:T(8,128)(2,1)S(1)}, bf16[64,768]{1,0:T(8,128)(2,1)S(1)}, u32[]{:S(2)}, u32[]{:S(2)}) collective-permute-start(bf16[64,768]{1,0:T(8,128)(2,1)S(1)} %slice.40), channel_id=1, source_target_pairs={{0,256},{256,0},{1,257},{257,1},{2,258},{258,2},{3,259},{259,3},{4... | collective-permute-start | bytes 294920 | tf_op jit(solution)/shard_map/ppermute | solution.py:42
  101.2 3.1 %collective-permute-done.3 = bf16[64,768]{1,0:T(8,128)(2,1)S(1)} collective-permute-done((bf16[64,768]{1,0:T(8,128)(2,1)S(1)}, bf16[64,768]{1,0:T(8,128)(2,1)S(1)}, u32[]{:S(2)}, u32[]{:S(2)}) %collective-permute-start.3) | collective-permute-done | bytes 98336 | tf_op jit(solution)/shard_map/ppermute | solution.py:55
  104.4 6.6 %collective-permute-start.4 = (bf16[64,768]{1,0:T(8,128)(2,1)S(1)}, bf16[64,768]{1,0:T(8,128)(2,1)S(1)}, u32[]{:S(2)}, u32[]{:S(2)}) collective-permute-start(bf16[64,768]{1,0:T(8,128)(2,1)S(1)} %add_convert_fusion), channel_id=1, source_target_pairs={{0,256},{256,0},{1,257},{257,1},{2,258},{258,2},{3,259},{259,3},{4... | collective-permute-start | bytes 294920 | tf_op jit(solution)/shard_map/ppermute | solution.py:42
  111.0 0.0 copy-done.2
  111.0 0.1 dynamic_slice.37
  111.1 0.0 collective-permute-done.5
  111.1 10.2 %collective-permute-done.4 = bf16[64,768]{1,0:T(8,128)(2,1)S(1)} collective-permute-done((bf16[64,768]{1,0:T(8,128)(2,1)S(1)}, bf16[64,768]{1,0:T(8,128)(2,1)S(1)}, u32[]{:S(2)}, u32[]{:S(2)}) %collective-permute-start.4) | collective-permute-done | bytes 98336 | tf_op jit(solution)/shard_map/ppermute | solution.py:42
  121.3 0.2 fusion.14
  121.5 1.9 collective-permute-start.6
  123.4 7.6 %collective-permute-done.6 = bf16[64,768]{1,0:T(8,128)(2,1)S(1)} collective-permute-done((bf16[64,768]{1,0:T(8,128)(2,1)S(1)}, bf16[64,768]{1,0:T(8,128)(2,1)S(1)}, u32[]{:S(2)}, u32[]{:S(2)}) %collective-permute-start.6) | collective-permute-done | bytes 98336 | tf_op jit(solution)/shard_map/ppermute | solution.py:55
  131.1 1.1 broadcast_in_dim.5
  132.2 3.5 %all-to-all-start.2 = ((bf16[4,64,2304]{2,1,0:T(8,128)(2,1)}), bf16[4,64,2304]{2,1,0:T(8,128)(2,1)S(1)}, u32[]{:S(2)}, u32[]{:S(2)}) async-start(bf16[4,64,2304]{2,1,0:T(8,128)(2,1)} %broadcast_in_dim.5), calls=%async_computation.2 | async-start | bytes 2359296 | tf_op jit(solution)/shard_map/all_to_all | solution.py:66
  135.8 0.0 copy-start
  135.8 1.0 slice.25
  136.8 0.7 constant_dynamic-slice_fusion
  137.5 3.3 %collective-permute-start.11 = (bf16[256,384]{1,0:T(8,128)(2,1)}, bf16[256,384]{1,0:T(8,128)(2,1)}, u32[]{:S(2)}, u32[]{:S(2)}) collective-permute-start(bf16[256,384]{1,0:T(8,128)(2,1)} %constant_dynamic-slice_fusion), channel_id=1, source_target_pairs={{0,1},{1,0},{2,3},{3,2},{4,5},{5,4},{6,7},{7,6},{8,9},{9,8},{10,11... | collective-permute-start | bytes 589832 | tf_op jit(solution)/shard_map/ppermute | solution.py:42
  140.9 0.0 copy-done
  140.9 1.9 collective-permute-start.8
  142.8 20.9 %all-to-all-done.2 = bf16[4,64,2304]{2,1,0:T(8,128)(2,1)S(1)} async-done(((bf16[4,64,2304]{2,1,0:T(8,128)(2,1)}), bf16[4,64,2304]{2,1,0:T(8,128)(2,1)S(1)}, u32[]{:S(2)}, u32[]{:S(2)}) %all-to-all-start.2) | async-done | bytes 1179680 | tf_op jit(solution)/shard_map/all_to_all | solution.py:66
  163.8 3.3 %convolution_convert_fusion = bf16[256,1536]{1,0:T(8,128)(2,1)} fusion(bf16[1536,384]{1,0:T(8,128)(2,1)} %collective-permute-done.1, bf16[1536,384]{1,0:T(8,128)(2,1)S(1)} %copy-done.4, pred[]{:T(512)S(6)} %eq.9, bf16[256,2304]{1,0:T(8,128)(2,1)S(1)} %bitcast.14), kind=kOutput, calls=%fused_computation.4 | convolution fusion | flops 614989824 | bytes 3538945 | tf_op jit(solution)/shard_map/dot_general | solution.py:30
  167.1 1.0 slice.30
  168.1 3.6 %all-to-all-start.3 = ((bf16[16,16,1536]{2,1,0:T(8,128)(2,1)}), bf16[16,16,1536]{2,1,0:T(8,128)(2,1)S(1)}, u32[]{:S(2)}, u32[]{:S(2)}) async-start(bf16[16,16,1536]{2,1,0:T(8,128)(2,1)} %bitcast.18), calls=%async_computation.3 | async-start | bytes 1572864 | tf_op jit(solution)/shard_map/all_to_all | solution.py:72
  171.8 3.5 %collective-permute-start.9 = (bf16[256,384]{1,0:T(8,128)(2,1)S(1)}, bf16[256,384]{1,0:T(8,128)(2,1)}, u32[]{:S(2)}, u32[]{:S(2)}) collective-permute-start(bf16[256,384]{1,0:T(8,128)(2,1)S(1)} %constant_dynamic-slice_fusion.1), channel_id=1, source_target_pairs={{0,1},{1,0},{2,3},{3,2},{4,5},{5,4},{6,7},{7,6},{8,9},{9,8},{10,11... | collective-permute-start | bytes 589832 | tf_op jit(solution)/shard_map/ppermute | solution.py:42
  175.3 0.6 fusion.17
  175.9 1.9 collective-permute-start.10
  177.8 0.1 convert_reduce_fusion.3
  177.9 0.0 copy-done.1
  177.9 1.7 fusion.15
  179.6 0.0 collective-permute-done.8
  179.6 0.0 collective-permute-done.9
  179.6 2.8 %fusion = bf16[1536,384]{1,0:T(8,128)(2,1)} fusion(f32[1536,384]{1,0:T(8,128)S(1)} %fusion.17, bf16[256,1536]{1,0:T(8,128)(2,1)} %collective-permute-done.8, bf16[256,384]{1,0:T(8,128)(2,1)} %collective-permute-done.9), kind=kOutput, calls=%fused_computation.2 | convolution fusion | flops 303169536 | bytes 4521984 | tf_op jit(solution)/shard_map/dot_general | solution.py:34
  182.4 2.1 %all-to-all-done.3 = bf16[16,16,1536]{2,1,0:T(8,128)(2,1)S(1)} async-done(((bf16[16,16,1536]{2,1,0:T(8,128)(2,1)}), bf16[16,16,1536]{2,1,0:T(8,128)(2,1)S(1)}, u32[]{:S(2)}, u32[]{:S(2)}) %all-to-all-start.3) | async-done | bytes 786464 | tf_op jit(solution)/shard_map/all_to_all | solution.py:72
  184.5 0.1 convert_reduce_fusion.1
  184.6 6.8 %collective-permute-start.7 = (bf16[8,1536]{1,0:T(8,128)(2,1)S(1)}, bf16[8,1536]{1,0:T(8,128)(2,1)S(1)}, u32[]{:S(2)}, u32[]{:S(2)}) collective-permute-start(bf16[8,1536]{1,0:T(8,128)(2,1)S(1)} %dynamic-slice_convert_fusion.1), channel_id=1, source_target_pairs={{0,2},{2,0},{1,3},{3,1},{4,6},{6,4},{5,7},{7,5},{8,10},{10,8},{9,1... | collective-permute-start | bytes 73736 | tf_op jit(solution)/shard_map/ppermute | solution.py:42
  191.5 1.0 convert_reduce_fusion.2
  192.5 0.6 add.82
  193.1 4.9 %collective-permute-done.7 = bf16[8,1536]{1,0:T(8,128)(2,1)S(1)} collective-permute-done((bf16[8,1536]{1,0:T(8,128)(2,1)S(1)}, bf16[8,1536]{1,0:T(8,128)(2,1)S(1)}, u32[]{:S(2)}, u32[]{:S(2)}) %collective-permute-start.7) | collective-permute-done | bytes 24608 | tf_op jit(solution)/shard_map/ppermute | solution.py:42
  198.0 0.6 add_convert_fusion.1
  198.6 0.0 collective-permute-done.11
  198.6 0.0 collective-permute-done.10
  198.6 2.8 %fusion.1 = bf16[1536,384]{1,0:T(8,128)(2,1)} fusion(f32[1536,384]{1,0:T(8,128)S(1)} %fusion.15, bf16[256,1536]{1,0:T(8,128)(2,1)} %collective-permute-done.10, bf16[256,384]{1,0:T(8,128)(2,1)} %collective-permute-done.11), kind=kOutput, calls=%fused_computation.3 | convolution fusion | flops 303169536 | bytes 4521984 | tf_op jit(solution)/shard_map/dot_general | solution.py:34
  (11 shorter events, 0.3 us)
Async XLA Ops:
  0.6 50.1 %copy-start.3 = (bf16[1536,384]{1,0:T(8,128)(2,1)S(1)}, bf16[1536,384]{1,0:T(8,128)(2,1)}, u32[]{:S(2)}) copy-start(bf16[1536,384]{1,0:T(8,128)(2,1)} %param.9) | copy-start | bytes 3538948
  0.6 31.4 %copy-start.4 = (bf16[1536,384]{1,0:T(8,128)(2,1)S(1)}, bf16[1536,384]{1,0:T(8,128)(2,1)}, u32[]{:S(2)}) copy-start(bf16[1536,384]{1,0:T(8,128)(2,1)} %param.7) | copy-start | bytes 3538948
  2.3 17.7 %collective-permute-start = (bf16[8,2304]{1,0:T(8,128)(2,1)S(1)}, bf16[8,2304]{1,0:T(8,128)(2,1)S(1)}, u32[]{:S(2)}, u32[]{:S(2)}) collective-permute-start(bf16[8,2304]{1,0:T(8,128)(2,1)S(1)} %pad_maximum_fusion.2), channel_id=1, source_target_pairs={{0,2},{2,0},{1,3},{3,1},{4,6},{6,4},{5,7},{7,5},{8,10},{10,8},{9,1... | collective-permute-start | bytes 110600 | tf_op jit(solution)/shard_map/ppermute | solution.py:42
  20.0 30.7 %collective-permute-start.2 = (bf16[1536,384]{1,0:T(8,128)(2,1)}, bf16[1536,384]{1,0:T(8,128)(2,1)}, u32[]{:S(2)}, u32[]{:S(2)}) collective-permute-start(bf16[1536,384]{1,0:T(8,128)(2,1)} %param.9), channel_id=1, source_target_pairs={{0,1},{1,0},{2,3},{3,2},{4,5},{5,4},{6,7},{7,6},{8,9},{9,8},{10,11... | collective-permute-start | bytes 3538952 | tf_op jit(solution)/shard_map/ppermute | solution.py:42
  27.6 23.2 %all-to-all-start = ((bf16[16,16,2304]{2,1,0:T(8,128)(2,1)}), bf16[16,16,2304]{2,1,0:T(8,128)(2,1)S(1)}, u32[]{:S(2)}, u32[]{:S(2)}) async-start(bf16[16,16,2304]{2,1,0:T(8,128)(2,1)} %broadcast_in_dim.4), calls=%async_computation | async-start | bytes 2359296 | tf_op jit(solution)/shard_map/all_to_all | solution.py:66
  32.1 21.2 %collective-permute-start.1 = (bf16[1536,384]{1,0:T(8,128)(2,1)S(1)}, bf16[1536,384]{1,0:T(8,128)(2,1)}, u32[]{:S(2)}, u32[]{:S(2)}) collective-permute-start(bf16[1536,384]{1,0:T(8,128)(2,1)S(1)} %copy-done.4), channel_id=1, source_target_pairs={{0,1},{1,0},{2,3},{3,2},{4,5},{5,4},{6,7},{7,6},{8,9},{9,8},{10,11... | collective-permute-start | bytes 3538952 | tf_op jit(solution)/shard_map/ppermute | solution.py:42
  55.8 55.2 %copy-start.2 = (f32[1536]{0:T(1024)S(1)}, f32[1536]{0:T(1024)}, u32[]{:S(2)}) copy-start(f32[1536]{0:T(1024)} %param.8) | copy-start | bytes 18436
  86.5 17.9 %collective-permute-start.3 = (bf16[64,768]{1,0:T(8,128)(2,1)S(1)}, bf16[64,768]{1,0:T(8,128)(2,1)S(1)}, u32[]{:S(2)}, u32[]{:S(2)}) collective-permute-start(bf16[64,768]{1,0:T(8,128)(2,1)S(1)} %dynamic-slice_convert_fusion), channel_id=1, source_target_pairs={{0,258},{2,256},{256,2},{258,0},{1,259},{3,257},{257,3},{259,1},{4... | collective-permute-start | bytes 294920 | tf_op jit(solution)/shard_map/ppermute | solution.py:55
  96.2 14.9 %collective-permute-start.5 = (bf16[64,768]{1,0:T(8,128)(2,1)S(1)}, bf16[64,768]{1,0:T(8,128)(2,1)S(1)}, u32[]{:S(2)}, u32[]{:S(2)}) collective-permute-start(bf16[64,768]{1,0:T(8,128)(2,1)S(1)} %slice.40), channel_id=1, source_target_pairs={{0,256},{256,0},{1,257},{257,1},{2,258},{258,2},{3,259},{259,3},{4... | collective-permute-start | bytes 294920 | tf_op jit(solution)/shard_map/ppermute | solution.py:42
  104.4 16.9 %collective-permute-start.4 = (bf16[64,768]{1,0:T(8,128)(2,1)S(1)}, bf16[64,768]{1,0:T(8,128)(2,1)S(1)}, u32[]{:S(2)}, u32[]{:S(2)}) collective-permute-start(bf16[64,768]{1,0:T(8,128)(2,1)S(1)} %add_convert_fusion), channel_id=1, source_target_pairs={{0,256},{256,0},{1,257},{257,1},{2,258},{258,2},{3,259},{259,3},{4... | collective-permute-start | bytes 294920 | tf_op jit(solution)/shard_map/ppermute | solution.py:42
  121.5 9.6 %collective-permute-start.6 = (bf16[64,768]{1,0:T(8,128)(2,1)S(1)}, bf16[64,768]{1,0:T(8,128)(2,1)S(1)}, u32[]{:S(2)}, u32[]{:S(2)}) collective-permute-start(bf16[64,768]{1,0:T(8,128)(2,1)S(1)} %get-tuple-element.17), channel_id=1, source_target_pairs={{0,258},{2,256},{256,2},{258,0},{1,259},{3,257},{257,3},{259,1},{4... | collective-permute-start | bytes 294920 | tf_op jit(solution)/shard_map/ppermute | solution.py:55
  132.2 31.5 %all-to-all-start.2 = ((bf16[4,64,2304]{2,1,0:T(8,128)(2,1)}), bf16[4,64,2304]{2,1,0:T(8,128)(2,1)S(1)}, u32[]{:S(2)}, u32[]{:S(2)}) async-start(bf16[4,64,2304]{2,1,0:T(8,128)(2,1)} %broadcast_in_dim.5), calls=%async_computation.2 | async-start | bytes 2359296 | tf_op jit(solution)/shard_map/all_to_all | solution.py:66
  135.8 5.1 %copy-start = (bf16[256,768]{1,0:T(8,128)(2,1)}, bf16[256,768]{1,0:T(8,128)(2,1)S(1)}, u32[]{:S(2)}) copy-start(bf16[256,768]{1,0:T(8,128)(2,1)S(1)} %slice.26) | copy-start | bytes 1179652
  137.5 61.1 %collective-permute-start.11 = (bf16[256,384]{1,0:T(8,128)(2,1)}, bf16[256,384]{1,0:T(8,128)(2,1)}, u32[]{:S(2)}, u32[]{:S(2)}) collective-permute-start(bf16[256,384]{1,0:T(8,128)(2,1)} %constant_dynamic-slice_fusion), channel_id=1, source_target_pairs={{0,1},{1,0},{2,3},{3,2},{4,5},{5,4},{6,7},{7,6},{8,9},{9,8},{10,11... | collective-permute-start | bytes 589832 | tf_op jit(solution)/shard_map/ppermute | solution.py:42
  140.9 38.7 %collective-permute-start.8 = (bf16[256,1536]{1,0:T(8,128)(2,1)}, bf16[256,1536]{1,0:T(8,128)(2,1)}, u32[]{:S(2)}, u32[]{:S(2)}) collective-permute-start(bf16[256,1536]{1,0:T(8,128)(2,1)} %slice.25), channel_id=1, source_target_pairs={{0,1},{1,0},{2,3},{3,2},{4,5},{5,4},{6,7},{7,6},{8,9},{9,8},{10,11... | collective-permute-start | bytes 2359304 | tf_op jit(solution)/shard_map/ppermute | solution.py:42
  168.1 16.4 %all-to-all-start.3 = ((bf16[16,16,1536]{2,1,0:T(8,128)(2,1)}), bf16[16,16,1536]{2,1,0:T(8,128)(2,1)S(1)}, u32[]{:S(2)}, u32[]{:S(2)}) async-start(bf16[16,16,1536]{2,1,0:T(8,128)(2,1)} %bitcast.18), calls=%async_computation.3 | async-start | bytes 1572864 | tf_op jit(solution)/shard_map/all_to_all | solution.py:72
  171.7 6.2 %copy-start.1 = (bf16[256,768]{1,0:T(8,128)(2,1)S(1)}, bf16[256,768]{1,0:T(8,128)(2,1)}, u32[]{:S(2)}) copy-start(bf16[256,768]{1,0:T(8,128)(2,1)} %copy-done) | copy-start | bytes 1179652
  171.8 7.9 %collective-permute-start.9 = (bf16[256,384]{1,0:T(8,128)(2,1)S(1)}, bf16[256,384]{1,0:T(8,128)(2,1)}, u32[]{:S(2)}, u32[]{:S(2)}) collective-permute-start(bf16[256,384]{1,0:T(8,128)(2,1)S(1)} %constant_dynamic-slice_fusion.1), channel_id=1, source_target_pairs={{0,1},{1,0},{2,3},{3,2},{4,5},{5,4},{6,7},{7,6},{8,9},{9,8},{10,11... | collective-permute-start | bytes 589832 | tf_op jit(solution)/shard_map/ppermute | solution.py:42
  175.9 22.8 %collective-permute-start.10 = (bf16[256,1536]{1,0:T(8,128)(2,1)}, bf16[256,1536]{1,0:T(8,128)(2,1)}, u32[]{:S(2)}, u32[]{:S(2)}) collective-permute-start(bf16[256,1536]{1,0:T(8,128)(2,1)} %slice.30), channel_id=1, source_target_pairs={{0,1},{1,0},{2,3},{3,2},{4,5},{5,4},{6,7},{7,6},{8,9},{9,8},{10,11... | collective-permute-start | bytes 2359304 | tf_op jit(solution)/shard_map/ppermute | solution.py:42
  184.6 13.4 %collective-permute-start.7 = (bf16[8,1536]{1,0:T(8,128)(2,1)S(1)}, bf16[8,1536]{1,0:T(8,128)(2,1)S(1)}, u32[]{:S(2)}, u32[]{:S(2)}) collective-permute-start(bf16[8,1536]{1,0:T(8,128)(2,1)S(1)} %dynamic-slice_convert_fusion.1), channel_id=1, source_target_pairs={{0,2},{2,0},{1,3},{3,1},{4,6},{6,4},{5,7},{7,5},{8,10},{10,8},{9,1... | collective-permute-start | bytes 73736 | tf_op jit(solution)/shard_map/ppermute | solution.py:42

commit v4 on v3

--- a/solution.py
+++ b/solution.py
@@ -51,13 +51,18 @@
     )
 
 
+def cut(part, axis, dim):
+    size = part.shape[dim] // 2
+    at = lax.axis_index(axis)
+    return part_of(part, at, size, dim), part_of(part, 1 - at, size, dim).astype(bf16)
+
+
 def cross(value):
     return lax.ppermute(value, ("rh", "zh"), CROSS)
 
 
-def both_sum(part, axis):
-    part = part.astype(bf16)
-    return part.astype(f32) + swap(part, axis).astype(f32)
+def widen(mine, axis, dim):
+    return join(mine, swap(mine, axis), axis, dim)
 
 
 def spread(rows, axes):
@@ -70,7 +75,12 @@
 def deal(part, axes):
     n = lax.axis_size(axes)
     got = lax.all_to_all(part.reshape(n, -1, part.shape[1]), axes, 0, 0, tiled=True)
-    return jnp.sum(got.astype(f32), axis=0)
+    if n > 4:
+        return jnp.sum(got.astype(f32), axis=0)
+    total = got[0].astype(f32)
+    for at in range(1, n):
+        total = total + got[at].astype(f32)
+    return total
 
 
 def shards(tokens, cotangent, w_in, b_in, w_out):
@@ -89,27 +99,35 @@
     out_pair = join(w_out, swap(w_out, "core"), "core", 1)
     in_pair = join(w_in, swap(w_in, "core"), "core", 1)
 
-    every = spread(join(kept, got, "zh", 0), GRID)
-    every_x, every_g = every[:, :feat], every[:, feat:]
-    pre = dot(every_x, in_pair).astype(bf16)
+    rows = join(kept, got, "zh", 0)
+    every_x = spread(rows[:, :feat], GRID)
+    pre = dot(every_x, in_pair).reshape(2, 2, -1, half_h)
+    pre_kept, pre_sent = cut(pre, "rl", 1)
+    pre_sent, g_rows = lax.optimization_barrier((pre_sent, rows[:, feat:]))
+    pre_kept, pre_sent = cut(pre_kept + swap(pre_sent, "rl").astype(f32), "rm", 0)
+    every_g = spread(g_rows, GRID)
+    pre_sent, every_g = lax.optimization_barrier((pre_sent, every_g))
+    pre = (pre_kept + swap(pre_sent, "rm").astype(f32))[0, 0].astype(bf16)
     back = against(every_g, out_pair).astype(bf16)
-    sums = deal(jnp.concatenate([pre, back], 1), ROW4)
-    back = sums[:, half_h:]
-    back_kept = part_of(back, zh, half_h, 1)
-    back_sent = part_of(back, 1 - zh, half_h, 1).astype(bf16)
-    pre = both_sum(sums[:, :half_h], "rh")
-    back = both_sum(back_kept + cross(back_sent).astype(f32), "rh")
+    pre, back = lax.optimization_barrier((pre, back))
+    sums = deal(back, ROW4).astype(bf16)
+    pre = pre.astype(f32) + swap(pre, "rh").astype(f32)
 
     act_f, slope = gelu_pair(pre + part_of(b_in, zh, half_h, 0))
     act = act_f.astype(bf16)
-    act = join(act, cross(act), "zh", 1)
-    grad = (back * slope).astype(bf16)
-    gathered = spread(jnp.concatenate([grad, act], 1), ROW4)
-    grad, act = gathered[:, :half_h], gathered[:, half_h:]
+    back_kept = part_of(sums, zh, half_h, 1)
+    back_sent = part_of(sums, 1 - zh, half_h, 1)
+    back_kept, back_sent, act = lax.optimization_barrier((back_kept, back_sent, act))
+    near = back_kept.astype(f32) + swap(back_kept, "rh").astype(f32)
+    far = cross(back_sent).astype(f32) + swap(back_sent, "zh").astype(f32)
+    grad = ((near + far) * slope).astype(bf16)
+    act = join(act, cross(act), "zh", 1)[None, None]
 
+    grad = spread(grad, ROW4)
     part = against(grad, in_pair).astype(bf16)
     part, grad, act = lax.optimization_barrier((part, grad, act))
     summed = deal(part, GRID)
+    act = widen(widen(act, "rm", 0), "rl", 1).reshape(-1, act.shape[-1])
     out_rows = part_of(summed, 1 - zh, tok_dev, 0).astype(bf16)
     own_rows = part_of(summed, zh, tok_dev, 0)
     input_grad = (own_rows + swap(out_rows, "zh").astype(f32)).astype(bf16)

time: 203 us -> 202 us (level)
  starting transfers between devices: 76.5 us -> 116 us
  blocking collectives: 30.4 us -> 0 us
  waiting for transfers between devices: 66.9 us -> 58.6 us
    all_to_all x1 -> x0, blocking collectives: 30.4 us -> none  [deal(): lax.all_to_all(part.reshape(n, -1, part.shape[1]), axes, 0, 0, tiled=True)]
    ppermute x10 -> x15, starting transfers between devices: 53.2 us -> 82.5 us  [swap(): return lax.ppermute(value, axis, SWAP)]
    all_to_all x2 -> x3, waiting for transfers between devices: 37.4 us -> 19.1 us  [spread(): got = lax.all_to_all(sent, axes, 0, 0, tiled=True)]
    all_to_all x1 -> x2, waiting for transfers between devices: 2.07 us -> 10.8 us  [deal(): lax.all_to_all(part.reshape(n, -1, part.shape[1]), axes, 0, 0, tiled=True)]
    all_to_all x1 -> x2, starting transfers between devices: 3.61 us -> 11.5 us  [deal(): lax.all_to_all(part.reshape(n, -1, part.shape[1]), axes, 0, 0, tiled=True)]
    all_to_all x2 -> x3, starting transfers between devices: 8.03 us -> 12.1 us  [spread(): got = lax.all_to_all(sent, axes, 0, 0, tiled=True)]
    dot_general x2, matrix products: 5.82 us -> 8.44 us  [against(): lax.dot_general(left, right, (((1,), (1,)), ((), ())), preferred_element_...]
    dot_general x4, matrix products: 7.92 us -> 5.42 us  [over_rows(): lax.dot_general(left, right, (((0,), (0,)), ((), ())), preferred_element_...]
  transfers between devices with their start and end apart: 15 -> 22, of which waited for: 8 -> 9; matrix products, arithmetic and copies ran while one was open for 9% -> 10% of each run, Pallas kernels for 0% -> 0%
where the time goes in v4:
time: 202 us; the launch traced here: 201 us
  starting transfers between devices  116 us (57%)
  waiting for transfers between devices  58.6 us (29%)
  matrix products  16.3 us (8%)
  other arithmetic  4.68 us (2%)
  local copies, waits for them, and re-layouts  4.25 us (2%)
    ppermute x15, starting transfers between devices, swap(): return lax.ppermute(value, axis, SWAP)  82.5 us
    all_to_all x3, waiting for transfers between devices, spread(): got = lax.all_to_all(sent, axes, 0, 0, tiled=True)  19.1 us
    ppermute x15, waiting for transfers between devices, swap(): return lax.ppermute(value, axis, SWAP)  17.6 us
    all_to_all x3, starting transfers between devices, spread(): got = lax.all_to_all(sent, axes, 0, 0, tiled=True)  12.1 us
    all_to_all x2, starting transfers between devices, deal(): lax.all_to_all(part.reshape(n, -1, part.shape[1]), axes, 0, 0, tiled=True)  11.5 us
    ppermute x2, waiting for transfers between devices, cross(): return lax.ppermute(value, ('rh', 'zh'), CROSS)  11.2 us
    all_to_all x2, waiting for transfers between devices, deal(): lax.all_to_all(part.reshape(n, -1, part.shape[1]), axes, 0, 0, tiled=True)  10.8 us
    ppermute x2, starting transfers between devices, cross(): return lax.ppermute(value, ('rh', 'zh'), CROSS)  10.1 us
  transfers between devices with their start and end apart: 22, of which 9 were waited for; matrix products, arithmetic and copies ran while one was open for 10% of the time, Pallas kernels for 0%

profile of v4, /device:TPU:1, one launch (start us, length us, event | category | flops | bytes accessed | tf_op | source)
XLA Modules:
  0.0 201.2 jit_solution(14134720193342678430)
XLA Ops:
  0.6 0.0 copy-start.1
  0.7 0.8 constant_dynamic-slice_fusion.3
  1.5 0.7 pad_maximum_fusion
  2.2 16.3 %collective-permute-start = (bf16[8,2304]{1,0:T(8,128)(2,1)S(1)}, bf16[8,2304]{1,0:T(8,128)(2,1)S(1)}, u32[]{:S(2)}, u32[]{:S(2)}) collective-permute-start(bf16[8,2304]{1,0:T(8,128)(2,1)S(1)} %pad_maximum_fusion), channel_id=1, source_target_pairs={{0,2},{2,0},{1,3},{3,1},{4,6},{6,4},{5,7},{7,5},{8,10},{10,8},{9,1... | collective-permute-start | bytes 110600 | tf_op jit(solution)/shard_map/ppermute | solution.py:42
  18.5 1.5 collective-permute-done
  20.0 5.6 %collective-permute-start.1 = (bf16[1536,384]{1,0:T(8,128)(2,1)}, bf16[1536,384]{1,0:T(8,128)(2,1)}, u32[]{:S(2)}, u32[]{:S(2)}) collective-permute-start(bf16[1536,384]{1,0:T(8,128)(2,1)} %param.7), channel_id=1, source_target_pairs={{0,1},{1,0},{2,3},{3,2},{4,5},{5,4},{6,7},{7,6},{8,9},{9,8},{10,11... | collective-permute-start | bytes 3538952 | tf_op jit(solution)/shard_map/ppermute | solution.py:42
  25.6 0.8 maximum_select_fusion.8
  26.4 1.0 broadcast_in_dim.6
  27.4 4.5 %all-to-all-start = ((bf16[16,16,1536]{2,1,0:T(8,128)(2,1)}), bf16[16,16,1536]{2,1,0:T(8,128)(2,1)S(1)}, u32[]{:S(2)}, u32[]{:S(2)}) async-start(bf16[16,16,1536]{2,1,0:T(8,128)(2,1)} %broadcast_in_dim.6), calls=%async_computation | async-start | bytes 1572864 | tf_op jit(solution)/shard_map/all_to_all | solution.py:71
  31.9 2.2 %collective-permute-start.4 = (bf16[1536,384]{1,0:T(8,128)(2,1)}, bf16[1536,384]{1,0:T(8,128)(2,1)}, u32[]{:S(2)}, u32[]{:S(2)}) collective-permute-start(bf16[1536,384]{1,0:T(8,128)(2,1)} %param.9), channel_id=1, source_target_pairs={{0,1},{1,0},{2,3},{3,2},{4,5},{5,4},{6,7},{7,6},{8,9},{9,8},{10,11... | collective-permute-start | bytes 3538952 | tf_op jit(solution)/shard_map/ppermute | solution.py:42
  34.1 11.2 %all-to-all-done = bf16[16,16,1536]{2,1,0:T(8,128)(2,1)S(1)} async-done(((bf16[16,16,1536]{2,1,0:T(8,128)(2,1)}), bf16[16,16,1536]{2,1,0:T(8,128)(2,1)S(1)}, u32[]{:S(2)}, u32[]{:S(2)}) %all-to-all-start) | async-done | bytes 786464 | tf_op jit(solution)/shard_map/all_to_all | solution.py:71
  45.3 0.0 collective-permute-done.1
  45.3 2.4 %fusion.7 = f32[2,2,64,768]{3,2,1,0:T(8,128)S(1)} fusion(bf16[2,2,64,1536]{3,2,1,0:T(8,128)(2,1)S(1)} %bitcast.31, bf16[1536,384]{1,0:T(8,128)(2,1)} %collective-permute-done.1, bf16[1536,384]{1,0:T(8,128)(2,1)S(1)} %copy-done.1, pred[]{:T(512)S(6)} %eq.15), kind=kOutput, calls=%fused_computation.13 | convolution fusion | flops 614596608 | bytes 3932161 | tf_op jit(solution)/shard_map/dot_general | solution.py:26
  47.8 3.1 %collective-permute-start.2 = (bf16[2,1,64,768]{3,2,1,0:T(8,128)(2,1)S(1)}, bf16[2,1,64,768]{3,2,1,0:T(8,128)(2,1)S(1)}, u32[]{:S(2)}, u32[]{:S(2)}) collective-permute-start(bf16[2,1,64,768]{3,2,1,0:T(8,128)(2,1)S(1)} %dynamic-slice_convert_fusion), channel_id=1, source_target_pairs={{0,64},{64,0},{1,65},{65,1},{2,66},{66,2},{3,67},{67,3},{4,68},{68... | collective-permute-start | bytes 589832 | tf_op jit(solution)/shard_map/ppermute | solution.py:42
  51.0 0.8 broadcast_in_dim.7
  51.7 4.1 %all-to-all-start.1 = ((bf16[16,16,768]{2,1,0:T(8,128)(2,1)}), bf16[16,16,768]{2,1,0:T(8,128)(2,1)S(1)}, u32[]{:S(2)}, u32[]{:S(2)}) async-start(bf16[16,16,768]{2,1,0:T(8,128)(2,1)} %broadcast_in_dim.7), calls=%async_computation.1 | async-start | bytes 786432 | tf_op jit(solution)/shard_map/all_to_all | solution.py:71
  55.9 0.0 collective-permute-done.2
  55.9 7.9 %all-to-all-done.1 = bf16[16,16,768]{2,1,0:T(8,128)(2,1)S(1)} async-done(((bf16[16,16,768]{2,1,0:T(8,128)(2,1)}), bf16[16,16,768]{2,1,0:T(8,128)(2,1)S(1)}, u32[]{:S(2)}, u32[]{:S(2)}) %all-to-all-start.1) | async-done | bytes 393248 | tf_op jit(solution)/shard_map/all_to_all | solution.py:71
  63.8 2.7 %collective-permute-start.3 = (bf16[1,1,64,768]{3,2,1,0:T(8,128)(2,1)S(1)}, bf16[1,1,64,768]{3,2,1,0:T(8,128)(2,1)S(1)}, u32[]{:S(2)}, u32[]{:S(2)}) collective-permute-start(bf16[1,1,64,768]{3,2,1,0:T(8,128)(2,1)S(1)} %dynamic-slice_convert_fusion.1), channel_id=1, source_target_pairs={{0,128},{128,0},{1,129},{129,1},{2,130},{130,2},{3,131},{131,3},{4... | collective-permute-start | bytes 294920 | tf_op jit(solution)/shard_map/ppermute | solution.py:42
  66.6 0.0 collective-permute-done.4
  66.6 4.3 %convolution_convert_fusion.1 = bf16[256,1536]{1,0:T(8,128)(2,1)} fusion(bf16[256,768]{1,0:T(8,128)(2,1)S(1)} %bitcast.38, bf16[1536,384]{1,0:T(8,128)(2,1)} %collective-permute-done.4, bf16[1536,384]{1,0:T(8,128)(2,1)} %param.9, pred[]{:T(512)S(6)} %eq.15), kind=kOutput, calls=%fused_computation.5 | convolution fusion | flops 614989824 | bytes 3538945 | tf_op jit(solution)/shard_map/dot_general | solution.py:30
  70.9 0.4 collective-permute-done.3
  71.3 3.5 %all-to-all-start.2 = ((bf16[4,64,1536]{2,1,0:T(8,128)(2,1)}), bf16[4,64,1536]{2,1,0:T(8,128)(2,1)S(1)}, u32[]{:S(2)}, u32[]{:S(2)}) async-start(bf16[4,64,1536]{2,1,0:T(8,128)(2,1)} %bitcast.5), calls=%async_computation.2 | async-start | bytes 1572864 | tf_op jit(solution)/shard_map/all_to_all | solution.py:77
  74.8 8.1 %collective-permute-start.5 = (bf16[64,768]{1,0:T(8,128)(2,1)S(1)}, bf16[64,768]{1,0:T(8,128)(2,1)S(1)}, u32[]{:S(2)}, u32[]{:S(2)}) collective-permute-start(bf16[64,768]{1,0:T(8,128)(2,1)S(1)} %fusion.20), channel_id=1, source_target_pairs={{0,256},{256,0},{1,257},{257,1},{2,258},{258,2},{3,259},{259,3},{4... | collective-permute-start | bytes 294920 | tf_op jit(solution)/shard_map/ppermute | solution.py:42
  82.9 0.1 dynamic_slice.59
  83.0 3.0 %collective-permute-done.5 = bf16[64,768]{1,0:T(8,128)(2,1)S(1)} collective-permute-done((bf16[64,768]{1,0:T(8,128)(2,1)S(1)}, bf16[64,768]{1,0:T(8,128)(2,1)S(1)}, u32[]{:S(2)}, u32[]{:S(2)}) %collective-permute-start.5) | collective-permute-done | bytes 98336 | tf_op jit(solution)/shard_map/ppermute | solution.py:42
  85.9 0.1 multiply_convert_fusion
  86.0 10.8 %all-to-all-done.2 = bf16[4,64,1536]{2,1,0:T(8,128)(2,1)S(1)} async-done(((bf16[4,64,1536]{2,1,0:T(8,128)(2,1)}), bf16[4,64,1536]{2,1,0:T(8,128)(2,1)S(1)}, u32[]{:S(2)}, u32[]{:S(2)}) %all-to-all-start.2) | async-done | bytes 786464 | tf_op jit(solution)/shard_map/all_to_all | solution.py:77
  96.8 0.1 add_convert_fusion
  96.9 12.4 %collective-permute-start.8 = (bf16[64,768]{1,0:T(8,128)(2,1)S(1)}, bf16[64,768]{1,0:T(8,128)(2,1)S(1)}, u32[]{:S(2)}, u32[]{:S(2)}) collective-permute-start(bf16[64,768]{1,0:T(8,128)(2,1)S(1)} %get-tuple-element.29), channel_id=1, source_target_pairs={{0,2},{2,0},{1,3},{3,1},{4,6},{6,4},{5,7},{7,5},{8,10},{10,8},{9,1... | collective-permute-start | bytes 294920 | tf_op jit(solution)/shard_map/ppermute | solution.py:42
  109.4 1.9 collective-permute-start.7
  111.3 2.2 %collective-permute-start.6 = (bf16[64,768]{1,0:T(8,128)(2,1)S(1)}, bf16[64,768]{1,0:T(8,128)(2,1)S(1)}, u32[]{:S(2)}, u32[]{:S(2)}) collective-permute-start(bf16[64,768]{1,0:T(8,128)(2,1)S(1)} %get-tuple-element.28), channel_id=1, source_target_pairs={{0,256},{256,0},{1,257},{257,1},{2,258},{258,2},{3,259},{259,3},{4... | collective-permute-start | bytes 294920 | tf_op jit(solution)/shard_map/ppermute | solution.py:42
  113.5 11.2 %collective-permute-done.7 = bf16[64,768]{1,0:T(8,128)(2,1)S(1)} collective-permute-done((bf16[64,768]{1,0:T(8,128)(2,1)S(1)}, bf16[64,768]{1,0:T(8,128)(2,1)S(1)}, u32[]{:S(2)}, u32[]{:S(2)}) %collective-permute-start.7) | collective-permute-done | bytes 98336 | tf_op jit(solution)/shard_map/ppermute | solution.py:61
  124.7 0.0 collective-permute-done.6
  124.7 0.2 fusion.16
  124.9 0.8 broadcast_in_dim.8
  125.7 3.5 %all-to-all-start.3 = ((bf16[4,64,768]{2,1,0:T(8,128)(2,1)}), bf16[4,64,768]{2,1,0:T(8,128)(2,1)S(1)}, u32[]{:S(2)}, u32[]{:S(2)}) async-start(bf16[4,64,768]{2,1,0:T(8,128)(2,1)} %broadcast_in_dim.8), calls=%async_computation.3 | async-start | bytes 786432 | tf_op jit(solution)/shard_map/all_to_all | solution.py:71
  129.2 8.2 %collective-permute-start.9 = (bf16[64,768]{1,0:T(8,128)(2,1)S(1)}, bf16[64,768]{1,0:T(8,128)(2,1)S(1)}, u32[]{:S(2)}, u32[]{:S(2)}) collective-permute-start(bf16[64,768]{1,0:T(8,128)(2,1)S(1)} %multiply_convert_fusion), channel_id=1, source_target_pairs={{0,258},{2,256},{256,2},{258,0},{1,259},{3,257},{257,3},{259,1},{4... | collective-permute-start | bytes 294920 | tf_op jit(solution)/shard_map/ppermute | solution.py:61
  137.4 5.0 %collective-permute-start.11 = (bf16[256,1536]{1,0:T(8,128)(2,1)S(1)}, bf16[256,1536]{1,0:T(8,128)(2,1)S(1)}, u32[]{:S(2)}, u32[]{:S(2)}) collective-permute-start(bf16[256,1536]{1,0:T(8,128)(2,1)S(1)} %bitcast.32), channel_id=1, source_target_pairs={{0,1},{1,0},{2,3},{3,2},{4,5},{5,4},{6,7},{7,6},{8,9},{9,8},{10,11... | collective-permute-start | bytes 2359304 | tf_op jit(solution)/shard_map/ppermute | solution.py:42
  142.4 0.0 collective-permute-done.9
  142.5 4.1 %convolution_convert_fusion = bf16[256,1536]{1,0:T(8,128)(2,1)} fusion(bf16[256,768]{1,0:T(8,128)(2,1)S(1)} %bitcast.34, bf16[1536,384]{1,0:T(8,128)(2,1)} %collective-permute-done.1, bf16[1536,384]{1,0:T(8,128)(2,1)} %param.7, pred[]{:T(512)S(6)} %eq.15), kind=kOutput, calls=%fused_computation.4 | convolution fusion | flops 614989824 | bytes 3538945 | tf_op jit(solution)/shard_map/dot_general | solution.py:30
  146.6 4.5 %collective-permute-start.13 = (bf16[1,1,64,1536]{3,2,1,0:T(8,128)(2,1)S(1)}, bf16[1,1,64,1536]{3,2,1,0:T(8,128)(2,1)}, u32[]{:S(2)}, u32[]{:S(2)}) collective-permute-start(bf16[1,1,64,1536]{3,2,1,0:T(8,128)(2,1)S(1)} %maximum_select_fusion.7), channel_id=1, source_target_pairs={{0,128},{128,0},{1,129},{129,1},{2,130},{130,2},{3,131},{131,3},{4... | collective-permute-start | bytes 589832 | tf_op jit(solution)/shard_map/ppermute | solution.py:42
  151.2 0.7 constant_dynamic-slice_fusion
  151.9 5.3 %collective-permute-start.16 = (bf16[256,384]{1,0:T(8,128)(2,1)}, bf16[256,384]{1,0:T(8,128)(2,1)}, u32[]{:S(2)}, u32[]{:S(2)}) collective-permute-start(bf16[256,384]{1,0:T(8,128)(2,1)} %constant_dynamic-slice_fusion), channel_id=1, source_target_pairs={{0,1},{1,0},{2,3},{3,2},{4,5},{5,4},{6,7},{7,6},{8,9},{9,8},{10,11... | collective-permute-start | bytes 589832 | tf_op jit(solution)/shard_map/ppermute | solution.py:42
  157.1 8.0 %all-to-all-start.4 = ((bf16[16,16,1536]{2,1,0:T(8,128)(2,1)}), bf16[16,16,1536]{2,1,0:T(8,128)(2,1)S(1)}, u32[]{:S(2)}, u32[]{:S(2)}) async-start(bf16[16,16,1536]{2,1,0:T(8,128)(2,1)} %bitcast.11), calls=%async_computation.4 | async-start | bytes 1572864 | tf_op jit(solution)/shard_map/all_to_all | solution.py:77
  165.2 2.2 %collective-permute-start.12 = (bf16[256,384]{1,0:T(8,128)(2,1)S(1)}, bf16[256,384]{1,0:T(8,128)(2,1)S(1)}, u32[]{:S(2)}, u32[]{:S(2)}) collective-permute-start(bf16[256,384]{1,0:T(8,128)(2,1)S(1)} %constant_dynamic-slice_fusion.1), channel_id=1, source_target_pairs={{0,1},{1,0},{2,3},{3,2},{4,5},{5,4},{6,7},{7,6},{8,9},{9,8},{10,11... | collective-permute-start | bytes 589832 | tf_op jit(solution)/shard_map/ppermute | solution.py:42
  167.4 0.0 collective-permute-done.13
  167.4 1.1 maximum_select_fusion.6
  168.5 1.9 collective-permute-start.14
  170.4 0.6 fusion.18
  171.0 0.1 convert_reduce_fusion.2
  171.1 0.0 collective-permute-done.12
  171.1 1.6 fusion
  172.8 8.1 %collective-permute-done.14 = bf16[2,1,64,1536]{3,2,1,0:T(8,128)(2,1)S(1)} collective-permute-done((bf16[2,1,64,1536]{3,2,1,0:T(8,128)(2,1)S(1)}, bf16[2,1,64,1536]{3,2,1,0:T(8,128)(2,1)S(1)}, u32[]{:S(2)}, u32[]{:S(2)}) %collective-permute-start.14) | collective-permute-done | bytes 393248 | tf_op jit(solution)/shard_map/ppermute | solution.py:42
  180.9 0.1 maximum_select_fusion.3
  181.0 2.9 %collective-permute-start.15 = (bf16[256,1536]{1,0:T(8,128)(2,1)S(1)}, bf16[256,1536]{1,0:T(8,128)(2,1)S(1)}, u32[]{:S(2)}, u32[]{:S(2)}) collective-permute-start(bf16[256,1536]{1,0:T(8,128)(2,1)S(1)} %bitcast.29), channel_id=1, source_target_pairs={{0,1},{1,0},{2,3},{3,2},{4,5},{5,4},{6,7},{7,6},{8,9},{9,8},{10,11... | collective-permute-start | bytes 2359304 | tf_op jit(solution)/shard_map/ppermute | solution.py:42
  184.0 0.1 convert_reduce_fusion
  184.1 8.0 %collective-permute-start.10 = (bf16[8,1536]{1,0:T(8,128)(2,1)S(1)}, bf16[8,1536]{1,0:T(8,128)(2,1)S(1)}, u32[]{:S(2)}, u32[]{:S(2)}) collective-permute-start(bf16[8,1536]{1,0:T(8,128)(2,1)S(1)} %dynamic-slice_convert_fusion.2), channel_id=1, source_target_pairs={{0,2},{2,0},{1,3},{3,1},{4,6},{6,4},{5,7},{7,5},{8,10},{10,8},{9,1... | collective-permute-start | bytes 73736 | tf_op jit(solution)/shard_map/ppermute | solution.py:42
  192.1 0.1 convert_reduce_fusion.1
  192.2 0.6 add.127
  192.8 4.6 %collective-permute-done.10 = bf16[8,1536]{1,0:T(8,128)(2,1)S(1)} collective-permute-done((bf16[8,1536]{1,0:T(8,128)(2,1)S(1)}, bf16[8,1536]{1,0:T(8,128)(2,1)S(1)}, u32[]{:S(2)}, u32[]{:S(2)}) %collective-permute-start.10) | collective-permute-done | bytes 24608 | tf_op jit(solution)/shard_map/ppermute | solution.py:42
  197.4 0.6 add_convert_fusion.2
  198.0 1.5 fusion.26
  199.5 1.7 fusion.1
  (19 shorter events, 0.3 us)
Async XLA Ops:
  0.6 44.7 %copy-start.1 = (bf16[1536,384]{1,0:T(8,128)(2,1)S(1)}, bf16[1536,384]{1,0:T(8,128)(2,1)}, u32[]{:S(2)}) copy-start(bf16[1536,384]{1,0:T(8,128)(2,1)} %param.7) | copy-start | bytes 3538948
  2.2 17.7 %collective-permute-start = (bf16[8,2304]{1,0:T(8,128)(2,1)S(1)}, bf16[8,2304]{1,0:T(8,128)(2,1)S(1)}, u32[]{:S(2)}, u32[]{:S(2)}) collective-permute-start(bf16[8,2304]{1,0:T(8,128)(2,1)S(1)} %pad_maximum_fusion), channel_id=1, source_target_pairs={{0,2},{2,0},{1,3},{3,1},{4,6},{6,4},{5,7},{7,5},{8,10},{10,8},{9,1... | collective-permute-start | bytes 110600 | tf_op jit(solution)/shard_map/ppermute | solution.py:42
  20.0 25.4 %collective-permute-start.1 = (bf16[1536,384]{1,0:T(8,128)(2,1)}, bf16[1536,384]{1,0:T(8,128)(2,1)}, u32[]{:S(2)}, u32[]{:S(2)}) collective-permute-start(bf16[1536,384]{1,0:T(8,128)(2,1)} %param.7), channel_id=1, source_target_pairs={{0,1},{1,0},{2,3},{3,2},{4,5},{5,4},{6,7},{7,6},{8,9},{9,8},{10,11... | collective-permute-start | bytes 3538952 | tf_op jit(solution)/shard_map/ppermute | solution.py:42
  27.4 18.0 %all-to-all-start = ((bf16[16,16,1536]{2,1,0:T(8,128)(2,1)}), bf16[16,16,1536]{2,1,0:T(8,128)(2,1)S(1)}, u32[]{:S(2)}, u32[]{:S(2)}) async-start(bf16[16,16,1536]{2,1,0:T(8,128)(2,1)} %broadcast_in_dim.6), calls=%async_computation | async-start | bytes 1572864 | tf_op jit(solution)/shard_map/all_to_all | solution.py:71
  31.9 34.7 %collective-permute-start.4 = (bf16[1536,384]{1,0:T(8,128)(2,1)}, bf16[1536,384]{1,0:T(8,128)(2,1)}, u32[]{:S(2)}, u32[]{:S(2)}) collective-permute-start(bf16[1536,384]{1,0:T(8,128)(2,1)} %param.9), channel_id=1, source_target_pairs={{0,1},{1,0},{2,3},{3,2},{4,5},{5,4},{6,7},{7,6},{8,9},{9,8},{10,11... | collective-permute-start | bytes 3538952 | tf_op jit(solution)/shard_map/ppermute | solution.py:42
  47.8 8.0 %collective-permute-start.2 = (bf16[2,1,64,768]{3,2,1,0:T(8,128)(2,1)S(1)}, bf16[2,1,64,768]{3,2,1,0:T(8,128)(2,1)S(1)}, u32[]{:S(2)}, u32[]{:S(2)}) collective-permute-start(bf16[2,1,64,768]{3,2,1,0:T(8,128)(2,1)S(1)} %dynamic-slice_convert_fusion), channel_id=1, source_target_pairs={{0,64},{64,0},{1,65},{65,1},{2,66},{66,2},{3,67},{67,3},{4,68},{68... | collective-permute-start | bytes 589832 | tf_op jit(solution)/shard_map/ppermute | solution.py:42
  51.7 12.1 %all-to-all-start.1 = ((bf16[16,16,768]{2,1,0:T(8,128)(2,1)}), bf16[16,16,768]{2,1,0:T(8,128)(2,1)S(1)}, u32[]{:S(2)}, u32[]{:S(2)}) async-start(bf16[16,16,768]{2,1,0:T(8,128)(2,1)} %broadcast_in_dim.7), calls=%async_computation.1 | async-start | bytes 786432 | tf_op jit(solution)/shard_map/all_to_all | solution.py:71
  63.8 19.1 %copy-start = (f32[1536]{0:T(1024)S(1)}, f32[1536]{0:T(1024)}, u32[]{:S(2)}) copy-start(f32[1536]{0:T(1024)} %param.8) | copy-start | bytes 18436
  63.8 7.4 %collective-permute-start.3 = (bf16[1,1,64,768]{3,2,1,0:T(8,128)(2,1)S(1)}, bf16[1,1,64,768]{3,2,1,0:T(8,128)(2,1)S(1)}, u32[]{:S(2)}, u32[]{:S(2)}) collective-permute-start(bf16[1,1,64,768]{3,2,1,0:T(8,128)(2,1)S(1)} %dynamic-slice_convert_fusion.1), channel_id=1, source_target_pairs={{0,128},{128,0},{1,129},{129,1},{2,130},{130,2},{3,131},{131,3},{4... | collective-permute-start | bytes 294920 | tf_op jit(solution)/shard_map/ppermute | solution.py:42
  71.3 25.5 %all-to-all-start.2 = ((bf16[4,64,1536]{2,1,0:T(8,128)(2,1)}), bf16[4,64,1536]{2,1,0:T(8,128)(2,1)S(1)}, u32[]{:S(2)}, u32[]{:S(2)}) async-start(bf16[4,64,1536]{2,1,0:T(8,128)(2,1)} %bitcast.5), calls=%async_computation.2 | async-start | bytes 1572864 | tf_op jit(solution)/shard_map/all_to_all | solution.py:77
  74.8 11.1 %collective-permute-start.5 = (bf16[64,768]{1,0:T(8,128)(2,1)S(1)}, bf16[64,768]{1,0:T(8,128)(2,1)S(1)}, u32[]{:S(2)}, u32[]{:S(2)}) collective-permute-start(bf16[64,768]{1,0:T(8,128)(2,1)S(1)} %fusion.20), channel_id=1, source_target_pairs={{0,256},{256,0},{1,257},{257,1},{2,258},{258,2},{3,259},{259,3},{4... | collective-permute-start | bytes 294920 | tf_op jit(solution)/shard_map/ppermute | solution.py:42
  96.9 16.6 %collective-permute-start.8 = (bf16[64,768]{1,0:T(8,128)(2,1)S(1)}, bf16[64,768]{1,0:T(8,128)(2,1)S(1)}, u32[]{:S(2)}, u32[]{:S(2)}) collective-permute-start(bf16[64,768]{1,0:T(8,128)(2,1)S(1)} %get-tuple-element.29), channel_id=1, source_target_pairs={{0,2},{2,0},{1,3},{3,1},{4,6},{6,4},{5,7},{7,5},{8,10},{10,8},{9,1... | collective-permute-start | bytes 294920 | tf_op jit(solution)/shard_map/ppermute | solution.py:42
  109.4 15.4 %collective-permute-start.7 = (bf16[64,768]{1,0:T(8,128)(2,1)S(1)}, bf16[64,768]{1,0:T(8,128)(2,1)S(1)}, u32[]{:S(2)}, u32[]{:S(2)}) collective-permute-start(bf16[64,768]{1,0:T(8,128)(2,1)S(1)} %get-tuple-element.29), channel_id=1, source_target_pairs={{0,258},{2,256},{256,2},{258,0},{1,259},{3,257},{257,3},{259,1},{4... | collective-permute-start | bytes 294920 | tf_op jit(solution)/shard_map/ppermute | solution.py:61
  111.3 13.4 %collective-permute-start.6 = (bf16[64,768]{1,0:T(8,128)(2,1)S(1)}, bf16[64,768]{1,0:T(8,128)(2,1)S(1)}, u32[]{:S(2)}, u32[]{:S(2)}) collective-permute-start(bf16[64,768]{1,0:T(8,128)(2,1)S(1)} %get-tuple-element.28), channel_id=1, source_target_pairs={{0,256},{256,0},{1,257},{257,1},{2,258},{258,2},{3,259},{259,3},{4... | collective-permute-start | bytes 294920 | tf_op jit(solution)/shard_map/ppermute | solution.py:42
  125.7 16.8 %all-to-all-start.3 = ((bf16[4,64,768]{2,1,0:T(8,128)(2,1)}), bf16[4,64,768]{2,1,0:T(8,128)(2,1)S(1)}, u32[]{:S(2)}, u32[]{:S(2)}) async-start(bf16[4,64,768]{2,1,0:T(8,128)(2,1)} %broadcast_in_dim.8), calls=%async_computation.3 | async-start | bytes 786432 | tf_op jit(solution)/shard_map/all_to_all | solution.py:71
  129.2 13.2 %collective-permute-start.9 = (bf16[64,768]{1,0:T(8,128)(2,1)S(1)}, bf16[64,768]{1,0:T(8,128)(2,1)S(1)}, u32[]{:S(2)}, u32[]{:S(2)}) collective-permute-start(bf16[64,768]{1,0:T(8,128)(2,1)S(1)} %multiply_convert_fusion), channel_id=1, source_target_pairs={{0,258},{2,256},{256,2},{258,0},{1,259},{3,257},{257,3},{259,1},{4... | collective-permute-start | bytes 294920 | tf_op jit(solution)/shard_map/ppermute | solution.py:61
  137.4 33.7 %collective-permute-start.11 = (bf16[256,1536]{1,0:T(8,128)(2,1)S(1)}, bf16[256,1536]{1,0:T(8,128)(2,1)S(1)}, u32[]{:S(2)}, u32[]{:S(2)}) collective-permute-start(bf16[256,1536]{1,0:T(8,128)(2,1)S(1)} %bitcast.32), channel_id=1, source_target_pairs={{0,1},{1,0},{2,3},{3,2},{4,5},{5,4},{6,7},{7,6},{8,9},{9,8},{10,11... | collective-permute-start | bytes 2359304 | tf_op jit(solution)/shard_map/ppermute | solution.py:42
  146.6 20.8 %collective-permute-start.13 = (bf16[1,1,64,1536]{3,2,1,0:T(8,128)(2,1)S(1)}, bf16[1,1,64,1536]{3,2,1,0:T(8,128)(2,1)}, u32[]{:S(2)}, u32[]{:S(2)}) collective-permute-start(bf16[1,1,64,1536]{3,2,1,0:T(8,128)(2,1)S(1)} %maximum_select_fusion.7), channel_id=1, source_target_pairs={{0,128},{128,0},{1,129},{129,1},{2,130},{130,2},{3,131},{131,3},{4... | collective-permute-start | bytes 589832 | tf_op jit(solution)/shard_map/ppermute | solution.py:42
  151.9 46.1 %collective-permute-start.16 = (bf16[256,384]{1,0:T(8,128)(2,1)}, bf16[256,384]{1,0:T(8,128)(2,1)}, u32[]{:S(2)}, u32[]{:S(2)}) collective-permute-start(bf16[256,384]{1,0:T(8,128)(2,1)} %constant_dynamic-slice_fusion), channel_id=1, source_target_pairs={{0,1},{1,0},{2,3},{3,2},{4,5},{5,4},{6,7},{7,6},{8,9},{9,8},{10,11... | collective-permute-start | bytes 589832 | tf_op jit(solution)/shard_map/ppermute | solution.py:42
  157.1 26.8 %all-to-all-start.4 = ((bf16[16,16,1536]{2,1,0:T(8,128)(2,1)}), bf16[16,16,1536]{2,1,0:T(8,128)(2,1)S(1)}, u32[]{:S(2)}, u32[]{:S(2)}) async-start(bf16[16,16,1536]{2,1,0:T(8,128)(2,1)} %bitcast.11), calls=%async_computation.4 | async-start | bytes 1572864 | tf_op jit(solution)/shard_map/all_to_all | solution.py:77
  165.2 5.9 %collective-permute-start.12 = (bf16[256,384]{1,0:T(8,128)(2,1)S(1)}, bf16[256,384]{1,0:T(8,128)(2,1)S(1)}, u32[]{:S(2)}, u32[]{:S(2)}) collective-permute-start(bf16[256,384]{1,0:T(8,128)(2,1)S(1)} %constant_dynamic-slice_fusion.1), channel_id=1, source_target_pairs={{0,1},{1,0},{2,3},{3,2},{4,5},{5,4},{6,7},{7,6},{8,9},{9,8},{10,11... | collective-permute-start | bytes 589832 | tf_op jit(solution)/shard_map/ppermute | solution.py:42
  168.5 12.4 %collective-permute-start.14 = (bf16[2,1,64,1536]{3,2,1,0:T(8,128)(2,1)S(1)}, bf16[2,1,64,1536]{3,2,1,0:T(8,128)(2,1)S(1)}, u32[]{:S(2)}, u32[]{:S(2)}) collective-permute-start(bf16[2,1,64,1536]{3,2,1,0:T(8,128)(2,1)S(1)} %maximum_select_fusion.6), channel_id=1, source_target_pairs={{0,64},{64,0},{1,65},{65,1},{2,66},{66,2},{3,67},{67,3},{4,68},{68... | collective-permute-start | bytes 1179656 | tf_op jit(solution)/shard_map/ppermute | solution.py:42
  181.0 17.0 %collective-permute-start.15 = (bf16[256,1536]{1,0:T(8,128)(2,1)S(1)}, bf16[256,1536]{1,0:T(8,128)(2,1)S(1)}, u32[]{:S(2)}, u32[]{:S(2)}) collective-permute-start(bf16[256,1536]{1,0:T(8,128)(2,1)S(1)} %bitcast.29), channel_id=1, source_target_pairs={{0,1},{1,0},{2,3},{3,2},{4,5},{5,4},{6,7},{7,6},{8,9},{9,8},{10,11... | collective-permute-start | bytes 2359304 | tf_op jit(solution)/shard_map/ppermute | solution.py:42
  184.1 13.3 %collective-permute-start.10 = (bf16[8,1536]{1,0:T(8,128)(2,1)S(1)}, bf16[8,1536]{1,0:T(8,128)(2,1)S(1)}, u32[]{:S(2)}, u32[]{:S(2)}) collective-permute-start(bf16[8,1536]{1,0:T(8,128)(2,1)S(1)} %dynamic-slice_convert_fusion.2), channel_id=1, source_target_pairs={{0,2},{2,0},{1,3},{3,1},{4,6},{6,4},{5,7},{7,5},{8,10},{10,8},{9,1... | collective-permute-start | bytes 73736 | tf_op jit(solution)/shard_map/ppermute | solution.py:42

commit v5 on v4

--- a/solution.py
+++ b/solution.py
@@ -10,6 +10,7 @@
 CROSS = [(0, 3), (1, 2), (2, 1), (3, 0)]
 GRID = ("x", "y")
 ROW4 = ("rm", "rl")
+RING4 = ("rh", "zh")
 
 
 def gelu_pair(pre):
@@ -92,54 +93,58 @@
     quarter_d = w_out.shape[1]
     half_d = 2 * quarter_d
 
+    kept = jnp.concatenate([tokens, part_of(cotangent, zh, half_d, 1)], 1)
     sent = jnp.concatenate([tokens, part_of(cotangent, 1 - zh, half_d, 1)], 1)
-    kept = jnp.concatenate([tokens, part_of(cotangent, zh, half_d, 1)], 1)
     got = swap(sent, "zh")
-    w_out, w_in, got = lax.optimization_barrier((w_out, w_in, got))
+    own = spread(kept, GRID)
+    got, own, w_in, w_out = lax.optimization_barrier((got, own, w_in, w_out))
+    in_pair = join(w_in, swap(w_in, "core"), "core", 1)
     out_pair = join(w_out, swap(w_out, "core"), "core", 1)
-    in_pair = join(w_in, swap(w_in, "core"), "core", 1)
+    other = spread(got, GRID)
 
-    rows = join(kept, got, "zh", 0)
-    every_x = spread(rows[:, :feat], GRID)
-    pre = dot(every_x, in_pair).reshape(2, 2, -1, half_h)
-    pre_kept, pre_sent = cut(pre, "rl", 1)
-    pre_sent, g_rows = lax.optimization_barrier((pre_sent, rows[:, feat:]))
-    pre_kept, pre_sent = cut(pre_kept + swap(pre_sent, "rl").astype(f32), "rm", 0)
-    every_g = spread(g_rows, GRID)
-    pre_sent, every_g = lax.optimization_barrier((pre_sent, every_g))
-    pre = (pre_kept + swap(pre_sent, "rm").astype(f32))[0, 0].astype(bf16)
+    def by_token(mine, theirs):
+        mine, theirs = (v.reshape(-1, tok_dev, v.shape[1]) for v in (mine, theirs))
+        return join(mine, theirs, "zh", 1).reshape(-1, mine.shape[2])
+
+    every = by_token(own, other)
+    every_x, every_g = every[:, :feat], every[:, feat:]
+    pre = dot(every_x, in_pair).astype(bf16)
     back = against(every_g, out_pair).astype(bf16)
+    pre = deal(pre, ROW4).astype(bf16)
     pre, back = lax.optimization_barrier((pre, back))
+    pre = pre.astype(f32) + swap(pre, "rh").astype(f32)
     sums = deal(back, ROW4).astype(bf16)
-    pre = pre.astype(f32) + swap(pre, "rh").astype(f32)
 
     act_f, slope = gelu_pair(pre + part_of(b_in, zh, half_h, 0))
     act = act_f.astype(bf16)
-    back_kept = part_of(sums, zh, half_h, 1)
-    back_sent = part_of(sums, 1 - zh, half_h, 1)
-    back_kept, back_sent, act = lax.optimization_barrier((back_kept, back_sent, act))
-    near = back_kept.astype(f32) + swap(back_kept, "rh").astype(f32)
-    far = cross(back_sent).astype(f32) + swap(back_sent, "zh").astype(f32)
-    grad = ((near + far) * slope).astype(bf16)
-    act = join(act, cross(act), "zh", 1)[None, None]
+    crossed = cross(act)
+    pair_x = swap(every_x, "core")
+    pair_g = swap(part_of(every_g, 1 - core, quarter_d, 1), "core")
+    sums, slope, crossed, pair_x, pair_g = lax.optimization_barrier(
+        (sums, slope, crossed, pair_x, pair_g)
+    )
+    act = join(act, crossed, "zh", 1)[None, None]
+    halves = jnp.stack([sums[:, :half_h], sums[:, half_h:]])
+    halves = jnp.concatenate([halves, halves], 0).reshape(-1, half_h)
+    grad = (deal(halves, RING4) * slope).astype(bf16)
 
     grad = spread(grad, ROW4)
     part = against(grad, in_pair).astype(bf16)
     part, grad, act = lax.optimization_barrier((part, grad, act))
     summed = deal(part, GRID)
-    act = widen(widen(act, "rm", 0), "rl", 1).reshape(-1, act.shape[-1])
+    act = widen(act, "rm", 0)
+    grad_sent, act = lax.optimization_barrier((part_of(grad, 1 - core, quarter, 1), act))
+    act = widen(act, "rl", 1).reshape(-1, act.shape[-1])
     out_rows = part_of(summed, 1 - zh, tok_dev, 0).astype(bf16)
     own_rows = part_of(summed, zh, tok_dev, 0)
     input_grad = (own_rows + swap(out_rows, "zh").astype(f32)).astype(bf16)
 
-    pair_x = swap(every_x, "core")
     own_grad = part_of(grad, core, quarter, 1)
-    pair_grad = swap(part_of(grad, 1 - core, quarter, 1), "core")
+    pair_grad = swap(grad_sent, "core")
     w_in_grad = (over_rows(every_x, own_grad) + over_rows(pair_x, pair_grad)).astype(bf16)
     b_in_grad = jnp.sum(own_grad.astype(f32), 0) + jnp.sum(pair_grad.astype(f32), 0)
 
     own_g = part_of(every_g, core, quarter_d, 1)
-    pair_g = swap(part_of(every_g, 1 - core, quarter_d, 1), "core")
     pair_act = swap(act, "core")
     w_out_grad = (over_rows(act, own_g) + over_rows(pair_act, pair_g)).astype(bf16)
     return (input_grad, w_in_grad, b_in_grad, w_out_grad)

time: 202 us -> 206 us (1.020)
  blocking collectives: 0 us -> 23.2 us
  starting transfers between devices: 116 us -> 105 us
  waiting for transfers between devices: 58.6 us -> 48.6 us
    ppermute x15 -> x11, starting transfers between devices: 82.5 us -> 50.6 us  [swap(): return lax.ppermute(value, axis, SWAP)]
    all_to_all x0 -> x1, blocking collectives: none -> 23.2 us  [deal(): lax.all_to_all(part.reshape(n, -1, part.shape[1]), axes, 0, 0, tiled=True)]
    all_to_all x3, starting transfers between devices: 12.1 us -> 32.2 us  [spread(): got = lax.all_to_all(sent, axes, 0, 0, tiled=True)]
    ppermute x2 -> x1, waiting for transfers between devices: 11.2 us -> 2.17 us  [cross(): return lax.ppermute(value, ('rh', 'zh'), CROSS)]
    ppermute x15 -> x11, waiting for transfers between devices: 17.6 us -> 23.7 us  [swap(): return lax.ppermute(value, axis, SWAP)]
    all_to_all x2 -> x3, waiting for transfers between devices: 10.8 us -> 5.63 us  [deal(): lax.all_to_all(part.reshape(n, -1, part.shape[1]), axes, 0, 0, tiled=True)]
    all_to_all x2 -> x3, starting transfers between devices: 11.5 us -> 12.3 us  [deal(): lax.all_to_all(part.reshape(n, -1, part.shape[1]), axes, 0, 0, tiled=True)]
    ppermute x2 -> x1, starting transfers between devices: 10.1 us -> 9.65 us  [cross(): return lax.ppermute(value, ('rh', 'zh'), CROSS)]
  transfers between devices with their start and end apart: 22 -> 18, of which waited for: 9 -> 9; matrix products, arithmetic and copies ran while one was open for 10% -> 8% of each run, Pallas kernels for 0% -> 0%
where the time goes in v5:
time: 206 us; the launch traced here: 205 us
  starting transfers between devices  105 us (51%)
  waiting for transfers between devices  48.6 us (24%)
  blocking collectives  23.2 us (11%)
  matrix products  18.2 us (9%)
  other arithmetic  4.68 us (2%)
  local copies, waits for them, and re-layouts  4.23 us (2%)
    ppermute x11, starting transfers between devices, swap(): return lax.ppermute(value, axis, SWAP)  50.6 us
    all_to_all x3, starting transfers between devices, spread(): got = lax.all_to_all(sent, axes, 0, 0, tiled=True)  32.2 us
    ppermute x11, waiting for transfers between devices, swap(): return lax.ppermute(value, axis, SWAP)  23.7 us
    all_to_all x1, blocking collectives, deal(): lax.all_to_all(part.reshape(n, -1, part.shape[1]), axes, 0, 0, tiled=True)  23.2 us
    all_to_all x3, waiting for transfers between devices, spread(): got = lax.all_to_all(sent, axes, 0, 0, tiled=True)  17.1 us
    all_to_all x3, starting transfers between devices, deal(): lax.all_to_all(part.reshape(n, -1, part.shape[1]), axes, 0, 0, tiled=True)  12.3 us
    ppermute x1, starting transfers between devices, cross(): return lax.ppermute(value, ('rh', 'zh'), CROSS)  9.65 us
    dot_general x2, matrix products, against(): lax.dot_general(left, right, (((1,), (1,)), ((), ())), preferred_element_...  7.46 us
  transfers between devices with their start and end apart: 18, of which 9 were waited for; matrix products, arithmetic and copies ran while one was open for 8% of the time, Pallas kernels for 0%

profile of v5, /device:TPU:1, one launch (start us, length us, event | category | flops | bytes accessed | tf_op | source)
XLA Modules:
  0.0 204.6 jit_solution(673692072552920572)
XLA Ops:
  0.6 0.8 constant_dynamic-slice_fusion.2
  1.5 0.7 pad_maximum_fusion.1
  2.2 0.9 broadcast_in_dim.6
  3.1 7.6 %all-to-all-start = ((bf16[16,8,2304]{2,1,0:T(8,128)(2,1)}), bf16[16,8,2304]{2,1,0:T(8,128)(2,1)S(1)}, u32[]{:S(2)}, u32[]{:S(2)}) async-start(bf16[16,8,2304]{2,1,0:T(8,128)(2,1)} %broadcast_in_dim.6), calls=%async_computation | async-start | bytes 1179648 | tf_op jit(solution)/shard_map/all_to_all | solution.py:72
  10.7 15.4 %collective-permute-start = (bf16[8,2304]{1,0:T(8,128)(2,1)S(1)}, bf16[8,2304]{1,0:T(8,128)(2,1)S(1)}, u32[]{:S(2)}, u32[]{:S(2)}) collective-permute-start(bf16[8,2304]{1,0:T(8,128)(2,1)S(1)} %get-tuple-element.41), channel_id=1, source_target_pairs={{0,2},{2,0},{1,3},{3,1},{4,6},{6,4},{5,7},{7,5},{8,10},{10,8},{9,1... | collective-permute-start | bytes 110600 | tf_op jit(solution)/shard_map/ppermute | solution.py:43
  26.1 1.4 collective-permute-done
  27.6 0.0 all-to-all-done
  27.6 3.6 %collective-permute-start.1 = (bf16[1536,384]{1,0:T(8,128)(2,1)}, bf16[1536,384]{1,0:T(8,128)(2,1)}, u32[]{:S(2)}, u32[]{:S(2)}) collective-permute-start(bf16[1536,384]{1,0:T(8,128)(2,1)} %param.7), channel_id=1, source_target_pairs={{0,1},{1,0},{2,3},{3,2},{4,5},{5,4},{6,7},{7,6},{8,9},{9,8},{10,11... | collective-permute-start | bytes 3538952 | tf_op jit(solution)/shard_map/ppermute | solution.py:43
  31.2 0.9 broadcast_in_dim.7
  32.0 6.9 %all-to-all-start.1 = ((bf16[16,8,2304]{2,1,0:T(8,128)(2,1)}), bf16[16,8,2304]{2,1,0:T(8,128)(2,1)S(1)}, u32[]{:S(2)}, u32[]{:S(2)}) async-start(bf16[16,8,2304]{2,1,0:T(8,128)(2,1)} %broadcast_in_dim.7), calls=%async_computation.1 | async-start | bytes 1179648 | tf_op jit(solution)/shard_map/all_to_all | solution.py:72
  39.0 2.2 %collective-permute-start.2 = (bf16[1536,384]{1,0:T(8,128)(2,1)S(1)}, bf16[1536,384]{1,0:T(8,128)(2,1)}, u32[]{:S(2)}, u32[]{:S(2)}) collective-permute-start(bf16[1536,384]{1,0:T(8,128)(2,1)S(1)} %copy-done.1), channel_id=1, source_target_pairs={{0,1},{1,0},{2,3},{3,2},{4,5},{5,4},{6,7},{7,6},{8,9},{9,8},{10,11... | collective-permute-start | bytes 3538952 | tf_op jit(solution)/shard_map/ppermute | solution.py:43
  41.2 8.5 %all-to-all-done.1 = bf16[16,8,2304]{2,1,0:T(8,128)(2,1)S(1)} async-done(((bf16[16,8,2304]{2,1,0:T(8,128)(2,1)}), bf16[16,8,2304]{2,1,0:T(8,128)(2,1)S(1)}, u32[]{:S(2)}, u32[]{:S(2)}) %all-to-all-start.1) | async-done | bytes 589856 | tf_op jit(solution)/shard_map/all_to_all | solution.py:72
  49.7 0.2 maximum_select_fusion.3
  50.0 0.0 collective-permute-done.1
  50.0 4.0 %convolution_convert_fusion.2 = bf16[256,768]{1,0:T(8,128)(2,1)} fusion(bf16[1536,384]{1,0:T(8,128)(2,1)} %collective-permute-done.1, bf16[1536,384]{1,0:T(8,128)(2,1)} %param.7, pred[]{:T(512)S(6)} %eq.15, bf16[256,2304]{1,0:T(8,128)(2,1)S(1)} %bitcast.28), kind=kOutput, calls=%fused_computation.15 | convolution fusion | flops 614793216 | bytes 3538945 | tf_op jit(solution)/shard_map/dot_general | solution.py:27
  54.0 3.5 %all-to-all-start.2 = ((bf16[4,64,768]{2,1,0:T(8,128)(2,1)}), bf16[4,64,768]{2,1,0:T(8,128)(2,1)S(1)}, u32[]{:S(2)}, u32[]{:S(2)}) async-start(bf16[4,64,768]{2,1,0:T(8,128)(2,1)} %bitcast.3), calls=%async_computation.2 | async-start | bytes 786432 | tf_op jit(solution)/shard_map/all_to_all | solution.py:78
  57.4 0.0 copy-start
  57.4 0.0 collective-permute-done.2
  57.5 3.3 %convolution_convert_fusion.1 = bf16[256,1536]{1,0:T(8,128)(2,1)} fusion(bf16[1536,384]{1,0:T(8,128)(2,1)} %collective-permute-done.2, bf16[1536,384]{1,0:T(8,128)(2,1)S(1)} %copy-done.1, pred[]{:T(512)S(6)} %eq.15, bf16[256,2304]{1,0:T(8,128)(2,1)S(1)} %bitcast.29), kind=kOutput, calls=%fused_computation.5 | convolution fusion | flops 614989824 | bytes 3538945 | tf_op jit(solution)/shard_map/dot_general | solution.py:31
  60.8 5.6 %all-to-all-done.2 = bf16[4,64,768]{2,1,0:T(8,128)(2,1)S(1)} async-done(((bf16[4,64,768]{2,1,0:T(8,128)(2,1)}), bf16[4,64,768]{2,1,0:T(8,128)(2,1)S(1)}, u32[]{:S(2)}, u32[]{:S(2)}) %all-to-all-start.2) | async-done | bytes 393248 | tf_op jit(solution)/shard_map/all_to_all | solution.py:78
  66.4 0.1 fusion.18
  66.5 4.2 %all-to-all-start.3 = ((bf16[4,64,1536]{2,1,0:T(8,128)(2,1)}), bf16[4,64,1536]{2,1,0:T(8,128)(2,1)S(1)}, u32[]{:S(2)}, u32[]{:S(2)}) async-start(bf16[4,64,1536]{2,1,0:T(8,128)(2,1)} %bitcast.5), calls=%async_computation.3 | async-start | bytes 1572864 | tf_op jit(solution)/shard_map/all_to_all | solution.py:78
  70.7 0.1 dynamic_slice.29
  70.8 0.1 slice.64
  70.9 4.8 %collective-permute-start.5 = (bf16[256,1536]{1,0:T(8,128)(2,1)S(1)}, bf16[256,1536]{1,0:T(8,128)(2,1)}, u32[]{:S(2)}, u32[]{:S(2)}) collective-permute-start(bf16[256,1536]{1,0:T(8,128)(2,1)S(1)} %slice.64), channel_id=1, source_target_pairs={{0,1},{1,0},{2,3},{3,2},{4,5},{5,4},{6,7},{7,6},{8,9},{9,8},{10,11... | collective-permute-start | bytes 2359304 | tf_op jit(solution)/shard_map/ppermute | solution.py:43
  75.7 7.9 %collective-permute-start.3 = (bf16[64,768]{1,0:T(8,128)(2,1)S(1)}, bf16[64,768]{1,0:T(8,128)(2,1)S(1)}, u32[]{:S(2)}, u32[]{:S(2)}) collective-permute-start(bf16[64,768]{1,0:T(8,128)(2,1)S(1)} %fusion.18), channel_id=1, source_target_pairs={{0,256},{256,0},{1,257},{257,1},{2,258},{258,2},{3,259},{259,3},{4... | collective-permute-start | bytes 294920 | tf_op jit(solution)/shard_map/ppermute | solution.py:43
  83.6 0.7 constant_dynamic-slice_fusion.1
  84.3 2.2 %collective-permute-start.6 = (bf16[256,384]{1,0:T(8,128)(2,1)}, bf16[256,384]{1,0:T(8,128)(2,1)}, u32[]{:S(2)}, u32[]{:S(2)}) collective-permute-start(bf16[256,384]{1,0:T(8,128)(2,1)} %constant_dynamic-slice_fusion.1), channel_id=1, source_target_pairs={{0,1},{1,0},{2,3},{3,2},{4,5},{5,4},{6,7},{7,6},{8,9},{9,8},{10,11... | collective-permute-start | bytes 589832 | tf_op jit(solution)/shard_map/ppermute | solution.py:43
  86.5 0.3 collective-permute-done.3
  86.8 0.8 multiply_convert_fusion
  87.6 9.6 %collective-permute-start.4 = (bf16[64,768]{1,0:T(8,128)(2,1)}, bf16[64,768]{1,0:T(8,128)(2,1)}, u32[]{:S(2)}, u32[]{:S(2)}) collective-permute-start(bf16[64,768]{1,0:T(8,128)(2,1)} %get-tuple-element.36), channel_id=1, source_target_pairs={{0,258},{2,256},{256,2},{258,0},{1,259},{3,257},{257,3},{259,1},{4... | collective-permute-start | bytes 294920 | tf_op jit(solution)/shard_map/ppermute | solution.py:62
  97.3 0.0 all-to-all-done.3
  97.3 0.1 fusion.13
  97.4 0.0 collective-permute-done.6
  97.4 2.2 %collective-permute-done.4 = bf16[64,768]{1,0:T(8,128)(2,1)} collective-permute-done((bf16[64,768]{1,0:T(8,128)(2,1)}, bf16[64,768]{1,0:T(8,128)(2,1)}, u32[]{:S(2)}, u32[]{:S(2)}) %collective-permute-start.4) | collective-permute-done | bytes 98336 | tf_op jit(solution)/shard_map/ppermute | solution.py:62
  99.6 0.1 pad_maximum_fusion
  99.7 23.2 %all_to_all.35 = bf16[4,64,768]{2,1,0:T(8,128)(2,1)S(1)} all-to-all(bf16[4,64,768]{2,1,0:T(8,128)(2,1)S(1)} %pad_maximum_fusion), channel_id=1, replica_groups=mesh['rh'=2,'rm'=2,'rl'=2,'x'=4,'y'=4,'zh'=2,'core'=2] {'rh','zh'}, dimensions={0} | all-to-all | bytes 786432 | tf_op jit(solution)/shard_map/all_to_all | solution.py:78
  122.9 0.1 fusion.14
  123.0 0.8 broadcast_in_dim.8
  123.7 17.6 %all-to-all-start.5 = ((bf16[4,64,768]{2,1,0:T(8,128)(2,1)}), bf16[4,64,768]{2,1,0:T(8,128)(2,1)S(1)}, u32[]{:S(2)}, u32[]{:S(2)}) async-start(bf16[4,64,768]{2,1,0:T(8,128)(2,1)} %broadcast_in_dim.8), calls=%async_computation.5 | async-start | bytes 786432 | tf_op jit(solution)/shard_map/all_to_all | solution.py:72
  141.4 1.1 maximum_select_fusion.8
  142.5 8.6 %all-to-all-done.5 = bf16[4,64,768]{2,1,0:T(8,128)(2,1)S(1)} async-done(((bf16[4,64,768]{2,1,0:T(8,128)(2,1)}), bf16[4,64,768]{2,1,0:T(8,128)(2,1)S(1)}, u32[]{:S(2)}, u32[]{:S(2)}) %all-to-all-start.5) | async-done | bytes 393248 | tf_op jit(solution)/shard_map/all_to_all | solution.py:72
  151.0 4.1 %convolution_convert_fusion = bf16[256,1536]{1,0:T(8,128)(2,1)} fusion(bf16[256,768]{1,0:T(8,128)(2,1)S(1)} %bitcast.35, bf16[1536,384]{1,0:T(8,128)(2,1)} %collective-permute-done.1, bf16[1536,384]{1,0:T(8,128)(2,1)} %param.7, pred[]{:T(512)S(6)} %eq.15), kind=kOutput, calls=%fused_computation.4 | convolution fusion | flops 614989824 | bytes 3538945 | tf_op jit(solution)/shard_map/dot_general | solution.py:31
  155.2 2.9 %collective-permute-start.8 = (bf16[1,1,64,1536]{3,2,1,0:T(8,128)(2,1)S(1)}, bf16[1,1,64,1536]{3,2,1,0:T(8,128)(2,1)S(1)}, u32[]{:S(2)}, u32[]{:S(2)}) collective-permute-start(bf16[1,1,64,1536]{3,2,1,0:T(8,128)(2,1)S(1)} %maximum_select_fusion.8), channel_id=1, source_target_pairs={{0,128},{128,0},{1,129},{129,1},{2,130},{130,2},{3,131},{131,3},{4... | collective-permute-start | bytes 589832 | tf_op jit(solution)/shard_map/ppermute | solution.py:43
  158.1 4.6 %all-to-all-start.6 = ((bf16[16,16,1536]{2,1,0:T(8,128)(2,1)}), bf16[16,16,1536]{2,1,0:T(8,128)(2,1)S(1)}, u32[]{:S(2)}, u32[]{:S(2)}) async-start(bf16[16,16,1536]{2,1,0:T(8,128)(2,1)} %bitcast.13), calls=%async_computation.6 | async-start | bytes 1572864 | tf_op jit(solution)/shard_map/all_to_all | solution.py:78
  162.7 4.6 %collective-permute-done.8 = bf16[1,1,64,1536]{3,2,1,0:T(8,128)(2,1)S(1)} collective-permute-done((bf16[1,1,64,1536]{3,2,1,0:T(8,128)(2,1)S(1)}, bf16[1,1,64,1536]{3,2,1,0:T(8,128)(2,1)S(1)}, u32[]{:S(2)}, u32[]{:S(2)}) %collective-permute-start.8) | collective-permute-done | bytes 196640 | tf_op jit(solution)/shard_map/ppermute | solution.py:43
  167.3 4.1 %collective-permute-start.9 = (bf16[256,384]{1,0:T(8,128)(2,1)S(1)}, bf16[256,384]{1,0:T(8,128)(2,1)S(1)}, u32[]{:S(2)}, u32[]{:S(2)}) collective-permute-start(bf16[256,384]{1,0:T(8,128)(2,1)S(1)} %constant_dynamic-slice_fusion), channel_id=1, source_target_pairs={{0,1},{1,0},{2,3},{3,2},{4,5},{5,4},{6,7},{7,6},{8,9},{9,8},{10,11... | collective-permute-start | bytes 589832 | tf_op jit(solution)/shard_map/ppermute | solution.py:43
  171.4 1.9 collective-permute-start.10
  173.4 0.6 fusion.16
  174.0 0.1 convert_reduce_fusion.2
  174.0 0.0 collective-permute-done.9
  174.0 2.8 %fusion = bf16[1536,384]{1,0:T(8,128)(2,1)} fusion(f32[1536,384]{1,0:T(8,128)S(1)} %fusion.16, bf16[256,1536]{1,0:T(8,128)(2,1)} %collective-permute-done.5, bf16[256,384]{1,0:T(8,128)(2,1)S(1)} %collective-permute-done.9), kind=kOutput, calls=%fused_computation.2 | convolution fusion | flops 303169536 | bytes 4521984 | tf_op jit(solution)/shard_map/dot_general | solution.py:35
  176.8 7.3 %collective-permute-done.10 = bf16[2,1,64,1536]{3,2,1,0:T(8,128)(2,1)S(1)} collective-permute-done((bf16[2,1,64,1536]{3,2,1,0:T(8,128)(2,1)S(1)}, bf16[2,1,64,1536]{3,2,1,0:T(8,128)(2,1)S(1)}, u32[]{:S(2)}, u32[]{:S(2)}) %collective-permute-start.10) | collective-permute-done | bytes 393248 | tf_op jit(solution)/shard_map/ppermute | solution.py:43
  184.1 0.1 maximum_select_fusion.4
  184.2 2.7 %collective-permute-start.11 = (bf16[256,1536]{1,0:T(8,128)(2,1)S(1)}, bf16[256,1536]{1,0:T(8,128)(2,1)}, u32[]{:S(2)}, u32[]{:S(2)}) collective-permute-start(bf16[256,1536]{1,0:T(8,128)(2,1)S(1)} %bitcast.33), channel_id=1, source_target_pairs={{0,1},{1,0},{2,3},{3,2},{4,5},{5,4},{6,7},{7,6},{8,9},{9,8},{10,11... | collective-permute-start | bytes 2359304 | tf_op jit(solution)/shard_map/ppermute | solution.py:43
  186.9 0.1 convert_reduce_fusion
  187.0 2.8 %collective-permute-start.7 = (bf16[8,1536]{1,0:T(8,128)(2,1)S(1)}, bf16[8,1536]{1,0:T(8,128)(2,1)S(1)}, u32[]{:S(2)}, u32[]{:S(2)}) collective-permute-start(bf16[8,1536]{1,0:T(8,128)(2,1)S(1)} %dynamic-slice_convert_fusion), channel_id=1, source_target_pairs={{0,2},{2,0},{1,3},{3,1},{4,6},{6,4},{5,7},{7,5},{8,10},{10,8},{9,1... | collective-permute-start | bytes 73736 | tf_op jit(solution)/shard_map/ppermute | solution.py:43
  189.8 0.1 convert_reduce_fusion.1
  189.9 0.6 add.126
  190.5 10.1 %collective-permute-done.7 = bf16[8,1536]{1,0:T(8,128)(2,1)S(1)} collective-permute-done((bf16[8,1536]{1,0:T(8,128)(2,1)S(1)}, bf16[8,1536]{1,0:T(8,128)(2,1)S(1)}, u32[]{:S(2)}, u32[]{:S(2)}) %collective-permute-start.7) | collective-permute-done | bytes 24608 | tf_op jit(solution)/shard_map/ppermute | solution.py:43
  200.5 0.6 add_convert_fusion.2
  201.1 0.0 collective-permute-done.11
  201.1 1.8 fusion.27
  202.9 1.6 fusion.1
  (10 shorter events, 0.1 us)
Async XLA Ops:
  0.6 38.4 %copy-start.1 = (bf16[1536,384]{1,0:T(8,128)(2,1)S(1)}, bf16[1536,384]{1,0:T(8,128)(2,1)}, u32[]{:S(2)}) copy-start(bf16[1536,384]{1,0:T(8,128)(2,1)} %param.9) | copy-start | bytes 3538948
  3.1 24.5 %all-to-all-start = ((bf16[16,8,2304]{2,1,0:T(8,128)(2,1)}), bf16[16,8,2304]{2,1,0:T(8,128)(2,1)S(1)}, u32[]{:S(2)}, u32[]{:S(2)}) async-start(bf16[16,8,2304]{2,1,0:T(8,128)(2,1)} %broadcast_in_dim.6), calls=%async_computation | async-start | bytes 1179648 | tf_op jit(solution)/shard_map/all_to_all | solution.py:72
  10.7 16.9 %collective-permute-start = (bf16[8,2304]{1,0:T(8,128)(2,1)S(1)}, bf16[8,2304]{1,0:T(8,128)(2,1)S(1)}, u32[]{:S(2)}, u32[]{:S(2)}) collective-permute-start(bf16[8,2304]{1,0:T(8,128)(2,1)S(1)} %get-tuple-element.41), channel_id=1, source_target_pairs={{0,2},{2,0},{1,3},{3,1},{4,6},{6,4},{5,7},{7,5},{8,10},{10,8},{9,1... | collective-permute-start | bytes 110600 | tf_op jit(solution)/shard_map/ppermute | solution.py:43
  27.6 22.4 %collective-permute-start.1 = (bf16[1536,384]{1,0:T(8,128)(2,1)}, bf16[1536,384]{1,0:T(8,128)(2,1)}, u32[]{:S(2)}, u32[]{:S(2)}) collective-permute-start(bf16[1536,384]{1,0:T(8,128)(2,1)} %param.7), channel_id=1, source_target_pairs={{0,1},{1,0},{2,3},{3,2},{4,5},{5,4},{6,7},{7,6},{8,9},{9,8},{10,11... | collective-permute-start | bytes 3538952 | tf_op jit(solution)/shard_map/ppermute | solution.py:43
  32.0 17.7 %all-to-all-start.1 = ((bf16[16,8,2304]{2,1,0:T(8,128)(2,1)}), bf16[16,8,2304]{2,1,0:T(8,128)(2,1)S(1)}, u32[]{:S(2)}, u32[]{:S(2)}) async-start(bf16[16,8,2304]{2,1,0:T(8,128)(2,1)} %broadcast_in_dim.7), calls=%async_computation.1 | async-start | bytes 1179648 | tf_op jit(solution)/shard_map/all_to_all | solution.py:72
  39.0 18.5 %collective-permute-start.2 = (bf16[1536,384]{1,0:T(8,128)(2,1)S(1)}, bf16[1536,384]{1,0:T(8,128)(2,1)}, u32[]{:S(2)}, u32[]{:S(2)}) collective-permute-start(bf16[1536,384]{1,0:T(8,128)(2,1)S(1)} %copy-done.1), channel_id=1, source_target_pairs={{0,1},{1,0},{2,3},{3,2},{4,5},{5,4},{6,7},{7,6},{8,9},{9,8},{10,11... | collective-permute-start | bytes 3538952 | tf_op jit(solution)/shard_map/ppermute | solution.py:43
  54.0 12.5 %all-to-all-start.2 = ((bf16[4,64,768]{2,1,0:T(8,128)(2,1)}), bf16[4,64,768]{2,1,0:T(8,128)(2,1)S(1)}, u32[]{:S(2)}, u32[]{:S(2)}) async-start(bf16[4,64,768]{2,1,0:T(8,128)(2,1)} %bitcast.3), calls=%async_computation.2 | async-start | bytes 786432 | tf_op jit(solution)/shard_map/all_to_all | solution.py:78
  57.4 13.3 %copy-start = (f32[1536]{0:T(1024)S(1)}, f32[1536]{0:T(1024)}, u32[]{:S(2)}) copy-start(f32[1536]{0:T(1024)} %param.8) | copy-start | bytes 18436
  66.5 30.8 %all-to-all-start.3 = ((bf16[4,64,1536]{2,1,0:T(8,128)(2,1)}), bf16[4,64,1536]{2,1,0:T(8,128)(2,1)S(1)}, u32[]{:S(2)}, u32[]{:S(2)}) async-start(bf16[4,64,1536]{2,1,0:T(8,128)(2,1)} %bitcast.5), calls=%async_computation.3 | async-start | bytes 1572864 | tf_op jit(solution)/shard_map/all_to_all | solution.py:78
  70.9 26.5 %collective-permute-start.5 = (bf16[256,1536]{1,0:T(8,128)(2,1)S(1)}, bf16[256,1536]{1,0:T(8,128)(2,1)}, u32[]{:S(2)}, u32[]{:S(2)}) collective-permute-start(bf16[256,1536]{1,0:T(8,128)(2,1)S(1)} %slice.64), channel_id=1, source_target_pairs={{0,1},{1,0},{2,3},{3,2},{4,5},{5,4},{6,7},{7,6},{8,9},{9,8},{10,11... | collective-permute-start | bytes 2359304 | tf_op jit(solution)/shard_map/ppermute | solution.py:43
  75.7 11.1 %collective-permute-start.3 = (bf16[64,768]{1,0:T(8,128)(2,1)S(1)}, bf16[64,768]{1,0:T(8,128)(2,1)S(1)}, u32[]{:S(2)}, u32[]{:S(2)}) collective-permute-start(bf16[64,768]{1,0:T(8,128)(2,1)S(1)} %fusion.18), channel_id=1, source_target_pairs={{0,256},{256,0},{1,257},{257,1},{2,258},{258,2},{3,259},{259,3},{4... | collective-permute-start | bytes 294920 | tf_op jit(solution)/shard_map/ppermute | solution.py:43
  84.3 13.1 %collective-permute-start.6 = (bf16[256,384]{1,0:T(8,128)(2,1)}, bf16[256,384]{1,0:T(8,128)(2,1)}, u32[]{:S(2)}, u32[]{:S(2)}) collective-permute-start(bf16[256,384]{1,0:T(8,128)(2,1)} %constant_dynamic-slice_fusion.1), channel_id=1, source_target_pairs={{0,1},{1,0},{2,3},{3,2},{4,5},{5,4},{6,7},{7,6},{8,9},{9,8},{10,11... | collective-permute-start | bytes 589832 | tf_op jit(solution)/shard_map/ppermute | solution.py:43
  87.6 12.0 %collective-permute-start.4 = (bf16[64,768]{1,0:T(8,128)(2,1)}, bf16[64,768]{1,0:T(8,128)(2,1)}, u32[]{:S(2)}, u32[]{:S(2)}) collective-permute-start(bf16[64,768]{1,0:T(8,128)(2,1)} %get-tuple-element.36), channel_id=1, source_target_pairs={{0,258},{2,256},{256,2},{258,0},{1,259},{3,257},{257,3},{259,1},{4... | collective-permute-start | bytes 294920 | tf_op jit(solution)/shard_map/ppermute | solution.py:62
  123.7 27.3 %all-to-all-start.5 = ((bf16[4,64,768]{2,1,0:T(8,128)(2,1)}), bf16[4,64,768]{2,1,0:T(8,128)(2,1)S(1)}, u32[]{:S(2)}, u32[]{:S(2)}) async-start(bf16[4,64,768]{2,1,0:T(8,128)(2,1)} %broadcast_in_dim.8), calls=%async_computation.5 | async-start | bytes 786432 | tf_op jit(solution)/shard_map/all_to_all | solution.py:72
  155.2 12.1 %collective-permute-start.8 = (bf16[1,1,64,1536]{3,2,1,0:T(8,128)(2,1)S(1)}, bf16[1,1,64,1536]{3,2,1,0:T(8,128)(2,1)S(1)}, u32[]{:S(2)}, u32[]{:S(2)}) collective-permute-start(bf16[1,1,64,1536]{3,2,1,0:T(8,128)(2,1)S(1)} %maximum_select_fusion.8), channel_id=1, source_target_pairs={{0,128},{128,0},{1,129},{129,1},{2,130},{130,2},{3,131},{131,3},{4... | collective-permute-start | bytes 589832 | tf_op jit(solution)/shard_map/ppermute | solution.py:43
  158.1 28.8 %all-to-all-start.6 = ((bf16[16,16,1536]{2,1,0:T(8,128)(2,1)}), bf16[16,16,1536]{2,1,0:T(8,128)(2,1)S(1)}, u32[]{:S(2)}, u32[]{:S(2)}) async-start(bf16[16,16,1536]{2,1,0:T(8,128)(2,1)} %bitcast.13), calls=%async_computation.6 | async-start | bytes 1572864 | tf_op jit(solution)/shard_map/all_to_all | solution.py:78
  167.3 6.7 %collective-permute-start.9 = (bf16[256,384]{1,0:T(8,128)(2,1)S(1)}, bf16[256,384]{1,0:T(8,128)(2,1)S(1)}, u32[]{:S(2)}, u32[]{:S(2)}) collective-permute-start(bf16[256,384]{1,0:T(8,128)(2,1)S(1)} %constant_dynamic-slice_fusion), channel_id=1, source_target_pairs={{0,1},{1,0},{2,3},{3,2},{4,5},{5,4},{6,7},{7,6},{8,9},{9,8},{10,11... | collective-permute-start | bytes 589832 | tf_op jit(solution)/shard_map/ppermute | solution.py:43
  171.4 12.6 %collective-permute-start.10 = (bf16[2,1,64,1536]{3,2,1,0:T(8,128)(2,1)S(1)}, bf16[2,1,64,1536]{3,2,1,0:T(8,128)(2,1)S(1)}, u32[]{:S(2)}, u32[]{:S(2)}) collective-permute-start(bf16[2,1,64,1536]{3,2,1,0:T(8,128)(2,1)S(1)} %maximum_select_fusion.7), channel_id=1, source_target_pairs={{0,64},{64,0},{1,65},{65,1},{2,66},{66,2},{3,67},{67,3},{4,68},{68... | collective-permute-start | bytes 1179656 | tf_op jit(solution)/shard_map/ppermute | solution.py:43
  184.2 17.0 %collective-permute-start.11 = (bf16[256,1536]{1,0:T(8,128)(2,1)S(1)}, bf16[256,1536]{1,0:T(8,128)(2,1)}, u32[]{:S(2)}, u32[]{:S(2)}) collective-permute-start(bf16[256,1536]{1,0:T(8,128)(2,1)S(1)} %bitcast.33), channel_id=1, source_target_pairs={{0,1},{1,0},{2,3},{3,2},{4,5},{5,4},{6,7},{7,6},{8,9},{9,8},{10,11... | collective-permute-start | bytes 2359304 | tf_op jit(solution)/shard_map/ppermute | solution.py:43
  187.0 13.5 %collective-permute-start.7 = (bf16[8,1536]{1,0:T(8,128)(2,1)S(1)}, bf16[8,1536]{1,0:T(8,128)(2,1)S(1)}, u32[]{:S(2)}, u32[]{:S(2)}) collective-permute-start(bf16[8,1536]{1,0:T(8,128)(2,1)S(1)} %dynamic-slice_convert_fusion), channel_id=1, source_target_pairs={{0,2},{2,0},{1,3},{3,1},{4,6},{6,4},{5,7},{7,5},{8,10},{10,8},{9,1... | collective-permute-start | bytes 73736 | tf_op jit(solution)/shard_map/ppermute | solution.py:43

commit v6 on v5

--- a/solution.py
+++ b/solution.py
@@ -10,7 +10,6 @@
 CROSS = [(0, 3), (1, 2), (2, 1), (3, 0)]
 GRID = ("x", "y")
 ROW4 = ("rm", "rl")
-RING4 = ("rh", "zh")
 
 
 def gelu_pair(pre):
@@ -50,6 +49,11 @@
         jnp.concatenate([mine, other], dim),
         jnp.concatenate([other, mine], dim),
     )
+
+
+def after(first, *values):
+    kept = lax.optimization_barrier((first, *values))[1:]
+    return kept[0] if len(kept) == 1 else kept
 
 
 def cut(part, axis, dim):
@@ -96,44 +100,39 @@
     kept = jnp.concatenate([tokens, part_of(cotangent, zh, half_d, 1)], 1)
     sent = jnp.concatenate([tokens, part_of(cotangent, 1 - zh, half_d, 1)], 1)
     got = swap(sent, "zh")
-    own = spread(kept, GRID)
-    got, own, w_in, w_out = lax.optimization_barrier((got, own, w_in, w_out))
+    w_out, w_in = after(got, w_out, w_in)
+    out_pair = join(w_out, swap(w_out, "core"), "core", 1)
     in_pair = join(w_in, swap(w_in, "core"), "core", 1)
-    out_pair = join(w_out, swap(w_out, "core"), "core", 1)
-    other = spread(got, GRID)
+    in_pair, out_pair = after(got, in_pair, out_pair)
+    rows = join(kept, got, "zh", 0)
 
-    def by_token(mine, theirs):
-        mine, theirs = (v.reshape(-1, tok_dev, v.shape[1]) for v in (mine, theirs))
-        return join(mine, theirs, "zh", 1).reshape(-1, mine.shape[2])
+    every_g = spread(rows[:, feat:], GRID)
+    every_x = spread(after(every_g, rows[:, :feat]), GRID)
 
-    every = by_token(own, other)
-    every_x, every_g = every[:, :feat], every[:, feat:]
+    back = against(every_g, out_pair).reshape(2, 2, -1, 2 * half_h)
+    back_kept, back_sent = cut(back, "rl", 1)
+    back_kept, back_sent = cut(back_kept + swap(back_sent, "rl").astype(f32), "rm", 0)
+    every_x = after(back_sent, every_x)
     pre = dot(every_x, in_pair).astype(bf16)
-    back = against(every_g, out_pair).astype(bf16)
+    back = (back_kept + swap(back_sent, "rm").astype(f32))[0, 0]
     pre = deal(pre, ROW4).astype(bf16)
-    pre, back = lax.optimization_barrier((pre, back))
+
+    back_kept, back_sent = cut(back, "zh", 1)
+    back = (back_kept + after(pre, cross(back_sent)).astype(f32)).astype(bf16)
+    pair_x = swap(every_x, "core")
+    pair_g = swap(part_of(every_g, 1 - core, quarter_d, 1), "core")
+    pre = after((pair_x, pair_g), pre)
     pre = pre.astype(f32) + swap(pre, "rh").astype(f32)
-    sums = deal(back, ROW4).astype(bf16)
+    back = back.astype(f32) + swap(back, "rh").astype(f32)
 
     act_f, slope = gelu_pair(pre + part_of(b_in, zh, half_h, 0))
     act = act_f.astype(bf16)
-    crossed = cross(act)
-    pair_x = swap(every_x, "core")
-    pair_g = swap(part_of(every_g, 1 - core, quarter_d, 1), "core")
-    sums, slope, crossed, pair_x, pair_g = lax.optimization_barrier(
-        (sums, slope, crossed, pair_x, pair_g)
-    )
-    act = join(act, crossed, "zh", 1)[None, None]
-    halves = jnp.stack([sums[:, :half_h], sums[:, half_h:]])
-    halves = jnp.concatenate([halves, halves], 0).reshape(-1, half_h)
-    grad = (deal(halves, RING4) * slope).astype(bf16)
-
-    grad = spread(grad, ROW4)
+    act = join(act, cross(act), "zh", 1)[None, None]
+    grad = spread((back * slope).astype(bf16), ROW4)
     part = against(grad, in_pair).astype(bf16)
-    part, grad, act = lax.optimization_barrier((part, grad, act))
     summed = deal(part, GRID)
-    act = widen(act, "rm", 0)
-    grad_sent, act = lax.optimization_barrier((part_of(grad, 1 - core, quarter, 1), act))
+    act = widen(after(part, act), "rm", 0)
+    grad_sent = after(act, part_of(grad, 1 - core, quarter, 1))
     act = widen(act, "rl", 1).reshape(-1, act.shape[-1])
     out_rows = part_of(summed, 1 - zh, tok_dev, 0).astype(bf16)
     own_rows = part_of(summed, zh, tok_dev, 0)

time: 206 us -> 194 us (0.942)
  blocking collectives: 23.2 us -> 0 us
  waiting for transfers between devices: 48.6 us -> 59.7 us
  other arithmetic: 4.68 us -> 10.5 us
  matrix products: 18.2 us -> 12.8 us
    all_to_all x1 -> x0, blocking collectives: 23.2 us -> none  [deal(): lax.all_to_all(part.reshape(n, -1, part.shape[1]), axes, 0, 0, tiled=True)]
    ppermute x11 -> x14, starting transfers between devices: 50.6 us -> 73.3 us  [swap(): return lax.ppermute(value, axis, SWAP)]
    all_to_all x3, starting transfers between devices: 32.2 us -> 11.6 us  [spread(): got = lax.all_to_all(sent, axes, 0, 0, tiled=True)]
    ppermute x11 -> x14, waiting for transfers between devices: 23.7 us -> 34.6 us  [swap(): return lax.ppermute(value, axis, SWAP)]
    ppermute x1 -> x2, waiting for transfers between devices: 2.17 us -> 9.14 us  [cross(): return lax.ppermute(value, ('rh', 'zh'), CROSS)]
    all_to_all x3 -> x2, waiting for transfers between devices: 5.63 us -> 0.01 us  [deal(): lax.all_to_all(part.reshape(n, -1, part.shape[1]), axes, 0, 0, tiled=True)]
    all_to_all x3 -> x2, starting transfers between devices: 12.3 us -> 7.45 us  [deal(): lax.all_to_all(part.reshape(n, -1, part.shape[1]), axes, 0, 0, tiled=True)]
    select_n x4 -> x6, other arithmetic: 1.45 us -> 6.01 us  [join(): jnp.where(first, jnp.concatenate([mine, other], dim), jnp.concatenate([ot...]
  transfers between devices with their start and end apart: 18 -> 21, of which waited for: 9 -> 12; matrix products, arithmetic and copies ran while one was open for 8% -> 7% of each run, Pallas kernels for 0% -> 0%
where the time goes in v6:
time: 194 us; the launch traced here: 193 us
  starting transfers between devices  103 us (53%)
  waiting for transfers between devices  59.7 us (31%)
  matrix products  12.8 us (7%)
  other arithmetic  10.5 us (5%)
  local copies, waits for them, and re-layouts  5.41 us (3%)
    ppermute x14, starting transfers between devices, swap(): return lax.ppermute(value, axis, SWAP)  73.3 us
    ppermute x14, waiting for transfers between devices, swap(): return lax.ppermute(value, axis, SWAP)  34.6 us
    all_to_all x3, waiting for transfers between devices, spread(): got = lax.all_to_all(sent, axes, 0, 0, tiled=True)  16 us
    all_to_all x3, starting transfers between devices, spread(): got = lax.all_to_all(sent, axes, 0, 0, tiled=True)  11.6 us
    ppermute x2, starting transfers between devices, cross(): return lax.ppermute(value, ('rh', 'zh'), CROSS)  11 us
    ppermute x2, waiting for transfers between devices, cross(): return lax.ppermute(value, ('rh', 'zh'), CROSS)  9.14 us
    all_to_all x2, starting transfers between devices, deal(): lax.all_to_all(part.reshape(n, -1, part.shape[1]), axes, 0, 0, tiled=True)  7.45 us
    select_n x6, other arithmetic, join(): jnp.where(first, jnp.concatenate([mine, other], dim), jnp.concatenate([ot...  6.01 us
  transfers between devices with their start and end apart: 21, of which 12 were waited for; matrix products, arithmetic and copies ran while one was open for 7% of the time, Pallas kernels for 0%

profile of v6, /device:TPU:1, one launch (start us, length us, event | category | flops | bytes accessed | tf_op | source)
XLA Modules:
  0.0 192.8 jit_solution(2118508874625238750)
XLA Ops:
  0.6 0.0 copy-start.2
  0.7 0.8 constant_dynamic-slice_fusion.3
  1.5 0.7 pad_maximum_fusion
  2.2 16.3 %collective-permute-start = (bf16[8,2304]{1,0:T(8,128)(2,1)S(1)}, bf16[8,2304]{1,0:T(8,128)(2,1)S(1)}, u32[]{:S(2)}, u32[]{:S(2)}) collective-permute-start(bf16[8,2304]{1,0:T(8,128)(2,1)S(1)} %pad_maximum_fusion), channel_id=1, source_target_pairs={{0,2},{2,0},{1,3},{3,1},{4,6},{6,4},{5,7},{7,5},{8,10},{10,8},{9,1... | collective-permute-start | bytes 110600 | tf_op jit(solution)/shard_map/ppermute | solution.py:42
  18.5 1.5 collective-permute-done
  20.0 5.6 %collective-permute-start.1 = (bf16[1536,384]{1,0:T(8,128)(2,1)}, bf16[1536,384]{1,0:T(8,128)(2,1)S(1)}, u32[]{:S(2)}, u32[]{:S(2)}) collective-permute-start(bf16[1536,384]{1,0:T(8,128)(2,1)} %param.7), channel_id=1, source_target_pairs={{0,1},{1,0},{2,3},{3,2},{4,5},{5,4},{6,7},{7,6},{8,9},{9,8},{10,11... | collective-permute-start | bytes 3538952 | tf_op jit(solution)/shard_map/ppermute | solution.py:42
  25.6 1.9 collective-permute-start.2
  27.5 0.8 maximum_select_fusion.5
  28.3 0.8 broadcast_in_dim.6
  29.1 4.5 %all-to-all-start = ((bf16[16,16,768]{2,1,0:T(8,128)(2,1)}), bf16[16,16,768]{2,1,0:T(8,128)(2,1)S(1)}, u32[]{:S(2)}, u32[]{:S(2)}) async-start(bf16[16,16,768]{2,1,0:T(8,128)(2,1)} %broadcast_in_dim.6), calls=%async_computation | async-start | bytes 786432 | tf_op jit(solution)/shard_map/all_to_all | solution.py:76
  33.6 0.0 copy-start.3
  33.7 1.7 maximum_select_fusion
  35.4 2.2 %maximum_select_fusion.1 = bf16[1536,768]{1,0:T(8,128)(2,1)S(1)} fusion(bf16[1536,384]{1,0:T(8,128)(2,1)} %collective-permute-done.2, bf16[1536,384]{1,0:T(8,128)(2,1)S(1)} %copy-done.3, pred[]{:T(512)S(6)} %eq.15), kind=kLoop, calls=%fused_computation.6 | loop fusion | flops 10616832 | bytes 4718593 | tf_op jit(solution)/shard_map/jit(_where)/select_n | solution.py:47
  37.6 5.0 %all-to-all-done = bf16[16,16,768]{2,1,0:T(8,128)(2,1)S(1)} async-done(((bf16[16,16,768]{2,1,0:T(8,128)(2,1)}), bf16[16,16,768]{2,1,0:T(8,128)(2,1)S(1)}, u32[]{:S(2)}, u32[]{:S(2)}) %all-to-all-start) | async-done | bytes 393248 | tf_op jit(solution)/shard_map/all_to_all | solution.py:76
  42.7 0.8 fusion.2
  43.5 1.1 copy-done
  44.7 3.2 %collective-permute-start.3 = (bf16[2,1,64,1536]{3,2,1,0:T(8,128)(2,1)S(1)}, bf16[2,1,64,1536]{3,2,1,0:T(8,128)(2,1)}, u32[]{:S(2)}, u32[]{:S(2)}) collective-permute-start(bf16[2,1,64,1536]{3,2,1,0:T(8,128)(2,1)S(1)} %dynamic-slice_convert_fusion), channel_id=1, source_target_pairs={{0,64},{64,0},{1,65},{65,1},{2,66},{66,2},{3,67},{67,3},{4,68},{68... | collective-permute-start | bytes 1179656 | tf_op jit(solution)/shard_map/ppermute | solution.py:42
  47.9 1.0 broadcast_in_dim.7
  48.9 3.6 %all-to-all-start.1 = ((bf16[16,16,1536]{2,1,0:T(8,128)(2,1)}), bf16[16,16,1536]{2,1,0:T(8,128)(2,1)S(1)}, u32[]{:S(2)}, u32[]{:S(2)}) async-start(bf16[16,16,1536]{2,1,0:T(8,128)(2,1)} %broadcast_in_dim.7), calls=%async_computation.1 | async-start | bytes 1572864 | tf_op jit(solution)/shard_map/all_to_all | solution.py:76
  52.5 3.2 %collective-permute-done.3 = bf16[2,1,64,1536]{3,2,1,0:T(8,128)(2,1)} collective-permute-done((bf16[2,1,64,1536]{3,2,1,0:T(8,128)(2,1)S(1)}, bf16[2,1,64,1536]{3,2,1,0:T(8,128)(2,1)}, u32[]{:S(2)}, u32[]{:S(2)}) %collective-permute-start.3) | collective-permute-done | bytes 393248 | tf_op jit(solution)/shard_map/ppermute | solution.py:42
  55.7 1.1 convert_add_fusion
  56.8 7.7 %all-to-all-done.1 = bf16[16,16,1536]{2,1,0:T(8,128)(2,1)S(1)} async-done(((bf16[16,16,1536]{2,1,0:T(8,128)(2,1)}), bf16[16,16,1536]{2,1,0:T(8,128)(2,1)S(1)}, u32[]{:S(2)}, u32[]{:S(2)}) %all-to-all-start.1) | async-done | bytes 786464 | tf_op jit(solution)/shard_map/all_to_all | solution.py:76
  64.5 3.2 %convolution_convert_fusion.1 = bf16[256,768]{1,0:T(8,128)(2,1)} fusion(bf16[256,1536]{1,0:T(8,128)(2,1)S(1)} %bitcast.38, bf16[1536,768]{1,0:T(8,128)(2,1)} %maximum_select_fusion), kind=kOutput, calls=%fused_computation.10 | convolution fusion | flops 604176384 | bytes 3538944 | tf_op jit(solution)/shard_map/dot_general | solution.py:26
  67.6 3.6 %all-to-all-start.2 = ((bf16[4,64,768]{2,1,0:T(8,128)(2,1)}), bf16[4,64,768]{2,1,0:T(8,128)(2,1)S(1)}, u32[]{:S(2)}, u32[]{:S(2)}) async-start(bf16[4,64,768]{2,1,0:T(8,128)(2,1)} %bitcast.6), calls=%async_computation.2 | async-start | bytes 786432 | tf_op jit(solution)/shard_map/all_to_all | solution.py:82
  71.2 4.2 %collective-permute-start.4 = (bf16[1,1,64,1536]{3,2,1,0:T(8,128)(2,1)S(1)}, bf16[1,1,64,1536]{3,2,1,0:T(8,128)(2,1)}, u32[]{:S(2)}, u32[]{:S(2)}) collective-permute-start(bf16[1,1,64,1536]{3,2,1,0:T(8,128)(2,1)S(1)} %dynamic-slice_convert_fusion.1), channel_id=1, source_target_pairs={{0,128},{128,0},{1,129},{129,1},{2,130},{130,2},{3,131},{131,3},{4... | collective-permute-start | bytes 589832 | tf_op jit(solution)/shard_map/ppermute | solution.py:42
  75.5 0.7 constant_dynamic-slice_fusion.1
  76.2 5.7 %collective-permute-start.8 = (bf16[256,384]{1,0:T(8,128)(2,1)}, bf16[256,384]{1,0:T(8,128)(2,1)}, u32[]{:S(2)}, u32[]{:S(2)}) collective-permute-start(bf16[256,384]{1,0:T(8,128)(2,1)} %constant_dynamic-slice_fusion.1), channel_id=1, source_target_pairs={{0,1},{1,0},{2,3},{3,2},{4,5},{5,4},{6,7},{7,6},{8,9},{9,8},{10,11... | collective-permute-start | bytes 589832 | tf_op jit(solution)/shard_map/ppermute | solution.py:42
  81.9 1.9 collective-permute-start.7
  83.9 5.8 %collective-permute-done.4 = bf16[1,1,64,1536]{3,2,1,0:T(8,128)(2,1)} collective-permute-done((bf16[1,1,64,1536]{3,2,1,0:T(8,128)(2,1)S(1)}, bf16[1,1,64,1536]{3,2,1,0:T(8,128)(2,1)}, u32[]{:S(2)}, u32[]{:S(2)}) %collective-permute-start.4) | collective-permute-done | bytes 196640 | tf_op jit(solution)/shard_map/ppermute | solution.py:42
  89.7 1.0 convert_add_fusion.1
  90.7 9.0 %collective-permute-start.5 = (bf16[64,768]{1,0:T(8,128)(2,1)S(1)}, bf16[64,768]{1,0:T(8,128)(2,1)S(1)}, u32[]{:S(2)}, u32[]{:S(2)}) collective-permute-start(bf16[64,768]{1,0:T(8,128)(2,1)S(1)} %fusion.16), channel_id=1, source_target_pairs={{0,258},{2,256},{256,2},{258,0},{1,259},{3,257},{257,3},{259,1},{4... | collective-permute-start | bytes 294920 | tf_op jit(solution)/shard_map/ppermute | solution.py:66
  99.8 0.1 fusion.15
  99.8 5.2 %collective-permute-start.9 = (bf16[64,768]{1,0:T(8,128)(2,1)S(1)}, bf16[64,768]{1,0:T(8,128)(2,1)S(1)}, u32[]{:S(2)}, u32[]{:S(2)}) collective-permute-start(bf16[64,768]{1,0:T(8,128)(2,1)S(1)} %fusion.15), channel_id=1, source_target_pairs={{0,256},{256,0},{1,257},{257,1},{2,258},{258,2},{3,259},{259,3},{4... | collective-permute-start | bytes 294920 | tf_op jit(solution)/shard_map/ppermute | solution.py:42
  105.0 1.5 collective-permute-done.5
  106.6 6.3 %collective-permute-start.6 = (bf16[64,768]{1,0:T(8,128)(2,1)S(1)}, bf16[64,768]{1,0:T(8,128)(2,1)S(1)}, u32[]{:S(2)}, u32[]{:S(2)}) collective-permute-start(bf16[64,768]{1,0:T(8,128)(2,1)S(1)} %fusion.11), channel_id=1, source_target_pairs={{0,256},{256,0},{1,257},{257,1},{2,258},{258,2},{3,259},{259,3},{4... | collective-permute-start | bytes 294920 | tf_op jit(solution)/shard_map/ppermute | solution.py:42
  112.9 0.1 dynamic_slice.57
  113.0 10.9 %collective-permute-done.6 = bf16[64,768]{1,0:T(8,128)(2,1)S(1)} collective-permute-done((bf16[64,768]{1,0:T(8,128)(2,1)S(1)}, bf16[64,768]{1,0:T(8,128)(2,1)S(1)}, u32[]{:S(2)}, u32[]{:S(2)}) %collective-permute-start.6) | collective-permute-done | bytes 98336 | tf_op jit(solution)/shard_map/ppermute | solution.py:42
  123.9 0.2 multiply_convert_fusion
  124.1 0.8 broadcast_in_dim.8
  124.8 3.5 %all-to-all-start.3 = ((bf16[4,64,768]{2,1,0:T(8,128)(2,1)}), bf16[4,64,768]{2,1,0:T(8,128)(2,1)S(1)}, u32[]{:S(2)}, u32[]{:S(2)}) async-start(bf16[4,64,768]{2,1,0:T(8,128)(2,1)} %broadcast_in_dim.8), calls=%async_computation.3 | async-start | bytes 786432 | tf_op jit(solution)/shard_map/all_to_all | solution.py:76
  128.3 1.9 collective-permute-start.11
  130.2 7.6 %collective-permute-done.11 = bf16[64,768]{1,0:T(8,128)(2,1)S(1)} collective-permute-done((bf16[64,768]{1,0:T(8,128)(2,1)S(1)}, bf16[64,768]{1,0:T(8,128)(2,1)S(1)}, u32[]{:S(2)}, u32[]{:S(2)}) %collective-permute-start.11) | collective-permute-done | bytes 98336 | tf_op jit(solution)/shard_map/ppermute | solution.py:66
  137.9 3.3 %all-to-all-done.3 = bf16[4,64,768]{2,1,0:T(8,128)(2,1)S(1)} async-done(((bf16[4,64,768]{2,1,0:T(8,128)(2,1)}), bf16[4,64,768]{2,1,0:T(8,128)(2,1)S(1)}, u32[]{:S(2)}, u32[]{:S(2)}) %all-to-all-start.3) | async-done | bytes 393248 | tf_op jit(solution)/shard_map/all_to_all | solution.py:76
  141.3 3.4 %convolution_convert_fusion = bf16[256,1536]{1,0:T(8,128)(2,1)} fusion(bf16[256,768]{1,0:T(8,128)(2,1)S(1)} %bitcast.41, bf16[1536,768]{1,0:T(8,128)(2,1)} %maximum_select_fusion), kind=kOutput, calls=%fused_computation.4 | convolution fusion | flops 604372992 | bytes 3538944 | tf_op jit(solution)/shard_map/dot_general | solution.py:30
  144.6 5.9 %collective-permute-start.12 = (bf16[1,1,64,1536]{3,2,1,0:T(8,128)(2,1)S(1)}, bf16[1,1,64,1536]{3,2,1,0:T(8,128)(2,1)}, u32[]{:S(2)}, u32[]{:S(2)}) collective-permute-start(bf16[1,1,64,1536]{3,2,1,0:T(8,128)(2,1)S(1)} %maximum_select_fusion.4), channel_id=1, source_target_pairs={{0,128},{128,0},{1,129},{129,1},{2,130},{130,2},{3,131},{131,3},{4... | collective-permute-start | bytes 589832 | tf_op jit(solution)/shard_map/ppermute | solution.py:42
  150.5 3.9 %all-to-all-start.4 = ((bf16[16,16,1536]{2,1,0:T(8,128)(2,1)}), bf16[16,16,1536]{2,1,0:T(8,128)(2,1)S(1)}, u32[]{:S(2)}, u32[]{:S(2)}) async-start(bf16[16,16,1536]{2,1,0:T(8,128)(2,1)} %bitcast.10), calls=%async_computation.4 | async-start | bytes 1572864 | tf_op jit(solution)/shard_map/all_to_all | solution.py:82
  154.4 1.1 maximum_select_fusion.3
  155.5 8.0 %collective-permute-start.14 = (bf16[2,1,64,1536]{3,2,1,0:T(8,128)(2,1)S(1)}, bf16[2,1,64,1536]{3,2,1,0:T(8,128)(2,1)S(1)}, u32[]{:S(2)}, u32[]{:S(2)}) collective-permute-start(bf16[2,1,64,1536]{3,2,1,0:T(8,128)(2,1)S(1)} %maximum_select_fusion.3), channel_id=1, source_target_pairs={{0,64},{64,0},{1,65},{65,1},{2,66},{66,2},{3,67},{67,3},{4,68},{68... | collective-permute-start | bytes 1179656 | tf_op jit(solution)/shard_map/ppermute | solution.py:42
  163.5 2.7 %collective-permute-start.13 = (bf16[256,384]{1,0:T(8,128)(2,1)S(1)}, bf16[256,384]{1,0:T(8,128)(2,1)S(1)}, u32[]{:S(2)}, u32[]{:S(2)}) collective-permute-start(bf16[256,384]{1,0:T(8,128)(2,1)S(1)} %constant_dynamic-slice_fusion), channel_id=1, source_target_pairs={{0,1},{1,0},{2,3},{3,2},{4,5},{5,4},{6,7},{7,6},{8,9},{9,8},{10,11... | collective-permute-start | bytes 589832 | tf_op jit(solution)/shard_map/ppermute | solution.py:42
  166.2 0.6 fusion.13
  166.8 0.1 convert_reduce_fusion.2
  166.8 0.4 collective-permute-done.13
  167.2 1.6 fusion
  168.9 2.6 %collective-permute-done.14 = bf16[2,1,64,1536]{3,2,1,0:T(8,128)(2,1)S(1)} collective-permute-done((bf16[2,1,64,1536]{3,2,1,0:T(8,128)(2,1)S(1)}, bf16[2,1,64,1536]{3,2,1,0:T(8,128)(2,1)S(1)}, u32[]{:S(2)}, u32[]{:S(2)}) %collective-permute-start.14) | collective-permute-done | bytes 393248 | tf_op jit(solution)/shard_map/ppermute | solution.py:42
  171.5 0.1 maximum_select_fusion.2
  171.6 4.0 %collective-permute-start.15 = (bf16[256,1536]{1,0:T(8,128)(2,1)S(1)}, bf16[256,1536]{1,0:T(8,128)(2,1)S(1)}, u32[]{:S(2)}, u32[]{:S(2)}) collective-permute-start(bf16[256,1536]{1,0:T(8,128)(2,1)S(1)} %bitcast.36), channel_id=1, source_target_pairs={{0,1},{1,0},{2,3},{3,2},{4,5},{5,4},{6,7},{7,6},{8,9},{9,8},{10,11... | collective-permute-start | bytes 2359304 | tf_op jit(solution)/shard_map/ppermute | solution.py:42
  175.6 0.1 convert_reduce_fusion
  175.7 2.4 %collective-permute-start.10 = (bf16[8,1536]{1,0:T(8,128)(2,1)S(1)}, bf16[8,1536]{1,0:T(8,128)(2,1)S(1)}, u32[]{:S(2)}, u32[]{:S(2)}) collective-permute-start(bf16[8,1536]{1,0:T(8,128)(2,1)S(1)} %dynamic-slice_convert_fusion.3), channel_id=1, source_target_pairs={{0,2},{2,0},{1,3},{3,1},{4,6},{6,4},{5,7},{7,5},{8,10},{10,8},{9,1... | collective-permute-start | bytes 73736 | tf_op jit(solution)/shard_map/ppermute | solution.py:42
  178.1 0.1 convert_reduce_fusion.1
  178.2 0.6 add.126
  178.8 10.2 %collective-permute-done.10 = bf16[8,1536]{1,0:T(8,128)(2,1)S(1)} collective-permute-done((bf16[8,1536]{1,0:T(8,128)(2,1)S(1)}, bf16[8,1536]{1,0:T(8,128)(2,1)S(1)}, u32[]{:S(2)}, u32[]{:S(2)}) %collective-permute-start.10) | collective-permute-done | bytes 24608 | tf_op jit(solution)/shard_map/ppermute | solution.py:42
  189.0 0.6 add_convert_fusion.1
  189.6 1.5 fusion.19
  191.1 1.7 fusion.1
  (25 shorter events, 0.3 us)
Async XLA Ops:
  0.6 33.0 %copy-start.2 = (bf16[1536,384]{1,0:T(8,128)(2,1)S(1)}, bf16[1536,384]{1,0:T(8,128)(2,1)}, u32[]{:S(2)}) copy-start(bf16[1536,384]{1,0:T(8,128)(2,1)} %param.7) | copy-start | bytes 3538948
  2.2 17.7 %collective-permute-start = (bf16[8,2304]{1,0:T(8,128)(2,1)S(1)}, bf16[8,2304]{1,0:T(8,128)(2,1)S(1)}, u32[]{:S(2)}, u32[]{:S(2)}) collective-permute-start(bf16[8,2304]{1,0:T(8,128)(2,1)S(1)} %pad_maximum_fusion), channel_id=1, source_target_pairs={{0,2},{2,0},{1,3},{3,1},{4,6},{6,4},{5,7},{7,5},{8,10},{10,8},{9,1... | collective-permute-start | bytes 110600 | tf_op jit(solution)/shard_map/ppermute | solution.py:42
  20.0 13.7 %collective-permute-start.1 = (bf16[1536,384]{1,0:T(8,128)(2,1)}, bf16[1536,384]{1,0:T(8,128)(2,1)S(1)}, u32[]{:S(2)}, u32[]{:S(2)}) collective-permute-start(bf16[1536,384]{1,0:T(8,128)(2,1)} %param.7), channel_id=1, source_target_pairs={{0,1},{1,0},{2,3},{3,2},{4,5},{5,4},{6,7},{7,6},{8,9},{9,8},{10,11... | collective-permute-start | bytes 3538952 | tf_op jit(solution)/shard_map/ppermute | solution.py:42
  25.6 9.9 %collective-permute-start.2 = (bf16[1536,384]{1,0:T(8,128)(2,1)}, bf16[1536,384]{1,0:T(8,128)(2,1)}, u32[]{:S(2)}, u32[]{:S(2)}) collective-permute-start(bf16[1536,384]{1,0:T(8,128)(2,1)} %param.9), channel_id=1, source_target_pairs={{0,1},{1,0},{2,3},{3,2},{4,5},{5,4},{6,7},{7,6},{8,9},{9,8},{10,11... | collective-permute-start | bytes 3538952 | tf_op jit(solution)/shard_map/ppermute | solution.py:42
  29.1 13.6 %all-to-all-start = ((bf16[16,16,768]{2,1,0:T(8,128)(2,1)}), bf16[16,16,768]{2,1,0:T(8,128)(2,1)S(1)}, u32[]{:S(2)}, u32[]{:S(2)}) async-start(bf16[16,16,768]{2,1,0:T(8,128)(2,1)} %broadcast_in_dim.6), calls=%async_computation | async-start | bytes 786432 | tf_op jit(solution)/shard_map/all_to_all | solution.py:76
  33.6 1.8 copy-start.3
  43.5 1.1 copy-start
  44.7 11.0 %copy-start.1 = (f32[2,2,64,1536]{3,2,1,0:T(8,128)S(1)}, f32[2,2,64,1536]{3,2,1,0:T(8,128)}, u32[]{:S(2)}) copy-start(f32[2,2,64,1536]{3,2,1,0:T(8,128)} %copy-done) | copy-start | bytes 4718596
  44.7 11.0 %collective-permute-start.3 = (bf16[2,1,64,1536]{3,2,1,0:T(8,128)(2,1)S(1)}, bf16[2,1,64,1536]{3,2,1,0:T(8,128)(2,1)}, u32[]{:S(2)}, u32[]{:S(2)}) collective-permute-start(bf16[2,1,64,1536]{3,2,1,0:T(8,128)(2,1)S(1)} %dynamic-slice_convert_fusion), channel_id=1, source_target_pairs={{0,64},{64,0},{1,65},{65,1},{2,66},{66,2},{3,67},{67,3},{4,68},{68... | collective-permute-start | bytes 1179656 | tf_op jit(solution)/shard_map/ppermute | solution.py:42
  48.9 15.6 %all-to-all-start.1 = ((bf16[16,16,1536]{2,1,0:T(8,128)(2,1)}), bf16[16,16,1536]{2,1,0:T(8,128)(2,1)S(1)}, u32[]{:S(2)}, u32[]{:S(2)}) async-start(bf16[16,16,1536]{2,1,0:T(8,128)(2,1)} %broadcast_in_dim.7), calls=%async_computation.1 | async-start | bytes 1572864 | tf_op jit(solution)/shard_map/all_to_all | solution.py:76
  67.6 45.2 %copy-start.4 = (f32[1536]{0:T(1024)S(1)}, f32[1536]{0:T(1024)}, u32[]{:S(2)}) copy-start(f32[1536]{0:T(1024)} %param.8) | copy-start | bytes 18436
  67.6 32.1 %all-to-all-start.2 = ((bf16[4,64,768]{2,1,0:T(8,128)(2,1)}), bf16[4,64,768]{2,1,0:T(8,128)(2,1)S(1)}, u32[]{:S(2)}, u32[]{:S(2)}) async-start(bf16[4,64,768]{2,1,0:T(8,128)(2,1)} %bitcast.6), calls=%async_computation.2 | async-start | bytes 786432 | tf_op jit(solution)/shard_map/all_to_all | solution.py:82
  71.2 18.5 %collective-permute-start.4 = (bf16[1,1,64,1536]{3,2,1,0:T(8,128)(2,1)S(1)}, bf16[1,1,64,1536]{3,2,1,0:T(8,128)(2,1)}, u32[]{:S(2)}, u32[]{:S(2)}) collective-permute-start(bf16[1,1,64,1536]{3,2,1,0:T(8,128)(2,1)S(1)} %dynamic-slice_convert_fusion.1), channel_id=1, source_target_pairs={{0,128},{128,0},{1,129},{129,1},{2,130},{130,2},{3,131},{131,3},{4... | collective-permute-start | bytes 589832 | tf_op jit(solution)/shard_map/ppermute | solution.py:42
  76.2 23.6 %collective-permute-start.8 = (bf16[256,384]{1,0:T(8,128)(2,1)}, bf16[256,384]{1,0:T(8,128)(2,1)}, u32[]{:S(2)}, u32[]{:S(2)}) collective-permute-start(bf16[256,384]{1,0:T(8,128)(2,1)} %constant_dynamic-slice_fusion.1), channel_id=1, source_target_pairs={{0,1},{1,0},{2,3},{3,2},{4,5},{5,4},{6,7},{7,6},{8,9},{9,8},{10,11... | collective-permute-start | bytes 589832 | tf_op jit(solution)/shard_map/ppermute | solution.py:42
  81.9 17.9 %collective-permute-start.7 = (bf16[256,1536]{1,0:T(8,128)(2,1)S(1)}, bf16[256,1536]{1,0:T(8,128)(2,1)S(1)}, u32[]{:S(2)}, u32[]{:S(2)}) collective-permute-start(bf16[256,1536]{1,0:T(8,128)(2,1)S(1)} %bitcast.39), channel_id=1, source_target_pairs={{0,1},{1,0},{2,3},{3,2},{4,5},{5,4},{6,7},{7,6},{8,9},{9,8},{10,11... | collective-permute-start | bytes 2359304 | tf_op jit(solution)/shard_map/ppermute | solution.py:42
  90.7 15.8 %collective-permute-start.5 = (bf16[64,768]{1,0:T(8,128)(2,1)S(1)}, bf16[64,768]{1,0:T(8,128)(2,1)S(1)}, u32[]{:S(2)}, u32[]{:S(2)}) collective-permute-start(bf16[64,768]{1,0:T(8,128)(2,1)S(1)} %fusion.16), channel_id=1, source_target_pairs={{0,258},{2,256},{256,2},{258,0},{1,259},{3,257},{257,3},{259,1},{4... | collective-permute-start | bytes 294920 | tf_op jit(solution)/shard_map/ppermute | solution.py:66
  99.8 13.1 %collective-permute-start.9 = (bf16[64,768]{1,0:T(8,128)(2,1)S(1)}, bf16[64,768]{1,0:T(8,128)(2,1)S(1)}, u32[]{:S(2)}, u32[]{:S(2)}) collective-permute-start(bf16[64,768]{1,0:T(8,128)(2,1)S(1)} %fusion.15), channel_id=1, source_target_pairs={{0,256},{256,0},{1,257},{257,1},{2,258},{258,2},{3,259},{259,3},{4... | collective-permute-start | bytes 294920 | tf_op jit(solution)/shard_map/ppermute | solution.py:42
  106.6 17.3 %collective-permute-start.6 = (bf16[64,768]{1,0:T(8,128)(2,1)S(1)}, bf16[64,768]{1,0:T(8,128)(2,1)S(1)}, u32[]{:S(2)}, u32[]{:S(2)}) collective-permute-start(bf16[64,768]{1,0:T(8,128)(2,1)S(1)} %fusion.11), channel_id=1, source_target_pairs={{0,256},{256,0},{1,257},{257,1},{2,258},{258,2},{3,259},{259,3},{4... | collective-permute-start | bytes 294920 | tf_op jit(solution)/shard_map/ppermute | solution.py:42
  124.8 16.4 %all-to-all-start.3 = ((bf16[4,64,768]{2,1,0:T(8,128)(2,1)}), bf16[4,64,768]{2,1,0:T(8,128)(2,1)S(1)}, u32[]{:S(2)}, u32[]{:S(2)}) async-start(bf16[4,64,768]{2,1,0:T(8,128)(2,1)} %broadcast_in_dim.8), calls=%async_computation.3 | async-start | bytes 786432 | tf_op jit(solution)/shard_map/all_to_all | solution.py:76
  128.3 9.6 %collective-permute-start.11 = (bf16[64,768]{1,0:T(8,128)(2,1)S(1)}, bf16[64,768]{1,0:T(8,128)(2,1)S(1)}, u32[]{:S(2)}, u32[]{:S(2)}) collective-permute-start(bf16[64,768]{1,0:T(8,128)(2,1)S(1)} %get-tuple-element.24), channel_id=1, source_target_pairs={{0,258},{2,256},{256,2},{258,0},{1,259},{3,257},{257,3},{259,1},{4... | collective-permute-start | bytes 294920 | tf_op jit(solution)/shard_map/ppermute | solution.py:66
  144.6 9.8 %collective-permute-start.12 = (bf16[1,1,64,1536]{3,2,1,0:T(8,128)(2,1)S(1)}, bf16[1,1,64,1536]{3,2,1,0:T(8,128)(2,1)}, u32[]{:S(2)}, u32[]{:S(2)}) collective-permute-start(bf16[1,1,64,1536]{3,2,1,0:T(8,128)(2,1)S(1)} %maximum_select_fusion.4), channel_id=1, source_target_pairs={{0,128},{128,0},{1,129},{129,1},{2,130},{130,2},{3,131},{131,3},{4... | collective-permute-start | bytes 589832 | tf_op jit(solution)/shard_map/ppermute | solution.py:42
  150.5 25.0 %all-to-all-start.4 = ((bf16[16,16,1536]{2,1,0:T(8,128)(2,1)}), bf16[16,16,1536]{2,1,0:T(8,128)(2,1)S(1)}, u32[]{:S(2)}, u32[]{:S(2)}) async-start(bf16[16,16,1536]{2,1,0:T(8,128)(2,1)} %bitcast.10), calls=%async_computation.4 | async-start | bytes 1572864 | tf_op jit(solution)/shard_map/all_to_all | solution.py:82
  155.5 16.0 %collective-permute-start.14 = (bf16[2,1,64,1536]{3,2,1,0:T(8,128)(2,1)S(1)}, bf16[2,1,64,1536]{3,2,1,0:T(8,128)(2,1)S(1)}, u32[]{:S(2)}, u32[]{:S(2)}) collective-permute-start(bf16[2,1,64,1536]{3,2,1,0:T(8,128)(2,1)S(1)} %maximum_select_fusion.3), channel_id=1, source_target_pairs={{0,64},{64,0},{1,65},{65,1},{2,66},{66,2},{3,67},{67,3},{4,68},{68... | collective-permute-start | bytes 1179656 | tf_op jit(solution)/shard_map/ppermute | solution.py:42
  163.5 3.7 %collective-permute-start.13 = (bf16[256,384]{1,0:T(8,128)(2,1)S(1)}, bf16[256,384]{1,0:T(8,128)(2,1)S(1)}, u32[]{:S(2)}, u32[]{:S(2)}) collective-permute-start(bf16[256,384]{1,0:T(8,128)(2,1)S(1)} %constant_dynamic-slice_fusion), channel_id=1, source_target_pairs={{0,1},{1,0},{2,3},{3,2},{4,5},{5,4},{6,7},{7,6},{8,9},{9,8},{10,11... | collective-permute-start | bytes 589832 | tf_op jit(solution)/shard_map/ppermute | solution.py:42
  171.6 18.0 %collective-permute-start.15 = (bf16[256,1536]{1,0:T(8,128)(2,1)S(1)}, bf16[256,1536]{1,0:T(8,128)(2,1)S(1)}, u32[]{:S(2)}, u32[]{:S(2)}) collective-permute-start(bf16[256,1536]{1,0:T(8,128)(2,1)S(1)} %bitcast.36), channel_id=1, source_target_pairs={{0,1},{1,0},{2,3},{3,2},{4,5},{5,4},{6,7},{7,6},{8,9},{9,8},{10,11... | collective-permute-start | bytes 2359304 | tf_op jit(solution)/shard_map/ppermute | solution.py:42
  175.7 13.3 %collective-permute-start.10 = (bf16[8,1536]{1,0:T(8,128)(2,1)S(1)}, bf16[8,1536]{1,0:T(8,128)(2,1)S(1)}, u32[]{:S(2)}, u32[]{:S(2)}) collective-permute-start(bf16[8,1536]{1,0:T(8,128)(2,1)S(1)} %dynamic-slice_convert_fusion.3), channel_id=1, source_target_pairs={{0,2},{2,0},{1,3},{3,1},{4,6},{6,4},{5,7},{7,5},{8,10},{10,8},{9,1... | collective-permute-start | bytes 73736 | tf_op jit(solution)/shard_map/ppermute | solution.py:42

commit v7 on v6

--- a/solution.py
+++ b/solution.py
@@ -66,10 +66,6 @@
     return lax.ppermute(value, ("rh", "zh"), CROSS)
 
 
-def widen(mine, axis, dim):
-    return join(mine, swap(mine, axis), axis, dim)
-
-
 def spread(rows, axes):
     n = lax.axis_size(axes)
     sent = jnp.broadcast_to(rows[None], (n,) + rows.shape)
@@ -100,30 +96,30 @@
     kept = jnp.concatenate([tokens, part_of(cotangent, zh, half_d, 1)], 1)
     sent = jnp.concatenate([tokens, part_of(cotangent, 1 - zh, half_d, 1)], 1)
     got = swap(sent, "zh")
-    w_out, w_in = after(got, w_out, w_in)
-    out_pair = join(w_out, swap(w_out, "core"), "core", 1)
-    in_pair = join(w_in, swap(w_in, "core"), "core", 1)
-    in_pair, out_pair = after(got, in_pair, out_pair)
     rows = join(kept, got, "zh", 0)
+    w_out = after(rows, w_out)
+    out_pair = after(rows, join(w_out, swap(w_out, "core"), "core", 1))
 
     every_g = spread(rows[:, feat:], GRID)
     every_x = spread(after(every_g, rows[:, :feat]), GRID)
+    w_in = after(every_g, w_in)
+    in_pair = after(rows, join(w_in, swap(w_in, "core"), "core", 1))
 
     back = against(every_g, out_pair).reshape(2, 2, -1, 2 * half_h)
     back_kept, back_sent = cut(back, "rl", 1)
     back_kept, back_sent = cut(back_kept + swap(back_sent, "rl").astype(f32), "rm", 0)
     every_x = after(back_sent, every_x)
     pre = dot(every_x, in_pair).astype(bf16)
-    back = (back_kept + swap(back_sent, "rm").astype(f32))[0, 0]
-    pre = deal(pre, ROW4).astype(bf16)
-
-    back_kept, back_sent = cut(back, "zh", 1)
-    back = (back_kept + after(pre, cross(back_sent)).astype(f32)).astype(bf16)
+    back_got = swap(back_sent, "rm")
+    pre = deal(after(back_got, pre), ROW4).astype(bf16)
+    back_kept, back_sent = cut((back_kept + back_got.astype(f32))[0, 0], "zh", 1)
+    back = (back_kept + cross(back_sent).astype(f32)).astype(bf16)
     pair_x = swap(every_x, "core")
     pair_g = swap(part_of(every_g, 1 - core, quarter_d, 1), "core")
     pre = after((pair_x, pair_g), pre)
-    pre = pre.astype(f32) + swap(pre, "rh").astype(f32)
-    back = back.astype(f32) + swap(back, "rh").astype(f32)
+    met = jnp.concatenate([pre, back], 1)
+    met = met.astype(f32) + swap(met, "rh").astype(f32)
+    pre, back = met[:, :half_h], met[:, half_h:]
 
     act_f, slope = gelu_pair(pre + part_of(b_in, zh, half_h, 0))
     act = act_f.astype(bf16)
@@ -131,12 +127,11 @@
     grad = spread((back * slope).astype(bf16), ROW4)
     part = against(grad, in_pair).astype(bf16)
     summed = deal(part, GRID)
-    act = widen(after(part, act), "rm", 0)
+    act = join(act, after(part, swap(act, "rm")), "rm", 0)
     grad_sent = after(act, part_of(grad, 1 - core, quarter, 1))
-    act = widen(act, "rl", 1).reshape(-1, act.shape[-1])
+    act = join(act, swap(act, "rl"), "rl", 1).reshape(-1, act.shape[-1])
     out_rows = part_of(summed, 1 - zh, tok_dev, 0).astype(bf16)
     own_rows = part_of(summed, zh, tok_dev, 0)
-    input_grad = (own_rows + swap(out_rows, "zh").astype(f32)).astype(bf16)
 
     own_grad = part_of(grad, core, quarter, 1)
     pair_grad = swap(grad_sent, "core")
@@ -146,6 +141,8 @@
     own_g = part_of(every_g, core, quarter_d, 1)
     pair_act = swap(act, "core")
     w_out_grad = (over_rows(act, own_g) + over_rows(pair_act, pair_g)).astype(bf16)
+    got_rows = after(w_out_grad, swap(out_rows, "zh"))
+    input_grad = (own_rows + got_rows.astype(f32)).astype(bf16)
     return (input_grad, w_in_grad, b_in_grad, w_out_grad)
 
 

time: 194 us -> 194 us (level)
  waiting for transfers between devices: 59.7 us -> 30.3 us
  starting transfers between devices: 103 us -> 121 us
  blocking collectives: 0 us -> 13.4 us
    ppermute x14 -> x13, waiting for transfers between devices: 34.6 us -> 11.8 us  [swap(): return lax.ppermute(value, axis, SWAP)]
    all_to_all x0 -> x1, blocking collectives: none -> 13.4 us  [spread(): got = lax.all_to_all(sent, axes, 0, 0, tiled=True)]
    all_to_all x3 -> x2, waiting for transfers between devices: 16 us -> 2.99 us  [spread(): got = lax.all_to_all(sent, axes, 0, 0, tiled=True)]
    ppermute x2, starting transfers between devices: 11 us -> 21 us  [cross(): return lax.ppermute(value, ('rh', 'zh'), CROSS)]
    all_to_all x3 -> x2, starting transfers between devices: 11.6 us -> 20.8 us  [spread(): got = lax.all_to_all(sent, axes, 0, 0, tiled=True)]
    all_to_all x2, waiting for transfers between devices: 0.01 us -> 7.07 us  [deal(): lax.all_to_all(part.reshape(n, -1, part.shape[1]), axes, 0, 0, tiled=True)]
    ppermute x14 -> x13, starting transfers between devices: 73.3 us -> 71 us  [swap(): return lax.ppermute(value, axis, SWAP)]
  transfers between devices with their start and end apart: 21 -> 19, of which waited for: 12 -> 10; matrix products, arithmetic and copies ran while one was open for 7% -> 11% of each run, Pallas kernels for 0% -> 0%
where the time goes in v7:
time: 194 us; the launch traced here: 192 us
  starting transfers between devices  121 us (62%)
  waiting for transfers between devices  30.3 us (16%)
  blocking collectives  13.4 us (7%)
  matrix products  13 us (7%)
  other arithmetic  9.36 us (5%)
  local copies, waits for them, and re-layouts  3.53 us (2%)
    ppermute x13, starting transfers between devices, swap(): return lax.ppermute(value, axis, SWAP)  71 us
    ppermute x2, starting transfers between devices, cross(): return lax.ppermute(value, ('rh', 'zh'), CROSS)  21 us
    all_to_all x2, starting transfers between devices, spread(): got = lax.all_to_all(sent, axes, 0, 0, tiled=True)  20.8 us
    all_to_all x1, blocking collectives, spread(): got = lax.all_to_all(sent, axes, 0, 0, tiled=True)  13.4 us
    ppermute x13, waiting for transfers between devices, swap(): return lax.ppermute(value, axis, SWAP)  11.8 us
    all_to_all x2, starting transfers between devices, deal(): lax.all_to_all(part.reshape(n, -1, part.shape[1]), axes, 0, 0, tiled=True)  8.59 us
    ppermute x2, waiting for transfers between devices, cross(): return lax.ppermute(value, ('rh', 'zh'), CROSS)  8.43 us
    all_to_all x2, waiting for transfers between devices, deal(): lax.all_to_all(part.reshape(n, -1, part.shape[1]), axes, 0, 0, tiled=True)  7.07 us
  transfers between devices with their start and end apart: 19, of which 10 were waited for; matrix products, arithmetic and copies ran while one was open for 11% of the time, Pallas kernels for 0%

profile of v7, /device:TPU:1, one launch (start us, length us, event | category | flops | bytes accessed | tf_op | source)
XLA Modules:
  0.0 192.0 jit_solution(15917547733183123074)
XLA Ops:
  0.6 0.0 copy-start
  0.7 0.8 constant_dynamic-slice_fusion.3
  1.5 0.7 pad_maximum_fusion.1
  2.2 16.3 %collective-permute-start = (bf16[8,2304]{1,0:T(8,128)(2,1)S(1)}, bf16[8,2304]{1,0:T(8,128)(2,1)S(1)}, u32[]{:S(2)}, u32[]{:S(2)}) collective-permute-start(bf16[8,2304]{1,0:T(8,128)(2,1)S(1)} %pad_maximum_fusion.1), channel_id=1, source_target_pairs={{0,2},{2,0},{1,3},{3,1},{4,6},{6,4},{5,7},{7,5},{8,10},{10,8},{9,1... | collective-permute-start | bytes 110600 | tf_op jit(solution)/shard_map/ppermute | solution.py:42
  18.5 1.5 collective-permute-done
  20.0 0.8 maximum_select_fusion.6
  20.8 5.6 %collective-permute-start.1 = (bf16[1536,384]{1,0:T(8,128)(2,1)}, bf16[1536,384]{1,0:T(8,128)(2,1)S(1)}, u32[]{:S(2)}, u32[]{:S(2)}) collective-permute-start(bf16[1536,384]{1,0:T(8,128)(2,1)} %param.9), channel_id=1, source_target_pairs={{0,1},{1,0},{2,3},{3,2},{4,5},{5,4},{6,7},{7,6},{8,9},{9,8},{10,11... | collective-permute-start | bytes 3538952 | tf_op jit(solution)/shard_map/ppermute | solution.py:42
  26.4 13.4 %all_to_all.25 = bf16[16,16,768]{2,1,0:T(8,128)(2,1)S(1)} all-to-all(bf16[16,16,768]{2,1,0:T(8,128)(2,1)S(1)} %broadcast_in_dim.6), channel_id=1, replica_groups=mesh['rh'=2,'rm'=2,'rl'=2,'x'=4,'y'=4,'zh'=2,'core'=2] {'x','y'}, dimensions={0} | all-to-all | bytes 786432 | tf_op jit(solution)/shard_map/all_to_all | solution.py:72
  39.8 3.6 %collective-permute-start.6 = (bf16[1536,384]{1,0:T(8,128)(2,1)}, bf16[1536,384]{1,0:T(8,128)(2,1)}, u32[]{:S(2)}, u32[]{:S(2)}) collective-permute-start(bf16[1536,384]{1,0:T(8,128)(2,1)} %param.7), channel_id=1, source_target_pairs={{0,1},{1,0},{2,3},{3,2},{4,5},{5,4},{6,7},{7,6},{8,9},{9,8},{10,11... | collective-permute-start | bytes 3538952 | tf_op jit(solution)/shard_map/ppermute | solution.py:42
  43.4 0.0 collective-permute-done.1
  43.5 0.6 maximum_select_fusion
  44.1 0.8 fusion.2
  44.9 0.1 dynamic-slice_convert_fusion
  45.0 3.1 %collective-permute-start.2 = (bf16[2,1,64,1536]{3,2,1,0:T(8,128)(2,1)S(1)}, bf16[2,1,64,1536]{3,2,1,0:T(8,128)(2,1)}, u32[]{:S(2)}, u32[]{:S(2)}) collective-permute-start(bf16[2,1,64,1536]{3,2,1,0:T(8,128)(2,1)S(1)} %dynamic-slice_convert_fusion), channel_id=1, source_target_pairs={{0,64},{64,0},{1,65},{65,1},{2,66},{66,2},{3,67},{67,3},{4,68},{68... | collective-permute-start | bytes 1179656 | tf_op jit(solution)/shard_map/ppermute | solution.py:42
  48.1 1.0 broadcast_in_dim.7
  49.0 3.6 %all-to-all-start.1 = ((bf16[16,16,1536]{2,1,0:T(8,128)(2,1)}), bf16[16,16,1536]{2,1,0:T(8,128)(2,1)S(1)}, u32[]{:S(2)}, u32[]{:S(2)}) async-start(bf16[16,16,1536]{2,1,0:T(8,128)(2,1)} %broadcast_in_dim.7), calls=%async_computation.1 | async-start | bytes 1572864 | tf_op jit(solution)/shard_map/all_to_all | solution.py:72
  52.7 0.0 collective-permute-done.6
  52.7 4.1 %maximum_select_fusion.1 = bf16[1536,768]{1,0:T(8,128)(2,1)} fusion(bf16[1536,384]{1,0:T(8,128)(2,1)} %collective-permute-done.6, bf16[1536,384]{1,0:T(8,128)(2,1)} %param.7, pred[]{:T(512)S(6)} %eq.15), kind=kLoop, calls=%fused_computation.6 | loop fusion | flops 10616832 | bytes 4718593 | tf_op jit(solution)/shard_map/jit(_where)/select_n | solution.py:47
  56.8 0.9 collective-permute-done.2
  57.7 1.1 convert_add_fusion
  58.8 3.6 %collective-permute-start.5 = (bf16[1,1,64,1536]{3,2,1,0:T(8,128)(2,1)S(1)}, bf16[1,1,64,1536]{3,2,1,0:T(8,128)(2,1)S(1)}, u32[]{:S(2)}, u32[]{:S(2)}) collective-permute-start(bf16[1,1,64,1536]{3,2,1,0:T(8,128)(2,1)S(1)} %dynamic-slice_convert_fusion.1), channel_id=1, source_target_pairs={{0,128},{128,0},{1,129},{129,1},{2,130},{130,2},{3,131},{131,3},{4... | collective-permute-start | bytes 589832 | tf_op jit(solution)/shard_map/ppermute | solution.py:42
  62.4 3.0 %all-to-all-done.1 = bf16[16,16,1536]{2,1,0:T(8,128)(2,1)S(1)} async-done(((bf16[16,16,1536]{2,1,0:T(8,128)(2,1)}), bf16[16,16,1536]{2,1,0:T(8,128)(2,1)S(1)}, u32[]{:S(2)}, u32[]{:S(2)}) %all-to-all-start.1) | async-done | bytes 786464 | tf_op jit(solution)/shard_map/all_to_all | solution.py:72
  65.4 3.2 %convolution_convert_fusion.1 = bf16[256,768]{1,0:T(8,128)(2,1)} fusion(bf16[256,1536]{1,0:T(8,128)(2,1)S(1)} %bitcast.42, bf16[1536,768]{1,0:T(8,128)(2,1)} %maximum_select_fusion.1), kind=kOutput, calls=%fused_computation.10 | convolution fusion | flops 604176384 | bytes 3538944 | tf_op jit(solution)/shard_map/dot_general | solution.py:26
  68.6 3.1 %collective-permute-done.5 = bf16[1,1,64,1536]{3,2,1,0:T(8,128)(2,1)S(1)} collective-permute-done((bf16[1,1,64,1536]{3,2,1,0:T(8,128)(2,1)S(1)}, bf16[1,1,64,1536]{3,2,1,0:T(8,128)(2,1)S(1)}, u32[]{:S(2)}, u32[]{:S(2)}) %collective-permute-start.5) | collective-permute-done | bytes 196640 | tf_op jit(solution)/shard_map/ppermute | solution.py:42
  71.7 3.5 %all-to-all-start.2 = ((bf16[4,64,768]{2,1,0:T(8,128)(2,1)}), bf16[4,64,768]{2,1,0:T(8,128)(2,1)S(1)}, u32[]{:S(2)}, u32[]{:S(2)}) async-start(bf16[4,64,768]{2,1,0:T(8,128)(2,1)} %bitcast.5), calls=%async_computation.2 | async-start | bytes 786432 | tf_op jit(solution)/shard_map/all_to_all | solution.py:78
  75.2 3.4 %collective-permute-start.3 = (bf16[256,1536]{1,0:T(8,128)(2,1)S(1)}, bf16[256,1536]{1,0:T(8,128)(2,1)}, u32[]{:S(2)}, u32[]{:S(2)}) collective-permute-start(bf16[256,1536]{1,0:T(8,128)(2,1)S(1)} %bitcast.43), channel_id=1, source_target_pairs={{0,1},{1,0},{2,3},{3,2},{4,5},{5,4},{6,7},{7,6},{8,9},{9,8},{10,11... | collective-permute-start | bytes 2359304 | tf_op jit(solution)/shard_map/ppermute | solution.py:42
  78.6 9.4 %collective-permute-start.7 = (bf16[64,768]{1,0:T(8,128)(2,1)S(1)}, bf16[64,768]{1,0:T(8,128)(2,1)S(1)}, u32[]{:S(2)}, u32[]{:S(2)}) collective-permute-start(bf16[64,768]{1,0:T(8,128)(2,1)S(1)} %fusion.17), channel_id=1, source_target_pairs={{0,258},{2,256},{256,2},{258,0},{1,259},{3,257},{257,3},{259,1},{4... | collective-permute-start | bytes 294920 | tf_op jit(solution)/shard_map/ppermute | solution.py:66
  88.1 2.2 %collective-permute-start.4 = (bf16[256,384]{1,0:T(8,128)(2,1)S(1)}, bf16[256,384]{1,0:T(8,128)(2,1)S(1)}, u32[]{:S(2)}, u32[]{:S(2)}) collective-permute-start(bf16[256,384]{1,0:T(8,128)(2,1)S(1)} %constant_dynamic-slice_fusion.1), channel_id=1, source_target_pairs={{0,1},{1,0},{2,3},{3,2},{4,5},{5,4},{6,7},{7,6},{8,9},{9,8},{10,11... | collective-permute-start | bytes 589832 | tf_op jit(solution)/shard_map/ppermute | solution.py:42
  90.3 1.3 collective-permute-done.7
  91.6 0.0 all-to-all-done.2
  91.7 0.1 fusion.16
  91.7 0.0 collective-permute-done.4
  91.7 0.0 collective-permute-done.3
  91.8 6.0 %collective-permute-start.8 = (bf16[64,1536]{1,0:T(8,128)(2,1)S(1)}, bf16[64,1536]{1,0:T(8,128)(2,1)S(1)}, u32[]{:S(2)}, u32[]{:S(2)}) collective-permute-start(bf16[64,1536]{1,0:T(8,128)(2,1)S(1)} %pad_maximum_fusion), channel_id=1, source_target_pairs={{0,256},{256,0},{1,257},{257,1},{2,258},{258,2},{3,259},{259,3},{4... | collective-permute-start | bytes 589832 | tf_op jit(solution)/shard_map/ppermute | solution.py:42
  97.8 0.1 dynamic_slice.57
  97.9 4.2 %collective-permute-done.8 = bf16[64,1536]{1,0:T(8,128)(2,1)S(1)} collective-permute-done((bf16[64,1536]{1,0:T(8,128)(2,1)S(1)}, bf16[64,1536]{1,0:T(8,128)(2,1)S(1)}, u32[]{:S(2)}, u32[]{:S(2)}) %collective-permute-start.8) | collective-permute-done | bytes 196640 | tf_op jit(solution)/shard_map/ppermute | solution.py:42
  102.1 0.2 multiply_convert_fusion
  102.3 0.8 broadcast_in_dim.8
  103.1 17.2 %all-to-all-start.3 = ((bf16[4,64,768]{2,1,0:T(8,128)(2,1)}), bf16[4,64,768]{2,1,0:T(8,128)(2,1)S(1)}, u32[]{:S(2)}, u32[]{:S(2)}) async-start(bf16[4,64,768]{2,1,0:T(8,128)(2,1)} %broadcast_in_dim.8), calls=%async_computation.3 | async-start | bytes 786432 | tf_op jit(solution)/shard_map/all_to_all | solution.py:72
  120.3 11.5 %collective-permute-start.9 = (bf16[64,768]{1,0:T(8,128)(2,1)S(1)}, bf16[64,768]{1,0:T(8,128)(2,1)S(1)}, u32[]{:S(2)}, u32[]{:S(2)}) collective-permute-start(bf16[64,768]{1,0:T(8,128)(2,1)S(1)} %get-tuple-element.26), channel_id=1, source_target_pairs={{0,258},{2,256},{256,2},{258,0},{1,259},{3,257},{257,3},{259,1},{4... | collective-permute-start | bytes 294920 | tf_op jit(solution)/shard_map/ppermute | solution.py:66
  131.8 7.1 %collective-permute-done.9 = bf16[64,768]{1,0:T(8,128)(2,1)S(1)} collective-permute-done((bf16[64,768]{1,0:T(8,128)(2,1)S(1)}, bf16[64,768]{1,0:T(8,128)(2,1)S(1)}, u32[]{:S(2)}, u32[]{:S(2)}) %collective-permute-start.9) | collective-permute-done | bytes 98336 | tf_op jit(solution)/shard_map/ppermute | solution.py:66
  139.0 3.1 %collective-permute-start.10 = (bf16[1,1,64,1536]{3,2,1,0:T(8,128)(2,1)S(1)}, bf16[1,1,64,1536]{3,2,1,0:T(8,128)(2,1)S(1)}, u32[]{:S(2)}, u32[]{:S(2)}) collective-permute-start(bf16[1,1,64,1536]{3,2,1,0:T(8,128)(2,1)S(1)} %maximum_select_fusion.5), channel_id=1, source_target_pairs={{0,128},{128,0},{1,129},{129,1},{2,130},{130,2},{3,131},{131,3},{4... | collective-permute-start | bytes 589832 | tf_op jit(solution)/shard_map/ppermute | solution.py:42
  142.2 3.4 %convolution_convert_fusion = bf16[256,1536]{1,0:T(8,128)(2,1)} fusion(bf16[256,768]{1,0:T(8,128)(2,1)S(1)} %bitcast.45, bf16[1536,768]{1,0:T(8,128)(2,1)} %maximum_select_fusion.1), kind=kOutput, calls=%fused_computation.4 | convolution fusion | flops 604372992 | bytes 3538944 | tf_op jit(solution)/shard_map/dot_general | solution.py:30
  145.5 0.8 collective-permute-done.10
  146.3 7.1 %collective-permute-start.11 = (bf16[2,1,64,1536]{3,2,1,0:T(8,128)(2,1)S(1)}, bf16[2,1,64,1536]{3,2,1,0:T(8,128)(2,1)S(1)}, u32[]{:S(2)}, u32[]{:S(2)}) collective-permute-start(bf16[2,1,64,1536]{3,2,1,0:T(8,128)(2,1)S(1)} %maximum_select_fusion.3), channel_id=1, source_target_pairs={{0,64},{64,0},{1,65},{65,1},{2,66},{66,2},{3,67},{67,3},{4,68},{68... | collective-permute-start | bytes 1179656 | tf_op jit(solution)/shard_map/ppermute | solution.py:42
  153.5 0.7 constant_dynamic-slice_fusion
  154.2 5.1 %collective-permute-start.14 = (bf16[256,384]{1,0:T(8,128)(2,1)}, bf16[256,384]{1,0:T(8,128)(2,1)S(1)}, u32[]{:S(2)}, u32[]{:S(2)}) collective-permute-start(bf16[256,384]{1,0:T(8,128)(2,1)} %constant_dynamic-slice_fusion), channel_id=1, source_target_pairs={{0,1},{1,0},{2,3},{3,2},{4,5},{5,4},{6,7},{7,6},{8,9},{9,8},{10,11... | collective-permute-start | bytes 589832 | tf_op jit(solution)/shard_map/ppermute | solution.py:42
  159.3 5.1 %all-to-all-start.4 = ((bf16[16,16,1536]{2,1,0:T(8,128)(2,1)}), bf16[16,16,1536]{2,1,0:T(8,128)(2,1)S(1)}, u32[]{:S(2)}, u32[]{:S(2)}) async-start(bf16[16,16,1536]{2,1,0:T(8,128)(2,1)} %bitcast.51), calls=%async_computation.4 | async-start | bytes 1572864 | tf_op jit(solution)/shard_map/all_to_all | solution.py:78
  164.4 0.6 fusion.14
  165.0 0.1 convert_reduce_fusion.2
  165.1 0.1 maximum_select_fusion.2
  165.2 2.2 %collective-permute-start.12 = (bf16[256,1536]{1,0:T(8,128)(2,1)S(1)}, bf16[256,1536]{1,0:T(8,128)(2,1)S(1)}, u32[]{:S(2)}, u32[]{:S(2)}) collective-permute-start(bf16[256,1536]{1,0:T(8,128)(2,1)S(1)} %bitcast.40), channel_id=1, source_target_pairs={{0,1},{1,0},{2,3},{3,2},{4,5},{5,4},{6,7},{7,6},{8,9},{9,8},{10,11... | collective-permute-start | bytes 2359304 | tf_op jit(solution)/shard_map/ppermute | solution.py:42
  167.4 0.0 collective-permute-done.14
  167.4 0.1 convert_reduce_fusion.1
  167.5 0.6 add.123
  168.1 2.8 %fusion.1 = bf16[1536,384]{1,0:T(8,128)(2,1)} fusion(f32[1536,384]{1,0:T(8,128)S(1)} %fusion.14, bf16[256,1536]{1,0:T(8,128)(2,1)} %collective-permute-done.3, bf16[256,384]{1,0:T(8,128)(2,1)S(1)} %collective-permute-done.14), kind=kOutput, calls=%fused_computation.3 | convolution fusion | flops 303169536 | bytes 4521984 | tf_op jit(solution)/shard_map/dot_general | solution.py:34
  170.8 7.1 %all-to-all-done.4 = bf16[16,16,1536]{2,1,0:T(8,128)(2,1)S(1)} async-done(((bf16[16,16,1536]{2,1,0:T(8,128)(2,1)}), bf16[16,16,1536]{2,1,0:T(8,128)(2,1)S(1)}, u32[]{:S(2)}, u32[]{:S(2)}) %all-to-all-start.4) | async-done | bytes 786464 | tf_op jit(solution)/shard_map/all_to_all | solution.py:78
  177.9 0.1 convert_reduce_fusion
  178.0 9.8 %collective-permute-start.13 = (bf16[8,1536]{1,0:T(8,128)(2,1)S(1)}, bf16[8,1536]{1,0:T(8,128)(2,1)S(1)}, u32[]{:S(2)}, u32[]{:S(2)}) collective-permute-start(bf16[8,1536]{1,0:T(8,128)(2,1)S(1)} %dynamic-slice_convert_fusion.3), channel_id=1, source_target_pairs={{0,2},{2,0},{1,3},{3,1},{4,6},{6,4},{5,7},{7,5},{8,10},{10,8},{9,1... | collective-permute-start | bytes 73736 | tf_op jit(solution)/shard_map/ppermute | solution.py:42
  187.8 0.0 collective-permute-done.12
  187.8 0.6 fusion.20
  188.4 1.6 fusion
  190.1 1.4 collective-permute-done.13
  191.4 0.6 add_convert_fusion.1
  (19 shorter events, 0.4 us)
Async XLA Ops:
  0.6 42.8 %copy-start = (bf16[1536,384]{1,0:T(8,128)(2,1)S(1)}, bf16[1536,384]{1,0:T(8,128)(2,1)}, u32[]{:S(2)}) copy-start(bf16[1536,384]{1,0:T(8,128)(2,1)} %param.9) | copy-start | bytes 3538948
  2.2 17.7 %collective-permute-start = (bf16[8,2304]{1,0:T(8,128)(2,1)S(1)}, bf16[8,2304]{1,0:T(8,128)(2,1)S(1)}, u32[]{:S(2)}, u32[]{:S(2)}) collective-permute-start(bf16[8,2304]{1,0:T(8,128)(2,1)S(1)} %pad_maximum_fusion.1), channel_id=1, source_target_pairs={{0,2},{2,0},{1,3},{3,1},{4,6},{6,4},{5,7},{7,5},{8,10},{10,8},{9,1... | collective-permute-start | bytes 110600 | tf_op jit(solution)/shard_map/ppermute | solution.py:42
  20.8 22.7 %collective-permute-start.1 = (bf16[1536,384]{1,0:T(8,128)(2,1)}, bf16[1536,384]{1,0:T(8,128)(2,1)S(1)}, u32[]{:S(2)}, u32[]{:S(2)}) collective-permute-start(bf16[1536,384]{1,0:T(8,128)(2,1)} %param.9), channel_id=1, source_target_pairs={{0,1},{1,0},{2,3},{3,2},{4,5},{5,4},{6,7},{7,6},{8,9},{9,8},{10,11... | collective-permute-start | bytes 3538952 | tf_op jit(solution)/shard_map/ppermute | solution.py:42
  39.8 12.8 %collective-permute-start.6 = (bf16[1536,384]{1,0:T(8,128)(2,1)}, bf16[1536,384]{1,0:T(8,128)(2,1)}, u32[]{:S(2)}, u32[]{:S(2)}) collective-permute-start(bf16[1536,384]{1,0:T(8,128)(2,1)} %param.7), channel_id=1, source_target_pairs={{0,1},{1,0},{2,3},{3,2},{4,5},{5,4},{6,7},{7,6},{8,9},{9,8},{10,11... | collective-permute-start | bytes 3538952 | tf_op jit(solution)/shard_map/ppermute | solution.py:42
  45.0 12.7 %collective-permute-start.2 = (bf16[2,1,64,1536]{3,2,1,0:T(8,128)(2,1)S(1)}, bf16[2,1,64,1536]{3,2,1,0:T(8,128)(2,1)}, u32[]{:S(2)}, u32[]{:S(2)}) collective-permute-start(bf16[2,1,64,1536]{3,2,1,0:T(8,128)(2,1)S(1)} %dynamic-slice_convert_fusion), channel_id=1, source_target_pairs={{0,64},{64,0},{1,65},{65,1},{2,66},{66,2},{3,67},{67,3},{4,68},{68... | collective-permute-start | bytes 1179656 | tf_op jit(solution)/shard_map/ppermute | solution.py:42
  49.0 16.4 %all-to-all-start.1 = ((bf16[16,16,1536]{2,1,0:T(8,128)(2,1)}), bf16[16,16,1536]{2,1,0:T(8,128)(2,1)S(1)}, u32[]{:S(2)}, u32[]{:S(2)}) async-start(bf16[16,16,1536]{2,1,0:T(8,128)(2,1)} %broadcast_in_dim.7), calls=%async_computation.1 | async-start | bytes 1572864 | tf_op jit(solution)/shard_map/all_to_all | solution.py:72
  58.8 12.9 %collective-permute-start.5 = (bf16[1,1,64,1536]{3,2,1,0:T(8,128)(2,1)S(1)}, bf16[1,1,64,1536]{3,2,1,0:T(8,128)(2,1)S(1)}, u32[]{:S(2)}, u32[]{:S(2)}) collective-permute-start(bf16[1,1,64,1536]{3,2,1,0:T(8,128)(2,1)S(1)} %dynamic-slice_convert_fusion.1), channel_id=1, source_target_pairs={{0,128},{128,0},{1,129},{129,1},{2,130},{130,2},{3,131},{131,3},{4... | collective-permute-start | bytes 589832 | tf_op jit(solution)/shard_map/ppermute | solution.py:42
  68.6 29.2 %copy-start.1 = (f32[1536]{0:T(1024)S(1)}, f32[1536]{0:T(1024)}, u32[]{:S(2)}) copy-start(f32[1536]{0:T(1024)} %param.8) | copy-start | bytes 18436
  71.7 20.0 %all-to-all-start.2 = ((bf16[4,64,768]{2,1,0:T(8,128)(2,1)}), bf16[4,64,768]{2,1,0:T(8,128)(2,1)S(1)}, u32[]{:S(2)}, u32[]{:S(2)}) async-start(bf16[4,64,768]{2,1,0:T(8,128)(2,1)} %bitcast.5), calls=%async_computation.2 | async-start | bytes 786432 | tf_op jit(solution)/shard_map/all_to_all | solution.py:78
  75.2 16.6 %collective-permute-start.3 = (bf16[256,1536]{1,0:T(8,128)(2,1)S(1)}, bf16[256,1536]{1,0:T(8,128)(2,1)}, u32[]{:S(2)}, u32[]{:S(2)}) collective-permute-start(bf16[256,1536]{1,0:T(8,128)(2,1)S(1)} %bitcast.43), channel_id=1, source_target_pairs={{0,1},{1,0},{2,3},{3,2},{4,5},{5,4},{6,7},{7,6},{8,9},{9,8},{10,11... | collective-permute-start | bytes 2359304 | tf_op jit(solution)/shard_map/ppermute | solution.py:42
  78.6 13.0 %collective-permute-start.7 = (bf16[64,768]{1,0:T(8,128)(2,1)S(1)}, bf16[64,768]{1,0:T(8,128)(2,1)S(1)}, u32[]{:S(2)}, u32[]{:S(2)}) collective-permute-start(bf16[64,768]{1,0:T(8,128)(2,1)S(1)} %fusion.17), channel_id=1, source_target_pairs={{0,258},{2,256},{256,2},{258,0},{1,259},{3,257},{257,3},{259,1},{4... | collective-permute-start | bytes 294920 | tf_op jit(solution)/shard_map/ppermute | solution.py:66
  88.1 3.6 %collective-permute-start.4 = (bf16[256,384]{1,0:T(8,128)(2,1)S(1)}, bf16[256,384]{1,0:T(8,128)(2,1)S(1)}, u32[]{:S(2)}, u32[]{:S(2)}) collective-permute-start(bf16[256,384]{1,0:T(8,128)(2,1)S(1)} %constant_dynamic-slice_fusion.1), channel_id=1, source_target_pairs={{0,1},{1,0},{2,3},{3,2},{4,5},{5,4},{6,7},{7,6},{8,9},{9,8},{10,11... | collective-permute-start | bytes 589832 | tf_op jit(solution)/shard_map/ppermute | solution.py:42
  91.8 10.3 %collective-permute-start.8 = (bf16[64,1536]{1,0:T(8,128)(2,1)S(1)}, bf16[64,1536]{1,0:T(8,128)(2,1)S(1)}, u32[]{:S(2)}, u32[]{:S(2)}) collective-permute-start(bf16[64,1536]{1,0:T(8,128)(2,1)S(1)} %pad_maximum_fusion), channel_id=1, source_target_pairs={{0,256},{256,0},{1,257},{257,1},{2,258},{258,2},{3,259},{259,3},{4... | collective-permute-start | bytes 589832 | tf_op jit(solution)/shard_map/ppermute | solution.py:42
  103.1 39.1 %all-to-all-start.3 = ((bf16[4,64,768]{2,1,0:T(8,128)(2,1)}), bf16[4,64,768]{2,1,0:T(8,128)(2,1)S(1)}, u32[]{:S(2)}, u32[]{:S(2)}) async-start(bf16[4,64,768]{2,1,0:T(8,128)(2,1)} %broadcast_in_dim.8), calls=%async_computation.3 | async-start | bytes 786432 | tf_op jit(solution)/shard_map/all_to_all | solution.py:72
  120.3 18.7 %collective-permute-start.9 = (bf16[64,768]{1,0:T(8,128)(2,1)S(1)}, bf16[64,768]{1,0:T(8,128)(2,1)S(1)}, u32[]{:S(2)}, u32[]{:S(2)}) collective-permute-start(bf16[64,768]{1,0:T(8,128)(2,1)S(1)} %get-tuple-element.26), channel_id=1, source_target_pairs={{0,258},{2,256},{256,2},{258,0},{1,259},{3,257},{257,3},{259,1},{4... | collective-permute-start | bytes 294920 | tf_op jit(solution)/shard_map/ppermute | solution.py:66
  139.0 7.3 %collective-permute-start.10 = (bf16[1,1,64,1536]{3,2,1,0:T(8,128)(2,1)S(1)}, bf16[1,1,64,1536]{3,2,1,0:T(8,128)(2,1)S(1)}, u32[]{:S(2)}, u32[]{:S(2)}) collective-permute-start(bf16[1,1,64,1536]{3,2,1,0:T(8,128)(2,1)S(1)} %maximum_select_fusion.5), channel_id=1, source_target_pairs={{0,128},{128,0},{1,129},{129,1},{2,130},{130,2},{3,131},{131,3},{4... | collective-permute-start | bytes 589832 | tf_op jit(solution)/shard_map/ppermute | solution.py:42
  146.3 18.8 %collective-permute-start.11 = (bf16[2,1,64,1536]{3,2,1,0:T(8,128)(2,1)S(1)}, bf16[2,1,64,1536]{3,2,1,0:T(8,128)(2,1)S(1)}, u32[]{:S(2)}, u32[]{:S(2)}) collective-permute-start(bf16[2,1,64,1536]{3,2,1,0:T(8,128)(2,1)S(1)} %maximum_select_fusion.3), channel_id=1, source_target_pairs={{0,64},{64,0},{1,65},{65,1},{2,66},{66,2},{3,67},{67,3},{4,68},{68... | collective-permute-start | bytes 1179656 | tf_op jit(solution)/shard_map/ppermute | solution.py:42
  154.2 13.2 %collective-permute-start.14 = (bf16[256,384]{1,0:T(8,128)(2,1)}, bf16[256,384]{1,0:T(8,128)(2,1)S(1)}, u32[]{:S(2)}, u32[]{:S(2)}) collective-permute-start(bf16[256,384]{1,0:T(8,128)(2,1)} %constant_dynamic-slice_fusion), channel_id=1, source_target_pairs={{0,1},{1,0},{2,3},{3,2},{4,5},{5,4},{6,7},{7,6},{8,9},{9,8},{10,11... | collective-permute-start | bytes 589832 | tf_op jit(solution)/shard_map/ppermute | solution.py:42
  159.3 18.6 %all-to-all-start.4 = ((bf16[16,16,1536]{2,1,0:T(8,128)(2,1)}), bf16[16,16,1536]{2,1,0:T(8,128)(2,1)S(1)}, u32[]{:S(2)}, u32[]{:S(2)}) async-start(bf16[16,16,1536]{2,1,0:T(8,128)(2,1)} %bitcast.51), calls=%async_computation.4 | async-start | bytes 1572864 | tf_op jit(solution)/shard_map/all_to_all | solution.py:78
  165.2 22.6 %collective-permute-start.12 = (bf16[256,1536]{1,0:T(8,128)(2,1)S(1)}, bf16[256,1536]{1,0:T(8,128)(2,1)S(1)}, u32[]{:S(2)}, u32[]{:S(2)}) collective-permute-start(bf16[256,1536]{1,0:T(8,128)(2,1)S(1)} %bitcast.40), channel_id=1, source_target_pairs={{0,1},{1,0},{2,3},{3,2},{4,5},{5,4},{6,7},{7,6},{8,9},{9,8},{10,11... | collective-permute-start | bytes 2359304 | tf_op jit(solution)/shard_map/ppermute | solution.py:42
  178.0 13.4 %collective-permute-start.13 = (bf16[8,1536]{1,0:T(8,128)(2,1)S(1)}, bf16[8,1536]{1,0:T(8,128)(2,1)S(1)}, u32[]{:S(2)}, u32[]{:S(2)}) collective-permute-start(bf16[8,1536]{1,0:T(8,128)(2,1)S(1)} %dynamic-slice_convert_fusion.3), channel_id=1, source_target_pairs={{0,2},{2,0},{1,3},{3,1},{4,6},{6,4},{5,7},{7,5},{8,10},{10,8},{9,1... | collective-permute-start | bytes 73736 | tf_op jit(solution)/shard_map/ppermute | solution.py:42

commit v8 on v7

--- a/solution.py
+++ b/solution.py
@@ -76,8 +76,6 @@
 def deal(part, axes):
     n = lax.axis_size(axes)
     got = lax.all_to_all(part.reshape(n, -1, part.shape[1]), axes, 0, 0, tiled=True)
-    if n > 4:
-        return jnp.sum(got.astype(f32), axis=0)
     total = got[0].astype(f32)
     for at in range(1, n):
         total = total + got[at].astype(f32)
@@ -102,13 +100,13 @@
 
     every_g = spread(rows[:, feat:], GRID)
     every_x = spread(after(every_g, rows[:, :feat]), GRID)
-    w_in = after(every_g, w_in)
-    in_pair = after(rows, join(w_in, swap(w_in, "core"), "core", 1))
 
     back = against(every_g, out_pair).reshape(2, 2, -1, 2 * half_h)
     back_kept, back_sent = cut(back, "rl", 1)
+    w_in = after(back_sent, w_in)
+    in_pair = after(rows, join(w_in, swap(w_in, "core"), "core", 1))
     back_kept, back_sent = cut(back_kept + swap(back_sent, "rl").astype(f32), "rm", 0)
-    every_x = after(back_sent, every_x)
+    every_x = after((back_sent, in_pair), every_x)
     pre = dot(every_x, in_pair).astype(bf16)
     back_got = swap(back_sent, "rm")
     pre = deal(after(back_got, pre), ROW4).astype(bf16)
@@ -123,23 +121,25 @@
 
     act_f, slope = gelu_pair(pre + part_of(b_in, zh, half_h, 0))
     act = act_f.astype(bf16)
-    act = join(act, cross(act), "zh", 1)[None, None]
+    crossed = cross(act)
     grad = spread((back * slope).astype(bf16), ROW4)
     part = against(grad, in_pair).astype(bf16)
-    summed = deal(part, GRID)
-    act = join(act, after(part, swap(act, "rm")), "rm", 0)
-    grad_sent = after(act, part_of(grad, 1 - core, quarter, 1))
+    dealt = lax.all_to_all(part.reshape(-1, 2 * tok_dev, feat), GRID, 0, 0, tiled=True)
+
+    own_grad = part_of(grad, core, quarter, 1)
+    act = join(act, after(part, crossed), "zh", 1)[None, None]
+    act = join(act, swap(act, "rm"), "rm", 0)
+    own_part = over_rows(every_x, own_grad)
+    pair_grad = swap(after(act, part_of(grad, 1 - core, quarter, 1)), "core")
     act = join(act, swap(act, "rl"), "rl", 1).reshape(-1, act.shape[-1])
+    w_in_grad = (own_part + over_rows(pair_x, pair_grad)).astype(bf16)
+    b_in_grad = jnp.sum(own_grad.astype(f32), 0) + jnp.sum(pair_grad.astype(f32), 0)
+
+    summed = jnp.sum(after((w_in_grad, b_in_grad), dealt).astype(f32), axis=0)
     out_rows = part_of(summed, 1 - zh, tok_dev, 0).astype(bf16)
     own_rows = part_of(summed, zh, tok_dev, 0)
-
-    own_grad = part_of(grad, core, quarter, 1)
-    pair_grad = swap(grad_sent, "core")
-    w_in_grad = (over_rows(every_x, own_grad) + over_rows(pair_x, pair_grad)).astype(bf16)
-    b_in_grad = jnp.sum(own_grad.astype(f32), 0) + jnp.sum(pair_grad.astype(f32), 0)
-
     own_g = part_of(every_g, core, quarter_d, 1)
-    pair_act = swap(act, "core")
+    pair_act = swap(after(out_rows, act), "core")
     w_out_grad = (over_rows(act, own_g) + over_rows(pair_act, pair_g)).astype(bf16)
     got_rows = after(w_out_grad, swap(out_rows, "zh"))
     input_grad = (own_rows + got_rows.astype(f32)).astype(bf16)

time: 194 us -> 192 us (0.990)
  blocking collectives: 13.4 us -> 0 us
  starting transfers between devices: 121 us -> 126 us
  waiting for transfers between devices: 30.3 us -> 34.1 us
  local copies, waits for them, and re-layouts: 3.53 us -> 6.13 us
  other arithmetic: 9.36 us -> 11.7 us
    all_to_all x1 -> x0, blocking collectives: 13.4 us -> none  [spread(): got = lax.all_to_all(sent, axes, 0, 0, tiled=True)]
    ppermute x13, waiting for transfers between devices: 11.8 us -> 23.5 us  [swap(): return lax.ppermute(value, axis, SWAP)]
    all_to_all x2 -> x1, waiting for transfers between devices: 7.07 us -> 0.01 us  [deal(): lax.all_to_all(part.reshape(n, -1, part.shape[1]), axes, 0, 0, tiled=True)]
    all_to_all x2 -> x1, starting transfers between devices: 8.59 us -> 3.46 us  [deal(): lax.all_to_all(part.reshape(n, -1, part.shape[1]), axes, 0, 0, tiled=True)]
    all_to_all x2 -> x3, starting transfers between devices: 20.8 us -> 25.3 us  [spread(): got = lax.all_to_all(sent, axes, 0, 0, tiled=True)]
    ppermute x2, waiting for transfers between devices: 8.43 us -> 4.42 us  [cross(): return lax.ppermute(value, ('rh', 'zh'), CROSS)]
    all_to_all x0 -> x1, starting transfers between devices: none -> 3.61 us  [shards(): lax.all_to_all(part.reshape(-1, 2 * tok_dev, feat), GRID, 0, 0, tiled=True)]
    all_to_all x2 -> x3, waiting for transfers between devices: 2.99 us -> 6.18 us  [spread(): got = lax.all_to_all(sent, axes, 0, 0, tiled=True)]
  transfers between devices with their start and end apart: 19 -> 20, of which waited for: 10 -> 9; matrix products, arithmetic and copies ran while one was open for 11% -> 12% of each run, Pallas kernels for 0% -> 0%
where the time goes in v8:
time: 192 us; the launch traced here: 191 us
  starting transfers between devices  126 us (66%)
  waiting for transfers between devices  34.1 us (18%)
  matrix products  11.8 us (6%)
  other arithmetic  11.7 us (6%)
  local copies, waits for them, and re-layouts  6.13 us (3%)
    ppermute x13, starting transfers between devices, swap(): return lax.ppermute(value, axis, SWAP)  72.9 us
    all_to_all x3, starting transfers between devices, spread(): got = lax.all_to_all(sent, axes, 0, 0, tiled=True)  25.3 us
    ppermute x13, waiting for transfers between devices, swap(): return lax.ppermute(value, axis, SWAP)  23.5 us
    ppermute x2, starting transfers between devices, cross(): return lax.ppermute(value, ('rh', 'zh'), CROSS)  21 us
    select_n x6, other arithmetic, join(): jnp.where(first, jnp.concatenate([mine, other], dim), jnp.concatenate([ot...  8.08 us
    all_to_all x3, waiting for transfers between devices, spread(): got = lax.all_to_all(sent, axes, 0, 0, tiled=True)  6.18 us
    dot_general x4, matrix products, over_rows(): lax.dot_general(left, right, (((0,), (0,)), ((), ())), preferred_element_...  4.5 us
    ppermute x2, waiting for transfers between devices, cross(): return lax.ppermute(value, ('rh', 'zh'), CROSS)  4.42 us
  transfers between devices with their start and end apart: 20, of which 9 were waited for; matrix products, arithmetic and copies ran while one was open for 12% of the time, Pallas kernels for 0%

profile of v8, /device:TPU:1, one launch (start us, length us, event | category | flops | bytes accessed | tf_op | source)
XLA Modules:
  0.0 191.0 jit_solution(6283978018068815495)
XLA Ops:
  0.6 0.7 constant_dynamic-slice_fusion.3
  1.4 0.7 pad_maximum_fusion.1
  2.1 16.3 %collective-permute-start = (bf16[8,2304]{1,0:T(8,128)(2,1)S(1)}, bf16[8,2304]{1,0:T(8,128)(2,1)S(1)}, u32[]{:S(2)}, u32[]{:S(2)}) collective-permute-start(bf16[8,2304]{1,0:T(8,128)(2,1)S(1)} %pad_maximum_fusion.1), channel_id=1, source_target_pairs={{0,2},{2,0},{1,3},{3,1},{4,6},{6,4},{5,7},{7,5},{8,10},{10,8},{9,1... | collective-permute-start | bytes 110600 | tf_op jit(solution)/shard_map/ppermute | solution.py:42
  18.4 1.5 collective-permute-done
  19.9 0.8 maximum_select_fusion.6
  20.7 0.0 copy-start.2
  20.7 5.6 %collective-permute-start.1 = (bf16[1536,384]{1,0:T(8,128)(2,1)}, bf16[1536,384]{1,0:T(8,128)(2,1)}, u32[]{:S(2)}, u32[]{:S(2)}) collective-permute-start(bf16[1536,384]{1,0:T(8,128)(2,1)} %param.9), channel_id=1, source_target_pairs={{0,1},{1,0},{2,3},{3,2},{4,5},{5,4},{6,7},{7,6},{8,9},{9,8},{10,11... | collective-permute-start | bytes 3538952 | tf_op jit(solution)/shard_map/ppermute | solution.py:42
  26.3 0.8 broadcast_in_dim.6
  27.1 4.5 %all-to-all-start = ((bf16[16,16,768]{2,1,0:T(8,128)(2,1)}), bf16[16,16,768]{2,1,0:T(8,128)(2,1)S(1)}, u32[]{:S(2)}, u32[]{:S(2)}) async-start(bf16[16,16,768]{2,1,0:T(8,128)(2,1)} %broadcast_in_dim.6), calls=%async_computation | async-start | bytes 786432 | tf_op jit(solution)/shard_map/all_to_all | solution.py:72
  31.6 0.0 collective-permute-done.1
  31.6 2.9 %maximum_select_fusion = bf16[1536,768]{1,0:T(8,128)(2,1)S(1)} fusion(bf16[1536,384]{1,0:T(8,128)(2,1)} %collective-permute-done.1, bf16[1536,384]{1,0:T(8,128)(2,1)} %param.9, pred[]{:T(512)S(6)} %eq.15), kind=kLoop, calls=%fused_computation.5 | loop fusion | flops 10616832 | bytes 4718593 | tf_op jit(solution)/shard_map/jit(_where)/select_n | solution.py:47
  34.5 6.2 %all-to-all-done = bf16[16,16,768]{2,1,0:T(8,128)(2,1)S(1)} async-done(((bf16[16,16,768]{2,1,0:T(8,128)(2,1)}), bf16[16,16,768]{2,1,0:T(8,128)(2,1)S(1)}, u32[]{:S(2)}, u32[]{:S(2)}) %all-to-all-start) | async-done | bytes 393248 | tf_op jit(solution)/shard_map/all_to_all | solution.py:72
  40.7 0.8 fusion.2
  41.5 1.2 copy-done
  42.7 3.7 %collective-permute-start.3 = (bf16[1536,384]{1,0:T(8,128)(2,1)}, bf16[1536,384]{1,0:T(8,128)(2,1)}, u32[]{:S(2)}, u32[]{:S(2)}) collective-permute-start(bf16[1536,384]{1,0:T(8,128)(2,1)} %param.7), channel_id=1, source_target_pairs={{0,1},{1,0},{2,3},{3,2},{4,5},{5,4},{6,7},{7,6},{8,9},{9,8},{10,11... | collective-permute-start | bytes 3538952 | tf_op jit(solution)/shard_map/ppermute | solution.py:42
  46.5 3.1 %collective-permute-start.2 = (bf16[2,1,64,1536]{3,2,1,0:T(8,128)(2,1)S(1)}, bf16[2,1,64,1536]{3,2,1,0:T(8,128)(2,1)}, u32[]{:S(2)}, u32[]{:S(2)}) collective-permute-start(bf16[2,1,64,1536]{3,2,1,0:T(8,128)(2,1)S(1)} %dynamic-slice_convert_fusion), channel_id=1, source_target_pairs={{0,64},{64,0},{1,65},{65,1},{2,66},{66,2},{3,67},{67,3},{4,68},{68... | collective-permute-start | bytes 1179656 | tf_op jit(solution)/shard_map/ppermute | solution.py:42
  49.6 0.8 slice.33
  50.4 1.0 broadcast_in_dim.7
  51.3 3.6 %all-to-all-start.1 = ((bf16[16,16,1536]{2,1,0:T(8,128)(2,1)}), bf16[16,16,1536]{2,1,0:T(8,128)(2,1)S(1)}, u32[]{:S(2)}, u32[]{:S(2)}) async-start(bf16[16,16,1536]{2,1,0:T(8,128)(2,1)} %broadcast_in_dim.7), calls=%async_computation.1 | async-start | bytes 1572864 | tf_op jit(solution)/shard_map/all_to_all | solution.py:72
  55.0 4.2 %collective-permute-done.2 = bf16[2,1,64,1536]{3,2,1,0:T(8,128)(2,1)} collective-permute-done((bf16[2,1,64,1536]{3,2,1,0:T(8,128)(2,1)S(1)}, bf16[2,1,64,1536]{3,2,1,0:T(8,128)(2,1)}, u32[]{:S(2)}, u32[]{:S(2)}) %collective-permute-start.2) | collective-permute-done | bytes 393248 | tf_op jit(solution)/shard_map/ppermute | solution.py:42
  59.2 1.1 convert_add_fusion
  60.3 3.6 %collective-permute-start.6 = (bf16[1,1,64,1536]{3,2,1,0:T(8,128)(2,1)S(1)}, bf16[1,1,64,1536]{3,2,1,0:T(8,128)(2,1)S(1)}, u32[]{:S(2)}, u32[]{:S(2)}) collective-permute-start(bf16[1,1,64,1536]{3,2,1,0:T(8,128)(2,1)S(1)} %dynamic-slice_convert_fusion.1), channel_id=1, source_target_pairs={{0,128},{128,0},{1,129},{129,1},{2,130},{130,2},{3,131},{131,3},{4... | collective-permute-start | bytes 589832 | tf_op jit(solution)/shard_map/ppermute | solution.py:42
  63.9 0.0 collective-permute-done.3
  63.9 4.2 %maximum_select_fusion.1 = bf16[1536,768]{1,0:T(8,128)(2,1)} fusion(bf16[1536,384]{1,0:T(8,128)(2,1)} %collective-permute-done.3, bf16[1536,384]{1,0:T(8,128)(2,1)} %param.7, pred[]{:T(512)S(6)} %eq.15), kind=kLoop, calls=%fused_computation.6 | loop fusion | flops 10616832 | bytes 4718593 | tf_op jit(solution)/shard_map/jit(_where)/select_n | solution.py:47
  68.1 0.0 all-to-all-done.1
  68.1 3.2 %convolution_convert_fusion.1 = bf16[256,768]{1,0:T(8,128)(2,1)} fusion(bf16[256,1536]{1,0:T(8,128)(2,1)S(1)} %bitcast.42, bf16[1536,768]{1,0:T(8,128)(2,1)} %maximum_select_fusion.1), kind=kOutput, calls=%fused_computation.10 | convolution fusion | flops 604176384 | bytes 3538944 | tf_op jit(solution)/shard_map/dot_general | solution.py:26
  71.3 1.9 %collective-permute-done.6 = bf16[1,1,64,1536]{3,2,1,0:T(8,128)(2,1)S(1)} collective-permute-done((bf16[1,1,64,1536]{3,2,1,0:T(8,128)(2,1)S(1)}, bf16[1,1,64,1536]{3,2,1,0:T(8,128)(2,1)S(1)}, u32[]{:S(2)}, u32[]{:S(2)}) %collective-permute-start.6) | collective-permute-done | bytes 196640 | tf_op jit(solution)/shard_map/ppermute | solution.py:42
  73.2 3.5 %all-to-all-start.2 = ((bf16[4,64,768]{2,1,0:T(8,128)(2,1)}), bf16[4,64,768]{2,1,0:T(8,128)(2,1)S(1)}, u32[]{:S(2)}, u32[]{:S(2)}) async-start(bf16[4,64,768]{2,1,0:T(8,128)(2,1)} %bitcast.5), calls=%async_computation.2 | async-start | bytes 786432 | tf_op jit(solution)/shard_map/all_to_all | solution.py:78
  76.7 3.4 %collective-permute-start.4 = (bf16[256,1536]{1,0:T(8,128)(2,1)S(1)}, bf16[256,1536]{1,0:T(8,128)(2,1)S(1)}, u32[]{:S(2)}, u32[]{:S(2)}) collective-permute-start(bf16[256,1536]{1,0:T(8,128)(2,1)S(1)} %bitcast.43), channel_id=1, source_target_pairs={{0,1},{1,0},{2,3},{3,2},{4,5},{5,4},{6,7},{7,6},{8,9},{9,8},{10,11... | collective-permute-start | bytes 2359304 | tf_op jit(solution)/shard_map/ppermute | solution.py:42
  80.1 9.4 %collective-permute-start.7 = (bf16[64,768]{1,0:T(8,128)(2,1)S(1)}, bf16[64,768]{1,0:T(8,128)(2,1)S(1)}, u32[]{:S(2)}, u32[]{:S(2)}) collective-permute-start(bf16[64,768]{1,0:T(8,128)(2,1)S(1)} %fusion.17), channel_id=1, source_target_pairs={{0,258},{2,256},{256,2},{258,0},{1,259},{3,257},{257,3},{259,1},{4... | collective-permute-start | bytes 294920 | tf_op jit(solution)/shard_map/ppermute | solution.py:66
  89.6 2.2 %collective-permute-start.5 = (bf16[256,384]{1,0:T(8,128)(2,1)S(1)}, bf16[256,384]{1,0:T(8,128)(2,1)S(1)}, u32[]{:S(2)}, u32[]{:S(2)}) collective-permute-start(bf16[256,384]{1,0:T(8,128)(2,1)S(1)} %constant_dynamic-slice_fusion.1), channel_id=1, source_target_pairs={{0,1},{1,0},{2,3},{3,2},{4,5},{5,4},{6,7},{7,6},{8,9},{9,8},{10,11... | collective-permute-start | bytes 589832 | tf_op jit(solution)/shard_map/ppermute | solution.py:42
  91.8 1.4 collective-permute-done.7
  93.2 0.0 all-to-all-done.2
  93.2 0.1 fusion.16
  93.3 0.0 collective-permute-done.5
  93.3 0.0 collective-permute-done.4
  93.3 6.0 %collective-permute-start.8 = (bf16[64,1536]{1,0:T(8,128)(2,1)S(1)}, bf16[64,1536]{1,0:T(8,128)(2,1)S(1)}, u32[]{:S(2)}, u32[]{:S(2)}) collective-permute-start(bf16[64,1536]{1,0:T(8,128)(2,1)S(1)} %pad_maximum_fusion), channel_id=1, source_target_pairs={{0,256},{256,0},{1,257},{257,1},{2,258},{258,2},{3,259},{259,3},{4... | collective-permute-start | bytes 589832 | tf_op jit(solution)/shard_map/ppermute | solution.py:42
  99.3 0.1 dynamic_slice.57
  99.4 4.2 %collective-permute-done.8 = bf16[64,1536]{1,0:T(8,128)(2,1)S(1)} collective-permute-done((bf16[64,1536]{1,0:T(8,128)(2,1)S(1)}, bf16[64,1536]{1,0:T(8,128)(2,1)S(1)}, u32[]{:S(2)}, u32[]{:S(2)}) %collective-permute-start.8) | collective-permute-done | bytes 196640 | tf_op jit(solution)/shard_map/ppermute | solution.py:42
  103.7 0.2 multiply_convert_fusion
  103.8 0.8 broadcast_in_dim.8
  104.6 17.2 %all-to-all-start.3 = ((bf16[4,64,768]{2,1,0:T(8,128)(2,1)}), bf16[4,64,768]{2,1,0:T(8,128)(2,1)S(1)}, u32[]{:S(2)}, u32[]{:S(2)}) async-start(bf16[4,64,768]{2,1,0:T(8,128)(2,1)} %broadcast_in_dim.8), calls=%async_computation.3 | async-start | bytes 786432 | tf_op jit(solution)/shard_map/all_to_all | solution.py:72
  121.8 11.5 %collective-permute-start.9 = (bf16[64,768]{1,0:T(8,128)(2,1)S(1)}, bf16[64,768]{1,0:T(8,128)(2,1)S(1)}, u32[]{:S(2)}, u32[]{:S(2)}) collective-permute-start(bf16[64,768]{1,0:T(8,128)(2,1)S(1)} %get-tuple-element.30), channel_id=1, source_target_pairs={{0,258},{2,256},{256,2},{258,0},{1,259},{3,257},{257,3},{259,1},{4... | collective-permute-start | bytes 294920 | tf_op jit(solution)/shard_map/ppermute | solution.py:66
  133.3 3.4 %convolution_convert_fusion = bf16[256,1536]{1,0:T(8,128)(2,1)} fusion(bf16[256,768]{1,0:T(8,128)(2,1)S(1)} %bitcast.45, bf16[1536,768]{1,0:T(8,128)(2,1)} %maximum_select_fusion.1), kind=kOutput, calls=%fused_computation.4 | convolution fusion | flops 604372992 | bytes 3538944 | tf_op jit(solution)/shard_map/dot_general | solution.py:30
  136.7 0.7 constant_dynamic-slice_fusion
  137.4 3.1 %collective-permute-done.9 = bf16[64,768]{1,0:T(8,128)(2,1)S(1)} collective-permute-done((bf16[64,768]{1,0:T(8,128)(2,1)S(1)}, bf16[64,768]{1,0:T(8,128)(2,1)S(1)}, u32[]{:S(2)}, u32[]{:S(2)}) %collective-permute-start.9) | collective-permute-done | bytes 98336 | tf_op jit(solution)/shard_map/ppermute | solution.py:66
  140.4 3.6 %all-to-all-start.4 = ((bf16[16,16,1536]{2,1,0:T(8,128)(2,1)}), bf16[16,16,1536]{2,1,0:T(8,128)(2,1)S(1)}, u32[]{:S(2)}, u32[]{:S(2)}) async-start(bf16[16,16,1536]{2,1,0:T(8,128)(2,1)} %bitcast.15), calls=%async_computation.4 | async-start | bytes 1572864 | tf_op jit(solution)/shard_map/all_to_all | solution.py:127
  144.1 3.1 %collective-permute-start.10 = (bf16[1,1,64,1536]{3,2,1,0:T(8,128)(2,1)S(1)}, bf16[1,1,64,1536]{3,2,1,0:T(8,128)(2,1)S(1)}, u32[]{:S(2)}, u32[]{:S(2)}) collective-permute-start(bf16[1,1,64,1536]{3,2,1,0:T(8,128)(2,1)S(1)} %maximum_select_fusion.5), channel_id=1, source_target_pairs={{0,128},{128,0},{1,129},{129,1},{2,130},{130,2},{3,131},{131,3},{4... | collective-permute-start | bytes 589832 | tf_op jit(solution)/shard_map/ppermute | solution.py:42
  147.3 4.4 %collective-permute-done.10 = bf16[1,1,64,1536]{3,2,1,0:T(8,128)(2,1)S(1)} collective-permute-done((bf16[1,1,64,1536]{3,2,1,0:T(8,128)(2,1)S(1)}, bf16[1,1,64,1536]{3,2,1,0:T(8,128)(2,1)S(1)}, u32[]{:S(2)}, u32[]{:S(2)}) %collective-permute-start.10) | collective-permute-done | bytes 196640 | tf_op jit(solution)/shard_map/ppermute | solution.py:42
  151.8 7.4 %collective-permute-start.11 = (bf16[256,384]{1,0:T(8,128)(2,1)}, bf16[256,384]{1,0:T(8,128)(2,1)S(1)}, u32[]{:S(2)}, u32[]{:S(2)}) collective-permute-start(bf16[256,384]{1,0:T(8,128)(2,1)} %constant_dynamic-slice_fusion), channel_id=1, source_target_pairs={{0,1},{1,0},{2,3},{3,2},{4,5},{5,4},{6,7},{7,6},{8,9},{9,8},{10,11... | collective-permute-start | bytes 589832 | tf_op jit(solution)/shard_map/ppermute | solution.py:42
  159.1 0.6 fusion.14
  159.8 0.1 convert_reduce_fusion.2
  159.8 4.3 %collective-permute-start.12 = (bf16[2,1,64,1536]{3,2,1,0:T(8,128)(2,1)S(1)}, bf16[2,1,64,1536]{3,2,1,0:T(8,128)(2,1)S(1)}, u32[]{:S(2)}, u32[]{:S(2)}) collective-permute-start(bf16[2,1,64,1536]{3,2,1,0:T(8,128)(2,1)S(1)} %maximum_select_fusion.3), channel_id=1, source_target_pairs={{0,64},{64,0},{1,65},{65,1},{2,66},{66,2},{3,67},{67,3},{4,68},{68... | collective-permute-start | bytes 1179656 | tf_op jit(solution)/shard_map/ppermute | solution.py:42
  164.2 0.1 convert_reduce_fusion.1
  164.2 0.6 add.119
  164.8 1.6 fusion
  166.5 7.2 %collective-permute-done.12 = bf16[2,1,64,1536]{3,2,1,0:T(8,128)(2,1)S(1)} collective-permute-done((bf16[2,1,64,1536]{3,2,1,0:T(8,128)(2,1)S(1)}, bf16[2,1,64,1536]{3,2,1,0:T(8,128)(2,1)S(1)}, u32[]{:S(2)}, u32[]{:S(2)}) %collective-permute-start.12) | collective-permute-done | bytes 393248 | tf_op jit(solution)/shard_map/ppermute | solution.py:42
  173.6 0.1 maximum_select_fusion.2
  173.7 0.1 convert_reduce_fusion
  173.9 2.5 %collective-permute-start.13 = (bf16[256,1536]{1,0:T(8,128)(2,1)S(1)}, bf16[256,1536]{1,0:T(8,128)(2,1)S(1)}, u32[]{:S(2)}, u32[]{:S(2)}) collective-permute-start(bf16[256,1536]{1,0:T(8,128)(2,1)S(1)} %bitcast.40), channel_id=1, source_target_pairs={{0,1},{1,0},{2,3},{3,2},{4,5},{5,4},{6,7},{7,6},{8,9},{9,8},{10,11... | collective-permute-start | bytes 2359304 | tf_op jit(solution)/shard_map/ppermute | solution.py:42
  176.4 11.8 %collective-permute-start.14 = (bf16[8,1536]{1,0:T(8,128)(2,1)S(1)}, bf16[8,1536]{1,0:T(8,128)(2,1)S(1)}, u32[]{:S(2)}, u32[]{:S(2)}) collective-permute-start(bf16[8,1536]{1,0:T(8,128)(2,1)S(1)} %dynamic-slice_convert_fusion.3), channel_id=1, source_target_pairs={{0,2},{2,0},{1,3},{3,1},{4,6},{6,4},{5,7},{7,5},{8,10},{10,8},{9,1... | collective-permute-start | bytes 73736 | tf_op jit(solution)/shard_map/ppermute | solution.py:42
  188.2 0.6 fusion.20
  188.8 1.6 fusion.1
  190.4 0.6 add_convert_fusion.1
  (24 shorter events, 0.4 us)
Async XLA Ops:
  2.1 17.7 %collective-permute-start = (bf16[8,2304]{1,0:T(8,128)(2,1)S(1)}, bf16[8,2304]{1,0:T(8,128)(2,1)S(1)}, u32[]{:S(2)}, u32[]{:S(2)}) collective-permute-start(bf16[8,2304]{1,0:T(8,128)(2,1)S(1)} %pad_maximum_fusion.1), channel_id=1, source_target_pairs={{0,2},{2,0},{1,3},{3,1},{4,6},{6,4},{5,7},{7,5},{8,10},{10,8},{9,1... | collective-permute-start | bytes 110600 | tf_op jit(solution)/shard_map/ppermute | solution.py:42
  20.7 6.4 %copy-start.2 = (bf16[16,2304]{1,0:T(8,128)(2,1)}, bf16[16,2304]{1,0:T(8,128)(2,1)S(1)}, u32[]{:S(2)}) copy-start(bf16[16,2304]{1,0:T(8,128)(2,1)S(1)} %maximum_select_fusion.6) | copy-start | bytes 221188
  20.7 10.9 %collective-permute-start.1 = (bf16[1536,384]{1,0:T(8,128)(2,1)}, bf16[1536,384]{1,0:T(8,128)(2,1)}, u32[]{:S(2)}, u32[]{:S(2)}) collective-permute-start(bf16[1536,384]{1,0:T(8,128)(2,1)} %param.9), channel_id=1, source_target_pairs={{0,1},{1,0},{2,3},{3,2},{4,5},{5,4},{6,7},{7,6},{8,9},{9,8},{10,11... | collective-permute-start | bytes 3538952 | tf_op jit(solution)/shard_map/ppermute | solution.py:42
  27.1 13.6 %all-to-all-start = ((bf16[16,16,768]{2,1,0:T(8,128)(2,1)}), bf16[16,16,768]{2,1,0:T(8,128)(2,1)S(1)}, u32[]{:S(2)}, u32[]{:S(2)}) async-start(bf16[16,16,768]{2,1,0:T(8,128)(2,1)} %broadcast_in_dim.6), calls=%async_computation | async-start | bytes 786432 | tf_op jit(solution)/shard_map/all_to_all | solution.py:72
  41.5 1.2 copy-start
  42.7 16.5 %copy-start.1 = (f32[2,2,64,1536]{3,2,1,0:T(8,128)S(1)}, f32[2,2,64,1536]{3,2,1,0:T(8,128)}, u32[]{:S(2)}) copy-start(f32[2,2,64,1536]{3,2,1,0:T(8,128)} %copy-done) | copy-start | bytes 4718596
  42.7 21.2 %collective-permute-start.3 = (bf16[1536,384]{1,0:T(8,128)(2,1)}, bf16[1536,384]{1,0:T(8,128)(2,1)}, u32[]{:S(2)}, u32[]{:S(2)}) collective-permute-start(bf16[1536,384]{1,0:T(8,128)(2,1)} %param.7), channel_id=1, source_target_pairs={{0,1},{1,0},{2,3},{3,2},{4,5},{5,4},{6,7},{7,6},{8,9},{9,8},{10,11... | collective-permute-start | bytes 3538952 | tf_op jit(solution)/shard_map/ppermute | solution.py:42
  46.5 12.7 %collective-permute-start.2 = (bf16[2,1,64,1536]{3,2,1,0:T(8,128)(2,1)S(1)}, bf16[2,1,64,1536]{3,2,1,0:T(8,128)(2,1)}, u32[]{:S(2)}, u32[]{:S(2)}) collective-permute-start(bf16[2,1,64,1536]{3,2,1,0:T(8,128)(2,1)S(1)} %dynamic-slice_convert_fusion), channel_id=1, source_target_pairs={{0,64},{64,0},{1,65},{65,1},{2,66},{66,2},{3,67},{67,3},{4,68},{68... | collective-permute-start | bytes 1179656 | tf_op jit(solution)/shard_map/ppermute | solution.py:42
  51.3 16.8 %all-to-all-start.1 = ((bf16[16,16,1536]{2,1,0:T(8,128)(2,1)}), bf16[16,16,1536]{2,1,0:T(8,128)(2,1)S(1)}, u32[]{:S(2)}, u32[]{:S(2)}) async-start(bf16[16,16,1536]{2,1,0:T(8,128)(2,1)} %broadcast_in_dim.7), calls=%async_computation.1 | async-start | bytes 1572864 | tf_op jit(solution)/shard_map/all_to_all | solution.py:72
  60.3 12.9 %collective-permute-start.6 = (bf16[1,1,64,1536]{3,2,1,0:T(8,128)(2,1)S(1)}, bf16[1,1,64,1536]{3,2,1,0:T(8,128)(2,1)S(1)}, u32[]{:S(2)}, u32[]{:S(2)}) collective-permute-start(bf16[1,1,64,1536]{3,2,1,0:T(8,128)(2,1)S(1)} %dynamic-slice_convert_fusion.1), channel_id=1, source_target_pairs={{0,128},{128,0},{1,129},{129,1},{2,130},{130,2},{3,131},{131,3},{4... | collective-permute-start | bytes 589832 | tf_op jit(solution)/shard_map/ppermute | solution.py:42
  71.3 28.0 %copy-start.3 = (f32[1536]{0:T(1024)S(1)}, f32[1536]{0:T(1024)}, u32[]{:S(2)}) copy-start(f32[1536]{0:T(1024)} %param.8) | copy-start | bytes 18436
  73.2 20.0 %all-to-all-start.2 = ((bf16[4,64,768]{2,1,0:T(8,128)(2,1)}), bf16[4,64,768]{2,1,0:T(8,128)(2,1)S(1)}, u32[]{:S(2)}, u32[]{:S(2)}) async-start(bf16[4,64,768]{2,1,0:T(8,128)(2,1)} %bitcast.5), calls=%async_computation.2 | async-start | bytes 786432 | tf_op jit(solution)/shard_map/all_to_all | solution.py:78
  76.7 16.6 %collective-permute-start.4 = (bf16[256,1536]{1,0:T(8,128)(2,1)S(1)}, bf16[256,1536]{1,0:T(8,128)(2,1)S(1)}, u32[]{:S(2)}, u32[]{:S(2)}) collective-permute-start(bf16[256,1536]{1,0:T(8,128)(2,1)S(1)} %bitcast.43), channel_id=1, source_target_pairs={{0,1},{1,0},{2,3},{3,2},{4,5},{5,4},{6,7},{7,6},{8,9},{9,8},{10,11... | collective-permute-start | bytes 2359304 | tf_op jit(solution)/shard_map/ppermute | solution.py:42
  80.1 13.1 %collective-permute-start.7 = (bf16[64,768]{1,0:T(8,128)(2,1)S(1)}, bf16[64,768]{1,0:T(8,128)(2,1)S(1)}, u32[]{:S(2)}, u32[]{:S(2)}) collective-permute-start(bf16[64,768]{1,0:T(8,128)(2,1)S(1)} %fusion.17), channel_id=1, source_target_pairs={{0,258},{2,256},{256,2},{258,0},{1,259},{3,257},{257,3},{259,1},{4... | collective-permute-start | bytes 294920 | tf_op jit(solution)/shard_map/ppermute | solution.py:66
  89.6 3.7 %collective-permute-start.5 = (bf16[256,384]{1,0:T(8,128)(2,1)S(1)}, bf16[256,384]{1,0:T(8,128)(2,1)S(1)}, u32[]{:S(2)}, u32[]{:S(2)}) collective-permute-start(bf16[256,384]{1,0:T(8,128)(2,1)S(1)} %constant_dynamic-slice_fusion.1), channel_id=1, source_target_pairs={{0,1},{1,0},{2,3},{3,2},{4,5},{5,4},{6,7},{7,6},{8,9},{9,8},{10,11... | collective-permute-start | bytes 589832 | tf_op jit(solution)/shard_map/ppermute | solution.py:42
  93.3 10.3 %collective-permute-start.8 = (bf16[64,1536]{1,0:T(8,128)(2,1)S(1)}, bf16[64,1536]{1,0:T(8,128)(2,1)S(1)}, u32[]{:S(2)}, u32[]{:S(2)}) collective-permute-start(bf16[64,1536]{1,0:T(8,128)(2,1)S(1)} %pad_maximum_fusion), channel_id=1, source_target_pairs={{0,256},{256,0},{1,257},{257,1},{2,258},{258,2},{3,259},{259,3},{4... | collective-permute-start | bytes 589832 | tf_op jit(solution)/shard_map/ppermute | solution.py:42
  104.6 28.7 %all-to-all-start.3 = ((bf16[4,64,768]{2,1,0:T(8,128)(2,1)}), bf16[4,64,768]{2,1,0:T(8,128)(2,1)S(1)}, u32[]{:S(2)}, u32[]{:S(2)}) async-start(bf16[4,64,768]{2,1,0:T(8,128)(2,1)} %broadcast_in_dim.8), calls=%async_computation.3 | async-start | bytes 786432 | tf_op jit(solution)/shard_map/all_to_all | solution.py:72
  121.8 18.7 %collective-permute-start.9 = (bf16[64,768]{1,0:T(8,128)(2,1)S(1)}, bf16[64,768]{1,0:T(8,128)(2,1)S(1)}, u32[]{:S(2)}, u32[]{:S(2)}) collective-permute-start(bf16[64,768]{1,0:T(8,128)(2,1)S(1)} %get-tuple-element.30), channel_id=1, source_target_pairs={{0,258},{2,256},{256,2},{258,0},{1,259},{3,257},{257,3},{259,1},{4... | collective-permute-start | bytes 294920 | tf_op jit(solution)/shard_map/ppermute | solution.py:66
  140.4 33.3 %all-to-all-start.4 = ((bf16[16,16,1536]{2,1,0:T(8,128)(2,1)}), bf16[16,16,1536]{2,1,0:T(8,128)(2,1)S(1)}, u32[]{:S(2)}, u32[]{:S(2)}) async-start(bf16[16,16,1536]{2,1,0:T(8,128)(2,1)} %bitcast.15), calls=%async_computation.4 | async-start | bytes 1572864 | tf_op jit(solution)/shard_map/all_to_all | solution.py:127
  144.1 7.6 %collective-permute-start.10 = (bf16[1,1,64,1536]{3,2,1,0:T(8,128)(2,1)S(1)}, bf16[1,1,64,1536]{3,2,1,0:T(8,128)(2,1)S(1)}, u32[]{:S(2)}, u32[]{:S(2)}) collective-permute-start(bf16[1,1,64,1536]{3,2,1,0:T(8,128)(2,1)S(1)} %maximum_select_fusion.5), channel_id=1, source_target_pairs={{0,128},{128,0},{1,129},{129,1},{2,130},{130,2},{3,131},{131,3},{4... | collective-permute-start | bytes 589832 | tf_op jit(solution)/shard_map/ppermute | solution.py:42
  151.8 12.4 %collective-permute-start.11 = (bf16[256,384]{1,0:T(8,128)(2,1)}, bf16[256,384]{1,0:T(8,128)(2,1)S(1)}, u32[]{:S(2)}, u32[]{:S(2)}) collective-permute-start(bf16[256,384]{1,0:T(8,128)(2,1)} %constant_dynamic-slice_fusion), channel_id=1, source_target_pairs={{0,1},{1,0},{2,3},{3,2},{4,5},{5,4},{6,7},{7,6},{8,9},{9,8},{10,11... | collective-permute-start | bytes 589832 | tf_op jit(solution)/shard_map/ppermute | solution.py:42
  159.8 13.8 %collective-permute-start.12 = (bf16[2,1,64,1536]{3,2,1,0:T(8,128)(2,1)S(1)}, bf16[2,1,64,1536]{3,2,1,0:T(8,128)(2,1)S(1)}, u32[]{:S(2)}, u32[]{:S(2)}) collective-permute-start(bf16[2,1,64,1536]{3,2,1,0:T(8,128)(2,1)S(1)} %maximum_select_fusion.3), channel_id=1, source_target_pairs={{0,64},{64,0},{1,65},{65,1},{2,66},{66,2},{3,67},{67,3},{4,68},{68... | collective-permute-start | bytes 1179656 | tf_op jit(solution)/shard_map/ppermute | solution.py:42
  173.9 14.3 %collective-permute-start.13 = (bf16[256,1536]{1,0:T(8,128)(2,1)S(1)}, bf16[256,1536]{1,0:T(8,128)(2,1)S(1)}, u32[]{:S(2)}, u32[]{:S(2)}) collective-permute-start(bf16[256,1536]{1,0:T(8,128)(2,1)S(1)} %bitcast.40), channel_id=1, source_target_pairs={{0,1},{1,0},{2,3},{3,2},{4,5},{5,4},{6,7},{7,6},{8,9},{9,8},{10,11... | collective-permute-start | bytes 2359304 | tf_op jit(solution)/shard_map/ppermute | solution.py:42
  176.4 14.0 %collective-permute-start.14 = (bf16[8,1536]{1,0:T(8,128)(2,1)S(1)}, bf16[8,1536]{1,0:T(8,128)(2,1)S(1)}, u32[]{:S(2)}, u32[]{:S(2)}) collective-permute-start(bf16[8,1536]{1,0:T(8,128)(2,1)S(1)} %dynamic-slice_convert_fusion.3), channel_id=1, source_target_pairs={{0,2},{2,0},{1,3},{3,1},{4,6},{6,4},{5,7},{7,5},{8,10},{10,8},{9,1... | collective-permute-start | bytes 73736 | tf_op jit(solution)/shard_map/ppermute | solution.py:42

commit v9 on v8

--- a/solution.py
+++ b/solution.py
@@ -97,31 +97,32 @@
     rows = join(kept, got, "zh", 0)
     w_out = after(rows, w_out)
     out_pair = after(rows, join(w_out, swap(w_out, "core"), "core", 1))
+    w_in = after(out_pair, w_in)
+    in_pair = after(rows, join(w_in, swap(w_in, "core"), "core", 1))
 
     every_g = spread(rows[:, feat:], GRID)
     every_x = spread(after(every_g, rows[:, :feat]), GRID)
 
     back = against(every_g, out_pair).reshape(2, 2, -1, 2 * half_h)
     back_kept, back_sent = cut(back, "rl", 1)
-    w_in = after(back_sent, w_in)
-    in_pair = after(rows, join(w_in, swap(w_in, "core"), "core", 1))
     back_kept, back_sent = cut(back_kept + swap(back_sent, "rl").astype(f32), "rm", 0)
     every_x = after((back_sent, in_pair), every_x)
     pre = dot(every_x, in_pair).astype(bf16)
     back_got = swap(back_sent, "rm")
     pre = deal(after(back_got, pre), ROW4).astype(bf16)
     back_kept, back_sent = cut((back_kept + back_got.astype(f32))[0, 0], "zh", 1)
-    back = (back_kept + cross(back_sent).astype(f32)).astype(bf16)
-    pair_x = swap(every_x, "core")
-    pair_g = swap(part_of(every_g, 1 - core, quarter_d, 1), "core")
-    pre = after((pair_x, pair_g), pre)
-    met = jnp.concatenate([pre, back], 1)
-    met = met.astype(f32) + swap(met, "rh").astype(f32)
-    pre, back = met[:, :half_h], met[:, half_h:]
+    pre_got = swap(pre, "rh")
+    back = (back_kept + after(pre_got, cross(back_sent)).astype(f32)).astype(bf16)
+    pre = pre.astype(f32) + pre_got.astype(f32)
+    act_f, slope = gelu_pair(pre + part_of(b_in, zh, half_h, 0))
+    act, slope = lax.optimization_barrier((act_f.astype(bf16), slope))
+    crossed = cross(act)
+    pair_x = swap(after(back, every_x), "core")
+    pair_g = part_of(every_g, 1 - core, quarter_d, 1)
+    pair_g = swap(after(back, pair_g), "core")
+    back_got = after((act, pair_x, pair_g), swap(back, "rh"))
+    back = back.astype(f32) + back_got.astype(f32)
 
-    act_f, slope = gelu_pair(pre + part_of(b_in, zh, half_h, 0))
-    act = act_f.astype(bf16)
-    crossed = cross(act)
     grad = spread((back * slope).astype(bf16), ROW4)
     part = against(grad, in_pair).astype(bf16)
     dealt = lax.all_to_all(part.reshape(-1, 2 * tok_dev, feat), GRID, 0, 0, tiled=True)

time: 192 us -> 194 us (1.010)
  waiting for transfers between devices: 34.1 us -> 38.2 us
  starting transfers between devices: 126 us -> 124 us
  local copies, waits for them, and re-layouts: 6.13 us -> 4.17 us
    ppermute x13 -> x14, starting transfers between devices: 72.9 us -> 86.7 us  [swap(): return lax.ppermute(value, axis, SWAP)]
    all_to_all x3, starting transfers between devices: 25.3 us -> 11.6 us  [spread(): got = lax.all_to_all(sent, axes, 0, 0, tiled=True)]
    ppermute x13 -> x14, waiting for transfers between devices: 23.5 us -> 28.9 us  [swap(): return lax.ppermute(value, axis, SWAP)]
    ppermute x2, waiting for transfers between devices: 4.42 us -> 0.57 us  [cross(): return lax.ppermute(value, ('rh', 'zh'), CROSS)]
    all_to_all x3, waiting for transfers between devices: 6.18 us -> 8.7 us  [spread(): got = lax.all_to_all(sent, axes, 0, 0, tiled=True)]
    ppermute x2, starting transfers between devices: 21 us -> 18.7 us  [cross(): return lax.ppermute(value, ('rh', 'zh'), CROSS)]
  transfers between devices with their start and end apart: 20 -> 21, of which waited for: 9 -> 10; matrix products, arithmetic and copies ran while one was open for 12% -> 12% of each run, Pallas kernels for 0% -> 0%
where the time goes in v9:
time: 194 us; the launch traced here: 193 us
  starting transfers between devices  124 us (64%)
  waiting for transfers between devices  38.2 us (20%)
  other arithmetic  13.4 us (7%)
  matrix products  11.8 us (6%)
  local copies, waits for them, and re-layouts  4.17 us (2%)
    ppermute x14, starting transfers between devices, swap(): return lax.ppermute(value, axis, SWAP)  86.7 us
    ppermute x14, waiting for transfers between devices, swap(): return lax.ppermute(value, axis, SWAP)  28.9 us
    ppermute x2, starting transfers between devices, cross(): return lax.ppermute(value, ('rh', 'zh'), CROSS)  18.7 us
    all_to_all x3, starting transfers between devices, spread(): got = lax.all_to_all(sent, axes, 0, 0, tiled=True)  11.6 us
    select_n x6, other arithmetic, join(): jnp.where(first, jnp.concatenate([mine, other], dim), jnp.concatenate([ot...  9.79 us
    all_to_all x3, waiting for transfers between devices, spread(): got = lax.all_to_all(sent, axes, 0, 0, tiled=True)  8.7 us
    dot_general x4, matrix products, over_rows(): lax.dot_general(left, right, (((0,), (0,)), ((), ())), preferred_element_...  4.49 us
    dot_general x2, matrix products, against(): lax.dot_general(left, right, (((1,), (1,)), ((), ())), preferred_element_...  4.16 us
  transfers between devices with their start and end apart: 21, of which 10 were waited for; matrix products, arithmetic and copies ran while one was open for 12% of the time, Pallas kernels for 0%

profile of v9, /device:TPU:1, one launch (start us, length us, event | category | flops | bytes accessed | tf_op | source)
XLA Modules:
  0.0 192.8 jit_solution(9622986485301163827)
XLA Ops:
  0.6 0.7 constant_dynamic-slice_fusion.3
  1.4 0.7 pad_maximum_fusion
  2.1 16.3 %collective-permute-start = (bf16[8,2304]{1,0:T(8,128)(2,1)S(1)}, bf16[8,2304]{1,0:T(8,128)(2,1)S(1)}, u32[]{:S(2)}, u32[]{:S(2)}) collective-permute-start(bf16[8,2304]{1,0:T(8,128)(2,1)S(1)} %pad_maximum_fusion), channel_id=1, source_target_pairs={{0,2},{2,0},{1,3},{3,1},{4,6},{6,4},{5,7},{7,5},{8,10},{10,8},{9,1... | collective-permute-start | bytes 110600 | tf_op jit(solution)/shard_map/ppermute | solution.py:42
  18.4 1.5 collective-permute-done
  19.9 0.8 maximum_select_fusion.6
  20.7 5.6 %collective-permute-start.1 = (bf16[1536,384]{1,0:T(8,128)(2,1)}, bf16[1536,384]{1,0:T(8,128)(2,1)}, u32[]{:S(2)}, u32[]{:S(2)}) collective-permute-start(bf16[1536,384]{1,0:T(8,128)(2,1)} %param.9), channel_id=1, source_target_pairs={{0,1},{1,0},{2,3},{3,2},{4,5},{5,4},{6,7},{7,6},{8,9},{9,8},{10,11... | collective-permute-start | bytes 3538952 | tf_op jit(solution)/shard_map/ppermute | solution.py:42
  26.3 0.8 broadcast_in_dim.6
  27.1 4.5 %all-to-all-start = ((bf16[16,16,768]{2,1,0:T(8,128)(2,1)}), bf16[16,16,768]{2,1,0:T(8,128)(2,1)S(1)}, u32[]{:S(2)}, u32[]{:S(2)}) async-start(bf16[16,16,768]{2,1,0:T(8,128)(2,1)} %broadcast_in_dim.6), calls=%async_computation | async-start | bytes 786432 | tf_op jit(solution)/shard_map/all_to_all | solution.py:72
  31.6 2.9 %maximum_select_fusion = bf16[1536,768]{1,0:T(8,128)(2,1)S(1)} fusion(bf16[1536,384]{1,0:T(8,128)(2,1)} %collective-permute-done.1, bf16[1536,384]{1,0:T(8,128)(2,1)} %param.9, pred[]{:T(512)S(6)} %eq.15), kind=kLoop, calls=%fused_computation.5 | loop fusion | flops 10616832 | bytes 4718593 | tf_op jit(solution)/shard_map/jit(_where)/select_n | solution.py:47
  34.5 6.2 %all-to-all-done = bf16[16,16,768]{2,1,0:T(8,128)(2,1)S(1)} async-done(((bf16[16,16,768]{2,1,0:T(8,128)(2,1)}), bf16[16,16,768]{2,1,0:T(8,128)(2,1)S(1)}, u32[]{:S(2)}, u32[]{:S(2)}) %all-to-all-start) | async-done | bytes 393248 | tf_op jit(solution)/shard_map/all_to_all | solution.py:72
  40.7 0.8 fusion.2
  41.5 3.6 %collective-permute-start.3 = (bf16[1536,384]{1,0:T(8,128)(2,1)}, bf16[1536,384]{1,0:T(8,128)(2,1)}, u32[]{:S(2)}, u32[]{:S(2)}) collective-permute-start(bf16[1536,384]{1,0:T(8,128)(2,1)} %param.7), channel_id=1, source_target_pairs={{0,1},{1,0},{2,3},{3,2},{4,5},{5,4},{6,7},{7,6},{8,9},{9,8},{10,11... | collective-permute-start | bytes 3538952 | tf_op jit(solution)/shard_map/ppermute | solution.py:42
  45.1 0.1 dynamic-slice_convert_fusion
  45.2 3.2 %collective-permute-start.2 = (bf16[2,1,64,1536]{3,2,1,0:T(8,128)(2,1)S(1)}, bf16[2,1,64,1536]{3,2,1,0:T(8,128)(2,1)}, u32[]{:S(2)}, u32[]{:S(2)}) collective-permute-start(bf16[2,1,64,1536]{3,2,1,0:T(8,128)(2,1)S(1)} %dynamic-slice_convert_fusion), channel_id=1, source_target_pairs={{0,64},{64,0},{1,65},{65,1},{2,66},{66,2},{3,67},{67,3},{4,68},{68... | collective-permute-start | bytes 1179656 | tf_op jit(solution)/shard_map/ppermute | solution.py:42
  48.5 1.0 broadcast_in_dim.7
  49.4 3.6 %all-to-all-start.1 = ((bf16[16,16,1536]{2,1,0:T(8,128)(2,1)}), bf16[16,16,1536]{2,1,0:T(8,128)(2,1)S(1)}, u32[]{:S(2)}, u32[]{:S(2)}) async-start(bf16[16,16,1536]{2,1,0:T(8,128)(2,1)} %broadcast_in_dim.7), calls=%async_computation.1 | async-start | bytes 1572864 | tf_op jit(solution)/shard_map/all_to_all | solution.py:72
  53.0 5.0 %collective-permute-done.2 = bf16[2,1,64,1536]{3,2,1,0:T(8,128)(2,1)} collective-permute-done((bf16[2,1,64,1536]{3,2,1,0:T(8,128)(2,1)S(1)}, bf16[2,1,64,1536]{3,2,1,0:T(8,128)(2,1)}, u32[]{:S(2)}, u32[]{:S(2)}) %collective-permute-start.2) | collective-permute-done | bytes 393248 | tf_op jit(solution)/shard_map/ppermute | solution.py:42
  58.1 1.1 convert_add_fusion
  59.2 3.6 %collective-permute-start.4 = (bf16[1,1,64,1536]{3,2,1,0:T(8,128)(2,1)S(1)}, bf16[1,1,64,1536]{3,2,1,0:T(8,128)(2,1)S(1)}, u32[]{:S(2)}, u32[]{:S(2)}) collective-permute-start(bf16[1,1,64,1536]{3,2,1,0:T(8,128)(2,1)S(1)} %dynamic-slice_convert_fusion.1), channel_id=1, source_target_pairs={{0,128},{128,0},{1,129},{129,1},{2,130},{130,2},{3,131},{131,3},{4... | collective-permute-start | bytes 589832 | tf_op jit(solution)/shard_map/ppermute | solution.py:42
  62.8 4.2 %maximum_select_fusion.1 = bf16[1536,768]{1,0:T(8,128)(2,1)} fusion(bf16[1536,384]{1,0:T(8,128)(2,1)} %collective-permute-done.3, bf16[1536,384]{1,0:T(8,128)(2,1)} %param.7, pred[]{:T(512)S(6)} %eq.15), kind=kLoop, calls=%fused_computation.6 | loop fusion | flops 10616832 | bytes 4718593 | tf_op jit(solution)/shard_map/jit(_where)/select_n | solution.py:47
  67.0 3.2 %convolution_convert_fusion.1 = bf16[256,768]{1,0:T(8,128)(2,1)} fusion(bf16[256,1536]{1,0:T(8,128)(2,1)S(1)} %bitcast.44, bf16[1536,768]{1,0:T(8,128)(2,1)} %maximum_select_fusion.1), kind=kOutput, calls=%fused_computation.10 | convolution fusion | flops 604176384 | bytes 3538944 | tf_op jit(solution)/shard_map/dot_general | solution.py:26
  70.1 1.9 collective-permute-done.4
  72.1 3.5 %all-to-all-start.2 = ((bf16[4,64,768]{2,1,0:T(8,128)(2,1)}), bf16[4,64,768]{2,1,0:T(8,128)(2,1)S(1)}, u32[]{:S(2)}, u32[]{:S(2)}) async-start(bf16[4,64,768]{2,1,0:T(8,128)(2,1)} %bitcast.6), calls=%async_computation.2 | async-start | bytes 786432 | tf_op jit(solution)/shard_map/all_to_all | solution.py:78
  75.6 9.9 %collective-permute-start.6 = (bf16[64,768]{1,0:T(8,128)(2,1)S(1)}, bf16[64,768]{1,0:T(8,128)(2,1)S(1)}, u32[]{:S(2)}, u32[]{:S(2)}) collective-permute-start(bf16[64,768]{1,0:T(8,128)(2,1)S(1)} %fusion.15), channel_id=1, source_target_pairs={{0,258},{2,256},{256,2},{258,0},{1,259},{3,257},{257,3},{259,1},{4... | collective-permute-start | bytes 294920 | tf_op jit(solution)/shard_map/ppermute | solution.py:66
  85.5 0.1 fusion.14
  85.6 12.5 %collective-permute-start.5 = (bf16[64,768]{1,0:T(8,128)(2,1)S(1)}, bf16[64,768]{1,0:T(8,128)(2,1)S(1)}, u32[]{:S(2)}, u32[]{:S(2)}) collective-permute-start(bf16[64,768]{1,0:T(8,128)(2,1)S(1)} %fusion.14), channel_id=1, source_target_pairs={{0,256},{256,0},{1,257},{257,1},{2,258},{258,2},{3,259},{259,3},{4... | collective-permute-start | bytes 294920 | tf_op jit(solution)/shard_map/ppermute | solution.py:42
  98.1 7.1 %collective-permute-done.5 = bf16[64,768]{1,0:T(8,128)(2,1)S(1)} collective-permute-done((bf16[64,768]{1,0:T(8,128)(2,1)S(1)}, bf16[64,768]{1,0:T(8,128)(2,1)S(1)}, u32[]{:S(2)}, u32[]{:S(2)}) %collective-permute-start.5) | collective-permute-done | bytes 98336 | tf_op jit(solution)/shard_map/ppermute | solution.py:42
  105.2 2.8 %collective-permute-start.7 = (bf16[256,1536]{1,0:T(8,128)(2,1)S(1)}, bf16[256,1536]{1,0:T(8,128)(2,1)S(1)}, u32[]{:S(2)}, u32[]{:S(2)}) collective-permute-start(bf16[256,1536]{1,0:T(8,128)(2,1)S(1)} %bitcast.45), channel_id=1, source_target_pairs={{0,1},{1,0},{2,3},{3,2},{4,5},{5,4},{6,7},{7,6},{8,9},{9,8},{10,11... | collective-permute-start | bytes 2359304 | tf_op jit(solution)/shard_map/ppermute | solution.py:42
  108.1 0.1 dynamic_slice.56
  108.2 5.8 %collective-permute-start.9 = (bf16[64,768]{1,0:T(8,128)(2,1)S(1)}, bf16[64,768]{1,0:T(8,128)(2,1)S(1)}, u32[]{:S(2)}, u32[]{:S(2)}) collective-permute-start(bf16[64,768]{1,0:T(8,128)(2,1)S(1)} %fusion.10), channel_id=1, source_target_pairs={{0,256},{256,0},{1,257},{257,1},{2,258},{258,2},{3,259},{259,3},{4... | collective-permute-start | bytes 294920 | tf_op jit(solution)/shard_map/ppermute | solution.py:42
  114.1 2.2 %collective-permute-start.8 = (bf16[256,384]{1,0:T(8,128)(2,1)S(1)}, bf16[256,384]{1,0:T(8,128)(2,1)S(1)}, u32[]{:S(2)}, u32[]{:S(2)}) collective-permute-start(bf16[256,384]{1,0:T(8,128)(2,1)S(1)} %constant_dynamic-slice_fusion.1), channel_id=1, source_target_pairs={{0,1},{1,0},{2,3},{3,2},{4,5},{5,4},{6,7},{7,6},{8,9},{9,8},{10,11... | collective-permute-start | bytes 589832 | tf_op jit(solution)/shard_map/ppermute | solution.py:42
  116.3 0.2 fusion.8
  116.5 5.4 %collective-permute-done.9 = bf16[64,768]{1,0:T(8,128)(2,1)S(1)} collective-permute-done((bf16[64,768]{1,0:T(8,128)(2,1)S(1)}, bf16[64,768]{1,0:T(8,128)(2,1)S(1)}, u32[]{:S(2)}, u32[]{:S(2)}) %collective-permute-start.9) | collective-permute-done | bytes 98336 | tf_op jit(solution)/shard_map/ppermute | solution.py:42
  121.9 0.0 collective-permute-done.8
  121.9 0.0 collective-permute-done.7
  121.9 0.8 broadcast_in_dim.8
  122.7 3.5 %all-to-all-start.3 = ((bf16[4,64,768]{2,1,0:T(8,128)(2,1)}), bf16[4,64,768]{2,1,0:T(8,128)(2,1)S(1)}, u32[]{:S(2)}, u32[]{:S(2)}) async-start(bf16[4,64,768]{2,1,0:T(8,128)(2,1)} %broadcast_in_dim.8), calls=%async_computation.3 | async-start | bytes 786432 | tf_op jit(solution)/shard_map/all_to_all | solution.py:72
  126.2 8.8 %collective-permute-start.10 = (bf16[64,768]{1,0:T(8,128)(2,1)S(1)}, bf16[64,768]{1,0:T(8,128)(2,1)S(1)}, u32[]{:S(2)}, u32[]{:S(2)}) collective-permute-start(bf16[64,768]{1,0:T(8,128)(2,1)S(1)} %get-tuple-element.30), channel_id=1, source_target_pairs={{0,258},{2,256},{256,2},{258,0},{1,259},{3,257},{257,3},{259,1},{4... | collective-permute-start | bytes 294920 | tf_op jit(solution)/shard_map/ppermute | solution.py:66
  135.0 2.5 %all-to-all-done.3 = bf16[4,64,768]{2,1,0:T(8,128)(2,1)S(1)} async-done(((bf16[4,64,768]{2,1,0:T(8,128)(2,1)}), bf16[4,64,768]{2,1,0:T(8,128)(2,1)S(1)}, u32[]{:S(2)}, u32[]{:S(2)}) %all-to-all-start.3) | async-done | bytes 393248 | tf_op jit(solution)/shard_map/all_to_all | solution.py:72
  137.5 3.4 %convolution_convert_fusion = bf16[256,1536]{1,0:T(8,128)(2,1)} fusion(bf16[256,768]{1,0:T(8,128)(2,1)S(1)} %bitcast.47, bf16[1536,768]{1,0:T(8,128)(2,1)} %maximum_select_fusion.1), kind=kOutput, calls=%fused_computation.4 | convolution fusion | flops 604372992 | bytes 3538944 | tf_op jit(solution)/shard_map/dot_general | solution.py:30
  140.8 0.7 constant_dynamic-slice_fusion
  141.5 0.6 collective-permute-done.10
  142.1 0.7 maximum_select_fusion.5
  142.8 3.1 %collective-permute-start.11 = (bf16[1,1,64,1536]{3,2,1,0:T(8,128)(2,1)}, bf16[1,1,64,1536]{3,2,1,0:T(8,128)(2,1)}, u32[]{:S(2)}, u32[]{:S(2)}) collective-permute-start(bf16[1,1,64,1536]{3,2,1,0:T(8,128)(2,1)} %maximum_select_fusion.5), channel_id=1, source_target_pairs={{0,128},{128,0},{1,129},{129,1},{2,130},{130,2},{3,131},{131,3},{4... | collective-permute-start | bytes 589832 | tf_op jit(solution)/shard_map/ppermute | solution.py:42
  145.9 3.6 %all-to-all-start.4 = ((bf16[16,16,1536]{2,1,0:T(8,128)(2,1)}), bf16[16,16,1536]{2,1,0:T(8,128)(2,1)S(1)}, u32[]{:S(2)}, u32[]{:S(2)}) async-start(bf16[16,16,1536]{2,1,0:T(8,128)(2,1)} %bitcast.15), calls=%async_computation.4 | async-start | bytes 1572864 | tf_op jit(solution)/shard_map/all_to_all | solution.py:128
  149.6 0.9 collective-permute-done.11
  150.4 1.1 maximum_select_fusion.3
  151.5 5.4 %collective-permute-start.12 = (bf16[256,384]{1,0:T(8,128)(2,1)}, bf16[256,384]{1,0:T(8,128)(2,1)S(1)}, u32[]{:S(2)}, u32[]{:S(2)}) collective-permute-start(bf16[256,384]{1,0:T(8,128)(2,1)} %constant_dynamic-slice_fusion), channel_id=1, source_target_pairs={{0,1},{1,0},{2,3},{3,2},{4,5},{5,4},{6,7},{7,6},{8,9},{9,8},{10,11... | collective-permute-start | bytes 589832 | tf_op jit(solution)/shard_map/ppermute | solution.py:42
  157.0 0.6 fusion.12
  157.6 0.1 convert_reduce_fusion.2
  157.6 6.4 %collective-permute-start.13 = (bf16[2,1,64,1536]{3,2,1,0:T(8,128)(2,1)S(1)}, bf16[2,1,64,1536]{3,2,1,0:T(8,128)(2,1)S(1)}, u32[]{:S(2)}, u32[]{:S(2)}) collective-permute-start(bf16[2,1,64,1536]{3,2,1,0:T(8,128)(2,1)S(1)} %maximum_select_fusion.3), channel_id=1, source_target_pairs={{0,64},{64,0},{1,65},{65,1},{2,66},{66,2},{3,67},{67,3},{4,68},{68... | collective-permute-start | bytes 1179656 | tf_op jit(solution)/shard_map/ppermute | solution.py:42
  164.1 0.1 convert_reduce_fusion.1
  164.1 0.6 add.123
  164.7 1.6 fusion
  166.4 7.2 %collective-permute-done.13 = bf16[2,1,64,1536]{3,2,1,0:T(8,128)(2,1)S(1)} collective-permute-done((bf16[2,1,64,1536]{3,2,1,0:T(8,128)(2,1)S(1)}, bf16[2,1,64,1536]{3,2,1,0:T(8,128)(2,1)S(1)}, u32[]{:S(2)}, u32[]{:S(2)}) %collective-permute-start.13) | collective-permute-done | bytes 393248 | tf_op jit(solution)/shard_map/ppermute | solution.py:42
  173.5 0.1 maximum_select_fusion.2
  173.7 0.0 all-to-all-done.4
  173.7 0.1 convert_reduce_fusion
  173.8 2.5 %collective-permute-start.14 = (bf16[256,1536]{1,0:T(8,128)(2,1)S(1)}, bf16[256,1536]{1,0:T(8,128)(2,1)S(1)}, u32[]{:S(2)}, u32[]{:S(2)}) collective-permute-start(bf16[256,1536]{1,0:T(8,128)(2,1)S(1)} %bitcast.42), channel_id=1, source_target_pairs={{0,1},{1,0},{2,3},{3,2},{4,5},{5,4},{6,7},{7,6},{8,9},{9,8},{10,11... | collective-permute-start | bytes 2359304 | tf_op jit(solution)/shard_map/ppermute | solution.py:42
  176.3 13.6 %collective-permute-start.15 = (bf16[8,1536]{1,0:T(8,128)(2,1)S(1)}, bf16[8,1536]{1,0:T(8,128)(2,1)S(1)}, u32[]{:S(2)}, u32[]{:S(2)}) collective-permute-start(bf16[8,1536]{1,0:T(8,128)(2,1)S(1)} %dynamic-slice_convert_fusion.3), channel_id=1, source_target_pairs={{0,2},{2,0},{1,3},{3,1},{4,6},{6,4},{5,7},{7,5},{8,10},{10,8},{9,1... | collective-permute-start | bytes 73736 | tf_op jit(solution)/shard_map/ppermute | solution.py:42
  189.9 0.0 collective-permute-done.14
  189.9 0.6 fusion.18
  190.5 1.6 fusion.1
  192.1 0.6 add_convert_fusion.1
  (23 shorter events, 0.3 us)
Async XLA Ops:
  2.1 17.7 %collective-permute-start = (bf16[8,2304]{1,0:T(8,128)(2,1)S(1)}, bf16[8,2304]{1,0:T(8,128)(2,1)S(1)}, u32[]{:S(2)}, u32[]{:S(2)}) collective-permute-start(bf16[8,2304]{1,0:T(8,128)(2,1)S(1)} %pad_maximum_fusion), channel_id=1, source_target_pairs={{0,2},{2,0},{1,3},{3,1},{4,6},{6,4},{5,7},{7,5},{8,10},{10,8},{9,1... | collective-permute-start | bytes 110600 | tf_op jit(solution)/shard_map/ppermute | solution.py:42
  20.7 10.9 %collective-permute-start.1 = (bf16[1536,384]{1,0:T(8,128)(2,1)}, bf16[1536,384]{1,0:T(8,128)(2,1)}, u32[]{:S(2)}, u32[]{:S(2)}) collective-permute-start(bf16[1536,384]{1,0:T(8,128)(2,1)} %param.9), channel_id=1, source_target_pairs={{0,1},{1,0},{2,3},{3,2},{4,5},{5,4},{6,7},{7,6},{8,9},{9,8},{10,11... | collective-permute-start | bytes 3538952 | tf_op jit(solution)/shard_map/ppermute | solution.py:42
  27.1 13.6 %all-to-all-start = ((bf16[16,16,768]{2,1,0:T(8,128)(2,1)}), bf16[16,16,768]{2,1,0:T(8,128)(2,1)S(1)}, u32[]{:S(2)}, u32[]{:S(2)}) async-start(bf16[16,16,768]{2,1,0:T(8,128)(2,1)} %broadcast_in_dim.6), calls=%async_computation | async-start | bytes 786432 | tf_op jit(solution)/shard_map/all_to_all | solution.py:72
  41.5 3.6 %copy-start = (f32[2,2,64,1536]{3,2,1,0:T(8,128)}, f32[2,2,64,1536]{3,2,1,0:T(8,128)S(1)}, u32[]{:S(2)}) copy-start(f32[2,2,64,1536]{3,2,1,0:T(8,128)S(1)} %fusion.2) | copy-start | bytes 4718596
  41.5 21.3 %collective-permute-start.3 = (bf16[1536,384]{1,0:T(8,128)(2,1)}, bf16[1536,384]{1,0:T(8,128)(2,1)}, u32[]{:S(2)}, u32[]{:S(2)}) collective-permute-start(bf16[1536,384]{1,0:T(8,128)(2,1)} %param.7), channel_id=1, source_target_pairs={{0,1},{1,0},{2,3},{3,2},{4,5},{5,4},{6,7},{7,6},{8,9},{9,8},{10,11... | collective-permute-start | bytes 3538952 | tf_op jit(solution)/shard_map/ppermute | solution.py:42
  45.2 12.9 %copy-start.1 = (f32[2,2,64,1536]{3,2,1,0:T(8,128)S(1)}, f32[2,2,64,1536]{3,2,1,0:T(8,128)}, u32[]{:S(2)}) copy-start(f32[2,2,64,1536]{3,2,1,0:T(8,128)} %copy-done) | copy-start | bytes 4718596
  45.2 12.9 %collective-permute-start.2 = (bf16[2,1,64,1536]{3,2,1,0:T(8,128)(2,1)S(1)}, bf16[2,1,64,1536]{3,2,1,0:T(8,128)(2,1)}, u32[]{:S(2)}, u32[]{:S(2)}) collective-permute-start(bf16[2,1,64,1536]{3,2,1,0:T(8,128)(2,1)S(1)} %dynamic-slice_convert_fusion), channel_id=1, source_target_pairs={{0,64},{64,0},{1,65},{65,1},{2,66},{66,2},{3,67},{67,3},{4,68},{68... | collective-permute-start | bytes 1179656 | tf_op jit(solution)/shard_map/ppermute | solution.py:42
  49.4 17.5 %all-to-all-start.1 = ((bf16[16,16,1536]{2,1,0:T(8,128)(2,1)}), bf16[16,16,1536]{2,1,0:T(8,128)(2,1)S(1)}, u32[]{:S(2)}, u32[]{:S(2)}) async-start(bf16[16,16,1536]{2,1,0:T(8,128)(2,1)} %broadcast_in_dim.7), calls=%async_computation.1 | async-start | bytes 1572864 | tf_op jit(solution)/shard_map/all_to_all | solution.py:72
  59.2 12.9 %collective-permute-start.4 = (bf16[1,1,64,1536]{3,2,1,0:T(8,128)(2,1)S(1)}, bf16[1,1,64,1536]{3,2,1,0:T(8,128)(2,1)S(1)}, u32[]{:S(2)}, u32[]{:S(2)}) collective-permute-start(bf16[1,1,64,1536]{3,2,1,0:T(8,128)(2,1)S(1)} %dynamic-slice_convert_fusion.1), channel_id=1, source_target_pairs={{0,128},{128,0},{1,129},{129,1},{2,130},{130,2},{3,131},{131,3},{4... | collective-permute-start | bytes 589832 | tf_op jit(solution)/shard_map/ppermute | solution.py:42
  70.1 38.0 %copy-start.2 = (f32[1536]{0:T(1024)S(1)}, f32[1536]{0:T(1024)}, u32[]{:S(2)}) copy-start(f32[1536]{0:T(1024)} %param.8) | copy-start | bytes 18436
  72.1 13.5 %all-to-all-start.2 = ((bf16[4,64,768]{2,1,0:T(8,128)(2,1)}), bf16[4,64,768]{2,1,0:T(8,128)(2,1)S(1)}, u32[]{:S(2)}, u32[]{:S(2)}) async-start(bf16[4,64,768]{2,1,0:T(8,128)(2,1)} %bitcast.6), calls=%async_computation.2 | async-start | bytes 786432 | tf_op jit(solution)/shard_map/all_to_all | solution.py:78
  75.6 22.5 %collective-permute-start.6 = (bf16[64,768]{1,0:T(8,128)(2,1)S(1)}, bf16[64,768]{1,0:T(8,128)(2,1)S(1)}, u32[]{:S(2)}, u32[]{:S(2)}) collective-permute-start(bf16[64,768]{1,0:T(8,128)(2,1)S(1)} %fusion.15), channel_id=1, source_target_pairs={{0,258},{2,256},{256,2},{258,0},{1,259},{3,257},{257,3},{259,1},{4... | collective-permute-start | bytes 294920 | tf_op jit(solution)/shard_map/ppermute | solution.py:66
  85.6 19.6 %collective-permute-start.5 = (bf16[64,768]{1,0:T(8,128)(2,1)S(1)}, bf16[64,768]{1,0:T(8,128)(2,1)S(1)}, u32[]{:S(2)}, u32[]{:S(2)}) collective-permute-start(bf16[64,768]{1,0:T(8,128)(2,1)S(1)} %fusion.14), channel_id=1, source_target_pairs={{0,256},{256,0},{1,257},{257,1},{2,258},{258,2},{3,259},{259,3},{4... | collective-permute-start | bytes 294920 | tf_op jit(solution)/shard_map/ppermute | solution.py:42
  105.2 16.6 %collective-permute-start.7 = (bf16[256,1536]{1,0:T(8,128)(2,1)S(1)}, bf16[256,1536]{1,0:T(8,128)(2,1)S(1)}, u32[]{:S(2)}, u32[]{:S(2)}) collective-permute-start(bf16[256,1536]{1,0:T(8,128)(2,1)S(1)} %bitcast.45), channel_id=1, source_target_pairs={{0,1},{1,0},{2,3},{3,2},{4,5},{5,4},{6,7},{7,6},{8,9},{9,8},{10,11... | collective-permute-start | bytes 2359304 | tf_op jit(solution)/shard_map/ppermute | solution.py:42
  108.2 13.6 %collective-permute-start.9 = (bf16[64,768]{1,0:T(8,128)(2,1)S(1)}, bf16[64,768]{1,0:T(8,128)(2,1)S(1)}, u32[]{:S(2)}, u32[]{:S(2)}) collective-permute-start(bf16[64,768]{1,0:T(8,128)(2,1)S(1)} %fusion.10), channel_id=1, source_target_pairs={{0,256},{256,0},{1,257},{257,1},{2,258},{258,2},{3,259},{259,3},{4... | collective-permute-start | bytes 294920 | tf_op jit(solution)/shard_map/ppermute | solution.py:42
  114.1 7.8 %collective-permute-start.8 = (bf16[256,384]{1,0:T(8,128)(2,1)S(1)}, bf16[256,384]{1,0:T(8,128)(2,1)S(1)}, u32[]{:S(2)}, u32[]{:S(2)}) collective-permute-start(bf16[256,384]{1,0:T(8,128)(2,1)S(1)} %constant_dynamic-slice_fusion.1), channel_id=1, source_target_pairs={{0,1},{1,0},{2,3},{3,2},{4,5},{5,4},{6,7},{7,6},{8,9},{9,8},{10,11... | collective-permute-start | bytes 589832 | tf_op jit(solution)/shard_map/ppermute | solution.py:42
  122.7 14.8 %all-to-all-start.3 = ((bf16[4,64,768]{2,1,0:T(8,128)(2,1)}), bf16[4,64,768]{2,1,0:T(8,128)(2,1)S(1)}, u32[]{:S(2)}, u32[]{:S(2)}) async-start(bf16[4,64,768]{2,1,0:T(8,128)(2,1)} %broadcast_in_dim.8), calls=%async_computation.3 | async-start | bytes 786432 | tf_op jit(solution)/shard_map/all_to_all | solution.py:72
  126.2 15.9 %collective-permute-start.10 = (bf16[64,768]{1,0:T(8,128)(2,1)S(1)}, bf16[64,768]{1,0:T(8,128)(2,1)S(1)}, u32[]{:S(2)}, u32[]{:S(2)}) collective-permute-start(bf16[64,768]{1,0:T(8,128)(2,1)S(1)} %get-tuple-element.30), channel_id=1, source_target_pairs={{0,258},{2,256},{256,2},{258,0},{1,259},{3,257},{257,3},{259,1},{4... | collective-permute-start | bytes 294920 | tf_op jit(solution)/shard_map/ppermute | solution.py:66
  142.8 7.6 %collective-permute-start.11 = (bf16[1,1,64,1536]{3,2,1,0:T(8,128)(2,1)}, bf16[1,1,64,1536]{3,2,1,0:T(8,128)(2,1)}, u32[]{:S(2)}, u32[]{:S(2)}) collective-permute-start(bf16[1,1,64,1536]{3,2,1,0:T(8,128)(2,1)} %maximum_select_fusion.5), channel_id=1, source_target_pairs={{0,128},{128,0},{1,129},{129,1},{2,130},{130,2},{3,131},{131,3},{4... | collective-permute-start | bytes 589832 | tf_op jit(solution)/shard_map/ppermute | solution.py:42
  145.9 27.8 %all-to-all-start.4 = ((bf16[16,16,1536]{2,1,0:T(8,128)(2,1)}), bf16[16,16,1536]{2,1,0:T(8,128)(2,1)S(1)}, u32[]{:S(2)}, u32[]{:S(2)}) async-start(bf16[16,16,1536]{2,1,0:T(8,128)(2,1)} %bitcast.15), calls=%async_computation.4 | async-start | bytes 1572864 | tf_op jit(solution)/shard_map/all_to_all | solution.py:128
  151.5 12.6 %collective-permute-start.12 = (bf16[256,384]{1,0:T(8,128)(2,1)}, bf16[256,384]{1,0:T(8,128)(2,1)S(1)}, u32[]{:S(2)}, u32[]{:S(2)}) collective-permute-start(bf16[256,384]{1,0:T(8,128)(2,1)} %constant_dynamic-slice_fusion), channel_id=1, source_target_pairs={{0,1},{1,0},{2,3},{3,2},{4,5},{5,4},{6,7},{7,6},{8,9},{9,8},{10,11... | collective-permute-start | bytes 589832 | tf_op jit(solution)/shard_map/ppermute | solution.py:42
  157.6 15.9 %collective-permute-start.13 = (bf16[2,1,64,1536]{3,2,1,0:T(8,128)(2,1)S(1)}, bf16[2,1,64,1536]{3,2,1,0:T(8,128)(2,1)S(1)}, u32[]{:S(2)}, u32[]{:S(2)}) collective-permute-start(bf16[2,1,64,1536]{3,2,1,0:T(8,128)(2,1)S(1)} %maximum_select_fusion.3), channel_id=1, source_target_pairs={{0,64},{64,0},{1,65},{65,1},{2,66},{66,2},{3,67},{67,3},{4,68},{68... | collective-permute-start | bytes 1179656 | tf_op jit(solution)/shard_map/ppermute | solution.py:42
  173.8 16.1 %collective-permute-start.14 = (bf16[256,1536]{1,0:T(8,128)(2,1)S(1)}, bf16[256,1536]{1,0:T(8,128)(2,1)S(1)}, u32[]{:S(2)}, u32[]{:S(2)}) collective-permute-start(bf16[256,1536]{1,0:T(8,128)(2,1)S(1)} %bitcast.42), channel_id=1, source_target_pairs={{0,1},{1,0},{2,3},{3,2},{4,5},{5,4},{6,7},{7,6},{8,9},{9,8},{10,11... | collective-permute-start | bytes 2359304 | tf_op jit(solution)/shard_map/ppermute | solution.py:42
  176.3 15.8 %collective-permute-start.15 = (bf16[8,1536]{1,0:T(8,128)(2,1)S(1)}, bf16[8,1536]{1,0:T(8,128)(2,1)S(1)}, u32[]{:S(2)}, u32[]{:S(2)}) collective-permute-start(bf16[8,1536]{1,0:T(8,128)(2,1)S(1)} %dynamic-slice_convert_fusion.3), channel_id=1, source_target_pairs={{0,2},{2,0},{1,3},{3,1},{4,6},{6,4},{5,7},{7,5},{8,10},{10,8},{9,1... | collective-permute-start | bytes 73736 | tf_op jit(solution)/shard_map/ppermute | solution.py:42

commit v10 on v9

--- a/solution.py
+++ b/solution.py
@@ -42,13 +42,16 @@
     return lax.ppermute(value, axis, SWAP)
 
 
-def join(mine, other, axis, dim):
-    first = lax.axis_index(axis) == 0
+def joined(at, mine, other, dim):
     return jnp.where(
-        first,
+        at == 0,
         jnp.concatenate([mine, other], dim),
         jnp.concatenate([other, mine], dim),
     )
+
+
+def join(mine, other, axis, dim):
+    return joined(lax.axis_index(axis), mine, other, dim)
 
 
 def after(first, *values):
@@ -109,28 +112,35 @@
     every_x = after((back_sent, in_pair), every_x)
     pre = dot(every_x, in_pair).astype(bf16)
     back_got = swap(back_sent, "rm")
-    pre = deal(after(back_got, pre), ROW4).astype(bf16)
-    back_kept, back_sent = cut((back_kept + back_got.astype(f32))[0, 0], "zh", 1)
-    pre_got = swap(pre, "rh")
-    back = (back_kept + after(pre_got, cross(back_sent)).astype(f32)).astype(bf16)
-    pre = pre.astype(f32) + pre_got.astype(f32)
+    pre = deal(after(back_got, pre), ROW4)
+    back = (back_kept + back_got.astype(f32))[0, 0]
+    side = (lax.axis_index("rh") + zh) % 2
+    n_rows = back.shape[0] // 2
+    back_sent = part_of(back, 1 - side, n_rows, 0).astype(bf16)
+    back_half = part_of(back, side, n_rows, 0) + swap(back_sent, "rh").astype(f32)
+    back_kept, back_sent = cut(back_half, "zh", 1)
+    pre_got = swap(part_of(pre, 1 - side, n_rows, 0).astype(bf16), "rh")
+    pre = part_of(pre, side, n_rows, 0) + pre_got.astype(f32)
+    back = back_kept + after(pre_got, cross(back_sent)).astype(f32)
+
     act_f, slope = gelu_pair(pre + part_of(b_in, zh, half_h, 0))
     act, slope = lax.optimization_barrier((act_f.astype(bf16), slope))
     crossed = cross(act)
-    pair_x = swap(after(back, every_x), "core")
+    grad = (back * slope).astype(bf16)
+    grad = joined(side, grad, swap(grad, "rh"), 0)
+    act = join(act, after(grad, crossed), "zh", 1)
+    act_got = swap(act, "rh")
+    pair_x = swap(after(grad, every_x), "core")
     pair_g = part_of(every_g, 1 - core, quarter_d, 1)
-    pair_g = swap(after(back, pair_g), "core")
-    back_got = after((act, pair_x, pair_g), swap(back, "rh"))
-    back = back.astype(f32) + back_got.astype(f32)
-
-    grad = spread((back * slope).astype(bf16), ROW4)
+    pair_g = swap(after(grad, pair_g), "core")
+    grad = after((pair_x, pair_g), spread(grad, ROW4))
     part = against(grad, in_pair).astype(bf16)
     dealt = lax.all_to_all(part.reshape(-1, 2 * tok_dev, feat), GRID, 0, 0, tiled=True)
 
     own_grad = part_of(grad, core, quarter, 1)
-    act = join(act, after(part, crossed), "zh", 1)[None, None]
+    act = joined(side, act, after(part, act_got), 0)[None, None]
     act = join(act, swap(act, "rm"), "rm", 0)
-    own_part = over_rows(every_x, own_grad)
+    own_part = over_rows(every_x, after(act, own_grad))
     pair_grad = swap(after(act, part_of(grad, 1 - core, quarter, 1)), "core")
     act = join(act, swap(act, "rl"), "rl", 1).reshape(-1, act.shape[-1])
     w_in_grad = (own_part + over_rows(pair_x, pair_grad)).astype(bf16)

time: 194 us -> 207 us (1.067)
  starting transfers between devices: 124 us -> 133 us
  waiting for transfers between devices: 38.2 us -> 29.3 us
  other arithmetic: 13.4 us -> 21.9 us
  local copies, waits for them, and re-layouts: 4.17 us -> 6.72 us
    all_to_all x3, starting transfers between devices: 11.6 us -> 19.5 us  [spread(): got = lax.all_to_all(sent, axes, 0, 0, tiled=True)]
    ppermute x14 -> x16, waiting for transfers between devices: 28.9 us -> 22 us  [swap(): return lax.ppermute(value, axis, SWAP)]
    ppermute x14 -> x16, starting transfers between devices: 86.7 us -> 91.3 us  [swap(): return lax.ppermute(value, axis, SWAP)]
    ppermute x2, starting transfers between devices: 18.7 us -> 14.4 us  [cross(): return lax.ppermute(value, ('rh', 'zh'), CROSS)]
    all_to_all x3, waiting for transfers between devices: 8.7 us -> 6.13 us  [spread(): got = lax.all_to_all(sent, axes, 0, 0, tiled=True)]
    select_n x6 -> x8, other arithmetic: 9.79 us -> 11.6 us  [joined(): jnp.where(at == 0, jnp.concatenate([mine, other], dim), jnp.concatenate([...]
  transfers between devices with their start and end apart: 21 -> 23, of which waited for: 10 -> 12; matrix products, arithmetic and copies ran while one was open for 12% -> 16% of each run, Pallas kernels for 0% -> 0%
where the time goes in v10:
time: 207 us; the launch traced here: 205 us
  starting transfers between devices  133 us (64%)
  waiting for transfers between devices  29.3 us (14%)
  other arithmetic  21.9 us (11%)
  matrix products  13.2 us (6%)
  local copies, waits for them, and re-layouts  6.72 us (3%)
    ppermute x16, starting transfers between devices, swap(): return lax.ppermute(value, axis, SWAP)  91.3 us
    ppermute x16, waiting for transfers between devices, swap(): return lax.ppermute(value, axis, SWAP)  22 us
    all_to_all x3, starting transfers between devices, spread(): got = lax.all_to_all(sent, axes, 0, 0, tiled=True)  19.5 us
    ppermute x2, starting transfers between devices, cross(): return lax.ppermute(value, ('rh', 'zh'), CROSS)  14.4 us
    select_n x8, other arithmetic, joined(): jnp.where(at == 0, jnp.concatenate([mine, other], dim), jnp.concatenate([...  11.6 us
    dot_general x4, matrix products, over_rows(): lax.dot_general(left, right, (((0,), (0,)), ((), ())), preferred_element_...  6.55 us
    all_to_all x3, waiting for transfers between devices, spread(): got = lax.all_to_all(sent, axes, 0, 0, tiled=True)  6.13 us
  transfers between devices with their start and end apart: 23, of which 12 were waited for; matrix products, arithmetic and copies ran while one was open for 16% of the time, Pallas kernels for 0%

profile of v10, /device:TPU:1, one launch (start us, length us, event | category | flops | bytes accessed | tf_op | source)
XLA Modules:
  0.0 205.3 jit_solution(4389810768916516855)
XLA Ops:
  0.6 0.7 constant_dynamic-slice_fusion.4
  1.4 0.7 pad_maximum_fusion
  2.1 16.3 %collective-permute-start = (bf16[8,2304]{1,0:T(8,128)(2,1)S(1)}, bf16[8,2304]{1,0:T(8,128)(2,1)S(1)}, u32[]{:S(2)}, u32[]{:S(2)}) collective-permute-start(bf16[8,2304]{1,0:T(8,128)(2,1)S(1)} %pad_maximum_fusion), channel_id=1, source_target_pairs={{0,2},{2,0},{1,3},{3,1},{4,6},{6,4},{5,7},{7,5},{8,10},{10,8},{9,1... | collective-permute-start | bytes 110600 | tf_op jit(solution)/shard_map/ppermute | solution.py:42
  18.4 1.5 collective-permute-done
  19.9 0.8 maximum_select_fusion.8
  20.7 5.6 %collective-permute-start.1 = (bf16[1536,384]{1,0:T(8,128)(2,1)}, bf16[1536,384]{1,0:T(8,128)(2,1)}, u32[]{:S(2)}, u32[]{:S(2)}) collective-permute-start(bf16[1536,384]{1,0:T(8,128)(2,1)} %param.9), channel_id=1, source_target_pairs={{0,1},{1,0},{2,3},{3,2},{4,5},{5,4},{6,7},{7,6},{8,9},{9,8},{10,11... | collective-permute-start | bytes 3538952 | tf_op jit(solution)/shard_map/ppermute | solution.py:42
  26.3 0.8 broadcast_in_dim.6
  27.1 4.5 %all-to-all-start = ((bf16[16,16,768]{2,1,0:T(8,128)(2,1)}), bf16[16,16,768]{2,1,0:T(8,128)(2,1)S(1)}, u32[]{:S(2)}, u32[]{:S(2)}) async-start(bf16[16,16,768]{2,1,0:T(8,128)(2,1)} %broadcast_in_dim.6), calls=%async_computation | async-start | bytes 786432 | tf_op jit(solution)/shard_map/all_to_all | solution.py:75
  31.6 2.9 %maximum_select_fusion = bf16[1536,768]{1,0:T(8,128)(2,1)S(1)} fusion(bf16[1536,384]{1,0:T(8,128)(2,1)} %collective-permute-done.1, bf16[1536,384]{1,0:T(8,128)(2,1)} %param.9, pred[]{:T(512)S(6)} %eq.21), kind=kLoop, calls=%fused_computation.5 | loop fusion | flops 10616832 | bytes 4718593 | tf_op jit(solution)/shard_map/jit(_where)/select_n | solution.py:46
  34.6 6.1 %all-to-all-done = bf16[16,16,768]{2,1,0:T(8,128)(2,1)S(1)} async-done(((bf16[16,16,768]{2,1,0:T(8,128)(2,1)}), bf16[16,16,768]{2,1,0:T(8,128)(2,1)S(1)}, u32[]{:S(2)}, u32[]{:S(2)}) %all-to-all-start) | async-done | bytes 393248 | tf_op jit(solution)/shard_map/all_to_all | solution.py:75
  40.7 0.8 fusion.2
  41.5 3.6 %collective-permute-start.3 = (bf16[1536,384]{1,0:T(8,128)(2,1)}, bf16[1536,384]{1,0:T(8,128)(2,1)}, u32[]{:S(2)}, u32[]{:S(2)}) collective-permute-start(bf16[1536,384]{1,0:T(8,128)(2,1)} %param.7), channel_id=1, source_target_pairs={{0,1},{1,0},{2,3},{3,2},{4,5},{5,4},{6,7},{7,6},{8,9},{9,8},{10,11... | collective-permute-start | bytes 3538952 | tf_op jit(solution)/shard_map/ppermute | solution.py:42
  45.2 3.2 %collective-permute-start.2 = (bf16[2,1,64,1536]{3,2,1,0:T(8,128)(2,1)S(1)}, bf16[2,1,64,1536]{3,2,1,0:T(8,128)(2,1)}, u32[]{:S(2)}, u32[]{:S(2)}) collective-permute-start(bf16[2,1,64,1536]{3,2,1,0:T(8,128)(2,1)S(1)} %dynamic-slice_convert_fusion), channel_id=1, source_target_pairs={{0,64},{64,0},{1,65},{65,1},{2,66},{66,2},{3,67},{67,3},{4,68},{68... | collective-permute-start | bytes 1179656 | tf_op jit(solution)/shard_map/ppermute | solution.py:42
  48.5 1.0 broadcast_in_dim.7
  49.4 3.6 %all-to-all-start.1 = ((bf16[16,16,1536]{2,1,0:T(8,128)(2,1)}), bf16[16,16,1536]{2,1,0:T(8,128)(2,1)S(1)}, u32[]{:S(2)}, u32[]{:S(2)}) async-start(bf16[16,16,1536]{2,1,0:T(8,128)(2,1)} %broadcast_in_dim.7), calls=%async_computation.1 | async-start | bytes 1572864 | tf_op jit(solution)/shard_map/all_to_all | solution.py:75
  53.1 5.0 %collective-permute-done.2 = bf16[2,1,64,1536]{3,2,1,0:T(8,128)(2,1)} collective-permute-done((bf16[2,1,64,1536]{3,2,1,0:T(8,128)(2,1)S(1)}, bf16[2,1,64,1536]{3,2,1,0:T(8,128)(2,1)}, u32[]{:S(2)}, u32[]{:S(2)}) %collective-permute-start.2) | collective-permute-done | bytes 393248 | tf_op jit(solution)/shard_map/ppermute | solution.py:42
  58.1 1.1 convert_add_fusion
  59.2 3.6 %collective-permute-start.4 = (bf16[1,1,64,1536]{3,2,1,0:T(8,128)(2,1)S(1)}, bf16[1,1,64,1536]{3,2,1,0:T(8,128)(2,1)S(1)}, u32[]{:S(2)}, u32[]{:S(2)}) collective-permute-start(bf16[1,1,64,1536]{3,2,1,0:T(8,128)(2,1)S(1)} %dynamic-slice_convert_fusion.1), channel_id=1, source_target_pairs={{0,128},{128,0},{1,129},{129,1},{2,130},{130,2},{3,131},{131,3},{4... | collective-permute-start | bytes 589832 | tf_op jit(solution)/shard_map/ppermute | solution.py:42
  62.8 4.1 %maximum_select_fusion.1 = bf16[1536,768]{1,0:T(8,128)(2,1)} fusion(bf16[1536,384]{1,0:T(8,128)(2,1)} %collective-permute-done.3, bf16[1536,384]{1,0:T(8,128)(2,1)} %param.7, pred[]{:T(512)S(6)} %eq.21), kind=kLoop, calls=%fused_computation.6 | loop fusion | flops 10616832 | bytes 4718593 | tf_op jit(solution)/shard_map/jit(_where)/select_n | solution.py:46
  66.9 3.2 %convolution_convert_fusion.1 = bf16[256,768]{1,0:T(8,128)(2,1)} fusion(bf16[256,1536]{1,0:T(8,128)(2,1)S(1)} %bitcast.49, bf16[1536,768]{1,0:T(8,128)(2,1)} %maximum_select_fusion.1), kind=kOutput, calls=%fused_computation.10 | convolution fusion | flops 604176384 | bytes 3538944 | tf_op jit(solution)/shard_map/dot_general | solution.py:26
  70.1 1.9 collective-permute-done.4
  72.1 4.1 %all-to-all-start.2 = ((bf16[4,64,768]{2,1,0:T(8,128)(2,1)}), bf16[4,64,768]{2,1,0:T(8,128)(2,1)}, u32[]{:S(2)}, u32[]{:S(2)}) async-start(bf16[4,64,768]{2,1,0:T(8,128)(2,1)} %bitcast.5), calls=%async_computation.2 | async-start | bytes 786432 | tf_op jit(solution)/shard_map/all_to_all | solution.py:81
  76.3 0.7 copy-done.3
  77.0 0.6 fusion.11
  77.6 8.0 %collective-permute-start.6 = (bf16[32,1536]{1,0:T(8,128)(2,1)}, bf16[32,1536]{1,0:T(8,128)(2,1)}, u32[]{:S(2)}, u32[]{:S(2)}) collective-permute-start(bf16[32,1536]{1,0:T(8,128)(2,1)} %fusion.11), channel_id=1, source_target_pairs={{0,256},{256,0},{1,257},{257,1},{2,258},{258,2},{3,259},{259,3},{4... | collective-permute-start | bytes 294920 | tf_op jit(solution)/shard_map/ppermute | solution.py:42
  85.8 2.4 %collective-permute-done.6 = bf16[32,1536]{1,0:T(8,128)(2,1)} collective-permute-done((bf16[32,1536]{1,0:T(8,128)(2,1)}, bf16[32,1536]{1,0:T(8,128)(2,1)}, u32[]{:S(2)}, u32[]{:S(2)}) %collective-permute-start.6) | collective-permute-done | bytes 98336 | tf_op jit(solution)/shard_map/ppermute | solution.py:42
  88.2 1.7 bitcast_add_fusion
  89.9 1.1 convert_add_fusion.2
  91.0 7.4 %collective-permute-start.5 = (bf16[32,768]{1,0:T(8,128)(2,1)S(1)}, bf16[32,768]{1,0:T(8,128)(2,1)S(1)}, u32[]{:S(2)}, u32[]{:S(2)}) collective-permute-start(bf16[32,768]{1,0:T(8,128)(2,1)S(1)} %fusion.13), channel_id=1, source_target_pairs={{0,256},{256,0},{1,257},{257,1},{2,258},{258,2},{3,259},{259,3},{4... | collective-permute-start | bytes 147464 | tf_op jit(solution)/shard_map/ppermute | solution.py:42
  98.3 0.9 dynamic-slice_convert_fusion.3
  99.2 7.7 %collective-permute-start.7 = (bf16[32,768]{1,0:T(8,128)(2,1)S(1)}, bf16[32,768]{1,0:T(8,128)(2,1)S(1)}, u32[]{:S(2)}, u32[]{:S(2)}) collective-permute-start(bf16[32,768]{1,0:T(8,128)(2,1)S(1)} %dynamic-slice_convert_fusion.3), channel_id=1, source_target_pairs={{0,258},{2,256},{256,2},{258,0},{1,259},{3,257},{257,3},{259,1},{4... | collective-permute-start | bytes 147464 | tf_op jit(solution)/shard_map/ppermute | solution.py:69
  106.9 0.7 fusion.10
  107.6 0.7 collective-permute-done.7
  108.4 1.5 multiply_convert_fusion
  109.9 5.2 %collective-permute-start.8 = (bf16[32,768]{1,0:T(8,128)(2,1)}, bf16[32,768]{1,0:T(8,128)(2,1)}, u32[]{:S(2)}, u32[]{:S(2)}) collective-permute-start(bf16[32,768]{1,0:T(8,128)(2,1)} %multiply_convert_fusion), channel_id=1, source_target_pairs={{0,256},{256,0},{1,257},{257,1},{2,258},{258,2},{3,259},{259,3},{4... | collective-permute-start | bytes 147464 | tf_op jit(solution)/shard_map/ppermute | solution.py:42
  115.1 3.8 %collective-permute-done.8 = bf16[32,768]{1,0:T(8,128)(2,1)} collective-permute-done((bf16[32,768]{1,0:T(8,128)(2,1)}, bf16[32,768]{1,0:T(8,128)(2,1)}, u32[]{:S(2)}, u32[]{:S(2)}) %collective-permute-start.8) | collective-permute-done | bytes 49184 | tf_op jit(solution)/shard_map/ppermute | solution.py:42
  119.0 0.9 maximum_select_fusion.6
  119.9 0.8 broadcast_in_dim.8
  120.7 11.4 %all-to-all-start.3 = ((bf16[4,64,768]{2,1,0:T(8,128)(2,1)}), bf16[4,64,768]{2,1,0:T(8,128)(2,1)}, u32[]{:S(2)}, u32[]{:S(2)}) async-start(bf16[4,64,768]{2,1,0:T(8,128)(2,1)} %broadcast_in_dim.8), calls=%async_computation.3 | async-start | bytes 786432 | tf_op jit(solution)/shard_map/all_to_all | solution.py:75
  132.1 6.3 %collective-permute-start.10 = (bf16[256,1536]{1,0:T(8,128)(2,1)S(1)}, bf16[256,1536]{1,0:T(8,128)(2,1)}, u32[]{:S(2)}, u32[]{:S(2)}) collective-permute-start(bf16[256,1536]{1,0:T(8,128)(2,1)S(1)} %bitcast.50), channel_id=1, source_target_pairs={{0,1},{1,0},{2,3},{3,2},{4,5},{5,4},{6,7},{7,6},{8,9},{9,8},{10,11... | collective-permute-start | bytes 2359304 | tf_op jit(solution)/shard_map/ppermute | solution.py:42
  138.4 6.7 %collective-permute-start.9 = (bf16[32,768]{1,0:T(8,128)(2,1)}, bf16[32,768]{1,0:T(8,128)(2,1)S(1)}, u32[]{:S(2)}, u32[]{:S(2)}) collective-permute-start(bf16[32,768]{1,0:T(8,128)(2,1)} %get-tuple-element.31), channel_id=1, source_target_pairs={{0,258},{2,256},{256,2},{258,0},{1,259},{3,257},{257,3},{259,1},{4... | collective-permute-start | bytes 147464 | tf_op jit(solution)/shard_map/ppermute | solution.py:69
  145.1 2.2 %collective-permute-start.11 = (bf16[256,384]{1,0:T(8,128)(2,1)S(1)}, bf16[256,384]{1,0:T(8,128)(2,1)}, u32[]{:S(2)}, u32[]{:S(2)}) collective-permute-start(bf16[256,384]{1,0:T(8,128)(2,1)S(1)} %constant_dynamic-slice_fusion.2), channel_id=1, source_target_pairs={{0,1},{1,0},{2,3},{3,2},{4,5},{5,4},{6,7},{7,6},{8,9},{9,8},{10,11... | collective-permute-start | bytes 589832 | tf_op jit(solution)/shard_map/ppermute | solution.py:42
  147.8 1.5 maximum_select_fusion.7
  149.3 3.5 %collective-permute-start.12 = (bf16[32,1536]{1,0:T(8,128)(2,1)}, bf16[32,1536]{1,0:T(8,128)(2,1)}, u32[]{:S(2)}, u32[]{:S(2)}) collective-permute-start(bf16[32,1536]{1,0:T(8,128)(2,1)} %maximum_select_fusion.7), channel_id=1, source_target_pairs={{0,256},{256,0},{1,257},{257,1},{2,258},{258,2},{3,259},{259,3},{4... | collective-permute-start | bytes 294920 | tf_op jit(solution)/shard_map/ppermute | solution.py:42
  152.9 2.7 %convolution_convert_fusion = bf16[256,1536]{1,0:T(8,128)(2,1)} fusion(bf16[256,768]{1,0:T(8,128)(2,1)} %bitcast.11, bf16[1536,768]{1,0:T(8,128)(2,1)S(1)} %copy-done.2), kind=kOutput, calls=%fused_computation.4 | convolution fusion | flops 604372992 | bytes 3538944 | tf_op jit(solution)/shard_map/dot_general | solution.py:30
  155.6 0.9 constant_dynamic-slice_fusion
  156.5 2.3 %collective-permute-done.12 = bf16[32,1536]{1,0:T(8,128)(2,1)} collective-permute-done((bf16[32,1536]{1,0:T(8,128)(2,1)}, bf16[32,1536]{1,0:T(8,128)(2,1)}, u32[]{:S(2)}, u32[]{:S(2)}) %collective-permute-start.12) | collective-permute-done | bytes 98336 | tf_op jit(solution)/shard_map/ppermute | solution.py:42
  158.9 1.1 maximum_select_fusion.5
  160.0 7.5 %collective-permute-start.13 = (bf16[1,1,64,1536]{3,2,1,0:T(8,128)(2,1)S(1)}, bf16[1,1,64,1536]{3,2,1,0:T(8,128)(2,1)S(1)}, u32[]{:S(2)}, u32[]{:S(2)}) collective-permute-start(bf16[1,1,64,1536]{3,2,1,0:T(8,128)(2,1)S(1)} %maximum_select_fusion.5), channel_id=1, source_target_pairs={{0,128},{128,0},{1,129},{129,1},{2,130},{130,2},{3,131},{131,3},{4... | collective-permute-start | bytes 589832 | tf_op jit(solution)/shard_map/ppermute | solution.py:42
  167.4 1.0 convert_reduce_fusion.2
  168.4 3.6 %all-to-all-start.4 = ((bf16[16,16,1536]{2,1,0:T(8,128)(2,1)}), bf16[16,16,1536]{2,1,0:T(8,128)(2,1)S(1)}, u32[]{:S(2)}, u32[]{:S(2)}) async-start(bf16[16,16,1536]{2,1,0:T(8,128)(2,1)} %bitcast.52), calls=%async_computation.4 | async-start | bytes 1572864 | tf_op jit(solution)/shard_map/all_to_all | solution.py:138
  172.1 1.1 fusion.4
  173.1 2.2 %collective-permute-done.13 = bf16[1,1,64,1536]{3,2,1,0:T(8,128)(2,1)S(1)} collective-permute-done((bf16[1,1,64,1536]{3,2,1,0:T(8,128)(2,1)S(1)}, bf16[1,1,64,1536]{3,2,1,0:T(8,128)(2,1)S(1)}, u32[]{:S(2)}, u32[]{:S(2)}) %collective-permute-start.13) | collective-permute-done | bytes 196640 | tf_op jit(solution)/shard_map/ppermute | solution.py:42
  175.4 3.6 %collective-permute-start.15 = (bf16[2,1,64,1536]{3,2,1,0:T(8,128)(2,1)S(1)}, bf16[2,1,64,1536]{3,2,1,0:T(8,128)(2,1)S(1)}, u32[]{:S(2)}, u32[]{:S(2)}) collective-permute-start(bf16[2,1,64,1536]{3,2,1,0:T(8,128)(2,1)S(1)} %maximum_select_fusion.3), channel_id=1, source_target_pairs={{0,64},{64,0},{1,65},{65,1},{2,66},{66,2},{3,67},{67,3},{4,68},{68... | collective-permute-start | bytes 1179656 | tf_op jit(solution)/shard_map/ppermute | solution.py:42
  179.0 3.1 %collective-permute-start.14 = (bf16[256,384]{1,0:T(8,128)(2,1)S(1)}, bf16[256,384]{1,0:T(8,128)(2,1)S(1)}, u32[]{:S(2)}, u32[]{:S(2)}) collective-permute-start(bf16[256,384]{1,0:T(8,128)(2,1)S(1)} %constant_dynamic-slice_fusion), channel_id=1, source_target_pairs={{0,1},{1,0},{2,3},{3,2},{4,5},{5,4},{6,7},{7,6},{8,9},{9,8},{10,11... | collective-permute-start | bytes 589832 | tf_op jit(solution)/shard_map/ppermute | solution.py:42
  182.1 0.6 fusion.15
  183.2 0.6 add.139
  183.8 2.8 %fusion = bf16[1536,384]{1,0:T(8,128)(2,1)} fusion(f32[1536,384]{1,0:T(8,128)S(1)} %fusion.15, bf16[256,1536]{1,0:T(8,128)(2,1)} %collective-permute-done.10, bf16[256,384]{1,0:T(8,128)(2,1)S(1)} %collective-permute-done.14), kind=kOutput, calls=%fused_computation.2 | convolution fusion | flops 303169536 | bytes 4521984 | tf_op jit(solution)/shard_map/dot_general | solution.py:34
  186.8 4.4 %collective-permute-start.16 = (bf16[256,1536]{1,0:T(8,128)(2,1)S(1)}, bf16[256,1536]{1,0:T(8,128)(2,1)S(1)}, u32[]{:S(2)}, u32[]{:S(2)}) collective-permute-start(bf16[256,1536]{1,0:T(8,128)(2,1)S(1)} %bitcast.47), channel_id=1, source_target_pairs={{0,1},{1,0},{2,3},{3,2},{4,5},{5,4},{6,7},{7,6},{8,9},{9,8},{10,11... | collective-permute-start | bytes 2359304 | tf_op jit(solution)/shard_map/ppermute | solution.py:42
  191.2 7.9 %collective-permute-start.17 = (bf16[8,1536]{1,0:T(8,128)(2,1)S(1)}, bf16[8,1536]{1,0:T(8,128)(2,1)S(1)}, u32[]{:S(2)}, u32[]{:S(2)}) collective-permute-start(bf16[8,1536]{1,0:T(8,128)(2,1)S(1)} %dynamic-slice_convert_fusion.5), channel_id=1, source_target_pairs={{0,2},{2,0},{1,3},{3,1},{4,6},{6,4},{5,7},{7,5},{8,10},{10,8},{9,1... | collective-permute-start | bytes 73736 | tf_op jit(solution)/shard_map/ppermute | solution.py:42
  199.1 1.5 fusion.16
  200.7 1.6 fusion.1
  202.3 2.3 %collective-permute-done.17 = bf16[8,1536]{1,0:T(8,128)(2,1)S(1)} collective-permute-done((bf16[8,1536]{1,0:T(8,128)(2,1)S(1)}, bf16[8,1536]{1,0:T(8,128)(2,1)S(1)}, u32[]{:S(2)}, u32[]{:S(2)}) %collective-permute-start.17) | collective-permute-done | bytes 24608 | tf_op jit(solution)/shard_map/ppermute | solution.py:42
  204.7 0.6 add_convert_fusion
  (35 shorter events, 1.5 us)
Async XLA Ops:
  2.1 17.7 %collective-permute-start = (bf16[8,2304]{1,0:T(8,128)(2,1)S(1)}, bf16[8,2304]{1,0:T(8,128)(2,1)S(1)}, u32[]{:S(2)}, u32[]{:S(2)}) collective-permute-start(bf16[8,2304]{1,0:T(8,128)(2,1)S(1)} %pad_maximum_fusion), channel_id=1, source_target_pairs={{0,2},{2,0},{1,3},{3,1},{4,6},{6,4},{5,7},{7,5},{8,10},{10,8},{9,1... | collective-permute-start | bytes 110600 | tf_op jit(solution)/shard_map/ppermute | solution.py:42
  20.7 10.9 %collective-permute-start.1 = (bf16[1536,384]{1,0:T(8,128)(2,1)}, bf16[1536,384]{1,0:T(8,128)(2,1)}, u32[]{:S(2)}, u32[]{:S(2)}) collective-permute-start(bf16[1536,384]{1,0:T(8,128)(2,1)} %param.9), channel_id=1, source_target_pairs={{0,1},{1,0},{2,3},{3,2},{4,5},{5,4},{6,7},{7,6},{8,9},{9,8},{10,11... | collective-permute-start | bytes 3538952 | tf_op jit(solution)/shard_map/ppermute | solution.py:42
  27.1 13.6 %all-to-all-start = ((bf16[16,16,768]{2,1,0:T(8,128)(2,1)}), bf16[16,16,768]{2,1,0:T(8,128)(2,1)S(1)}, u32[]{:S(2)}, u32[]{:S(2)}) async-start(bf16[16,16,768]{2,1,0:T(8,128)(2,1)} %broadcast_in_dim.6), calls=%async_computation | async-start | bytes 786432 | tf_op jit(solution)/shard_map/all_to_all | solution.py:75
  41.5 3.6 %copy-start = (f32[2,2,64,1536]{3,2,1,0:T(8,128)}, f32[2,2,64,1536]{3,2,1,0:T(8,128)S(1)}, u32[]{:S(2)}) copy-start(f32[2,2,64,1536]{3,2,1,0:T(8,128)S(1)} %fusion.2) | copy-start | bytes 4718596
  41.5 21.3 %collective-permute-start.3 = (bf16[1536,384]{1,0:T(8,128)(2,1)}, bf16[1536,384]{1,0:T(8,128)(2,1)}, u32[]{:S(2)}, u32[]{:S(2)}) collective-permute-start(bf16[1536,384]{1,0:T(8,128)(2,1)} %param.7), channel_id=1, source_target_pairs={{0,1},{1,0},{2,3},{3,2},{4,5},{5,4},{6,7},{7,6},{8,9},{9,8},{10,11... | collective-permute-start | bytes 3538952 | tf_op jit(solution)/shard_map/ppermute | solution.py:42
  45.2 12.9 %copy-start.1 = (f32[2,2,64,1536]{3,2,1,0:T(8,128)S(1)}, f32[2,2,64,1536]{3,2,1,0:T(8,128)}, u32[]{:S(2)}) copy-start(f32[2,2,64,1536]{3,2,1,0:T(8,128)} %copy-done) | copy-start | bytes 4718596
  45.2 12.9 %collective-permute-start.2 = (bf16[2,1,64,1536]{3,2,1,0:T(8,128)(2,1)S(1)}, bf16[2,1,64,1536]{3,2,1,0:T(8,128)(2,1)}, u32[]{:S(2)}, u32[]{:S(2)}) collective-permute-start(bf16[2,1,64,1536]{3,2,1,0:T(8,128)(2,1)S(1)} %dynamic-slice_convert_fusion), channel_id=1, source_target_pairs={{0,64},{64,0},{1,65},{65,1},{2,66},{66,2},{3,67},{67,3},{4,68},{68... | collective-permute-start | bytes 1179656 | tf_op jit(solution)/shard_map/ppermute | solution.py:42
  49.4 17.5 %all-to-all-start.1 = ((bf16[16,16,1536]{2,1,0:T(8,128)(2,1)}), bf16[16,16,1536]{2,1,0:T(8,128)(2,1)S(1)}, u32[]{:S(2)}, u32[]{:S(2)}) async-start(bf16[16,16,1536]{2,1,0:T(8,128)(2,1)} %broadcast_in_dim.7), calls=%async_computation.1 | async-start | bytes 1572864 | tf_op jit(solution)/shard_map/all_to_all | solution.py:75
  59.2 12.9 %collective-permute-start.4 = (bf16[1,1,64,1536]{3,2,1,0:T(8,128)(2,1)S(1)}, bf16[1,1,64,1536]{3,2,1,0:T(8,128)(2,1)S(1)}, u32[]{:S(2)}, u32[]{:S(2)}) collective-permute-start(bf16[1,1,64,1536]{3,2,1,0:T(8,128)(2,1)S(1)} %dynamic-slice_convert_fusion.1), channel_id=1, source_target_pairs={{0,128},{128,0},{1,129},{129,1},{2,130},{130,2},{3,131},{131,3},{4... | collective-permute-start | bytes 589832 | tf_op jit(solution)/shard_map/ppermute | solution.py:42
  66.9 18.7 %copy-start.4 = (f32[1536]{0:T(1024)S(1)}, f32[1536]{0:T(1024)}, u32[]{:S(2)}) copy-start(f32[1536]{0:T(1024)} %param.8) | copy-start | bytes 18436
  72.1 17.8 %all-to-all-start.2 = ((bf16[4,64,768]{2,1,0:T(8,128)(2,1)}), bf16[4,64,768]{2,1,0:T(8,128)(2,1)}, u32[]{:S(2)}, u32[]{:S(2)}) async-start(bf16[4,64,768]{2,1,0:T(8,128)(2,1)} %bitcast.5), calls=%async_computation.2 | async-start | bytes 786432 | tf_op jit(solution)/shard_map/all_to_all | solution.py:81
  76.2 0.7 copy-start.3
  77.0 75.9 %copy-start.2 = (bf16[1536,768]{1,0:T(8,128)(2,1)S(1)}, bf16[1536,768]{1,0:T(8,128)(2,1)}, u32[]{:S(2)}) copy-start(bf16[1536,768]{1,0:T(8,128)(2,1)} %maximum_select_fusion.1) | copy-start | bytes 7077892
  77.6 10.5 %collective-permute-start.6 = (bf16[32,1536]{1,0:T(8,128)(2,1)}, bf16[32,1536]{1,0:T(8,128)(2,1)}, u32[]{:S(2)}, u32[]{:S(2)}) collective-permute-start(bf16[32,1536]{1,0:T(8,128)(2,1)} %fusion.11), channel_id=1, source_target_pairs={{0,256},{256,0},{1,257},{257,1},{2,258},{258,2},{3,259},{259,3},{4... | collective-permute-start | bytes 294920 | tf_op jit(solution)/shard_map/ppermute | solution.py:42
  91.0 16.0 %collective-permute-start.5 = (bf16[32,768]{1,0:T(8,128)(2,1)S(1)}, bf16[32,768]{1,0:T(8,128)(2,1)S(1)}, u32[]{:S(2)}, u32[]{:S(2)}) collective-permute-start(bf16[32,768]{1,0:T(8,128)(2,1)S(1)} %fusion.13), channel_id=1, source_target_pairs={{0,256},{256,0},{1,257},{257,1},{2,258},{258,2},{3,259},{259,3},{4... | collective-permute-start | bytes 147464 | tf_op jit(solution)/shard_map/ppermute | solution.py:42
  99.2 9.2 %collective-permute-start.7 = (bf16[32,768]{1,0:T(8,128)(2,1)S(1)}, bf16[32,768]{1,0:T(8,128)(2,1)S(1)}, u32[]{:S(2)}, u32[]{:S(2)}) collective-permute-start(bf16[32,768]{1,0:T(8,128)(2,1)S(1)} %dynamic-slice_convert_fusion.3), channel_id=1, source_target_pairs={{0,258},{2,256},{256,2},{258,0},{1,259},{3,257},{257,3},{259,1},{4... | collective-permute-start | bytes 147464 | tf_op jit(solution)/shard_map/ppermute | solution.py:69
  109.9 9.0 %collective-permute-start.8 = (bf16[32,768]{1,0:T(8,128)(2,1)}, bf16[32,768]{1,0:T(8,128)(2,1)}, u32[]{:S(2)}, u32[]{:S(2)}) collective-permute-start(bf16[32,768]{1,0:T(8,128)(2,1)} %multiply_convert_fusion), channel_id=1, source_target_pairs={{0,256},{256,0},{1,257},{257,1},{2,258},{258,2},{3,259},{259,3},{4... | collective-permute-start | bytes 147464 | tf_op jit(solution)/shard_map/ppermute | solution.py:42
  120.7 32.2 %all-to-all-start.3 = ((bf16[4,64,768]{2,1,0:T(8,128)(2,1)}), bf16[4,64,768]{2,1,0:T(8,128)(2,1)}, u32[]{:S(2)}, u32[]{:S(2)}) async-start(bf16[4,64,768]{2,1,0:T(8,128)(2,1)} %broadcast_in_dim.8), calls=%async_computation.3 | async-start | bytes 786432 | tf_op jit(solution)/shard_map/all_to_all | solution.py:75
  132.1 20.8 %collective-permute-start.10 = (bf16[256,1536]{1,0:T(8,128)(2,1)S(1)}, bf16[256,1536]{1,0:T(8,128)(2,1)}, u32[]{:S(2)}, u32[]{:S(2)}) collective-permute-start(bf16[256,1536]{1,0:T(8,128)(2,1)S(1)} %bitcast.50), channel_id=1, source_target_pairs={{0,1},{1,0},{2,3},{3,2},{4,5},{5,4},{6,7},{7,6},{8,9},{9,8},{10,11... | collective-permute-start | bytes 2359304 | tf_op jit(solution)/shard_map/ppermute | solution.py:42
  138.4 9.4 %collective-permute-start.9 = (bf16[32,768]{1,0:T(8,128)(2,1)}, bf16[32,768]{1,0:T(8,128)(2,1)S(1)}, u32[]{:S(2)}, u32[]{:S(2)}) collective-permute-start(bf16[32,768]{1,0:T(8,128)(2,1)} %get-tuple-element.31), channel_id=1, source_target_pairs={{0,258},{2,256},{256,2},{258,0},{1,259},{3,257},{257,3},{259,1},{4... | collective-permute-start | bytes 147464 | tf_op jit(solution)/shard_map/ppermute | solution.py:69
  145.1 7.7 %collective-permute-start.11 = (bf16[256,384]{1,0:T(8,128)(2,1)S(1)}, bf16[256,384]{1,0:T(8,128)(2,1)}, u32[]{:S(2)}, u32[]{:S(2)}) collective-permute-start(bf16[256,384]{1,0:T(8,128)(2,1)S(1)} %constant_dynamic-slice_fusion.2), channel_id=1, source_target_pairs={{0,1},{1,0},{2,3},{3,2},{4,5},{5,4},{6,7},{7,6},{8,9},{9,8},{10,11... | collective-permute-start | bytes 589832 | tf_op jit(solution)/shard_map/ppermute | solution.py:42
  149.3 9.6 %collective-permute-start.12 = (bf16[32,1536]{1,0:T(8,128)(2,1)}, bf16[32,1536]{1,0:T(8,128)(2,1)}, u32[]{:S(2)}, u32[]{:S(2)}) collective-permute-start(bf16[32,1536]{1,0:T(8,128)(2,1)} %maximum_select_fusion.7), channel_id=1, source_target_pairs={{0,256},{256,0},{1,257},{257,1},{2,258},{258,2},{3,259},{259,3},{4... | collective-permute-start | bytes 294920 | tf_op jit(solution)/shard_map/ppermute | solution.py:42
  160.0 15.4 %collective-permute-start.13 = (bf16[1,1,64,1536]{3,2,1,0:T(8,128)(2,1)S(1)}, bf16[1,1,64,1536]{3,2,1,0:T(8,128)(2,1)S(1)}, u32[]{:S(2)}, u32[]{:S(2)}) collective-permute-start(bf16[1,1,64,1536]{3,2,1,0:T(8,128)(2,1)S(1)} %maximum_select_fusion.5), channel_id=1, source_target_pairs={{0,128},{128,0},{1,129},{129,1},{2,130},{130,2},{3,131},{131,3},{4... | collective-permute-start | bytes 589832 | tf_op jit(solution)/shard_map/ppermute | solution.py:42
  168.4 18.2 %all-to-all-start.4 = ((bf16[16,16,1536]{2,1,0:T(8,128)(2,1)}), bf16[16,16,1536]{2,1,0:T(8,128)(2,1)S(1)}, u32[]{:S(2)}, u32[]{:S(2)}) async-start(bf16[16,16,1536]{2,1,0:T(8,128)(2,1)} %bitcast.52), calls=%async_computation.4 | async-start | bytes 1572864 | tf_op jit(solution)/shard_map/all_to_all | solution.py:138
  175.4 11.1 %collective-permute-start.15 = (bf16[2,1,64,1536]{3,2,1,0:T(8,128)(2,1)S(1)}, bf16[2,1,64,1536]{3,2,1,0:T(8,128)(2,1)S(1)}, u32[]{:S(2)}, u32[]{:S(2)}) collective-permute-start(bf16[2,1,64,1536]{3,2,1,0:T(8,128)(2,1)S(1)} %maximum_select_fusion.3), channel_id=1, source_target_pairs={{0,64},{64,0},{1,65},{65,1},{2,66},{66,2},{3,67},{67,3},{4,68},{68... | collective-permute-start | bytes 1179656 | tf_op jit(solution)/shard_map/ppermute | solution.py:42
  179.0 4.1 %collective-permute-start.14 = (bf16[256,384]{1,0:T(8,128)(2,1)S(1)}, bf16[256,384]{1,0:T(8,128)(2,1)S(1)}, u32[]{:S(2)}, u32[]{:S(2)}) collective-permute-start(bf16[256,384]{1,0:T(8,128)(2,1)S(1)} %constant_dynamic-slice_fusion), channel_id=1, source_target_pairs={{0,1},{1,0},{2,3},{3,2},{4,5},{5,4},{6,7},{7,6},{8,9},{9,8},{10,11... | collective-permute-start | bytes 589832 | tf_op jit(solution)/shard_map/ppermute | solution.py:42
  186.8 12.3 %collective-permute-start.16 = (bf16[256,1536]{1,0:T(8,128)(2,1)S(1)}, bf16[256,1536]{1,0:T(8,128)(2,1)S(1)}, u32[]{:S(2)}, u32[]{:S(2)}) collective-permute-start(bf16[256,1536]{1,0:T(8,128)(2,1)S(1)} %bitcast.47), channel_id=1, source_target_pairs={{0,1},{1,0},{2,3},{3,2},{4,5},{5,4},{6,7},{7,6},{8,9},{9,8},{10,11... | collective-permute-start | bytes 2359304 | tf_op jit(solution)/shard_map/ppermute | solution.py:42
  191.2 13.4 %collective-permute-start.17 = (bf16[8,1536]{1,0:T(8,128)(2,1)S(1)}, bf16[8,1536]{1,0:T(8,128)(2,1)S(1)}, u32[]{:S(2)}, u32[]{:S(2)}) collective-permute-start(bf16[8,1536]{1,0:T(8,128)(2,1)S(1)} %dynamic-slice_convert_fusion.5), channel_id=1, source_target_pairs={{0,2},{2,0},{1,3},{3,1},{4,6},{6,4},{5,7},{7,5},{8,10},{10,8},{9,1... | collective-permute-start | bytes 73736 | tf_op jit(solution)/shard_map/ppermute | solution.py:42

commit v11 on v8

--- a/solution.py
+++ b/solution.py
@@ -127,11 +127,11 @@
     dealt = lax.all_to_all(part.reshape(-1, 2 * tok_dev, feat), GRID, 0, 0, tiled=True)
 
     own_grad = part_of(grad, core, quarter, 1)
-    act = join(act, after(part, crossed), "zh", 1)[None, None]
-    act = join(act, swap(act, "rm"), "rm", 0)
+    act = join(act, crossed, "zh", 1)[None, None]
+    act = join(act, after(part, swap(act, "rm")), "rm", 0)
     own_part = over_rows(every_x, own_grad)
-    pair_grad = swap(after(act, part_of(grad, 1 - core, quarter, 1)), "core")
-    act = join(act, swap(act, "rl"), "rl", 1).reshape(-1, act.shape[-1])
+    pair_grad = swap(after(own_part, part_of(grad, 1 - core, quarter, 1)), "core")
+    act = join(act, after(dealt, swap(after(own_part, act), "rl")), "rl", 1).reshape(-1, act.shape[-1])
     w_in_grad = (own_part + over_rows(pair_x, pair_grad)).astype(bf16)
     b_in_grad = jnp.sum(own_grad.astype(f32), 0) + jnp.sum(pair_grad.astype(f32), 0)
 

time: 192 us -> 192 us (level)
  starting transfers between devices: 126 us -> 122 us
  other arithmetic: 11.7 us -> 14.5 us
    ppermute x13, starting transfers between devices: 72.9 us -> 68.7 us  [swap(): return lax.ppermute(value, axis, SWAP)]
    ppermute x2, waiting for transfers between devices: 4.42 us -> 8.46 us  [cross(): return lax.ppermute(value, ('rh', 'zh'), CROSS)]
    ppermute x13, waiting for transfers between devices: 23.5 us -> 20.5 us  [swap(): return lax.ppermute(value, axis, SWAP)]
    select_n x6, other arithmetic: 8.08 us -> 10.9 us  [join(): jnp.where(first, jnp.concatenate([mine, other], dim), jnp.concatenate([ot...]
  transfers between devices with their start and end apart: 20 -> 20, of which waited for: 9 -> 9; matrix products, arithmetic and copies ran while one was open for 12% -> 13% of each run, Pallas kernels for 0% -> 0%
where the time goes in v11:
time: 192 us; the launch traced here: 190 us
  starting transfers between devices  122 us (64%)
  waiting for transfers between devices  35.1 us (18%)
  other arithmetic  14.5 us (8%)
  matrix products  11.8 us (6%)
  local copies, waits for them, and re-layouts  5.45 us (3%)
    ppermute x13, starting transfers between devices, swap(): return lax.ppermute(value, axis, SWAP)  68.7 us
    all_to_all x3, starting transfers between devices, spread(): got = lax.all_to_all(sent, axes, 0, 0, tiled=True)  25.3 us
    ppermute x2, starting transfers between devices, cross(): return lax.ppermute(value, ('rh', 'zh'), CROSS)  21 us
    ppermute x13, waiting for transfers between devices, swap(): return lax.ppermute(value, axis, SWAP)  20.5 us
    select_n x6, other arithmetic, join(): jnp.where(first, jnp.concatenate([mine, other], dim), jnp.concatenate([ot...  10.9 us
    ppermute x2, waiting for transfers between devices, cross(): return lax.ppermute(value, ('rh', 'zh'), CROSS)  8.46 us
    all_to_all x3, waiting for transfers between devices, spread(): got = lax.all_to_all(sent, axes, 0, 0, tiled=True)  6.18 us
    dot_general x4, matrix products, over_rows(): lax.dot_general(left, right, (((0,), (0,)), ((), ())), preferred_element_...  4.49 us
  transfers between devices with their start and end apart: 20, of which 9 were waited for; matrix products, arithmetic and copies ran while one was open for 13% of the time, Pallas kernels for 0%

profile of v11, /device:TPU:1, one launch (start us, length us, event | category | flops | bytes accessed | tf_op | source)
XLA Modules:
  0.0 190.0 jit_solution(12670486634011822200)
XLA Ops:
  0.6 0.7 constant_dynamic-slice_fusion.3
  1.4 0.7 pad_maximum_fusion.1
  2.1 16.3 %collective-permute-start = (bf16[8,2304]{1,0:T(8,128)(2,1)S(1)}, bf16[8,2304]{1,0:T(8,128)(2,1)S(1)}, u32[]{:S(2)}, u32[]{:S(2)}) collective-permute-start(bf16[8,2304]{1,0:T(8,128)(2,1)S(1)} %pad_maximum_fusion.1), channel_id=1, source_target_pairs={{0,2},{2,0},{1,3},{3,1},{4,6},{6,4},{5,7},{7,5},{8,10},{10,8},{9,1... | collective-permute-start | bytes 110600 | tf_op jit(solution)/shard_map/ppermute | solution.py:42
  18.4 1.5 collective-permute-done
  19.9 0.8 maximum_select_fusion.6
  20.7 0.0 copy-start.2
  20.7 5.6 %collective-permute-start.1 = (bf16[1536,384]{1,0:T(8,128)(2,1)}, bf16[1536,384]{1,0:T(8,128)(2,1)}, u32[]{:S(2)}, u32[]{:S(2)}) collective-permute-start(bf16[1536,384]{1,0:T(8,128)(2,1)} %param.9), channel_id=1, source_target_pairs={{0,1},{1,0},{2,3},{3,2},{4,5},{5,4},{6,7},{7,6},{8,9},{9,8},{10,11... | collective-permute-start | bytes 3538952 | tf_op jit(solution)/shard_map/ppermute | solution.py:42
  26.3 0.8 broadcast_in_dim.6
  27.1 4.5 %all-to-all-start = ((bf16[16,16,768]{2,1,0:T(8,128)(2,1)}), bf16[16,16,768]{2,1,0:T(8,128)(2,1)S(1)}, u32[]{:S(2)}, u32[]{:S(2)}) async-start(bf16[16,16,768]{2,1,0:T(8,128)(2,1)} %broadcast_in_dim.6), calls=%async_computation | async-start | bytes 786432 | tf_op jit(solution)/shard_map/all_to_all | solution.py:72
  31.6 0.0 collective-permute-done.1
  31.6 2.9 %maximum_select_fusion = bf16[1536,768]{1,0:T(8,128)(2,1)S(1)} fusion(bf16[1536,384]{1,0:T(8,128)(2,1)} %collective-permute-done.1, bf16[1536,384]{1,0:T(8,128)(2,1)} %param.9, pred[]{:T(512)S(6)} %eq.15), kind=kLoop, calls=%fused_computation.5 | loop fusion | flops 10616832 | bytes 4718593 | tf_op jit(solution)/shard_map/jit(_where)/select_n | solution.py:47
  34.5 6.2 %all-to-all-done = bf16[16,16,768]{2,1,0:T(8,128)(2,1)S(1)} async-done(((bf16[16,16,768]{2,1,0:T(8,128)(2,1)}), bf16[16,16,768]{2,1,0:T(8,128)(2,1)S(1)}, u32[]{:S(2)}, u32[]{:S(2)}) %all-to-all-start) | async-done | bytes 393248 | tf_op jit(solution)/shard_map/all_to_all | solution.py:72
  40.7 0.8 fusion.2
  41.5 1.2 copy-done
  42.7 3.7 %collective-permute-start.3 = (bf16[1536,384]{1,0:T(8,128)(2,1)}, bf16[1536,384]{1,0:T(8,128)(2,1)}, u32[]{:S(2)}, u32[]{:S(2)}) collective-permute-start(bf16[1536,384]{1,0:T(8,128)(2,1)} %param.7), channel_id=1, source_target_pairs={{0,1},{1,0},{2,3},{3,2},{4,5},{5,4},{6,7},{7,6},{8,9},{9,8},{10,11... | collective-permute-start | bytes 3538952 | tf_op jit(solution)/shard_map/ppermute | solution.py:42
  46.5 3.1 %collective-permute-start.2 = (bf16[2,1,64,1536]{3,2,1,0:T(8,128)(2,1)S(1)}, bf16[2,1,64,1536]{3,2,1,0:T(8,128)(2,1)}, u32[]{:S(2)}, u32[]{:S(2)}) collective-permute-start(bf16[2,1,64,1536]{3,2,1,0:T(8,128)(2,1)S(1)} %dynamic-slice_convert_fusion), channel_id=1, source_target_pairs={{0,64},{64,0},{1,65},{65,1},{2,66},{66,2},{3,67},{67,3},{4,68},{68... | collective-permute-start | bytes 1179656 | tf_op jit(solution)/shard_map/ppermute | solution.py:42
  49.6 0.8 slice.33
  50.4 1.0 broadcast_in_dim.7
  51.3 3.6 %all-to-all-start.1 = ((bf16[16,16,1536]{2,1,0:T(8,128)(2,1)}), bf16[16,16,1536]{2,1,0:T(8,128)(2,1)S(1)}, u32[]{:S(2)}, u32[]{:S(2)}) async-start(bf16[16,16,1536]{2,1,0:T(8,128)(2,1)} %broadcast_in_dim.7), calls=%async_computation.1 | async-start | bytes 1572864 | tf_op jit(solution)/shard_map/all_to_all | solution.py:72
  55.0 4.2 %collective-permute-done.2 = bf16[2,1,64,1536]{3,2,1,0:T(8,128)(2,1)} collective-permute-done((bf16[2,1,64,1536]{3,2,1,0:T(8,128)(2,1)S(1)}, bf16[2,1,64,1536]{3,2,1,0:T(8,128)(2,1)}, u32[]{:S(2)}, u32[]{:S(2)}) %collective-permute-start.2) | collective-permute-done | bytes 393248 | tf_op jit(solution)/shard_map/ppermute | solution.py:42
  59.2 1.1 convert_add_fusion
  60.3 3.6 %collective-permute-start.6 = (bf16[1,1,64,1536]{3,2,1,0:T(8,128)(2,1)S(1)}, bf16[1,1,64,1536]{3,2,1,0:T(8,128)(2,1)S(1)}, u32[]{:S(2)}, u32[]{:S(2)}) collective-permute-start(bf16[1,1,64,1536]{3,2,1,0:T(8,128)(2,1)S(1)} %dynamic-slice_convert_fusion.1), channel_id=1, source_target_pairs={{0,128},{128,0},{1,129},{129,1},{2,130},{130,2},{3,131},{131,3},{4... | collective-permute-start | bytes 589832 | tf_op jit(solution)/shard_map/ppermute | solution.py:42
  63.9 0.0 collective-permute-done.3
  63.9 4.2 %maximum_select_fusion.1 = bf16[1536,768]{1,0:T(8,128)(2,1)} fusion(bf16[1536,384]{1,0:T(8,128)(2,1)} %collective-permute-done.3, bf16[1536,384]{1,0:T(8,128)(2,1)} %param.7, pred[]{:T(512)S(6)} %eq.15), kind=kLoop, calls=%fused_computation.6 | loop fusion | flops 10616832 | bytes 4718593 | tf_op jit(solution)/shard_map/jit(_where)/select_n | solution.py:47
  68.1 3.2 %convolution_convert_fusion.1 = bf16[256,768]{1,0:T(8,128)(2,1)} fusion(bf16[256,1536]{1,0:T(8,128)(2,1)S(1)} %bitcast.40, bf16[1536,768]{1,0:T(8,128)(2,1)} %maximum_select_fusion.1), kind=kOutput, calls=%fused_computation.10 | convolution fusion | flops 604176384 | bytes 3538944 | tf_op jit(solution)/shard_map/dot_general | solution.py:26
  71.3 1.9 %collective-permute-done.6 = bf16[1,1,64,1536]{3,2,1,0:T(8,128)(2,1)S(1)} collective-permute-done((bf16[1,1,64,1536]{3,2,1,0:T(8,128)(2,1)S(1)}, bf16[1,1,64,1536]{3,2,1,0:T(8,128)(2,1)S(1)}, u32[]{:S(2)}, u32[]{:S(2)}) %collective-permute-start.6) | collective-permute-done | bytes 196640 | tf_op jit(solution)/shard_map/ppermute | solution.py:42
  73.2 3.5 %all-to-all-start.2 = ((bf16[4,64,768]{2,1,0:T(8,128)(2,1)}), bf16[4,64,768]{2,1,0:T(8,128)(2,1)S(1)}, u32[]{:S(2)}, u32[]{:S(2)}) async-start(bf16[4,64,768]{2,1,0:T(8,128)(2,1)} %bitcast.5), calls=%async_computation.2 | async-start | bytes 786432 | tf_op jit(solution)/shard_map/all_to_all | solution.py:78
  76.7 3.4 %collective-permute-start.4 = (bf16[256,1536]{1,0:T(8,128)(2,1)S(1)}, bf16[256,1536]{1,0:T(8,128)(2,1)S(1)}, u32[]{:S(2)}, u32[]{:S(2)}) collective-permute-start(bf16[256,1536]{1,0:T(8,128)(2,1)S(1)} %bitcast.41), channel_id=1, source_target_pairs={{0,1},{1,0},{2,3},{3,2},{4,5},{5,4},{6,7},{7,6},{8,9},{9,8},{10,11... | collective-permute-start | bytes 2359304 | tf_op jit(solution)/shard_map/ppermute | solution.py:42
  80.1 9.4 %collective-permute-start.7 = (bf16[64,768]{1,0:T(8,128)(2,1)S(1)}, bf16[64,768]{1,0:T(8,128)(2,1)S(1)}, u32[]{:S(2)}, u32[]{:S(2)}) collective-permute-start(bf16[64,768]{1,0:T(8,128)(2,1)S(1)} %fusion.18), channel_id=1, source_target_pairs={{0,258},{2,256},{256,2},{258,0},{1,259},{3,257},{257,3},{259,1},{4... | collective-permute-start | bytes 294920 | tf_op jit(solution)/shard_map/ppermute | solution.py:66
  89.6 2.2 %collective-permute-start.5 = (bf16[256,384]{1,0:T(8,128)(2,1)S(1)}, bf16[256,384]{1,0:T(8,128)(2,1)S(1)}, u32[]{:S(2)}, u32[]{:S(2)}) collective-permute-start(bf16[256,384]{1,0:T(8,128)(2,1)S(1)} %constant_dynamic-slice_fusion.1), channel_id=1, source_target_pairs={{0,1},{1,0},{2,3},{3,2},{4,5},{5,4},{6,7},{7,6},{8,9},{9,8},{10,11... | collective-permute-start | bytes 589832 | tf_op jit(solution)/shard_map/ppermute | solution.py:42
  91.8 1.4 collective-permute-done.7
  93.2 0.1 fusion.17
  93.3 0.0 collective-permute-done.5
  93.3 6.0 %collective-permute-start.8 = (bf16[64,1536]{1,0:T(8,128)(2,1)S(1)}, bf16[64,1536]{1,0:T(8,128)(2,1)S(1)}, u32[]{:S(2)}, u32[]{:S(2)}) collective-permute-start(bf16[64,1536]{1,0:T(8,128)(2,1)S(1)} %pad_maximum_fusion), channel_id=1, source_target_pairs={{0,256},{256,0},{1,257},{257,1},{2,258},{258,2},{3,259},{259,3},{4... | collective-permute-start | bytes 589832 | tf_op jit(solution)/shard_map/ppermute | solution.py:42
  99.3 0.1 dynamic_slice.57
  99.4 4.2 %collective-permute-done.8 = bf16[64,1536]{1,0:T(8,128)(2,1)S(1)} collective-permute-done((bf16[64,1536]{1,0:T(8,128)(2,1)S(1)}, bf16[64,1536]{1,0:T(8,128)(2,1)S(1)}, u32[]{:S(2)}, u32[]{:S(2)}) %collective-permute-start.8) | collective-permute-done | bytes 196640 | tf_op jit(solution)/shard_map/ppermute | solution.py:42
  103.7 0.2 multiply_convert_fusion
  103.8 0.8 broadcast_in_dim.8
  104.6 17.2 %all-to-all-start.3 = ((bf16[4,64,768]{2,1,0:T(8,128)(2,1)}), bf16[4,64,768]{2,1,0:T(8,128)(2,1)S(1)}, u32[]{:S(2)}, u32[]{:S(2)}) async-start(bf16[4,64,768]{2,1,0:T(8,128)(2,1)} %broadcast_in_dim.8), calls=%async_computation.3 | async-start | bytes 786432 | tf_op jit(solution)/shard_map/all_to_all | solution.py:72
  121.8 11.5 %collective-permute-start.10 = (bf16[64,768]{1,0:T(8,128)(2,1)S(1)}, bf16[64,768]{1,0:T(8,128)(2,1)S(1)}, u32[]{:S(2)}, u32[]{:S(2)}) collective-permute-start(bf16[64,768]{1,0:T(8,128)(2,1)S(1)} %get-tuple-element.34), channel_id=1, source_target_pairs={{0,258},{2,256},{256,2},{258,0},{1,259},{3,257},{257,3},{259,1},{4... | collective-permute-start | bytes 294920 | tf_op jit(solution)/shard_map/ppermute | solution.py:66
  133.3 7.1 %collective-permute-done.10 = bf16[64,768]{1,0:T(8,128)(2,1)S(1)} collective-permute-done((bf16[64,768]{1,0:T(8,128)(2,1)S(1)}, bf16[64,768]{1,0:T(8,128)(2,1)S(1)}, u32[]{:S(2)}, u32[]{:S(2)}) %collective-permute-start.10) | collective-permute-done | bytes 98336 | tf_op jit(solution)/shard_map/ppermute | solution.py:66
  140.4 0.7 maximum_select_fusion.5
  141.2 3.1 %collective-permute-start.11 = (bf16[1,1,64,1536]{3,2,1,0:T(8,128)(2,1)}, bf16[1,1,64,1536]{3,2,1,0:T(8,128)(2,1)}, u32[]{:S(2)}, u32[]{:S(2)}) collective-permute-start(bf16[1,1,64,1536]{3,2,1,0:T(8,128)(2,1)} %maximum_select_fusion.5), channel_id=1, source_target_pairs={{0,128},{128,0},{1,129},{129,1},{2,130},{130,2},{3,131},{131,3},{4... | collective-permute-start | bytes 589832 | tf_op jit(solution)/shard_map/ppermute | solution.py:42
  144.3 3.4 %convolution_convert_fusion = bf16[256,1536]{1,0:T(8,128)(2,1)} fusion(bf16[256,768]{1,0:T(8,128)(2,1)S(1)} %bitcast.45, bf16[1536,768]{1,0:T(8,128)(2,1)} %maximum_select_fusion.1), kind=kOutput, calls=%fused_computation.4 | convolution fusion | flops 604372992 | bytes 3538944 | tf_op jit(solution)/shard_map/dot_general | solution.py:30
  147.7 3.6 %all-to-all-start.4 = ((bf16[16,16,1536]{2,1,0:T(8,128)(2,1)}), bf16[16,16,1536]{2,1,0:T(8,128)(2,1)S(1)}, u32[]{:S(2)}, u32[]{:S(2)}) async-start(bf16[16,16,1536]{2,1,0:T(8,128)(2,1)} %bitcast.10), calls=%async_computation.4 | async-start | bytes 1572864 | tf_op jit(solution)/shard_map/all_to_all | solution.py:127
  151.3 0.6 fusion.15
  152.0 0.0 collective-permute-done.11
  152.0 5.8 %collective-permute-start.9 = (bf16[256,384]{1,0:T(8,128)(2,1)S(1)}, bf16[256,384]{1,0:T(8,128)(2,1)S(1)}, u32[]{:S(2)}, u32[]{:S(2)}) collective-permute-start(bf16[256,384]{1,0:T(8,128)(2,1)S(1)} %constant_dynamic-slice_fusion), channel_id=1, source_target_pairs={{0,1},{1,0},{2,3},{3,2},{4,5},{5,4},{6,7},{7,6},{8,9},{9,8},{10,11... | collective-permute-start | bytes 589832 | tf_op jit(solution)/shard_map/ppermute | solution.py:42
  157.8 1.1 maximum_select_fusion.3
  158.8 3.9 %collective-permute-start.12 = (bf16[2,1,64,1536]{3,2,1,0:T(8,128)(2,1)S(1)}, bf16[2,1,64,1536]{3,2,1,0:T(8,128)(2,1)}, u32[]{:S(2)}, u32[]{:S(2)}) collective-permute-start(bf16[2,1,64,1536]{3,2,1,0:T(8,128)(2,1)S(1)} %maximum_select_fusion.3), channel_id=1, source_target_pairs={{0,64},{64,0},{1,65},{65,1},{2,66},{66,2},{3,67},{67,3},{4,68},{68... | collective-permute-start | bytes 1179656 | tf_op jit(solution)/shard_map/ppermute | solution.py:42
  162.7 0.1 convert_reduce_fusion.2
  162.8 0.1 convert_reduce_fusion.1
  162.8 0.6 add.119
  163.4 1.6 fusion
  165.1 0.0 all-to-all-done.4
  165.1 0.1 convert_reduce_fusion
  165.2 7.1 %collective-permute-done.12 = bf16[2,1,64,1536]{3,2,1,0:T(8,128)(2,1)} collective-permute-done((bf16[2,1,64,1536]{3,2,1,0:T(8,128)(2,1)S(1)}, bf16[2,1,64,1536]{3,2,1,0:T(8,128)(2,1)}, u32[]{:S(2)}, u32[]{:S(2)}) %collective-permute-start.12) | collective-permute-done | bytes 393248 | tf_op jit(solution)/shard_map/ppermute | solution.py:42
  172.3 1.2 maximum_select_fusion.2
  173.5 2.5 %collective-permute-start.13 = (bf16[256,1536]{1,0:T(8,128)(2,1)S(1)}, bf16[256,1536]{1,0:T(8,128)(2,1)S(1)}, u32[]{:S(2)}, u32[]{:S(2)}) collective-permute-start(bf16[256,1536]{1,0:T(8,128)(2,1)S(1)} %bitcast.43), channel_id=1, source_target_pairs={{0,1},{1,0},{2,3},{3,2},{4,5},{5,4},{6,7},{7,6},{8,9},{9,8},{10,11... | collective-permute-start | bytes 2359304 | tf_op jit(solution)/shard_map/ppermute | solution.py:42
  176.0 9.6 %collective-permute-start.14 = (bf16[8,1536]{1,0:T(8,128)(2,1)S(1)}, bf16[8,1536]{1,0:T(8,128)(2,1)S(1)}, u32[]{:S(2)}, u32[]{:S(2)}) collective-permute-start(bf16[8,1536]{1,0:T(8,128)(2,1)S(1)} %dynamic-slice_convert_fusion.3), channel_id=1, source_target_pairs={{0,2},{2,0},{1,3},{3,1},{4,6},{6,4},{5,7},{7,5},{8,10},{10,8},{9,1... | collective-permute-start | bytes 73736 | tf_op jit(solution)/shard_map/ppermute | solution.py:42
  185.6 0.6 fusion.13
  186.2 1.6 fusion.1
  187.9 1.5 collective-permute-done.14
  189.4 0.6 add_convert_fusion.1
  (24 shorter events, 0.4 us)
Async XLA Ops:
  2.1 17.7 %collective-permute-start = (bf16[8,2304]{1,0:T(8,128)(2,1)S(1)}, bf16[8,2304]{1,0:T(8,128)(2,1)S(1)}, u32[]{:S(2)}, u32[]{:S(2)}) collective-permute-start(bf16[8,2304]{1,0:T(8,128)(2,1)S(1)} %pad_maximum_fusion.1), channel_id=1, source_target_pairs={{0,2},{2,0},{1,3},{3,1},{4,6},{6,4},{5,7},{7,5},{8,10},{10,8},{9,1... | collective-permute-start | bytes 110600 | tf_op jit(solution)/shard_map/ppermute | solution.py:42
  20.7 6.4 %copy-start.2 = (bf16[16,2304]{1,0:T(8,128)(2,1)}, bf16[16,2304]{1,0:T(8,128)(2,1)S(1)}, u32[]{:S(2)}) copy-start(bf16[16,2304]{1,0:T(8,128)(2,1)S(1)} %maximum_select_fusion.6) | copy-start | bytes 221188
  20.7 10.9 %collective-permute-start.1 = (bf16[1536,384]{1,0:T(8,128)(2,1)}, bf16[1536,384]{1,0:T(8,128)(2,1)}, u32[]{:S(2)}, u32[]{:S(2)}) collective-permute-start(bf16[1536,384]{1,0:T(8,128)(2,1)} %param.9), channel_id=1, source_target_pairs={{0,1},{1,0},{2,3},{3,2},{4,5},{5,4},{6,7},{7,6},{8,9},{9,8},{10,11... | collective-permute-start | bytes 3538952 | tf_op jit(solution)/shard_map/ppermute | solution.py:42
  27.1 13.6 %all-to-all-start = ((bf16[16,16,768]{2,1,0:T(8,128)(2,1)}), bf16[16,16,768]{2,1,0:T(8,128)(2,1)S(1)}, u32[]{:S(2)}, u32[]{:S(2)}) async-start(bf16[16,16,768]{2,1,0:T(8,128)(2,1)} %broadcast_in_dim.6), calls=%async_computation | async-start | bytes 786432 | tf_op jit(solution)/shard_map/all_to_all | solution.py:72
  41.5 1.2 copy-start
  42.7 16.5 %copy-start.1 = (f32[2,2,64,1536]{3,2,1,0:T(8,128)S(1)}, f32[2,2,64,1536]{3,2,1,0:T(8,128)}, u32[]{:S(2)}) copy-start(f32[2,2,64,1536]{3,2,1,0:T(8,128)} %copy-done) | copy-start | bytes 4718596
  42.7 21.2 %collective-permute-start.3 = (bf16[1536,384]{1,0:T(8,128)(2,1)}, bf16[1536,384]{1,0:T(8,128)(2,1)}, u32[]{:S(2)}, u32[]{:S(2)}) collective-permute-start(bf16[1536,384]{1,0:T(8,128)(2,1)} %param.7), channel_id=1, source_target_pairs={{0,1},{1,0},{2,3},{3,2},{4,5},{5,4},{6,7},{7,6},{8,9},{9,8},{10,11... | collective-permute-start | bytes 3538952 | tf_op jit(solution)/shard_map/ppermute | solution.py:42
  46.5 12.7 %collective-permute-start.2 = (bf16[2,1,64,1536]{3,2,1,0:T(8,128)(2,1)S(1)}, bf16[2,1,64,1536]{3,2,1,0:T(8,128)(2,1)}, u32[]{:S(2)}, u32[]{:S(2)}) collective-permute-start(bf16[2,1,64,1536]{3,2,1,0:T(8,128)(2,1)S(1)} %dynamic-slice_convert_fusion), channel_id=1, source_target_pairs={{0,64},{64,0},{1,65},{65,1},{2,66},{66,2},{3,67},{67,3},{4,68},{68... | collective-permute-start | bytes 1179656 | tf_op jit(solution)/shard_map/ppermute | solution.py:42
  51.3 16.8 %all-to-all-start.1 = ((bf16[16,16,1536]{2,1,0:T(8,128)(2,1)}), bf16[16,16,1536]{2,1,0:T(8,128)(2,1)S(1)}, u32[]{:S(2)}, u32[]{:S(2)}) async-start(bf16[16,16,1536]{2,1,0:T(8,128)(2,1)} %broadcast_in_dim.7), calls=%async_computation.1 | async-start | bytes 1572864 | tf_op jit(solution)/shard_map/all_to_all | solution.py:72
  60.3 12.9 %collective-permute-start.6 = (bf16[1,1,64,1536]{3,2,1,0:T(8,128)(2,1)S(1)}, bf16[1,1,64,1536]{3,2,1,0:T(8,128)(2,1)S(1)}, u32[]{:S(2)}, u32[]{:S(2)}) collective-permute-start(bf16[1,1,64,1536]{3,2,1,0:T(8,128)(2,1)S(1)} %dynamic-slice_convert_fusion.1), channel_id=1, source_target_pairs={{0,128},{128,0},{1,129},{129,1},{2,130},{130,2},{3,131},{131,3},{4... | collective-permute-start | bytes 589832 | tf_op jit(solution)/shard_map/ppermute | solution.py:42
  71.3 28.0 %copy-start.3 = (f32[1536]{0:T(1024)S(1)}, f32[1536]{0:T(1024)}, u32[]{:S(2)}) copy-start(f32[1536]{0:T(1024)} %param.8) | copy-start | bytes 18436
  73.2 20.0 %all-to-all-start.2 = ((bf16[4,64,768]{2,1,0:T(8,128)(2,1)}), bf16[4,64,768]{2,1,0:T(8,128)(2,1)S(1)}, u32[]{:S(2)}, u32[]{:S(2)}) async-start(bf16[4,64,768]{2,1,0:T(8,128)(2,1)} %bitcast.5), calls=%async_computation.2 | async-start | bytes 786432 | tf_op jit(solution)/shard_map/all_to_all | solution.py:78
  76.7 16.6 %collective-permute-start.4 = (bf16[256,1536]{1,0:T(8,128)(2,1)S(1)}, bf16[256,1536]{1,0:T(8,128)(2,1)S(1)}, u32[]{:S(2)}, u32[]{:S(2)}) collective-permute-start(bf16[256,1536]{1,0:T(8,128)(2,1)S(1)} %bitcast.41), channel_id=1, source_target_pairs={{0,1},{1,0},{2,3},{3,2},{4,5},{5,4},{6,7},{7,6},{8,9},{9,8},{10,11... | collective-permute-start | bytes 2359304 | tf_op jit(solution)/shard_map/ppermute | solution.py:42
  80.1 13.1 %collective-permute-start.7 = (bf16[64,768]{1,0:T(8,128)(2,1)S(1)}, bf16[64,768]{1,0:T(8,128)(2,1)S(1)}, u32[]{:S(2)}, u32[]{:S(2)}) collective-permute-start(bf16[64,768]{1,0:T(8,128)(2,1)S(1)} %fusion.18), channel_id=1, source_target_pairs={{0,258},{2,256},{256,2},{258,0},{1,259},{3,257},{257,3},{259,1},{4... | collective-permute-start | bytes 294920 | tf_op jit(solution)/shard_map/ppermute | solution.py:66
  89.6 3.7 %collective-permute-start.5 = (bf16[256,384]{1,0:T(8,128)(2,1)S(1)}, bf16[256,384]{1,0:T(8,128)(2,1)S(1)}, u32[]{:S(2)}, u32[]{:S(2)}) collective-permute-start(bf16[256,384]{1,0:T(8,128)(2,1)S(1)} %constant_dynamic-slice_fusion.1), channel_id=1, source_target_pairs={{0,1},{1,0},{2,3},{3,2},{4,5},{5,4},{6,7},{7,6},{8,9},{9,8},{10,11... | collective-permute-start | bytes 589832 | tf_op jit(solution)/shard_map/ppermute | solution.py:42
  93.3 10.3 %collective-permute-start.8 = (bf16[64,1536]{1,0:T(8,128)(2,1)S(1)}, bf16[64,1536]{1,0:T(8,128)(2,1)S(1)}, u32[]{:S(2)}, u32[]{:S(2)}) collective-permute-start(bf16[64,1536]{1,0:T(8,128)(2,1)S(1)} %pad_maximum_fusion), channel_id=1, source_target_pairs={{0,256},{256,0},{1,257},{257,1},{2,258},{258,2},{3,259},{259,3},{4... | collective-permute-start | bytes 589832 | tf_op jit(solution)/shard_map/ppermute | solution.py:42
  104.6 39.7 %all-to-all-start.3 = ((bf16[4,64,768]{2,1,0:T(8,128)(2,1)}), bf16[4,64,768]{2,1,0:T(8,128)(2,1)S(1)}, u32[]{:S(2)}, u32[]{:S(2)}) async-start(bf16[4,64,768]{2,1,0:T(8,128)(2,1)} %broadcast_in_dim.8), calls=%async_computation.3 | async-start | bytes 786432 | tf_op jit(solution)/shard_map/all_to_all | solution.py:72
  121.8 18.7 %collective-permute-start.10 = (bf16[64,768]{1,0:T(8,128)(2,1)S(1)}, bf16[64,768]{1,0:T(8,128)(2,1)S(1)}, u32[]{:S(2)}, u32[]{:S(2)}) collective-permute-start(bf16[64,768]{1,0:T(8,128)(2,1)S(1)} %get-tuple-element.34), channel_id=1, source_target_pairs={{0,258},{2,256},{256,2},{258,0},{1,259},{3,257},{257,3},{259,1},{4... | collective-permute-start | bytes 294920 | tf_op jit(solution)/shard_map/ppermute | solution.py:66
  141.2 10.8 %collective-permute-start.11 = (bf16[1,1,64,1536]{3,2,1,0:T(8,128)(2,1)}, bf16[1,1,64,1536]{3,2,1,0:T(8,128)(2,1)}, u32[]{:S(2)}, u32[]{:S(2)}) collective-permute-start(bf16[1,1,64,1536]{3,2,1,0:T(8,128)(2,1)} %maximum_select_fusion.5), channel_id=1, source_target_pairs={{0,128},{128,0},{1,129},{129,1},{2,130},{130,2},{3,131},{131,3},{4... | collective-permute-start | bytes 589832 | tf_op jit(solution)/shard_map/ppermute | solution.py:42
  147.7 17.4 %all-to-all-start.4 = ((bf16[16,16,1536]{2,1,0:T(8,128)(2,1)}), bf16[16,16,1536]{2,1,0:T(8,128)(2,1)S(1)}, u32[]{:S(2)}, u32[]{:S(2)}) async-start(bf16[16,16,1536]{2,1,0:T(8,128)(2,1)} %bitcast.10), calls=%async_computation.4 | async-start | bytes 1572864 | tf_op jit(solution)/shard_map/all_to_all | solution.py:127
  152.0 10.8 %collective-permute-start.9 = (bf16[256,384]{1,0:T(8,128)(2,1)S(1)}, bf16[256,384]{1,0:T(8,128)(2,1)S(1)}, u32[]{:S(2)}, u32[]{:S(2)}) collective-permute-start(bf16[256,384]{1,0:T(8,128)(2,1)S(1)} %constant_dynamic-slice_fusion), channel_id=1, source_target_pairs={{0,1},{1,0},{2,3},{3,2},{4,5},{5,4},{6,7},{7,6},{8,9},{9,8},{10,11... | collective-permute-start | bytes 589832 | tf_op jit(solution)/shard_map/ppermute | solution.py:42
  158.8 13.4 %collective-permute-start.12 = (bf16[2,1,64,1536]{3,2,1,0:T(8,128)(2,1)S(1)}, bf16[2,1,64,1536]{3,2,1,0:T(8,128)(2,1)}, u32[]{:S(2)}, u32[]{:S(2)}) collective-permute-start(bf16[2,1,64,1536]{3,2,1,0:T(8,128)(2,1)S(1)} %maximum_select_fusion.3), channel_id=1, source_target_pairs={{0,64},{64,0},{1,65},{65,1},{2,66},{66,2},{3,67},{67,3},{4,68},{68... | collective-permute-start | bytes 1179656 | tf_op jit(solution)/shard_map/ppermute | solution.py:42
  173.5 12.7 %collective-permute-start.13 = (bf16[256,1536]{1,0:T(8,128)(2,1)S(1)}, bf16[256,1536]{1,0:T(8,128)(2,1)S(1)}, u32[]{:S(2)}, u32[]{:S(2)}) collective-permute-start(bf16[256,1536]{1,0:T(8,128)(2,1)S(1)} %bitcast.43), channel_id=1, source_target_pairs={{0,1},{1,0},{2,3},{3,2},{4,5},{5,4},{6,7},{7,6},{8,9},{9,8},{10,11... | collective-permute-start | bytes 2359304 | tf_op jit(solution)/shard_map/ppermute | solution.py:42
  176.0 13.4 %collective-permute-start.14 = (bf16[8,1536]{1,0:T(8,128)(2,1)S(1)}, bf16[8,1536]{1,0:T(8,128)(2,1)S(1)}, u32[]{:S(2)}, u32[]{:S(2)}) collective-permute-start(bf16[8,1536]{1,0:T(8,128)(2,1)S(1)} %dynamic-slice_convert_fusion.3), channel_id=1, source_target_pairs={{0,2},{2,0},{1,3},{3,1},{4,6},{6,4},{5,7},{7,5},{8,10},{10,8},{9,1... | collective-permute-start | bytes 73736 | tf_op jit(solution)/shard_map/ppermute | solution.py:42

commit v12 on v8

--- a/solution.py
+++ b/solution.py
@@ -131,18 +131,32 @@
     act = join(act, swap(act, "rm"), "rm", 0)
     own_part = over_rows(every_x, own_grad)
     pair_grad = swap(after(act, part_of(grad, 1 - core, quarter, 1)), "core")
-    act = join(act, swap(act, "rl"), "rl", 1).reshape(-1, act.shape[-1])
+    rest = swap(act, "rl")
+    pair_act = swap(act, "core")
     w_in_grad = (own_part + over_rows(pair_x, pair_grad)).astype(bf16)
     b_in_grad = jnp.sum(own_grad.astype(f32), 0) + jnp.sum(pair_grad.astype(f32), 0)
 
     summed = jnp.sum(after((w_in_grad, b_in_grad), dealt).astype(f32), axis=0)
     out_rows = part_of(summed, 1 - zh, tok_dev, 0).astype(bf16)
     own_rows = part_of(summed, zh, tok_dev, 0)
+    got_rows = swap(out_rows, "zh")
+    input_grad = (own_rows + got_rows.astype(f32)).astype(bf16)
+
+    rl = lax.axis_index("rl")
+
+    def rows_of(value, at):
+        value = value.reshape(2, 2, -1, value.shape[-1])
+        return part_of(value, at, 1, 1).reshape(-1, value.shape[-1])
+
+    def flat(value):
+        return value.reshape(-1, value.shape[-1])
+
     own_g = part_of(every_g, core, quarter_d, 1)
-    pair_act = swap(after(out_rows, act), "core")
-    w_out_grad = (over_rows(act, own_g) + over_rows(pair_act, pair_g)).astype(bf16)
-    got_rows = after(w_out_grad, swap(out_rows, "zh"))
-    input_grad = (own_rows + got_rows.astype(f32)).astype(bf16)
+    w_out_sum = over_rows(flat(act), rows_of(own_g, rl)) + over_rows(flat(pair_act), rows_of(pair_g, rl))
+    rest = flat(after(got_rows, rest))
+    pair_rest = swap(rest, "core")
+    w_out_sum = w_out_sum + over_rows(rest, rows_of(own_g, 1 - rl))
+    w_out_grad = (w_out_sum + over_rows(pair_rest, rows_of(pair_g, 1 - rl))).astype(bf16)
     return (input_grad, w_in_grad, b_in_grad, w_out_grad)
 
 

time: 192 us -> 198 us (1.031)
  waiting for transfers between devices: 34.1 us -> 29 us
  starting transfers between devices: 126 us -> 131 us
  other arithmetic: 11.7 us -> 16 us
    ppermute x13 -> x14, waiting for transfers between devices: 23.5 us -> 18.7 us  [swap(): return lax.ppermute(value, axis, SWAP)]
    ppermute x13 -> x14, starting transfers between devices: 72.9 us -> 76.2 us  [swap(): return lax.ppermute(value, axis, SWAP)]
    dot_general x4 -> x6, matrix products: 4.5 us -> 6.37 us  [over_rows(): lax.dot_general(left, right, (((0,), (0,)), ((), ())), preferred_element_...]
  transfers between devices with their start and end apart: 20 -> 21, of which waited for: 9 -> 9; matrix products, arithmetic and copies ran while one was open for 12% -> 14% of each run, Pallas kernels for 0% -> 0%
where the time goes in v12:
time: 198 us; the launch traced here: 196 us
  starting transfers between devices  131 us (66%)
  waiting for transfers between devices  29 us (15%)
  other arithmetic  16 us (8%)
  matrix products  12 us (6%)
  local copies, waits for them, and re-layouts  7.39 us (4%)
    ppermute x14, starting transfers between devices, swap(): return lax.ppermute(value, axis, SWAP)  76.2 us
    all_to_all x3, starting transfers between devices, spread(): got = lax.all_to_all(sent, axes, 0, 0, tiled=True)  25.8 us
    ppermute x2, starting transfers between devices, cross(): return lax.ppermute(value, ('rh', 'zh'), CROSS)  21 us
    ppermute x14, waiting for transfers between devices, swap(): return lax.ppermute(value, axis, SWAP)  18.7 us
    select_n x6, other arithmetic, join(): jnp.where(first, jnp.concatenate([mine, other], dim), jnp.concatenate([ot...  9.9 us
    dot_general x6, matrix products, over_rows(): lax.dot_general(left, right, (((0,), (0,)), ((), ())), preferred_element_...  6.37 us
    all_to_all x3, waiting for transfers between devices, spread(): got = lax.all_to_all(sent, axes, 0, 0, tiled=True)  6.17 us
    all_to_all x1, starting transfers between devices, deal(): lax.all_to_all(part.reshape(n, -1, part.shape[1]), axes, 0, 0, tiled=True)  4.11 us
  transfers between devices with their start and end apart: 21, of which 9 were waited for; matrix products, arithmetic and copies ran while one was open for 14% of the time, Pallas kernels for 0%

profile of v12, /device:TPU:1, one launch (start us, length us, event | category | flops | bytes accessed | tf_op | source)
XLA Modules:
  0.0 196.4 jit_solution(18382961510197091305)
XLA Ops:
  0.6 0.7 constant_dynamic-slice_fusion.5
  1.4 0.7 pad_maximum_fusion.1
  2.1 16.3 %collective-permute-start = (bf16[8,2304]{1,0:T(8,128)(2,1)S(1)}, bf16[8,2304]{1,0:T(8,128)(2,1)S(1)}, u32[]{:S(2)}, u32[]{:S(2)}) collective-permute-start(bf16[8,2304]{1,0:T(8,128)(2,1)S(1)} %pad_maximum_fusion.1), channel_id=1, source_target_pairs={{0,2},{2,0},{1,3},{3,1},{4,6},{6,4},{5,7},{7,5},{8,10},{10,8},{9,1... | collective-permute-start | bytes 110600 | tf_op jit(solution)/shard_map/ppermute | solution.py:42
  18.4 1.5 collective-permute-done
  19.9 0.8 maximum_select_fusion.7
  20.7 5.6 %collective-permute-start.1 = (bf16[1536,384]{1,0:T(8,128)(2,1)}, bf16[1536,384]{1,0:T(8,128)(2,1)}, u32[]{:S(2)}, u32[]{:S(2)}) collective-permute-start(bf16[1536,384]{1,0:T(8,128)(2,1)} %param.9), channel_id=1, source_target_pairs={{0,1},{1,0},{2,3},{3,2},{4,5},{5,4},{6,7},{7,6},{8,9},{9,8},{10,11... | collective-permute-start | bytes 3538952 | tf_op jit(solution)/shard_map/ppermute | solution.py:42
  26.3 0.8 broadcast_in_dim.6
  27.1 4.5 %all-to-all-start = ((bf16[16,16,768]{2,1,0:T(8,128)(2,1)}), bf16[16,16,768]{2,1,0:T(8,128)(2,1)S(1)}, u32[]{:S(2)}, u32[]{:S(2)}) async-start(bf16[16,16,768]{2,1,0:T(8,128)(2,1)} %broadcast_in_dim.6), calls=%async_computation | async-start | bytes 786432 | tf_op jit(solution)/shard_map/all_to_all | solution.py:72
  31.6 2.9 %maximum_select_fusion = bf16[1536,768]{1,0:T(8,128)(2,1)S(1)} fusion(bf16[1536,384]{1,0:T(8,128)(2,1)} %collective-permute-done.1, bf16[1536,384]{1,0:T(8,128)(2,1)} %param.9, pred[]{:T(512)S(6)} %eq.12), kind=kLoop, calls=%fused_computation.10 | loop fusion | flops 10616832 | bytes 4718593 | tf_op jit(solution)/shard_map/jit(_where)/select_n | solution.py:47
  34.5 6.2 %all-to-all-done = bf16[16,16,768]{2,1,0:T(8,128)(2,1)S(1)} async-done(((bf16[16,16,768]{2,1,0:T(8,128)(2,1)}), bf16[16,16,768]{2,1,0:T(8,128)(2,1)S(1)}, u32[]{:S(2)}, u32[]{:S(2)}) %all-to-all-start) | async-done | bytes 393248 | tf_op jit(solution)/shard_map/all_to_all | solution.py:72
  40.7 0.8 fusion.4
  41.5 1.2 copy-done
  42.8 3.7 %collective-permute-start.3 = (bf16[1536,384]{1,0:T(8,128)(2,1)}, bf16[1536,384]{1,0:T(8,128)(2,1)}, u32[]{:S(2)}, u32[]{:S(2)}) collective-permute-start(bf16[1536,384]{1,0:T(8,128)(2,1)} %param.7), channel_id=1, source_target_pairs={{0,1},{1,0},{2,3},{3,2},{4,5},{5,4},{6,7},{7,6},{8,9},{9,8},{10,11... | collective-permute-start | bytes 3538952 | tf_op jit(solution)/shard_map/ppermute | solution.py:42
  46.5 3.1 %collective-permute-start.2 = (bf16[2,1,64,1536]{3,2,1,0:T(8,128)(2,1)S(1)}, bf16[2,1,64,1536]{3,2,1,0:T(8,128)(2,1)}, u32[]{:S(2)}, u32[]{:S(2)}) collective-permute-start(bf16[2,1,64,1536]{3,2,1,0:T(8,128)(2,1)S(1)} %dynamic-slice_convert_fusion), channel_id=1, source_target_pairs={{0,64},{64,0},{1,65},{65,1},{2,66},{66,2},{3,67},{67,3},{4,68},{68... | collective-permute-start | bytes 1179656 | tf_op jit(solution)/shard_map/ppermute | solution.py:42
  49.6 1.0 broadcast_in_dim.7
  50.6 3.6 %all-to-all-start.1 = ((bf16[16,16,1536]{2,1,0:T(8,128)(2,1)}), bf16[16,16,1536]{2,1,0:T(8,128)(2,1)S(1)}, u32[]{:S(2)}, u32[]{:S(2)}) async-start(bf16[16,16,1536]{2,1,0:T(8,128)(2,1)} %broadcast_in_dim.7), calls=%async_computation.1 | async-start | bytes 1572864 | tf_op jit(solution)/shard_map/all_to_all | solution.py:72
  54.2 5.0 %collective-permute-done.2 = bf16[2,1,64,1536]{3,2,1,0:T(8,128)(2,1)} collective-permute-done((bf16[2,1,64,1536]{3,2,1,0:T(8,128)(2,1)S(1)}, bf16[2,1,64,1536]{3,2,1,0:T(8,128)(2,1)}, u32[]{:S(2)}, u32[]{:S(2)}) %collective-permute-start.2) | collective-permute-done | bytes 393248 | tf_op jit(solution)/shard_map/ppermute | solution.py:42
  59.2 1.1 convert_add_fusion
  60.3 3.6 %collective-permute-start.6 = (bf16[1,1,64,1536]{3,2,1,0:T(8,128)(2,1)S(1)}, bf16[1,1,64,1536]{3,2,1,0:T(8,128)(2,1)S(1)}, u32[]{:S(2)}, u32[]{:S(2)}) collective-permute-start(bf16[1,1,64,1536]{3,2,1,0:T(8,128)(2,1)S(1)} %dynamic-slice_convert_fusion.1), channel_id=1, source_target_pairs={{0,128},{128,0},{1,129},{129,1},{2,130},{130,2},{3,131},{131,3},{4... | collective-permute-start | bytes 589832 | tf_op jit(solution)/shard_map/ppermute | solution.py:42
  64.0 4.0 %maximum_select_fusion.1 = bf16[1536,768]{1,0:T(8,128)(2,1)} fusion(bf16[1536,384]{1,0:T(8,128)(2,1)} %collective-permute-done.3, bf16[1536,384]{1,0:T(8,128)(2,1)} %param.7, pred[]{:T(512)S(6)} %eq.12), kind=kLoop, calls=%fused_computation.11 | loop fusion | flops 10616832 | bytes 4718593 | tf_op jit(solution)/shard_map/jit(_where)/select_n | solution.py:47
  68.0 3.2 %convolution_convert_fusion.1 = bf16[256,768]{1,0:T(8,128)(2,1)} fusion(bf16[256,1536]{1,0:T(8,128)(2,1)S(1)} %bitcast.66, bf16[1536,768]{1,0:T(8,128)(2,1)} %maximum_select_fusion.1), kind=kOutput, calls=%fused_computation.15 | convolution fusion | flops 604176384 | bytes 3538944 | tf_op jit(solution)/shard_map/dot_general | solution.py:26
  71.2 2.1 %collective-permute-done.6 = bf16[1,1,64,1536]{3,2,1,0:T(8,128)(2,1)S(1)} collective-permute-done((bf16[1,1,64,1536]{3,2,1,0:T(8,128)(2,1)S(1)}, bf16[1,1,64,1536]{3,2,1,0:T(8,128)(2,1)S(1)}, u32[]{:S(2)}, u32[]{:S(2)}) %collective-permute-start.6) | collective-permute-done | bytes 196640 | tf_op jit(solution)/shard_map/ppermute | solution.py:42
  73.2 4.1 %all-to-all-start.2 = ((bf16[4,64,768]{2,1,0:T(8,128)(2,1)}), bf16[4,64,768]{2,1,0:T(8,128)(2,1)}, u32[]{:S(2)}, u32[]{:S(2)}) async-start(bf16[4,64,768]{2,1,0:T(8,128)(2,1)} %bitcast.5), calls=%async_computation.2 | async-start | bytes 786432 | tf_op jit(solution)/shard_map/all_to_all | solution.py:78
  77.3 3.4 %collective-permute-start.4 = (bf16[256,1536]{1,0:T(8,128)(2,1)S(1)}, bf16[256,1536]{1,0:T(8,128)(2,1)}, u32[]{:S(2)}, u32[]{:S(2)}) collective-permute-start(bf16[256,1536]{1,0:T(8,128)(2,1)S(1)} %bitcast.67), channel_id=1, source_target_pairs={{0,1},{1,0},{2,3},{3,2},{4,5},{5,4},{6,7},{7,6},{8,9},{9,8},{10,11... | collective-permute-start | bytes 2359304 | tf_op jit(solution)/shard_map/ppermute | solution.py:42
  80.8 9.5 %collective-permute-start.7 = (bf16[64,768]{1,0:T(8,128)(2,1)S(1)}, bf16[64,768]{1,0:T(8,128)(2,1)S(1)}, u32[]{:S(2)}, u32[]{:S(2)}) collective-permute-start(bf16[64,768]{1,0:T(8,128)(2,1)S(1)} %fusion.25), channel_id=1, source_target_pairs={{0,258},{2,256},{256,2},{258,0},{1,259},{3,257},{257,3},{259,1},{4... | collective-permute-start | bytes 294920 | tf_op jit(solution)/shard_map/ppermute | solution.py:66
  90.3 0.8 constant_dynamic-slice_fusion.1
  91.1 2.2 %collective-permute-start.5 = (bf16[256,384]{1,0:T(8,128)(2,1)}, bf16[256,384]{1,0:T(8,128)(2,1)S(1)}, u32[]{:S(2)}, u32[]{:S(2)}) collective-permute-start(bf16[256,384]{1,0:T(8,128)(2,1)} %get-tuple-element.31), channel_id=1, source_target_pairs={{0,1},{1,0},{2,3},{3,2},{4,5},{5,4},{6,7},{7,6},{8,9},{9,8},{10,11... | collective-permute-start | bytes 589832 | tf_op jit(solution)/shard_map/ppermute | solution.py:42
  93.3 0.2 collective-permute-done.7
  93.5 0.0 all-to-all-done.2
  93.5 1.1 fusion.24
  94.7 6.5 %collective-permute-start.8 = (bf16[64,1536]{1,0:T(8,128)(2,1)S(1)}, bf16[64,1536]{1,0:T(8,128)(2,1)S(1)}, u32[]{:S(2)}, u32[]{:S(2)}) collective-permute-start(bf16[64,1536]{1,0:T(8,128)(2,1)S(1)} %pad_maximum_fusion), channel_id=1, source_target_pairs={{0,256},{256,0},{1,257},{257,1},{2,258},{258,2},{3,259},{259,3},{4... | collective-permute-start | bytes 589832 | tf_op jit(solution)/shard_map/ppermute | solution.py:42
  101.3 0.1 dynamic_slice.69
  101.3 3.7 %collective-permute-done.8 = bf16[64,1536]{1,0:T(8,128)(2,1)S(1)} collective-permute-done((bf16[64,1536]{1,0:T(8,128)(2,1)S(1)}, bf16[64,1536]{1,0:T(8,128)(2,1)S(1)}, u32[]{:S(2)}, u32[]{:S(2)}) %collective-permute-start.8) | collective-permute-done | bytes 196640 | tf_op jit(solution)/shard_map/ppermute | solution.py:42
  105.0 0.9 convert_add_fusion.1
  105.9 0.8 multiply_convert_fusion
  106.7 0.8 broadcast_in_dim.8
  107.5 17.7 %all-to-all-start.3 = ((bf16[4,64,768]{2,1,0:T(8,128)(2,1)}), bf16[4,64,768]{2,1,0:T(8,128)(2,1)S(1)}, u32[]{:S(2)}, u32[]{:S(2)}) async-start(bf16[4,64,768]{2,1,0:T(8,128)(2,1)} %broadcast_in_dim.8), calls=%async_computation.3 | async-start | bytes 786432 | tf_op jit(solution)/shard_map/all_to_all | solution.py:72
  125.2 1.5 constant_dynamic-slice_fusion
  126.8 11.5 %collective-permute-start.9 = (bf16[64,768]{1,0:T(8,128)(2,1)}, bf16[64,768]{1,0:T(8,128)(2,1)}, u32[]{:S(2)}, u32[]{:S(2)}) collective-permute-start(bf16[64,768]{1,0:T(8,128)(2,1)} %get-tuple-element.28), channel_id=1, source_target_pairs={{0,258},{2,256},{256,2},{258,0},{1,259},{3,257},{257,3},{259,1},{4... | collective-permute-start | bytes 294920 | tf_op jit(solution)/shard_map/ppermute | solution.py:66
  138.3 1.7 convolution_convert_fusion
  140.0 0.1 convert_reduce_fusion.2
  140.1 3.9 %collective-permute-done.9 = bf16[64,768]{1,0:T(8,128)(2,1)} collective-permute-done((bf16[64,768]{1,0:T(8,128)(2,1)}, bf16[64,768]{1,0:T(8,128)(2,1)}, u32[]{:S(2)}, u32[]{:S(2)}) %collective-permute-start.9) | collective-permute-done | bytes 98336 | tf_op jit(solution)/shard_map/ppermute | solution.py:66
  144.0 3.6 %all-to-all-start.4 = ((bf16[16,16,1536]{2,1,0:T(8,128)(2,1)}), bf16[16,16,1536]{2,1,0:T(8,128)(2,1)S(1)}, u32[]{:S(2)}, u32[]{:S(2)}) async-start(bf16[16,16,1536]{2,1,0:T(8,128)(2,1)} %bitcast.78), calls=%async_computation.4 | async-start | bytes 1572864 | tf_op jit(solution)/shard_map/all_to_all | solution.py:127
  147.6 1.1 maximum_select_fusion.6
  148.7 5.4 %collective-permute-start.10 = (bf16[1,1,64,1536]{3,2,1,0:T(8,128)(2,1)S(1)}, bf16[1,1,64,1536]{3,2,1,0:T(8,128)(2,1)S(1)}, u32[]{:S(2)}, u32[]{:S(2)}) collective-permute-start(bf16[1,1,64,1536]{3,2,1,0:T(8,128)(2,1)S(1)} %maximum_select_fusion.6), channel_id=1, source_target_pairs={{0,128},{128,0},{1,129},{129,1},{2,130},{130,2},{3,131},{131,3},{4... | collective-permute-start | bytes 589832 | tf_op jit(solution)/shard_map/ppermute | solution.py:42
  154.1 1.0 maximum_select_fusion.5
  155.2 2.3 %collective-permute-done.10 = bf16[1,1,64,1536]{3,2,1,0:T(8,128)(2,1)S(1)} collective-permute-done((bf16[1,1,64,1536]{3,2,1,0:T(8,128)(2,1)S(1)}, bf16[1,1,64,1536]{3,2,1,0:T(8,128)(2,1)S(1)}, u32[]{:S(2)}, u32[]{:S(2)}) %collective-permute-start.10) | collective-permute-done | bytes 196640 | tf_op jit(solution)/shard_map/ppermute | solution.py:42
  157.5 10.2 %collective-permute-start.11 = (bf16[256,384]{1,0:T(8,128)(2,1)S(1)}, bf16[256,384]{1,0:T(8,128)(2,1)S(1)}, u32[]{:S(2)}, u32[]{:S(2)}) collective-permute-start(bf16[256,384]{1,0:T(8,128)(2,1)S(1)} %constant_dynamic-slice_fusion.2), channel_id=1, source_target_pairs={{0,1},{1,0},{2,3},{3,2},{4,5},{5,4},{6,7},{7,6},{8,9},{9,8},{10,11... | collective-permute-start | bytes 589832 | tf_op jit(solution)/shard_map/ppermute | solution.py:42
  167.7 0.6 fusion.22
  168.3 2.1 %collective-permute-start.14 = (bf16[2,1,64,1536]{3,2,1,0:T(8,128)(2,1)S(1)}, bf16[2,1,64,1536]{3,2,1,0:T(8,128)(2,1)S(1)}, u32[]{:S(2)}, u32[]{:S(2)}) collective-permute-start(bf16[2,1,64,1536]{3,2,1,0:T(8,128)(2,1)S(1)} %maximum_select_fusion.2), channel_id=1, source_target_pairs={{0,64},{64,0},{1,65},{65,1},{2,66},{66,2},{3,67},{67,3},{4,68},{68... | collective-permute-start | bytes 1179656 | tf_op jit(solution)/shard_map/ppermute | solution.py:42
  170.4 1.9 collective-permute-start.13
  172.3 2.8 %fusion.2 = bf16[1536,384]{1,0:T(8,128)(2,1)} fusion(f32[1536,384]{1,0:T(8,128)S(1)} %fusion.22, bf16[256,1536]{1,0:T(8,128)(2,1)} %collective-permute-done.4, bf16[256,384]{1,0:T(8,128)(2,1)S(1)} %collective-permute-done.11), kind=kOutput, calls=%fused_computation.7 | convolution fusion | flops 303169536 | bytes 4521984 | tf_op jit(solution)/shard_map/dot_general | solution.py:34
  175.1 0.1 convert_reduce_fusion.1
  175.2 0.6 add.129
  175.8 0.1 convert_reduce_fusion
  175.9 8.6 %collective-permute-start.12 = (bf16[8,1536]{1,0:T(8,128)(2,1)S(1)}, bf16[8,1536]{1,0:T(8,128)(2,1)S(1)}, u32[]{:S(2)}, u32[]{:S(2)}) collective-permute-start(bf16[8,1536]{1,0:T(8,128)(2,1)S(1)} %dynamic-slice_convert_fusion.3), channel_id=1, source_target_pairs={{0,2},{2,0},{1,3},{3,1},{4,6},{6,4},{5,7},{7,5},{8,10},{10,8},{9,1... | collective-permute-start | bytes 73736 | tf_op jit(solution)/shard_map/ppermute | solution.py:42
  184.5 0.5 convolution_bitcast_fusion.1
  185.0 4.2 %collective-permute-done.12 = bf16[8,1536]{1,0:T(8,128)(2,1)S(1)} collective-permute-done((bf16[8,1536]{1,0:T(8,128)(2,1)S(1)}, bf16[8,1536]{1,0:T(8,128)(2,1)S(1)}, u32[]{:S(2)}, u32[]{:S(2)}) %collective-permute-start.12) | collective-permute-done | bytes 24608 | tf_op jit(solution)/shard_map/ppermute | solution.py:42
  189.2 3.6 %collective-permute-start.15 = (bf16[128,1536]{1,0:T(8,128)(2,1)S(1)}, bf16[128,1536]{1,0:T(8,128)(2,1)S(1)}, u32[]{:S(2)}, u32[]{:S(2)}) collective-permute-start(bf16[128,1536]{1,0:T(8,128)(2,1)S(1)} %bitcast.80), channel_id=1, source_target_pairs={{0,1},{1,0},{2,3},{3,2},{4,5},{5,4},{6,7},{7,6},{8,9},{9,8},{10,11... | collective-permute-start | bytes 1179656 | tf_op jit(solution)/shard_map/ppermute | solution.py:42
  192.8 0.5 convolution_bitcast_fusion
  193.3 0.6 add_convert_fusion.1
  194.0 0.5 fusion.1
  194.5 0.4 copy-done.6
  194.9 1.5 fusion.3
  (40 shorter events, 0.3 us)
Async XLA Ops:
  2.1 17.7 %collective-permute-start = (bf16[8,2304]{1,0:T(8,128)(2,1)S(1)}, bf16[8,2304]{1,0:T(8,128)(2,1)S(1)}, u32[]{:S(2)}, u32[]{:S(2)}) collective-permute-start(bf16[8,2304]{1,0:T(8,128)(2,1)S(1)} %pad_maximum_fusion.1), channel_id=1, source_target_pairs={{0,2},{2,0},{1,3},{3,1},{4,6},{6,4},{5,7},{7,5},{8,10},{10,8},{9,1... | collective-permute-start | bytes 110600 | tf_op jit(solution)/shard_map/ppermute | solution.py:42
  20.7 10.9 %collective-permute-start.1 = (bf16[1536,384]{1,0:T(8,128)(2,1)}, bf16[1536,384]{1,0:T(8,128)(2,1)}, u32[]{:S(2)}, u32[]{:S(2)}) collective-permute-start(bf16[1536,384]{1,0:T(8,128)(2,1)} %param.9), channel_id=1, source_target_pairs={{0,1},{1,0},{2,3},{3,2},{4,5},{5,4},{6,7},{7,6},{8,9},{9,8},{10,11... | collective-permute-start | bytes 3538952 | tf_op jit(solution)/shard_map/ppermute | solution.py:42
  27.1 13.6 %all-to-all-start = ((bf16[16,16,768]{2,1,0:T(8,128)(2,1)}), bf16[16,16,768]{2,1,0:T(8,128)(2,1)S(1)}, u32[]{:S(2)}, u32[]{:S(2)}) async-start(bf16[16,16,768]{2,1,0:T(8,128)(2,1)} %broadcast_in_dim.6), calls=%async_computation | async-start | bytes 786432 | tf_op jit(solution)/shard_map/all_to_all | solution.py:72
  41.5 1.2 copy-start
  42.7 16.5 %copy-start.1 = (f32[2,2,64,1536]{3,2,1,0:T(8,128)S(1)}, f32[2,2,64,1536]{3,2,1,0:T(8,128)}, u32[]{:S(2)}) copy-start(f32[2,2,64,1536]{3,2,1,0:T(8,128)} %copy-done) | copy-start | bytes 4718596
  42.8 21.2 %collective-permute-start.3 = (bf16[1536,384]{1,0:T(8,128)(2,1)}, bf16[1536,384]{1,0:T(8,128)(2,1)}, u32[]{:S(2)}, u32[]{:S(2)}) collective-permute-start(bf16[1536,384]{1,0:T(8,128)(2,1)} %param.7), channel_id=1, source_target_pairs={{0,1},{1,0},{2,3},{3,2},{4,5},{5,4},{6,7},{7,6},{8,9},{9,8},{10,11... | collective-permute-start | bytes 3538952 | tf_op jit(solution)/shard_map/ppermute | solution.py:42
  46.5 12.7 %collective-permute-start.2 = (bf16[2,1,64,1536]{3,2,1,0:T(8,128)(2,1)S(1)}, bf16[2,1,64,1536]{3,2,1,0:T(8,128)(2,1)}, u32[]{:S(2)}, u32[]{:S(2)}) collective-permute-start(bf16[2,1,64,1536]{3,2,1,0:T(8,128)(2,1)S(1)} %dynamic-slice_convert_fusion), channel_id=1, source_target_pairs={{0,64},{64,0},{1,65},{65,1},{2,66},{66,2},{3,67},{67,3},{4,68},{68... | collective-permute-start | bytes 1179656 | tf_op jit(solution)/shard_map/ppermute | solution.py:42
  50.6 17.4 %all-to-all-start.1 = ((bf16[16,16,1536]{2,1,0:T(8,128)(2,1)}), bf16[16,16,1536]{2,1,0:T(8,128)(2,1)S(1)}, u32[]{:S(2)}, u32[]{:S(2)}) async-start(bf16[16,16,1536]{2,1,0:T(8,128)(2,1)} %broadcast_in_dim.7), calls=%async_computation.1 | async-start | bytes 1572864 | tf_op jit(solution)/shard_map/all_to_all | solution.py:72
  60.3 12.9 %collective-permute-start.6 = (bf16[1,1,64,1536]{3,2,1,0:T(8,128)(2,1)S(1)}, bf16[1,1,64,1536]{3,2,1,0:T(8,128)(2,1)S(1)}, u32[]{:S(2)}, u32[]{:S(2)}) collective-permute-start(bf16[1,1,64,1536]{3,2,1,0:T(8,128)(2,1)S(1)} %dynamic-slice_convert_fusion.1), channel_id=1, source_target_pairs={{0,128},{128,0},{1,129},{129,1},{2,130},{130,2},{3,131},{131,3},{4... | collective-permute-start | bytes 589832 | tf_op jit(solution)/shard_map/ppermute | solution.py:42
  71.2 30.1 %copy-start.9 = (f32[1536]{0:T(1024)S(1)}, f32[1536]{0:T(1024)}, u32[]{:S(2)}) copy-start(f32[1536]{0:T(1024)} %param.8) | copy-start | bytes 18436
  73.2 20.3 %all-to-all-start.2 = ((bf16[4,64,768]{2,1,0:T(8,128)(2,1)}), bf16[4,64,768]{2,1,0:T(8,128)(2,1)}, u32[]{:S(2)}, u32[]{:S(2)}) async-start(bf16[4,64,768]{2,1,0:T(8,128)(2,1)} %bitcast.5), calls=%async_computation.2 | async-start | bytes 786432 | tf_op jit(solution)/shard_map/all_to_all | solution.py:78
  77.3 17.3 %collective-permute-start.4 = (bf16[256,1536]{1,0:T(8,128)(2,1)S(1)}, bf16[256,1536]{1,0:T(8,128)(2,1)}, u32[]{:S(2)}, u32[]{:S(2)}) collective-permute-start(bf16[256,1536]{1,0:T(8,128)(2,1)S(1)} %bitcast.67), channel_id=1, source_target_pairs={{0,1},{1,0},{2,3},{3,2},{4,5},{5,4},{6,7},{7,6},{8,9},{9,8},{10,11... | collective-permute-start | bytes 2359304 | tf_op jit(solution)/shard_map/ppermute | solution.py:42
  80.8 57.5 %copy-start.2 = (bf16[1536,768]{1,0:T(8,128)(2,1)S(1)}, bf16[1536,768]{1,0:T(8,128)(2,1)}, u32[]{:S(2)}) copy-start(bf16[1536,768]{1,0:T(8,128)(2,1)} %maximum_select_fusion.1) | copy-start | bytes 7077892
  80.8 12.7 %collective-permute-start.7 = (bf16[64,768]{1,0:T(8,128)(2,1)S(1)}, bf16[64,768]{1,0:T(8,128)(2,1)S(1)}, u32[]{:S(2)}, u32[]{:S(2)}) collective-permute-start(bf16[64,768]{1,0:T(8,128)(2,1)S(1)} %fusion.25), channel_id=1, source_target_pairs={{0,258},{2,256},{256,2},{258,0},{1,259},{3,257},{257,3},{259,1},{4... | collective-permute-start | bytes 294920 | tf_op jit(solution)/shard_map/ppermute | solution.py:66
  91.1 3.6 %collective-permute-start.5 = (bf16[256,384]{1,0:T(8,128)(2,1)}, bf16[256,384]{1,0:T(8,128)(2,1)S(1)}, u32[]{:S(2)}, u32[]{:S(2)}) collective-permute-start(bf16[256,384]{1,0:T(8,128)(2,1)} %get-tuple-element.31), channel_id=1, source_target_pairs={{0,1},{1,0},{2,3},{3,2},{4,5},{5,4},{6,7},{7,6},{8,9},{9,8},{10,11... | collective-permute-start | bytes 589832 | tf_op jit(solution)/shard_map/ppermute | solution.py:42
  93.5 7.8 %copy-start.4 = (bf16[64,768]{1,0:T(8,128)(2,1)}, bf16[64,768]{1,0:T(8,128)(2,1)S(1)}, u32[]{:S(2)}) copy-start(bf16[64,768]{1,0:T(8,128)(2,1)S(1)} %fusion.21) | copy-start | bytes 294916
  94.6 6.7 %copy-start.7 = (bf16[256,384]{1,0:T(8,128)(2,1)}, bf16[256,384]{1,0:T(8,128)(2,1)S(1)}, u32[]{:S(2)}) copy-start(bf16[256,384]{1,0:T(8,128)(2,1)S(1)} %collective-permute-done.5) | copy-start | bytes 589828
  94.7 10.3 %collective-permute-start.8 = (bf16[64,1536]{1,0:T(8,128)(2,1)S(1)}, bf16[64,1536]{1,0:T(8,128)(2,1)S(1)}, u32[]{:S(2)}, u32[]{:S(2)}) collective-permute-start(bf16[64,1536]{1,0:T(8,128)(2,1)S(1)} %pad_maximum_fusion), channel_id=1, source_target_pairs={{0,256},{256,0},{1,257},{257,1},{2,258},{258,2},{3,259},{259,3},{4... | collective-permute-start | bytes 589832 | tf_op jit(solution)/shard_map/ppermute | solution.py:42
  107.5 30.8 %all-to-all-start.3 = ((bf16[4,64,768]{2,1,0:T(8,128)(2,1)}), bf16[4,64,768]{2,1,0:T(8,128)(2,1)S(1)}, u32[]{:S(2)}, u32[]{:S(2)}) async-start(bf16[4,64,768]{2,1,0:T(8,128)(2,1)} %broadcast_in_dim.8), calls=%async_computation.3 | async-start | bytes 786432 | tf_op jit(solution)/shard_map/all_to_all | solution.py:72
  126.8 17.2 %collective-permute-start.9 = (bf16[64,768]{1,0:T(8,128)(2,1)}, bf16[64,768]{1,0:T(8,128)(2,1)}, u32[]{:S(2)}, u32[]{:S(2)}) collective-permute-start(bf16[64,768]{1,0:T(8,128)(2,1)} %get-tuple-element.28), channel_id=1, source_target_pairs={{0,258},{2,256},{256,2},{258,0},{1,259},{3,257},{257,3},{259,1},{4... | collective-permute-start | bytes 294920 | tf_op jit(solution)/shard_map/ppermute | solution.py:66
  140.0 14.1 %copy-start.3 = (bf16[64,768]{1,0:T(8,128)(2,1)S(1)}, bf16[64,768]{1,0:T(8,128)(2,1)}, u32[]{:S(2)}) copy-start(bf16[64,768]{1,0:T(8,128)(2,1)} %get-tuple-element.28) | copy-start | bytes 294916
  144.0 31.8 %all-to-all-start.4 = ((bf16[16,16,1536]{2,1,0:T(8,128)(2,1)}), bf16[16,16,1536]{2,1,0:T(8,128)(2,1)S(1)}, u32[]{:S(2)}, u32[]{:S(2)}) async-start(bf16[16,16,1536]{2,1,0:T(8,128)(2,1)} %bitcast.78), calls=%async_computation.4 | async-start | bytes 1572864 | tf_op jit(solution)/shard_map/all_to_all | solution.py:127
  148.7 8.8 %collective-permute-start.10 = (bf16[1,1,64,1536]{3,2,1,0:T(8,128)(2,1)S(1)}, bf16[1,1,64,1536]{3,2,1,0:T(8,128)(2,1)S(1)}, u32[]{:S(2)}, u32[]{:S(2)}) collective-permute-start(bf16[1,1,64,1536]{3,2,1,0:T(8,128)(2,1)S(1)} %maximum_select_fusion.6), channel_id=1, source_target_pairs={{0,128},{128,0},{1,129},{129,1},{2,130},{130,2},{3,131},{131,3},{4... | collective-permute-start | bytes 589832 | tf_op jit(solution)/shard_map/ppermute | solution.py:42
  157.5 14.8 %collective-permute-start.11 = (bf16[256,384]{1,0:T(8,128)(2,1)S(1)}, bf16[256,384]{1,0:T(8,128)(2,1)S(1)}, u32[]{:S(2)}, u32[]{:S(2)}) collective-permute-start(bf16[256,384]{1,0:T(8,128)(2,1)S(1)} %constant_dynamic-slice_fusion.2), channel_id=1, source_target_pairs={{0,1},{1,0},{2,3},{3,2},{4,5},{5,4},{6,7},{7,6},{8,9},{9,8},{10,11... | collective-permute-start | bytes 589832 | tf_op jit(solution)/shard_map/ppermute | solution.py:42
  168.3 16.2 %copy-start.8 = (bf16[256,384]{1,0:T(8,128)(2,1)S(1)}, bf16[256,384]{1,0:T(8,128)(2,1)}, u32[]{:S(2)}) copy-start(bf16[256,384]{1,0:T(8,128)(2,1)} %copy-done.7) | copy-start | bytes 589828
  168.3 16.6 %collective-permute-start.14 = (bf16[2,1,64,1536]{3,2,1,0:T(8,128)(2,1)S(1)}, bf16[2,1,64,1536]{3,2,1,0:T(8,128)(2,1)S(1)}, u32[]{:S(2)}, u32[]{:S(2)}) collective-permute-start(bf16[2,1,64,1536]{3,2,1,0:T(8,128)(2,1)S(1)} %maximum_select_fusion.2), channel_id=1, source_target_pairs={{0,64},{64,0},{1,65},{65,1},{2,66},{66,2},{3,67},{67,3},{4,68},{68... | collective-permute-start | bytes 1179656 | tf_op jit(solution)/shard_map/ppermute | solution.py:42
  170.4 14.1 %collective-permute-start.13 = (bf16[2,1,64,1536]{3,2,1,0:T(8,128)(2,1)S(1)}, bf16[2,1,64,1536]{3,2,1,0:T(8,128)(2,1)S(1)}, u32[]{:S(2)}, u32[]{:S(2)}) collective-permute-start(bf16[2,1,64,1536]{3,2,1,0:T(8,128)(2,1)S(1)} %maximum_select_fusion.2), channel_id=1, source_target_pairs={{0,1},{1,0},{2,3},{3,2},{4,5},{5,4},{6,7},{7,6},{8,9},{9,8},{10,11... | collective-permute-start | bytes 1179656 | tf_op jit(solution)/shard_map/ppermute | solution.py:42
  175.1 17.7 %copy-start.5 = (bf16[256,384]{1,0:T(8,128)(2,1)S(1)}, bf16[256,384]{1,0:T(8,128)(2,1)}, u32[]{:S(2)}) copy-start(bf16[256,384]{1,0:T(8,128)(2,1)} %get-tuple-element.30) | copy-start | bytes 589828
  175.9 13.3 %collective-permute-start.12 = (bf16[8,1536]{1,0:T(8,128)(2,1)S(1)}, bf16[8,1536]{1,0:T(8,128)(2,1)S(1)}, u32[]{:S(2)}, u32[]{:S(2)}) collective-permute-start(bf16[8,1536]{1,0:T(8,128)(2,1)S(1)} %dynamic-slice_convert_fusion.3), channel_id=1, source_target_pairs={{0,2},{2,0},{1,3},{3,1},{4,6},{6,4},{5,7},{7,5},{8,10},{10,8},{9,1... | collective-permute-start | bytes 73736 | tf_op jit(solution)/shard_map/ppermute | solution.py:42
  189.2 5.3 %collective-permute-start.15 = (bf16[128,1536]{1,0:T(8,128)(2,1)S(1)}, bf16[128,1536]{1,0:T(8,128)(2,1)S(1)}, u32[]{:S(2)}, u32[]{:S(2)}) collective-permute-start(bf16[128,1536]{1,0:T(8,128)(2,1)S(1)} %bitcast.80), channel_id=1, source_target_pairs={{0,1},{1,0},{2,3},{3,2},{4,5},{5,4},{6,7},{7,6},{8,9},{9,8},{10,11... | collective-permute-start | bytes 1179656 | tf_op jit(solution)/shard_map/ppermute | solution.py:42
  194.0 0.9 copy-start.6

commit v13 on v8

--- a/solution.py
+++ b/solution.py
@@ -112,9 +112,6 @@
     pre = deal(after(back_got, pre), ROW4).astype(bf16)
     back_kept, back_sent = cut((back_kept + back_got.astype(f32))[0, 0], "zh", 1)
     back = (back_kept + cross(back_sent).astype(f32)).astype(bf16)
-    pair_x = swap(every_x, "core")
-    pair_g = swap(part_of(every_g, 1 - core, quarter_d, 1), "core")
-    pre = after((pair_x, pair_g), pre)
     met = jnp.concatenate([pre, back], 1)
     met = met.astype(f32) + swap(met, "rh").astype(f32)
     pre, back = met[:, :half_h], met[:, half_h:]
@@ -122,16 +119,19 @@
     act_f, slope = gelu_pair(pre + part_of(b_in, zh, half_h, 0))
     act = act_f.astype(bf16)
     crossed = cross(act)
+    pair_x = swap(after(act, every_x), "core")
+    pair_g = swap(after(act, part_of(every_g, 1 - core, quarter_d, 1)), "core")
     grad = spread((back * slope).astype(bf16), ROW4)
+    grad = after((pair_x, pair_g), grad)
     part = against(grad, in_pair).astype(bf16)
     dealt = lax.all_to_all(part.reshape(-1, 2 * tok_dev, feat), GRID, 0, 0, tiled=True)
 
     own_grad = part_of(grad, core, quarter, 1)
     act = join(act, after(part, crossed), "zh", 1)[None, None]
     act = join(act, swap(act, "rm"), "rm", 0)
-    own_part = over_rows(every_x, own_grad)
+    own_part = over_rows(every_x, after(act, own_grad))
     pair_grad = swap(after(act, part_of(grad, 1 - core, quarter, 1)), "core")
-    act = join(act, swap(act, "rl"), "rl", 1).reshape(-1, act.shape[-1])
+    act = join(act, swap(after(own_part, act), "rl"), "rl", 1).reshape(-1, act.shape[-1])
     w_in_grad = (own_part + over_rows(pair_x, pair_grad)).astype(bf16)
     b_in_grad = jnp.sum(own_grad.astype(f32), 0) + jnp.sum(pair_grad.astype(f32), 0)
 

time: 192 us -> 204 us (1.062)
  waiting for transfers between devices: 34.1 us -> 44.9 us
  starting transfers between devices: 126 us -> 118 us
  other arithmetic: 11.7 us -> 18.6 us
    ppermute x13, waiting for transfers between devices: 23.5 us -> 30.9 us  [swap(): return lax.ppermute(value, axis, SWAP)]
    ppermute x2, starting transfers between devices: 21 us -> 14.1 us  [cross(): return lax.ppermute(value, ('rh', 'zh'), CROSS)]
    ppermute x2, waiting for transfers between devices: 4.42 us -> 7.93 us  [cross(): return lax.ppermute(value, ('rh', 'zh'), CROSS)]
    dot_general x4, matrix products: 4.5 us -> 6.54 us  [over_rows(): lax.dot_general(left, right, (((0,), (0,)), ((), ())), preferred_element_...]
  transfers between devices with their start and end apart: 20 -> 20, of which waited for: 9 -> 10; matrix products, arithmetic and copies ran while one was open for 12% -> 14% of each run, Pallas kernels for 0% -> 0%
where the time goes in v13:
time: 204 us; the launch traced here: 202 us
  starting transfers between devices  118 us (58%)
  waiting for transfers between devices  44.9 us (22%)
  other arithmetic  18.6 us (9%)
  matrix products  13.2 us (6%)
  local copies, waits for them, and re-layouts  6.28 us (3%)
    ppermute x13, starting transfers between devices, swap(): return lax.ppermute(value, axis, SWAP)  71.4 us
    ppermute x13, waiting for transfers between devices, swap(): return lax.ppermute(value, axis, SWAP)  30.9 us
    all_to_all x3, starting transfers between devices, spread(): got = lax.all_to_all(sent, axes, 0, 0, tiled=True)  24.7 us
    ppermute x2, starting transfers between devices, cross(): return lax.ppermute(value, ('rh', 'zh'), CROSS)  14.1 us
    select_n x6, other arithmetic, join(): jnp.where(first, jnp.concatenate([mine, other], dim), jnp.concatenate([ot...  9.05 us
    ppermute x2, waiting for transfers between devices, cross(): return lax.ppermute(value, ('rh', 'zh'), CROSS)  7.93 us
    dot_general x4, matrix products, over_rows(): lax.dot_general(left, right, (((0,), (0,)), ((), ())), preferred_element_...  6.54 us
    all_to_all x3, waiting for transfers between devices, spread(): got = lax.all_to_all(sent, axes, 0, 0, tiled=True)  6.11 us
  transfers between devices with their start and end apart: 20, of which 10 were waited for; matrix products, arithmetic and copies ran while one was open for 14% of the time, Pallas kernels for 0%

profile of v13, /device:TPU:1, one launch (start us, length us, event | category | flops | bytes accessed | tf_op | source)
XLA Modules:
  0.0 202.1 jit_solution(596608338446524431)
XLA Ops:
  0.6 0.7 constant_dynamic-slice_fusion.4
  1.4 0.7 pad_maximum_fusion.1
  2.1 16.3 %collective-permute-start = (bf16[8,2304]{1,0:T(8,128)(2,1)S(1)}, bf16[8,2304]{1,0:T(8,128)(2,1)S(1)}, u32[]{:S(2)}, u32[]{:S(2)}) collective-permute-start(bf16[8,2304]{1,0:T(8,128)(2,1)S(1)} %pad_maximum_fusion.1), channel_id=1, source_target_pairs={{0,2},{2,0},{1,3},{3,1},{4,6},{6,4},{5,7},{7,5},{8,10},{10,8},{9,1... | collective-permute-start | bytes 110600 | tf_op jit(solution)/shard_map/ppermute | solution.py:42
  18.4 1.5 collective-permute-done
  19.9 0.8 maximum_select_fusion.6
  20.7 5.6 %collective-permute-start.1 = (bf16[1536,384]{1,0:T(8,128)(2,1)}, bf16[1536,384]{1,0:T(8,128)(2,1)}, u32[]{:S(2)}, u32[]{:S(2)}) collective-permute-start(bf16[1536,384]{1,0:T(8,128)(2,1)} %param.9), channel_id=1, source_target_pairs={{0,1},{1,0},{2,3},{3,2},{4,5},{5,4},{6,7},{7,6},{8,9},{9,8},{10,11... | collective-permute-start | bytes 3538952 | tf_op jit(solution)/shard_map/ppermute | solution.py:42
  26.3 0.8 broadcast_in_dim.6
  27.1 4.5 %all-to-all-start = ((bf16[16,16,768]{2,1,0:T(8,128)(2,1)}), bf16[16,16,768]{2,1,0:T(8,128)(2,1)S(1)}, u32[]{:S(2)}, u32[]{:S(2)}) async-start(bf16[16,16,768]{2,1,0:T(8,128)(2,1)} %broadcast_in_dim.6), calls=%async_computation | async-start | bytes 786432 | tf_op jit(solution)/shard_map/all_to_all | solution.py:72
  31.6 0.0 collective-permute-done.1
  31.6 3.0 %maximum_select_fusion = bf16[1536,768]{1,0:T(8,128)(2,1)S(1)} fusion(bf16[1536,384]{1,0:T(8,128)(2,1)} %collective-permute-done.1, bf16[1536,384]{1,0:T(8,128)(2,1)} %param.9, pred[]{:T(512)S(6)} %eq.15), kind=kLoop, calls=%fused_computation.5 | loop fusion | flops 10616832 | bytes 4718593 | tf_op jit(solution)/shard_map/jit(_where)/select_n | solution.py:47
  34.6 6.1 %all-to-all-done = bf16[16,16,768]{2,1,0:T(8,128)(2,1)S(1)} async-done(((bf16[16,16,768]{2,1,0:T(8,128)(2,1)}), bf16[16,16,768]{2,1,0:T(8,128)(2,1)S(1)}, u32[]{:S(2)}, u32[]{:S(2)}) %all-to-all-start) | async-done | bytes 393248 | tf_op jit(solution)/shard_map/all_to_all | solution.py:72
  40.7 0.8 fusion.2
  41.5 1.1 copy-done
  42.7 3.7 %collective-permute-start.3 = (bf16[1536,384]{1,0:T(8,128)(2,1)}, bf16[1536,384]{1,0:T(8,128)(2,1)}, u32[]{:S(2)}, u32[]{:S(2)}) collective-permute-start(bf16[1536,384]{1,0:T(8,128)(2,1)} %param.7), channel_id=1, source_target_pairs={{0,1},{1,0},{2,3},{3,2},{4,5},{5,4},{6,7},{7,6},{8,9},{9,8},{10,11... | collective-permute-start | bytes 3538952 | tf_op jit(solution)/shard_map/ppermute | solution.py:42
  46.4 3.1 %collective-permute-start.2 = (bf16[2,1,64,1536]{3,2,1,0:T(8,128)(2,1)S(1)}, bf16[2,1,64,1536]{3,2,1,0:T(8,128)(2,1)}, u32[]{:S(2)}, u32[]{:S(2)}) collective-permute-start(bf16[2,1,64,1536]{3,2,1,0:T(8,128)(2,1)S(1)} %dynamic-slice_convert_fusion), channel_id=1, source_target_pairs={{0,64},{64,0},{1,65},{65,1},{2,66},{66,2},{3,67},{67,3},{4,68},{68... | collective-permute-start | bytes 1179656 | tf_op jit(solution)/shard_map/ppermute | solution.py:42
  49.6 1.0 broadcast_in_dim.7
  50.5 3.6 %all-to-all-start.1 = ((bf16[16,16,1536]{2,1,0:T(8,128)(2,1)}), bf16[16,16,1536]{2,1,0:T(8,128)(2,1)S(1)}, u32[]{:S(2)}, u32[]{:S(2)}) async-start(bf16[16,16,1536]{2,1,0:T(8,128)(2,1)} %broadcast_in_dim.7), calls=%async_computation.1 | async-start | bytes 1572864 | tf_op jit(solution)/shard_map/all_to_all | solution.py:72
  54.2 5.0 %collective-permute-done.2 = bf16[2,1,64,1536]{3,2,1,0:T(8,128)(2,1)} collective-permute-done((bf16[2,1,64,1536]{3,2,1,0:T(8,128)(2,1)S(1)}, bf16[2,1,64,1536]{3,2,1,0:T(8,128)(2,1)}, u32[]{:S(2)}, u32[]{:S(2)}) %collective-permute-start.2) | collective-permute-done | bytes 393248 | tf_op jit(solution)/shard_map/ppermute | solution.py:42
  59.2 1.1 convert_add_fusion
  60.3 3.6 %collective-permute-start.4 = (bf16[1,1,64,1536]{3,2,1,0:T(8,128)(2,1)S(1)}, bf16[1,1,64,1536]{3,2,1,0:T(8,128)(2,1)S(1)}, u32[]{:S(2)}, u32[]{:S(2)}) collective-permute-start(bf16[1,1,64,1536]{3,2,1,0:T(8,128)(2,1)S(1)} %dynamic-slice_convert_fusion.1), channel_id=1, source_target_pairs={{0,128},{128,0},{1,129},{129,1},{2,130},{130,2},{3,131},{131,3},{4... | collective-permute-start | bytes 589832 | tf_op jit(solution)/shard_map/ppermute | solution.py:42
  63.9 4.1 %maximum_select_fusion.1 = bf16[1536,768]{1,0:T(8,128)(2,1)} fusion(bf16[1536,384]{1,0:T(8,128)(2,1)} %collective-permute-done.3, bf16[1536,384]{1,0:T(8,128)(2,1)} %param.7, pred[]{:T(512)S(6)} %eq.15), kind=kLoop, calls=%fused_computation.6 | loop fusion | flops 10616832 | bytes 4718593 | tf_op jit(solution)/shard_map/jit(_where)/select_n | solution.py:47
  68.0 3.2 %convolution_convert_fusion.1 = bf16[256,768]{1,0:T(8,128)(2,1)} fusion(bf16[256,1536]{1,0:T(8,128)(2,1)S(1)} %bitcast.43, bf16[1536,768]{1,0:T(8,128)(2,1)} %maximum_select_fusion.1), kind=kOutput, calls=%fused_computation.10 | convolution fusion | flops 604176384 | bytes 3538944 | tf_op jit(solution)/shard_map/dot_general | solution.py:26
  71.2 2.0 collective-permute-done.4
  73.2 4.1 %all-to-all-start.2 = ((bf16[4,64,768]{2,1,0:T(8,128)(2,1)}), bf16[4,64,768]{2,1,0:T(8,128)(2,1)}, u32[]{:S(2)}, u32[]{:S(2)}) async-start(bf16[4,64,768]{2,1,0:T(8,128)(2,1)} %bitcast.5), calls=%async_computation.2 | async-start | bytes 786432 | tf_op jit(solution)/shard_map/all_to_all | solution.py:78
  77.4 9.8 %collective-permute-start.5 = (bf16[64,768]{1,0:T(8,128)(2,1)S(1)}, bf16[64,768]{1,0:T(8,128)(2,1)S(1)}, u32[]{:S(2)}, u32[]{:S(2)}) collective-permute-start(bf16[64,768]{1,0:T(8,128)(2,1)S(1)} %fusion.15), channel_id=1, source_target_pairs={{0,258},{2,256},{256,2},{258,0},{1,259},{3,257},{257,3},{259,1},{4... | collective-permute-start | bytes 294920 | tf_op jit(solution)/shard_map/ppermute | solution.py:66
  87.2 6.0 %collective-permute-done.5 = bf16[64,768]{1,0:T(8,128)(2,1)S(1)} collective-permute-done((bf16[64,768]{1,0:T(8,128)(2,1)S(1)}, bf16[64,768]{1,0:T(8,128)(2,1)S(1)}, u32[]{:S(2)}, u32[]{:S(2)}) %collective-permute-start.5) | collective-permute-done | bytes 98336 | tf_op jit(solution)/shard_map/ppermute | solution.py:66
  93.2 0.7 fusion.12
  93.9 1.1 fusion.14
  95.0 0.9 pad_maximum_fusion
  95.9 4.7 %collective-permute-start.6 = (bf16[64,1536]{1,0:T(8,128)(2,1)S(1)}, bf16[64,1536]{1,0:T(8,128)(2,1)S(1)}, u32[]{:S(2)}, u32[]{:S(2)}) collective-permute-start(bf16[64,1536]{1,0:T(8,128)(2,1)S(1)} %pad_maximum_fusion), channel_id=1, source_target_pairs={{0,256},{256,0},{1,257},{257,1},{2,258},{258,2},{3,259},{259,3},{4... | collective-permute-start | bytes 589832 | tf_op jit(solution)/shard_map/ppermute | solution.py:42
  100.6 0.1 dynamic_slice.56
  100.6 5.6 %collective-permute-done.6 = bf16[64,1536]{1,0:T(8,128)(2,1)S(1)} collective-permute-done((bf16[64,1536]{1,0:T(8,128)(2,1)S(1)}, bf16[64,1536]{1,0:T(8,128)(2,1)S(1)}, u32[]{:S(2)}, u32[]{:S(2)}) %collective-permute-start.6) | collective-permute-done | bytes 196640 | tf_op jit(solution)/shard_map/ppermute | solution.py:42
  106.2 0.9 convert_add_fusion.1
  107.1 0.8 fusion.10
  107.9 0.8 broadcast_in_dim.8
  108.7 16.6 %all-to-all-start.3 = ((bf16[4,64,768]{2,1,0:T(8,128)(2,1)}), bf16[4,64,768]{2,1,0:T(8,128)(2,1)}, u32[]{:S(2)}, u32[]{:S(2)}) async-start(bf16[4,64,768]{2,1,0:T(8,128)(2,1)} %broadcast_in_dim.8), calls=%async_computation.3 | async-start | bytes 786432 | tf_op jit(solution)/shard_map/all_to_all | solution.py:72
  125.3 6.6 %collective-permute-start.7 = (bf16[256,1536]{1,0:T(8,128)(2,1)S(1)}, bf16[256,1536]{1,0:T(8,128)(2,1)}, u32[]{:S(2)}, u32[]{:S(2)}) collective-permute-start(bf16[256,1536]{1,0:T(8,128)(2,1)S(1)} %bitcast.44), channel_id=1, source_target_pairs={{0,1},{1,0},{2,3},{3,2},{4,5},{5,4},{6,7},{7,6},{8,9},{9,8},{10,11... | collective-permute-start | bytes 2359304 | tf_op jit(solution)/shard_map/ppermute | solution.py:42
  131.9 0.7 constant_dynamic-slice_fusion.2
  132.6 1.9 collective-permute-start.8
  134.6 4.4 %collective-permute-start.9 = (bf16[64,768]{1,0:T(8,128)(2,1)}, bf16[64,768]{1,0:T(8,128)(2,1)}, u32[]{:S(2)}, u32[]{:S(2)}) collective-permute-start(bf16[64,768]{1,0:T(8,128)(2,1)} %get-tuple-element.41), channel_id=1, source_target_pairs={{0,258},{2,256},{256,2},{258,0},{1,259},{3,257},{257,3},{259,1},{4... | collective-permute-start | bytes 294920 | tf_op jit(solution)/shard_map/ppermute | solution.py:66
  139.0 2.7 %convolution_convert_fusion = bf16[256,1536]{1,0:T(8,128)(2,1)} fusion(bf16[256,768]{1,0:T(8,128)(2,1)} %bitcast.10, bf16[1536,768]{1,0:T(8,128)(2,1)S(1)} %copy-done.2), kind=kOutput, calls=%fused_computation.4 | convolution fusion | flops 604372992 | bytes 3538944 | tf_op jit(solution)/shard_map/dot_general | solution.py:30
  141.7 1.0 constant_dynamic-slice_fusion
  142.7 1.9 collective-permute-done.9
  144.6 3.6 %all-to-all-start.4 = ((bf16[16,16,1536]{2,1,0:T(8,128)(2,1)}), bf16[16,16,1536]{2,1,0:T(8,128)(2,1)S(1)}, u32[]{:S(2)}, u32[]{:S(2)}) async-start(bf16[16,16,1536]{2,1,0:T(8,128)(2,1)} %bitcast.48), calls=%async_computation.4 | async-start | bytes 1572864 | tf_op jit(solution)/shard_map/all_to_all | solution.py:127
  148.2 1.0 convert_reduce_fusion.2
  149.2 1.0 maximum_select_fusion.5
  150.2 9.1 %collective-permute-start.10 = (bf16[1,1,64,1536]{3,2,1,0:T(8,128)(2,1)S(1)}, bf16[1,1,64,1536]{3,2,1,0:T(8,128)(2,1)S(1)}, u32[]{:S(2)}, u32[]{:S(2)}) collective-permute-start(bf16[1,1,64,1536]{3,2,1,0:T(8,128)(2,1)S(1)} %maximum_select_fusion.5), channel_id=1, source_target_pairs={{0,128},{128,0},{1,129},{129,1},{2,130},{130,2},{3,131},{131,3},{4... | collective-permute-start | bytes 589832 | tf_op jit(solution)/shard_map/ppermute | solution.py:42
  159.3 1.0 fusion.11
  160.3 7.8 %collective-permute-done.10 = bf16[1,1,64,1536]{3,2,1,0:T(8,128)(2,1)S(1)} collective-permute-done((bf16[1,1,64,1536]{3,2,1,0:T(8,128)(2,1)S(1)}, bf16[1,1,64,1536]{3,2,1,0:T(8,128)(2,1)S(1)}, u32[]{:S(2)}, u32[]{:S(2)}) %collective-permute-start.10) | collective-permute-done | bytes 196640 | tf_op jit(solution)/shard_map/ppermute | solution.py:42
  168.2 3.1 %collective-permute-start.11 = (bf16[256,384]{1,0:T(8,128)(2,1)S(1)}, bf16[256,384]{1,0:T(8,128)(2,1)S(1)}, u32[]{:S(2)}, u32[]{:S(2)}) collective-permute-start(bf16[256,384]{1,0:T(8,128)(2,1)S(1)} %constant_dynamic-slice_fusion), channel_id=1, source_target_pairs={{0,1},{1,0},{2,3},{3,2},{4,5},{5,4},{6,7},{7,6},{8,9},{9,8},{10,11... | collective-permute-start | bytes 589832 | tf_op jit(solution)/shard_map/ppermute | solution.py:42
  171.3 0.6 fusion.17
  171.9 2.3 %collective-permute-start.12 = (bf16[2,1,64,1536]{3,2,1,0:T(8,128)(2,1)S(1)}, bf16[2,1,64,1536]{3,2,1,0:T(8,128)(2,1)S(1)}, u32[]{:S(2)}, u32[]{:S(2)}) collective-permute-start(bf16[2,1,64,1536]{3,2,1,0:T(8,128)(2,1)S(1)} %maximum_select_fusion.3), channel_id=1, source_target_pairs={{0,64},{64,0},{1,65},{65,1},{2,66},{66,2},{3,67},{67,3},{4,68},{68... | collective-permute-start | bytes 1179656 | tf_op jit(solution)/shard_map/ppermute | solution.py:42
  174.3 0.1 convert_reduce_fusion.1
  174.3 0.6 add.119
  174.9 2.8 %fusion = bf16[1536,384]{1,0:T(8,128)(2,1)} fusion(f32[1536,384]{1,0:T(8,128)S(1)} %fusion.17, bf16[256,1536]{1,0:T(8,128)(2,1)} %collective-permute-done.7, bf16[256,384]{1,0:T(8,128)(2,1)S(1)} %collective-permute-done.11), kind=kOutput, calls=%fused_computation.2 | convolution fusion | flops 303169536 | bytes 4521984 | tf_op jit(solution)/shard_map/dot_general | solution.py:34
  177.7 6.9 %collective-permute-done.12 = bf16[2,1,64,1536]{3,2,1,0:T(8,128)(2,1)S(1)} collective-permute-done((bf16[2,1,64,1536]{3,2,1,0:T(8,128)(2,1)S(1)}, bf16[2,1,64,1536]{3,2,1,0:T(8,128)(2,1)S(1)}, u32[]{:S(2)}, u32[]{:S(2)}) %collective-permute-start.12) | collective-permute-done | bytes 393248 | tf_op jit(solution)/shard_map/ppermute | solution.py:42
  184.6 0.1 maximum_select_fusion.2
  184.7 0.1 convert_reduce_fusion
  184.8 2.7 %collective-permute-start.13 = (bf16[256,1536]{1,0:T(8,128)(2,1)S(1)}, bf16[256,1536]{1,0:T(8,128)(2,1)S(1)}, u32[]{:S(2)}, u32[]{:S(2)}) collective-permute-start(bf16[256,1536]{1,0:T(8,128)(2,1)S(1)} %bitcast.41), channel_id=1, source_target_pairs={{0,1},{1,0},{2,3},{3,2},{4,5},{5,4},{6,7},{7,6},{8,9},{9,8},{10,11... | collective-permute-start | bytes 2359304 | tf_op jit(solution)/shard_map/ppermute | solution.py:42
  187.5 8.7 %collective-permute-start.14 = (bf16[8,1536]{1,0:T(8,128)(2,1)S(1)}, bf16[8,1536]{1,0:T(8,128)(2,1)S(1)}, u32[]{:S(2)}, u32[]{:S(2)}) collective-permute-start(bf16[8,1536]{1,0:T(8,128)(2,1)S(1)} %dynamic-slice_convert_fusion.3), channel_id=1, source_target_pairs={{0,2},{2,0},{1,3},{3,1},{4,6},{6,4},{5,7},{7,5},{8,10},{10,8},{9,1... | collective-permute-start | bytes 73736 | tf_op jit(solution)/shard_map/ppermute | solution.py:42
  196.2 1.5 fusion.18
  197.7 1.6 fusion.1
  199.4 2.1 %collective-permute-done.14 = bf16[8,1536]{1,0:T(8,128)(2,1)S(1)} collective-permute-done((bf16[8,1536]{1,0:T(8,128)(2,1)S(1)}, bf16[8,1536]{1,0:T(8,128)(2,1)S(1)}, u32[]{:S(2)}, u32[]{:S(2)}) %collective-permute-start.14) | collective-permute-done | bytes 24608 | tf_op jit(solution)/shard_map/ppermute | solution.py:42
  201.5 0.6 add_convert_fusion.1
  (26 shorter events, 0.2 us)
Async XLA Ops:
  2.1 17.7 %collective-permute-start = (bf16[8,2304]{1,0:T(8,128)(2,1)S(1)}, bf16[8,2304]{1,0:T(8,128)(2,1)S(1)}, u32[]{:S(2)}, u32[]{:S(2)}) collective-permute-start(bf16[8,2304]{1,0:T(8,128)(2,1)S(1)} %pad_maximum_fusion.1), channel_id=1, source_target_pairs={{0,2},{2,0},{1,3},{3,1},{4,6},{6,4},{5,7},{7,5},{8,10},{10,8},{9,1... | collective-permute-start | bytes 110600 | tf_op jit(solution)/shard_map/ppermute | solution.py:42
  20.7 10.9 %collective-permute-start.1 = (bf16[1536,384]{1,0:T(8,128)(2,1)}, bf16[1536,384]{1,0:T(8,128)(2,1)}, u32[]{:S(2)}, u32[]{:S(2)}) collective-permute-start(bf16[1536,384]{1,0:T(8,128)(2,1)} %param.9), channel_id=1, source_target_pairs={{0,1},{1,0},{2,3},{3,2},{4,5},{5,4},{6,7},{7,6},{8,9},{9,8},{10,11... | collective-permute-start | bytes 3538952 | tf_op jit(solution)/shard_map/ppermute | solution.py:42
  27.1 13.6 %all-to-all-start = ((bf16[16,16,768]{2,1,0:T(8,128)(2,1)}), bf16[16,16,768]{2,1,0:T(8,128)(2,1)S(1)}, u32[]{:S(2)}, u32[]{:S(2)}) async-start(bf16[16,16,768]{2,1,0:T(8,128)(2,1)} %broadcast_in_dim.6), calls=%async_computation | async-start | bytes 786432 | tf_op jit(solution)/shard_map/all_to_all | solution.py:72
  41.5 1.2 copy-start
  42.7 16.5 %copy-start.1 = (f32[2,2,64,1536]{3,2,1,0:T(8,128)S(1)}, f32[2,2,64,1536]{3,2,1,0:T(8,128)}, u32[]{:S(2)}) copy-start(f32[2,2,64,1536]{3,2,1,0:T(8,128)} %copy-done) | copy-start | bytes 4718596
  42.7 21.2 %collective-permute-start.3 = (bf16[1536,384]{1,0:T(8,128)(2,1)}, bf16[1536,384]{1,0:T(8,128)(2,1)}, u32[]{:S(2)}, u32[]{:S(2)}) collective-permute-start(bf16[1536,384]{1,0:T(8,128)(2,1)} %param.7), channel_id=1, source_target_pairs={{0,1},{1,0},{2,3},{3,2},{4,5},{5,4},{6,7},{7,6},{8,9},{9,8},{10,11... | collective-permute-start | bytes 3538952 | tf_op jit(solution)/shard_map/ppermute | solution.py:42
  46.4 12.7 %collective-permute-start.2 = (bf16[2,1,64,1536]{3,2,1,0:T(8,128)(2,1)S(1)}, bf16[2,1,64,1536]{3,2,1,0:T(8,128)(2,1)}, u32[]{:S(2)}, u32[]{:S(2)}) collective-permute-start(bf16[2,1,64,1536]{3,2,1,0:T(8,128)(2,1)S(1)} %dynamic-slice_convert_fusion), channel_id=1, source_target_pairs={{0,64},{64,0},{1,65},{65,1},{2,66},{66,2},{3,67},{67,3},{4,68},{68... | collective-permute-start | bytes 1179656 | tf_op jit(solution)/shard_map/ppermute | solution.py:42
  50.5 17.5 %all-to-all-start.1 = ((bf16[16,16,1536]{2,1,0:T(8,128)(2,1)}), bf16[16,16,1536]{2,1,0:T(8,128)(2,1)S(1)}, u32[]{:S(2)}, u32[]{:S(2)}) async-start(bf16[16,16,1536]{2,1,0:T(8,128)(2,1)} %broadcast_in_dim.7), calls=%async_computation.1 | async-start | bytes 1572864 | tf_op jit(solution)/shard_map/all_to_all | solution.py:72
  60.3 12.9 %collective-permute-start.4 = (bf16[1,1,64,1536]{3,2,1,0:T(8,128)(2,1)S(1)}, bf16[1,1,64,1536]{3,2,1,0:T(8,128)(2,1)S(1)}, u32[]{:S(2)}, u32[]{:S(2)}) collective-permute-start(bf16[1,1,64,1536]{3,2,1,0:T(8,128)(2,1)S(1)} %dynamic-slice_convert_fusion.1), channel_id=1, source_target_pairs={{0,128},{128,0},{1,129},{129,1},{2,130},{130,2},{3,131},{131,3},{4... | collective-permute-start | bytes 589832 | tf_op jit(solution)/shard_map/ppermute | solution.py:42
  71.2 29.3 %copy-start.4 = (f32[1536]{0:T(1024)S(1)}, f32[1536]{0:T(1024)}, u32[]{:S(2)}) copy-start(f32[1536]{0:T(1024)} %param.8) | copy-start | bytes 18436
  73.2 20.7 %all-to-all-start.2 = ((bf16[4,64,768]{2,1,0:T(8,128)(2,1)}), bf16[4,64,768]{2,1,0:T(8,128)(2,1)}, u32[]{:S(2)}, u32[]{:S(2)}) async-start(bf16[4,64,768]{2,1,0:T(8,128)(2,1)} %bitcast.5), calls=%async_computation.2 | async-start | bytes 786432 | tf_op jit(solution)/shard_map/all_to_all | solution.py:78
  77.4 61.6 %copy-start.2 = (bf16[1536,768]{1,0:T(8,128)(2,1)S(1)}, bf16[1536,768]{1,0:T(8,128)(2,1)}, u32[]{:S(2)}) copy-start(bf16[1536,768]{1,0:T(8,128)(2,1)} %maximum_select_fusion.1) | copy-start | bytes 7077892
  77.4 15.8 %collective-permute-start.5 = (bf16[64,768]{1,0:T(8,128)(2,1)S(1)}, bf16[64,768]{1,0:T(8,128)(2,1)S(1)}, u32[]{:S(2)}, u32[]{:S(2)}) collective-permute-start(bf16[64,768]{1,0:T(8,128)(2,1)S(1)} %fusion.15), channel_id=1, source_target_pairs={{0,258},{2,256},{256,2},{258,0},{1,259},{3,257},{257,3},{259,1},{4... | collective-permute-start | bytes 294920 | tf_op jit(solution)/shard_map/ppermute | solution.py:66
  95.9 10.3 %collective-permute-start.6 = (bf16[64,1536]{1,0:T(8,128)(2,1)S(1)}, bf16[64,1536]{1,0:T(8,128)(2,1)S(1)}, u32[]{:S(2)}, u32[]{:S(2)}) collective-permute-start(bf16[64,1536]{1,0:T(8,128)(2,1)S(1)} %pad_maximum_fusion), channel_id=1, source_target_pairs={{0,256},{256,0},{1,257},{257,1},{2,258},{258,2},{3,259},{259,3},{4... | collective-permute-start | bytes 589832 | tf_op jit(solution)/shard_map/ppermute | solution.py:42
  108.7 30.3 %all-to-all-start.3 = ((bf16[4,64,768]{2,1,0:T(8,128)(2,1)}), bf16[4,64,768]{2,1,0:T(8,128)(2,1)}, u32[]{:S(2)}, u32[]{:S(2)}) async-start(bf16[4,64,768]{2,1,0:T(8,128)(2,1)} %broadcast_in_dim.8), calls=%async_computation.3 | async-start | bytes 786432 | tf_op jit(solution)/shard_map/all_to_all | solution.py:72
  125.3 13.7 %collective-permute-start.7 = (bf16[256,1536]{1,0:T(8,128)(2,1)S(1)}, bf16[256,1536]{1,0:T(8,128)(2,1)}, u32[]{:S(2)}, u32[]{:S(2)}) collective-permute-start(bf16[256,1536]{1,0:T(8,128)(2,1)S(1)} %bitcast.44), channel_id=1, source_target_pairs={{0,1},{1,0},{2,3},{3,2},{4,5},{5,4},{6,7},{7,6},{8,9},{9,8},{10,11... | collective-permute-start | bytes 2359304 | tf_op jit(solution)/shard_map/ppermute | solution.py:42
  132.6 6.3 %collective-permute-start.8 = (bf16[256,384]{1,0:T(8,128)(2,1)}, bf16[256,384]{1,0:T(8,128)(2,1)}, u32[]{:S(2)}, u32[]{:S(2)}) collective-permute-start(bf16[256,384]{1,0:T(8,128)(2,1)} %constant_dynamic-slice_fusion.2), channel_id=1, source_target_pairs={{0,1},{1,0},{2,3},{3,2},{4,5},{5,4},{6,7},{7,6},{8,9},{9,8},{10,11... | collective-permute-start | bytes 589832 | tf_op jit(solution)/shard_map/ppermute | solution.py:42
  134.6 10.0 %collective-permute-start.9 = (bf16[64,768]{1,0:T(8,128)(2,1)}, bf16[64,768]{1,0:T(8,128)(2,1)}, u32[]{:S(2)}, u32[]{:S(2)}) collective-permute-start(bf16[64,768]{1,0:T(8,128)(2,1)} %get-tuple-element.41), channel_id=1, source_target_pairs={{0,258},{2,256},{256,2},{258,0},{1,259},{3,257},{257,3},{259,1},{4... | collective-permute-start | bytes 294920 | tf_op jit(solution)/shard_map/ppermute | solution.py:66
  141.7 7.5 %copy-start.3 = (bf16[64,768]{1,0:T(8,128)(2,1)S(1)}, bf16[64,768]{1,0:T(8,128)(2,1)}, u32[]{:S(2)}) copy-start(bf16[64,768]{1,0:T(8,128)(2,1)} %get-tuple-element.41) | copy-start | bytes 294916
  144.6 40.1 %all-to-all-start.4 = ((bf16[16,16,1536]{2,1,0:T(8,128)(2,1)}), bf16[16,16,1536]{2,1,0:T(8,128)(2,1)S(1)}, u32[]{:S(2)}, u32[]{:S(2)}) async-start(bf16[16,16,1536]{2,1,0:T(8,128)(2,1)} %bitcast.48), calls=%async_computation.4 | async-start | bytes 1572864 | tf_op jit(solution)/shard_map/all_to_all | solution.py:127
  150.2 18.0 %collective-permute-start.10 = (bf16[1,1,64,1536]{3,2,1,0:T(8,128)(2,1)S(1)}, bf16[1,1,64,1536]{3,2,1,0:T(8,128)(2,1)S(1)}, u32[]{:S(2)}, u32[]{:S(2)}) collective-permute-start(bf16[1,1,64,1536]{3,2,1,0:T(8,128)(2,1)S(1)} %maximum_select_fusion.5), channel_id=1, source_target_pairs={{0,128},{128,0},{1,129},{129,1},{2,130},{130,2},{3,131},{131,3},{4... | collective-permute-start | bytes 589832 | tf_op jit(solution)/shard_map/ppermute | solution.py:42
  168.2 6.1 %collective-permute-start.11 = (bf16[256,384]{1,0:T(8,128)(2,1)S(1)}, bf16[256,384]{1,0:T(8,128)(2,1)S(1)}, u32[]{:S(2)}, u32[]{:S(2)}) collective-permute-start(bf16[256,384]{1,0:T(8,128)(2,1)S(1)} %constant_dynamic-slice_fusion), channel_id=1, source_target_pairs={{0,1},{1,0},{2,3},{3,2},{4,5},{5,4},{6,7},{7,6},{8,9},{9,8},{10,11... | collective-permute-start | bytes 589832 | tf_op jit(solution)/shard_map/ppermute | solution.py:42
  171.9 12.6 %collective-permute-start.12 = (bf16[2,1,64,1536]{3,2,1,0:T(8,128)(2,1)S(1)}, bf16[2,1,64,1536]{3,2,1,0:T(8,128)(2,1)S(1)}, u32[]{:S(2)}, u32[]{:S(2)}) collective-permute-start(bf16[2,1,64,1536]{3,2,1,0:T(8,128)(2,1)S(1)} %maximum_select_fusion.3), channel_id=1, source_target_pairs={{0,64},{64,0},{1,65},{65,1},{2,66},{66,2},{3,67},{67,3},{4,68},{68... | collective-permute-start | bytes 1179656 | tf_op jit(solution)/shard_map/ppermute | solution.py:42
  184.8 11.4 %collective-permute-start.13 = (bf16[256,1536]{1,0:T(8,128)(2,1)S(1)}, bf16[256,1536]{1,0:T(8,128)(2,1)S(1)}, u32[]{:S(2)}, u32[]{:S(2)}) collective-permute-start(bf16[256,1536]{1,0:T(8,128)(2,1)S(1)} %bitcast.41), channel_id=1, source_target_pairs={{0,1},{1,0},{2,3},{3,2},{4,5},{5,4},{6,7},{7,6},{8,9},{9,8},{10,11... | collective-permute-start | bytes 2359304 | tf_op jit(solution)/shard_map/ppermute | solution.py:42
  187.5 14.0 %collective-permute-start.14 = (bf16[8,1536]{1,0:T(8,128)(2,1)S(1)}, bf16[8,1536]{1,0:T(8,128)(2,1)S(1)}, u32[]{:S(2)}, u32[]{:S(2)}) collective-permute-start(bf16[8,1536]{1,0:T(8,128)(2,1)S(1)} %dynamic-slice_convert_fusion.3), channel_id=1, source_target_pairs={{0,2},{2,0},{1,3},{3,1},{4,6},{6,4},{5,7},{7,5},{8,10},{10,8},{9,1... | collective-permute-start | bytes 73736 | tf_op jit(solution)/shard_map/ppermute | solution.py:42

commit v14 on v11

--- a/solution.py
+++ b/solution.py
@@ -127,9 +127,9 @@
     dealt = lax.all_to_all(part.reshape(-1, 2 * tok_dev, feat), GRID, 0, 0, tiled=True)
 
     own_grad = part_of(grad, core, quarter, 1)
-    act = join(act, crossed, "zh", 1)[None, None]
-    act = join(act, after(part, swap(act, "rm")), "rm", 0)
-    own_part = over_rows(every_x, own_grad)
+    act = join(act, after(part, crossed), "zh", 1)[None, None]
+    act = join(act, swap(act, "rm"), "rm", 0)
+    own_part = over_rows(every_x, after(act, own_grad))
     pair_grad = swap(after(own_part, part_of(grad, 1 - core, quarter, 1)), "core")
     act = join(act, after(dealt, swap(after(own_part, act), "rl")), "rl", 1).reshape(-1, act.shape[-1])
     w_in_grad = (own_part + over_rows(pair_x, pair_grad)).astype(bf16)

time: 192 us -> 202 us (1.052)
  other arithmetic: 14.5 us -> 21.1 us
  starting transfers between devices: 122 us -> 126 us
  waiting for transfers between devices: 35.1 us -> 31.1 us
    ppermute x2, waiting for transfers between devices: 8.46 us -> 5 us  [cross(): return lax.ppermute(value, ('rh', 'zh'), CROSS)]
    dot_general x4, matrix products: 4.49 us -> 7.67 us  [over_rows(): lax.dot_general(left, right, (((0,), (0,)), ((), ())), preferred_element_...]
    ppermute x13, starting transfers between devices: 68.7 us -> 71.8 us  [swap(): return lax.ppermute(value, axis, SWAP)]
  transfers between devices with their start and end apart: 20 -> 20, of which waited for: 9 -> 10; matrix products, arithmetic and copies ran while one was open for 13% -> 16% of each run, Pallas kernels for 0% -> 0%
where the time goes in v14:
time: 202 us; the launch traced here: 201 us
  starting transfers between devices  126 us (62%)
  waiting for transfers between devices  31.1 us (15%)
  other arithmetic  21.1 us (10%)
  matrix products  13.6 us (7%)
  local copies, waits for them, and re-layouts  7.45 us (4%)
    ppermute x13, starting transfers between devices, swap(): return lax.ppermute(value, axis, SWAP)  71.8 us
    all_to_all x3, starting transfers between devices, spread(): got = lax.all_to_all(sent, axes, 0, 0, tiled=True)  25.9 us
    ppermute x2, starting transfers between devices, cross(): return lax.ppermute(value, ('rh', 'zh'), CROSS)  20.9 us
    ppermute x13, waiting for transfers between devices, swap(): return lax.ppermute(value, axis, SWAP)  20 us
    select_n x6, other arithmetic, join(): jnp.where(first, jnp.concatenate([mine, other], dim), jnp.concatenate([ot...  11.2 us
    dot_general x4, matrix products, over_rows(): lax.dot_general(left, right, (((0,), (0,)), ((), ())), preferred_element_...  7.67 us
    all_to_all x3, waiting for transfers between devices, spread(): got = lax.all_to_all(sent, axes, 0, 0, tiled=True)  6.17 us
    ppermute x2, waiting for transfers between devices, cross(): return lax.ppermute(value, ('rh', 'zh'), CROSS)  5 us
  transfers between devices with their start and end apart: 20, of which 10 were waited for; matrix products, arithmetic and copies ran while one was open for 16% of the time, Pallas kernels for 0%

profile of v14, /device:TPU:1, one launch (start us, length us, event | category | flops | bytes accessed | tf_op | source)
XLA Modules:
  0.0 200.7 jit_solution(1873602156576836464)
XLA Ops:
  0.6 0.7 constant_dynamic-slice_fusion.4
  1.4 0.7 pad_maximum_fusion.1
  2.1 16.3 %collective-permute-start = (bf16[8,2304]{1,0:T(8,128)(2,1)S(1)}, bf16[8,2304]{1,0:T(8,128)(2,1)S(1)}, u32[]{:S(2)}, u32[]{:S(2)}) collective-permute-start(bf16[8,2304]{1,0:T(8,128)(2,1)S(1)} %pad_maximum_fusion.1), channel_id=1, source_target_pairs={{0,2},{2,0},{1,3},{3,1},{4,6},{6,4},{5,7},{7,5},{8,10},{10,8},{9,1... | collective-permute-start | bytes 110600 | tf_op jit(solution)/shard_map/ppermute | solution.py:42
  18.4 1.5 collective-permute-done
  19.9 0.8 maximum_select_fusion.6
  20.7 5.6 %collective-permute-start.1 = (bf16[1536,384]{1,0:T(8,128)(2,1)}, bf16[1536,384]{1,0:T(8,128)(2,1)}, u32[]{:S(2)}, u32[]{:S(2)}) collective-permute-start(bf16[1536,384]{1,0:T(8,128)(2,1)} %param.9), channel_id=1, source_target_pairs={{0,1},{1,0},{2,3},{3,2},{4,5},{5,4},{6,7},{7,6},{8,9},{9,8},{10,11... | collective-permute-start | bytes 3538952 | tf_op jit(solution)/shard_map/ppermute | solution.py:42
  26.3 0.8 broadcast_in_dim.6
  27.1 4.5 %all-to-all-start = ((bf16[16,16,768]{2,1,0:T(8,128)(2,1)}), bf16[16,16,768]{2,1,0:T(8,128)(2,1)S(1)}, u32[]{:S(2)}, u32[]{:S(2)}) async-start(bf16[16,16,768]{2,1,0:T(8,128)(2,1)} %broadcast_in_dim.6), calls=%async_computation | async-start | bytes 786432 | tf_op jit(solution)/shard_map/all_to_all | solution.py:72
  31.6 2.9 %maximum_select_fusion = bf16[1536,768]{1,0:T(8,128)(2,1)S(1)} fusion(bf16[1536,384]{1,0:T(8,128)(2,1)} %collective-permute-done.1, bf16[1536,384]{1,0:T(8,128)(2,1)} %param.9, pred[]{:T(512)S(6)} %eq.15), kind=kLoop, calls=%fused_computation.5 | loop fusion | flops 10616832 | bytes 4718593 | tf_op jit(solution)/shard_map/jit(_where)/select_n | solution.py:47
  34.5 6.2 %all-to-all-done = bf16[16,16,768]{2,1,0:T(8,128)(2,1)S(1)} async-done(((bf16[16,16,768]{2,1,0:T(8,128)(2,1)}), bf16[16,16,768]{2,1,0:T(8,128)(2,1)S(1)}, u32[]{:S(2)}, u32[]{:S(2)}) %all-to-all-start) | async-done | bytes 393248 | tf_op jit(solution)/shard_map/all_to_all | solution.py:72
  40.7 0.8 fusion.2
  41.5 1.2 copy-done
  42.8 3.7 %collective-permute-start.3 = (bf16[1536,384]{1,0:T(8,128)(2,1)}, bf16[1536,384]{1,0:T(8,128)(2,1)}, u32[]{:S(2)}, u32[]{:S(2)}) collective-permute-start(bf16[1536,384]{1,0:T(8,128)(2,1)} %param.7), channel_id=1, source_target_pairs={{0,1},{1,0},{2,3},{3,2},{4,5},{5,4},{6,7},{7,6},{8,9},{9,8},{10,11... | collective-permute-start | bytes 3538952 | tf_op jit(solution)/shard_map/ppermute | solution.py:42
  46.5 3.1 %collective-permute-start.2 = (bf16[2,1,64,1536]{3,2,1,0:T(8,128)(2,1)S(1)}, bf16[2,1,64,1536]{3,2,1,0:T(8,128)(2,1)}, u32[]{:S(2)}, u32[]{:S(2)}) collective-permute-start(bf16[2,1,64,1536]{3,2,1,0:T(8,128)(2,1)S(1)} %dynamic-slice_convert_fusion), channel_id=1, source_target_pairs={{0,64},{64,0},{1,65},{65,1},{2,66},{66,2},{3,67},{67,3},{4,68},{68... | collective-permute-start | bytes 1179656 | tf_op jit(solution)/shard_map/ppermute | solution.py:42
  49.6 0.8 slice.33
  50.4 1.0 broadcast_in_dim.7
  51.4 3.6 %all-to-all-start.1 = ((bf16[16,16,1536]{2,1,0:T(8,128)(2,1)}), bf16[16,16,1536]{2,1,0:T(8,128)(2,1)S(1)}, u32[]{:S(2)}, u32[]{:S(2)}) async-start(bf16[16,16,1536]{2,1,0:T(8,128)(2,1)} %broadcast_in_dim.7), calls=%async_computation.1 | async-start | bytes 1572864 | tf_op jit(solution)/shard_map/all_to_all | solution.py:72
  55.0 4.2 %collective-permute-done.2 = bf16[2,1,64,1536]{3,2,1,0:T(8,128)(2,1)} collective-permute-done((bf16[2,1,64,1536]{3,2,1,0:T(8,128)(2,1)S(1)}, bf16[2,1,64,1536]{3,2,1,0:T(8,128)(2,1)}, u32[]{:S(2)}, u32[]{:S(2)}) %collective-permute-start.2) | collective-permute-done | bytes 393248 | tf_op jit(solution)/shard_map/ppermute | solution.py:42
  59.2 1.1 convert_add_fusion
  60.3 3.6 %collective-permute-start.6 = (bf16[1,1,64,1536]{3,2,1,0:T(8,128)(2,1)S(1)}, bf16[1,1,64,1536]{3,2,1,0:T(8,128)(2,1)S(1)}, u32[]{:S(2)}, u32[]{:S(2)}) collective-permute-start(bf16[1,1,64,1536]{3,2,1,0:T(8,128)(2,1)S(1)} %dynamic-slice_convert_fusion.1), channel_id=1, source_target_pairs={{0,128},{128,0},{1,129},{129,1},{2,130},{130,2},{3,131},{131,3},{4... | collective-permute-start | bytes 589832 | tf_op jit(solution)/shard_map/ppermute | solution.py:42
  64.0 4.1 %maximum_select_fusion.1 = bf16[1536,768]{1,0:T(8,128)(2,1)} fusion(bf16[1536,384]{1,0:T(8,128)(2,1)} %collective-permute-done.3, bf16[1536,384]{1,0:T(8,128)(2,1)} %param.7, pred[]{:T(512)S(6)} %eq.15), kind=kLoop, calls=%fused_computation.6 | loop fusion | flops 10616832 | bytes 4718593 | tf_op jit(solution)/shard_map/jit(_where)/select_n | solution.py:47
  68.0 3.5 %convolution_convert_fusion.1 = bf16[256,768]{1,0:T(8,128)(2,1)} fusion(bf16[256,1536]{1,0:T(8,128)(2,1)S(1)} %bitcast.41, bf16[1536,768]{1,0:T(8,128)(2,1)} %maximum_select_fusion.1), kind=kOutput, calls=%fused_computation.10 | convolution fusion | flops 604176384 | bytes 3538944 | tf_op jit(solution)/shard_map/dot_general | solution.py:26
  71.5 1.7 collective-permute-done.6
  73.2 4.1 %all-to-all-start.2 = ((bf16[4,64,768]{2,1,0:T(8,128)(2,1)}), bf16[4,64,768]{2,1,0:T(8,128)(2,1)}, u32[]{:S(2)}, u32[]{:S(2)}) async-start(bf16[4,64,768]{2,1,0:T(8,128)(2,1)} %bitcast.5), calls=%async_computation.2 | async-start | bytes 786432 | tf_op jit(solution)/shard_map/all_to_all | solution.py:78
  77.4 3.4 %collective-permute-start.4 = (bf16[256,1536]{1,0:T(8,128)(2,1)S(1)}, bf16[256,1536]{1,0:T(8,128)(2,1)}, u32[]{:S(2)}, u32[]{:S(2)}) collective-permute-start(bf16[256,1536]{1,0:T(8,128)(2,1)S(1)} %bitcast.42), channel_id=1, source_target_pairs={{0,1},{1,0},{2,3},{3,2},{4,5},{5,4},{6,7},{7,6},{8,9},{9,8},{10,11... | collective-permute-start | bytes 2359304 | tf_op jit(solution)/shard_map/ppermute | solution.py:42
  80.8 9.5 %collective-permute-start.7 = (bf16[64,768]{1,0:T(8,128)(2,1)S(1)}, bf16[64,768]{1,0:T(8,128)(2,1)S(1)}, u32[]{:S(2)}, u32[]{:S(2)}) collective-permute-start(bf16[64,768]{1,0:T(8,128)(2,1)S(1)} %fusion.16), channel_id=1, source_target_pairs={{0,258},{2,256},{256,2},{258,0},{1,259},{3,257},{257,3},{259,1},{4... | collective-permute-start | bytes 294920 | tf_op jit(solution)/shard_map/ppermute | solution.py:66
  90.3 0.7 constant_dynamic-slice_fusion.2
  91.0 2.2 %collective-permute-start.5 = (bf16[256,384]{1,0:T(8,128)(2,1)}, bf16[256,384]{1,0:T(8,128)(2,1)}, u32[]{:S(2)}, u32[]{:S(2)}) collective-permute-start(bf16[256,384]{1,0:T(8,128)(2,1)} %constant_dynamic-slice_fusion.2), channel_id=1, source_target_pairs={{0,1},{1,0},{2,3},{3,2},{4,5},{5,4},{6,7},{7,6},{8,9},{9,8},{10,11... | collective-permute-start | bytes 589832 | tf_op jit(solution)/shard_map/ppermute | solution.py:42
  93.2 0.3 collective-permute-done.7
  93.5 0.6 fusion.12
  94.1 1.1 fusion.15
  95.2 0.9 pad_maximum_fusion
  96.1 6.6 %collective-permute-start.8 = (bf16[64,1536]{1,0:T(8,128)(2,1)S(1)}, bf16[64,1536]{1,0:T(8,128)(2,1)S(1)}, u32[]{:S(2)}, u32[]{:S(2)}) collective-permute-start(bf16[64,1536]{1,0:T(8,128)(2,1)S(1)} %pad_maximum_fusion), channel_id=1, source_target_pairs={{0,256},{256,0},{1,257},{257,1},{2,258},{258,2},{3,259},{259,3},{4... | collective-permute-start | bytes 589832 | tf_op jit(solution)/shard_map/ppermute | solution.py:42
  102.8 3.7 %collective-permute-done.8 = bf16[64,1536]{1,0:T(8,128)(2,1)S(1)} collective-permute-done((bf16[64,1536]{1,0:T(8,128)(2,1)S(1)}, bf16[64,1536]{1,0:T(8,128)(2,1)S(1)}, u32[]{:S(2)}, u32[]{:S(2)}) %collective-permute-start.8) | collective-permute-done | bytes 196640 | tf_op jit(solution)/shard_map/ppermute | solution.py:42
  106.5 0.9 convert_add_fusion.1
  107.4 0.2 multiply_convert_fusion
  107.6 0.8 broadcast_in_dim.8
  108.3 17.7 %all-to-all-start.3 = ((bf16[4,64,768]{2,1,0:T(8,128)(2,1)}), bf16[4,64,768]{2,1,0:T(8,128)(2,1)S(1)}, u32[]{:S(2)}, u32[]{:S(2)}) async-start(bf16[4,64,768]{2,1,0:T(8,128)(2,1)} %broadcast_in_dim.8), calls=%async_computation.3 | async-start | bytes 786432 | tf_op jit(solution)/shard_map/all_to_all | solution.py:72
  126.1 11.5 %collective-permute-start.9 = (bf16[64,768]{1,0:T(8,128)(2,1)S(1)}, bf16[64,768]{1,0:T(8,128)(2,1)S(1)}, u32[]{:S(2)}, u32[]{:S(2)}) collective-permute-start(bf16[64,768]{1,0:T(8,128)(2,1)S(1)} %get-tuple-element.38), channel_id=1, source_target_pairs={{0,258},{2,256},{256,2},{258,0},{1,259},{3,257},{257,3},{259,1},{4... | collective-permute-start | bytes 294920 | tf_op jit(solution)/shard_map/ppermute | solution.py:66
  137.6 1.7 convolution_convert_fusion
  139.3 0.7 constant_dynamic-slice_fusion
  140.0 4.7 %collective-permute-done.9 = bf16[64,768]{1,0:T(8,128)(2,1)S(1)} collective-permute-done((bf16[64,768]{1,0:T(8,128)(2,1)S(1)}, bf16[64,768]{1,0:T(8,128)(2,1)S(1)}, u32[]{:S(2)}, u32[]{:S(2)}) %collective-permute-start.9) | collective-permute-done | bytes 98336 | tf_op jit(solution)/shard_map/ppermute | solution.py:66
  144.7 0.6 copy-done.7
  145.3 3.6 %all-to-all-start.4 = ((bf16[16,16,1536]{2,1,0:T(8,128)(2,1)}), bf16[16,16,1536]{2,1,0:T(8,128)(2,1)S(1)}, u32[]{:S(2)}, u32[]{:S(2)}) async-start(bf16[16,16,1536]{2,1,0:T(8,128)(2,1)} %bitcast.51), calls=%async_computation.4 | async-start | bytes 1572864 | tf_op jit(solution)/shard_map/all_to_all | solution.py:127
  149.0 1.0 convert_reduce_fusion.2
  149.9 1.1 maximum_select_fusion.5
  151.0 3.1 %collective-permute-start.10 = (bf16[1,1,64,1536]{3,2,1,0:T(8,128)(2,1)S(1)}, bf16[1,1,64,1536]{3,2,1,0:T(8,128)(2,1)S(1)}, u32[]{:S(2)}, u32[]{:S(2)}) collective-permute-start(bf16[1,1,64,1536]{3,2,1,0:T(8,128)(2,1)S(1)} %maximum_select_fusion.5), channel_id=1, source_target_pairs={{0,128},{128,0},{1,129},{129,1},{2,130},{130,2},{3,131},{131,3},{4... | collective-permute-start | bytes 589832 | tf_op jit(solution)/shard_map/ppermute | solution.py:42
  154.2 1.0 fusion.11
  155.2 3.5 %collective-permute-done.10 = bf16[1,1,64,1536]{3,2,1,0:T(8,128)(2,1)S(1)} collective-permute-done((bf16[1,1,64,1536]{3,2,1,0:T(8,128)(2,1)S(1)}, bf16[1,1,64,1536]{3,2,1,0:T(8,128)(2,1)S(1)}, u32[]{:S(2)}, u32[]{:S(2)}) %collective-permute-start.10) | collective-permute-done | bytes 196640 | tf_op jit(solution)/shard_map/ppermute | solution.py:42
  158.6 0.8 maximum_select_fusion.3
  159.4 1.7 fusion.18
  161.2 7.4 %collective-permute-start.11 = (bf16[256,384]{1,0:T(8,128)(2,1)}, bf16[256,384]{1,0:T(8,128)(2,1)}, u32[]{:S(2)}, u32[]{:S(2)}) collective-permute-start(bf16[256,384]{1,0:T(8,128)(2,1)} %constant_dynamic-slice_fusion), channel_id=1, source_target_pairs={{0,1},{1,0},{2,3},{3,2},{4,5},{5,4},{6,7},{7,6},{8,9},{9,8},{10,11... | collective-permute-start | bytes 589832 | tf_op jit(solution)/shard_map/ppermute | solution.py:42
  168.6 4.3 %collective-permute-start.12 = (bf16[2,1,64,1536]{3,2,1,0:T(8,128)(2,1)}, bf16[2,1,64,1536]{3,2,1,0:T(8,128)(2,1)}, u32[]{:S(2)}, u32[]{:S(2)}) collective-permute-start(bf16[2,1,64,1536]{3,2,1,0:T(8,128)(2,1)} %maximum_select_fusion.3), channel_id=1, source_target_pairs={{0,64},{64,0},{1,65},{65,1},{2,66},{66,2},{3,67},{67,3},{4,68},{68... | collective-permute-start | bytes 1179656 | tf_op jit(solution)/shard_map/ppermute | solution.py:42
  172.9 1.0 convert_reduce_fusion.1
  173.9 0.6 add.119
  174.5 2.8 %fusion = bf16[1536,384]{1,0:T(8,128)(2,1)} fusion(f32[1536,384]{1,0:T(8,128)S(1)} %fusion.18, bf16[256,1536]{1,0:T(8,128)(2,1)} %collective-permute-done.4, bf16[256,384]{1,0:T(8,128)(2,1)} %collective-permute-done.11), kind=kOutput, calls=%fused_computation.2 | convolution fusion | flops 303169536 | bytes 4521984 | tf_op jit(solution)/shard_map/dot_general | solution.py:34
  177.3 0.1 convert_reduce_fusion
  177.4 5.3 %collective-permute-done.12 = bf16[2,1,64,1536]{3,2,1,0:T(8,128)(2,1)} collective-permute-done((bf16[2,1,64,1536]{3,2,1,0:T(8,128)(2,1)}, bf16[2,1,64,1536]{3,2,1,0:T(8,128)(2,1)}, u32[]{:S(2)}, u32[]{:S(2)}) %collective-permute-start.12) | collective-permute-done | bytes 393248 | tf_op jit(solution)/shard_map/ppermute | solution.py:42
  182.7 1.5 maximum_select_fusion.2
  184.2 2.5 %collective-permute-start.13 = (bf16[256,1536]{1,0:T(8,128)(2,1)S(1)}, bf16[256,1536]{1,0:T(8,128)(2,1)S(1)}, u32[]{:S(2)}, u32[]{:S(2)}) collective-permute-start(bf16[256,1536]{1,0:T(8,128)(2,1)S(1)} %bitcast.44), channel_id=1, source_target_pairs={{0,1},{1,0},{2,3},{3,2},{4,5},{5,4},{6,7},{7,6},{8,9},{9,8},{10,11... | collective-permute-start | bytes 2359304 | tf_op jit(solution)/shard_map/ppermute | solution.py:42
  186.7 10.1 %collective-permute-start.14 = (bf16[8,1536]{1,0:T(8,128)(2,1)S(1)}, bf16[8,1536]{1,0:T(8,128)(2,1)S(1)}, u32[]{:S(2)}, u32[]{:S(2)}) collective-permute-start(bf16[8,1536]{1,0:T(8,128)(2,1)S(1)} %dynamic-slice_convert_fusion.3), channel_id=1, source_target_pairs={{0,2},{2,0},{1,3},{3,1},{4,6},{6,4},{5,7},{7,5},{8,10},{10,8},{9,1... | collective-permute-start | bytes 73736 | tf_op jit(solution)/shard_map/ppermute | solution.py:42
  196.8 0.6 fusion.13
  197.4 2.6 %fusion.1 = bf16[1536,384]{1,0:T(8,128)(2,1)} fusion(f32[1536,384]{1,0:T(8,128)S(1)} %fusion.13, bf16[256,1536]{1,0:T(8,128)(2,1)S(1)} %collective-permute-done.13, bf16[256,384]{1,0:T(8,128)(2,1)} %collective-permute-done.5), kind=kOutput, calls=%fused_computation.3 | convolution fusion | flops 303169536 | bytes 4521984 | tf_op jit(solution)/shard_map/dot_general | solution.py:34
  200.1 0.6 add_convert_fusion.1
  (36 shorter events, 0.4 us)
Async XLA Ops:
  2.1 17.7 %collective-permute-start = (bf16[8,2304]{1,0:T(8,128)(2,1)S(1)}, bf16[8,2304]{1,0:T(8,128)(2,1)S(1)}, u32[]{:S(2)}, u32[]{:S(2)}) collective-permute-start(bf16[8,2304]{1,0:T(8,128)(2,1)S(1)} %pad_maximum_fusion.1), channel_id=1, source_target_pairs={{0,2},{2,0},{1,3},{3,1},{4,6},{6,4},{5,7},{7,5},{8,10},{10,8},{9,1... | collective-permute-start | bytes 110600 | tf_op jit(solution)/shard_map/ppermute | solution.py:42
  20.7 6.4 %copy-start.8 = (bf16[16,2304]{1,0:T(8,128)(2,1)}, bf16[16,2304]{1,0:T(8,128)(2,1)S(1)}, u32[]{:S(2)}) copy-start(bf16[16,2304]{1,0:T(8,128)(2,1)S(1)} %maximum_select_fusion.6) | copy-start | bytes 221188
  20.7 10.9 %collective-permute-start.1 = (bf16[1536,384]{1,0:T(8,128)(2,1)}, bf16[1536,384]{1,0:T(8,128)(2,1)}, u32[]{:S(2)}, u32[]{:S(2)}) collective-permute-start(bf16[1536,384]{1,0:T(8,128)(2,1)} %param.9), channel_id=1, source_target_pairs={{0,1},{1,0},{2,3},{3,2},{4,5},{5,4},{6,7},{7,6},{8,9},{9,8},{10,11... | collective-permute-start | bytes 3538952 | tf_op jit(solution)/shard_map/ppermute | solution.py:42
  27.1 13.6 %all-to-all-start = ((bf16[16,16,768]{2,1,0:T(8,128)(2,1)}), bf16[16,16,768]{2,1,0:T(8,128)(2,1)S(1)}, u32[]{:S(2)}, u32[]{:S(2)}) async-start(bf16[16,16,768]{2,1,0:T(8,128)(2,1)} %broadcast_in_dim.6), calls=%async_computation | async-start | bytes 786432 | tf_op jit(solution)/shard_map/all_to_all | solution.py:72
  41.5 1.2 copy-start
  42.7 16.5 %copy-start.1 = (f32[2,2,64,1536]{3,2,1,0:T(8,128)S(1)}, f32[2,2,64,1536]{3,2,1,0:T(8,128)}, u32[]{:S(2)}) copy-start(f32[2,2,64,1536]{3,2,1,0:T(8,128)} %copy-done) | copy-start | bytes 4718596
  42.8 21.2 %collective-permute-start.3 = (bf16[1536,384]{1,0:T(8,128)(2,1)}, bf16[1536,384]{1,0:T(8,128)(2,1)}, u32[]{:S(2)}, u32[]{:S(2)}) collective-permute-start(bf16[1536,384]{1,0:T(8,128)(2,1)} %param.7), channel_id=1, source_target_pairs={{0,1},{1,0},{2,3},{3,2},{4,5},{5,4},{6,7},{7,6},{8,9},{9,8},{10,11... | collective-permute-start | bytes 3538952 | tf_op jit(solution)/shard_map/ppermute | solution.py:42
  46.5 12.7 %collective-permute-start.2 = (bf16[2,1,64,1536]{3,2,1,0:T(8,128)(2,1)S(1)}, bf16[2,1,64,1536]{3,2,1,0:T(8,128)(2,1)}, u32[]{:S(2)}, u32[]{:S(2)}) collective-permute-start(bf16[2,1,64,1536]{3,2,1,0:T(8,128)(2,1)S(1)} %dynamic-slice_convert_fusion), channel_id=1, source_target_pairs={{0,64},{64,0},{1,65},{65,1},{2,66},{66,2},{3,67},{67,3},{4,68},{68... | collective-permute-start | bytes 1179656 | tf_op jit(solution)/shard_map/ppermute | solution.py:42
  51.4 16.6 %all-to-all-start.1 = ((bf16[16,16,1536]{2,1,0:T(8,128)(2,1)}), bf16[16,16,1536]{2,1,0:T(8,128)(2,1)S(1)}, u32[]{:S(2)}, u32[]{:S(2)}) async-start(bf16[16,16,1536]{2,1,0:T(8,128)(2,1)} %broadcast_in_dim.7), calls=%async_computation.1 | async-start | bytes 1572864 | tf_op jit(solution)/shard_map/all_to_all | solution.py:72
  60.3 12.9 %collective-permute-start.6 = (bf16[1,1,64,1536]{3,2,1,0:T(8,128)(2,1)S(1)}, bf16[1,1,64,1536]{3,2,1,0:T(8,128)(2,1)S(1)}, u32[]{:S(2)}, u32[]{:S(2)}) collective-permute-start(bf16[1,1,64,1536]{3,2,1,0:T(8,128)(2,1)S(1)} %dynamic-slice_convert_fusion.1), channel_id=1, source_target_pairs={{0,128},{128,0},{1,129},{129,1},{2,130},{130,2},{3,131},{131,3},{4... | collective-permute-start | bytes 589832 | tf_op jit(solution)/shard_map/ppermute | solution.py:42
  68.0 9.3 %copy-start.2 = (bf16[16,16,1536]{2,1,0:T(8,128)(2,1)}, bf16[16,16,1536]{2,1,0:T(8,128)(2,1)S(1)}, u32[]{:S(2)}) copy-start(bf16[16,16,1536]{2,1,0:T(8,128)(2,1)S(1)} %all-to-all-done.1) | copy-start | bytes 2359300
  71.5 31.2 %copy-start.9 = (f32[1536]{0:T(1024)S(1)}, f32[1536]{0:T(1024)}, u32[]{:S(2)}) copy-start(f32[1536]{0:T(1024)} %param.8) | copy-start | bytes 18436
  73.2 20.9 %all-to-all-start.2 = ((bf16[4,64,768]{2,1,0:T(8,128)(2,1)}), bf16[4,64,768]{2,1,0:T(8,128)(2,1)}, u32[]{:S(2)}, u32[]{:S(2)}) async-start(bf16[4,64,768]{2,1,0:T(8,128)(2,1)} %bitcast.5), calls=%async_computation.2 | async-start | bytes 786432 | tf_op jit(solution)/shard_map/all_to_all | solution.py:78
  77.4 17.9 %collective-permute-start.4 = (bf16[256,1536]{1,0:T(8,128)(2,1)S(1)}, bf16[256,1536]{1,0:T(8,128)(2,1)}, u32[]{:S(2)}, u32[]{:S(2)}) collective-permute-start(bf16[256,1536]{1,0:T(8,128)(2,1)S(1)} %bitcast.42), channel_id=1, source_target_pairs={{0,1},{1,0},{2,3},{3,2},{4,5},{5,4},{6,7},{7,6},{8,9},{9,8},{10,11... | collective-permute-start | bytes 2359304 | tf_op jit(solution)/shard_map/ppermute | solution.py:42
  80.8 56.8 %copy-start.3 = (bf16[1536,768]{1,0:T(8,128)(2,1)S(1)}, bf16[1536,768]{1,0:T(8,128)(2,1)}, u32[]{:S(2)}) copy-start(bf16[1536,768]{1,0:T(8,128)(2,1)} %maximum_select_fusion.1) | copy-start | bytes 7077892
  80.8 12.7 %collective-permute-start.7 = (bf16[64,768]{1,0:T(8,128)(2,1)S(1)}, bf16[64,768]{1,0:T(8,128)(2,1)S(1)}, u32[]{:S(2)}, u32[]{:S(2)}) collective-permute-start(bf16[64,768]{1,0:T(8,128)(2,1)S(1)} %fusion.16), channel_id=1, source_target_pairs={{0,258},{2,256},{256,2},{258,0},{1,259},{3,257},{257,3},{259,1},{4... | collective-permute-start | bytes 294920 | tf_op jit(solution)/shard_map/ppermute | solution.py:66
  91.0 4.3 %collective-permute-start.5 = (bf16[256,384]{1,0:T(8,128)(2,1)}, bf16[256,384]{1,0:T(8,128)(2,1)}, u32[]{:S(2)}, u32[]{:S(2)}) collective-permute-start(bf16[256,384]{1,0:T(8,128)(2,1)} %constant_dynamic-slice_fusion.2), channel_id=1, source_target_pairs={{0,1},{1,0},{2,3},{3,2},{4,5},{5,4},{6,7},{7,6},{8,9},{9,8},{10,11... | collective-permute-start | bytes 589832 | tf_op jit(solution)/shard_map/ppermute | solution.py:42
  96.1 10.3 %collective-permute-start.8 = (bf16[64,1536]{1,0:T(8,128)(2,1)S(1)}, bf16[64,1536]{1,0:T(8,128)(2,1)S(1)}, u32[]{:S(2)}, u32[]{:S(2)}) collective-permute-start(bf16[64,1536]{1,0:T(8,128)(2,1)S(1)} %pad_maximum_fusion), channel_id=1, source_target_pairs={{0,256},{256,0},{1,257},{257,1},{2,258},{258,2},{3,259},{259,3},{4... | collective-permute-start | bytes 589832 | tf_op jit(solution)/shard_map/ppermute | solution.py:42
  107.6 31.7 %copy-start.5 = (bf16[64,768]{1,0:T(8,128)(2,1)}, bf16[64,768]{1,0:T(8,128)(2,1)S(1)}, u32[]{:S(2)}) copy-start(bf16[64,768]{1,0:T(8,128)(2,1)S(1)} %get-tuple-element.38) | copy-start | bytes 294916
  108.3 29.2 %all-to-all-start.3 = ((bf16[4,64,768]{2,1,0:T(8,128)(2,1)}), bf16[4,64,768]{2,1,0:T(8,128)(2,1)S(1)}, u32[]{:S(2)}, u32[]{:S(2)}) async-start(bf16[4,64,768]{2,1,0:T(8,128)(2,1)} %broadcast_in_dim.8), calls=%async_computation.3 | async-start | bytes 786432 | tf_op jit(solution)/shard_map/all_to_all | solution.py:72
  126.1 18.6 %collective-permute-start.9 = (bf16[64,768]{1,0:T(8,128)(2,1)S(1)}, bf16[64,768]{1,0:T(8,128)(2,1)S(1)}, u32[]{:S(2)}, u32[]{:S(2)}) collective-permute-start(bf16[64,768]{1,0:T(8,128)(2,1)S(1)} %get-tuple-element.38), channel_id=1, source_target_pairs={{0,258},{2,256},{256,2},{258,0},{1,259},{3,257},{257,3},{259,1},{4... | collective-permute-start | bytes 294920 | tf_op jit(solution)/shard_map/ppermute | solution.py:66
  137.6 7.1 %copy-start.4 = (bf16[4,64,768]{2,1,0:T(8,128)(2,1)}, bf16[4,64,768]{2,1,0:T(8,128)(2,1)S(1)}, u32[]{:S(2)}) copy-start(bf16[4,64,768]{2,1,0:T(8,128)(2,1)S(1)} %all-to-all-done.3) | copy-start | bytes 1179652
  140.0 14.1 %copy-start.6 = (bf16[64,768]{1,0:T(8,128)(2,1)S(1)}, bf16[64,768]{1,0:T(8,128)(2,1)}, u32[]{:S(2)}) copy-start(bf16[64,768]{1,0:T(8,128)(2,1)} %copy-done.5) | copy-start | bytes 294916
  144.7 0.6 copy-start.7
  145.3 31.9 %all-to-all-start.4 = ((bf16[16,16,1536]{2,1,0:T(8,128)(2,1)}), bf16[16,16,1536]{2,1,0:T(8,128)(2,1)S(1)}, u32[]{:S(2)}, u32[]{:S(2)}) async-start(bf16[16,16,1536]{2,1,0:T(8,128)(2,1)} %bitcast.51), calls=%async_computation.4 | async-start | bytes 1572864 | tf_op jit(solution)/shard_map/all_to_all | solution.py:127
  151.0 7.6 %collective-permute-start.10 = (bf16[1,1,64,1536]{3,2,1,0:T(8,128)(2,1)S(1)}, bf16[1,1,64,1536]{3,2,1,0:T(8,128)(2,1)S(1)}, u32[]{:S(2)}, u32[]{:S(2)}) collective-permute-start(bf16[1,1,64,1536]{3,2,1,0:T(8,128)(2,1)S(1)} %maximum_select_fusion.5), channel_id=1, source_target_pairs={{0,128},{128,0},{1,129},{129,1},{2,130},{130,2},{3,131},{131,3},{4... | collective-permute-start | bytes 589832 | tf_op jit(solution)/shard_map/ppermute | solution.py:42
  161.2 11.7 %collective-permute-start.11 = (bf16[256,384]{1,0:T(8,128)(2,1)}, bf16[256,384]{1,0:T(8,128)(2,1)}, u32[]{:S(2)}, u32[]{:S(2)}) collective-permute-start(bf16[256,384]{1,0:T(8,128)(2,1)} %constant_dynamic-slice_fusion), channel_id=1, source_target_pairs={{0,1},{1,0},{2,3},{3,2},{4,5},{5,4},{6,7},{7,6},{8,9},{9,8},{10,11... | collective-permute-start | bytes 589832 | tf_op jit(solution)/shard_map/ppermute | solution.py:42
  168.6 14.1 %collective-permute-start.12 = (bf16[2,1,64,1536]{3,2,1,0:T(8,128)(2,1)}, bf16[2,1,64,1536]{3,2,1,0:T(8,128)(2,1)}, u32[]{:S(2)}, u32[]{:S(2)}) collective-permute-start(bf16[2,1,64,1536]{3,2,1,0:T(8,128)(2,1)} %maximum_select_fusion.3), channel_id=1, source_target_pairs={{0,64},{64,0},{1,65},{65,1},{2,66},{66,2},{3,67},{67,3},{4,68},{68... | collective-permute-start | bytes 1179656 | tf_op jit(solution)/shard_map/ppermute | solution.py:42
  184.2 13.2 %collective-permute-start.13 = (bf16[256,1536]{1,0:T(8,128)(2,1)S(1)}, bf16[256,1536]{1,0:T(8,128)(2,1)S(1)}, u32[]{:S(2)}, u32[]{:S(2)}) collective-permute-start(bf16[256,1536]{1,0:T(8,128)(2,1)S(1)} %bitcast.44), channel_id=1, source_target_pairs={{0,1},{1,0},{2,3},{3,2},{4,5},{5,4},{6,7},{7,6},{8,9},{9,8},{10,11... | collective-permute-start | bytes 2359304 | tf_op jit(solution)/shard_map/ppermute | solution.py:42
  186.7 13.4 %collective-permute-start.14 = (bf16[8,1536]{1,0:T(8,128)(2,1)S(1)}, bf16[8,1536]{1,0:T(8,128)(2,1)S(1)}, u32[]{:S(2)}, u32[]{:S(2)}) collective-permute-start(bf16[8,1536]{1,0:T(8,128)(2,1)S(1)} %dynamic-slice_convert_fusion.3), channel_id=1, source_target_pairs={{0,2},{2,0},{1,3},{3,1},{4,6},{6,4},{5,7},{7,5},{8,10},{10,8},{9,1... | collective-permute-start | bytes 73736 | tf_op jit(solution)/shard_map/ppermute | solution.py:42
